TPU v7x, 128 devices: a whole 4x4x4 slice. The times are simulated.
128 devices in a mesh: gx: 8 (over x, z_lo), gy: 16 (over y, z_hi, core).
Axes of the slice: x: 4, y: 4, z: 4 (z_hi: 2, z_lo: 2; z = z_hi * 2 + z_lo), core: 2. Of those that a mesh axis runs over, the one named last changes fastest.
Arguments:
- images: bfloat16 [64, 2, 1024, 1024], P('gy', None, 'gx'), may hold values from -192 to 192
- rates: float32 [256], replicated, may hold values from 0.002 to 0.2
- smoothing: float32 [256], replicated, may hold values from 0.02 to 1
Outputs:
- spectra: float32 [2, 1024, 1024, 256], P(None, 'gx', 'gy')
All inputs are finite; a program needn't handle non-finite values.
Results may differ from a plain program's by a relative error of at most 0.0033.
Values may be sent and summed in bfloat16 or wider, within the bound.
A program may use at most 192 MiB of HBM per device.

v0:
```python
import jax
import jax.numpy as jnp
from jax import lax
from jax.sharding import PartitionSpec as P

E = 64
ITERS = 3


def padded_2(cells, sides, width):
    for axis, dim in sides:
        count = lax.axis_size(axis)
        ends = count - 1
        head = lax.slice_in_dim(cells, 0, width, axis=dim)
        tail = lax.slice_in_dim(cells, cells.shape[dim] - width, cells.shape[dim], axis=dim)
        cells = jnp.concatenate(
            [
                lax.ppermute(tail, axis, [(i, (i + 1) % count) for i in range(ends)]),
                cells,
                lax.ppermute(head, axis, [((i + 1) % count, i) for i in range(ends)]),
            ],
            axis=dim,
        )
    return cells


def kernel_parts(rates, smoothing):
    times = 10.0 * (jnp.arange(E, dtype=jnp.float32) + 1.0)
    raw = jnp.exp(-times[:, None] * rates[None, :])
    kernel = raw / jnp.sqrt(jnp.sum(raw * raw, axis=0))[None, :]
    gram = jnp.dot(kernel.T, kernel, precision=lax.Precision.HIGHEST)
    rowsum = jnp.sum(gram, axis=1)
    lam = smoothing * rowsum
    step = 1.0 / (rowsum + 8.0 * lam)
    return (kernel, gram, lam, step)


def project(piece, kernel_b):
    return jnp.einsum("esij,er->sijr", piece, kernel_b, preferred_element_type=jnp.float32)


def laplace(padded):
    center = padded[:, 1:-1, 1:-1]
    return (
        4.0 * center
        - padded[:, 2:, 1:-1]
        - padded[:, :-2, 1:-1]
        - padded[:, 1:-1, 2:]
        - padded[:, 1:-1, :-2]
    )


def curvature(field, gram):
    shape = field.shape
    flat = field.reshape(-1, shape[-1])
    result = jnp.dot(flat, gram, precision=lax.Precision.HIGHEST)
    return result.reshape(shape)


def per_device(images, rates, smoothing):
    kernel, gram, lam, step = kernel_parts(rates, smoothing)
    kernel_b = kernel.astype(jnp.bfloat16)
    proj = project(lax.all_to_all(images, "gy", split_axis=3, concat_axis=0, tiled=True), kernel_b)
    field = jnp.maximum(proj * step, 0.0)
    for count in range(ITERS - 1):
        padded = padded_2(field.astype(jnp.bfloat16), (("gx", 1), ("gy", 2)), 1).astype(field.dtype)
        grad = curvature(field, gram) - proj + lam * laplace(padded)
        field = jnp.maximum(field - step * grad, 0.0)
    return field


def solution(mesh):
    in_specs = (P("gy", None, "gx", None), P(), P())
    out_specs = P(None, "gx", "gy", None)
    return jax.shard_map(
        per_device, mesh=mesh, in_specs=in_specs, out_specs=out_specs, check_vma=False
    )
```

profile of v0, /device:TPU:1, one launch (start us, length us, event | category | flops | bytes accessed | tf_op | source)
XLA Modules:
  0.0 251.0 jit_solution(17120506668764002705)
XLA Ops:
  0.0 0.0 copy-start
  0.0 6.2 %copy.13 = bf16[4,2,128,1024]{2,1,0,3:T(2,128)(2,1)} copy(bf16[4,2,128,1024]{3,2,1,0:T(8,128)(2,1)} %param.3) | data formatting | bytes 4194304 | tf_op args[0]
  6.2 9.3 %all-to-all-start = ((bf16[4,2,128,1024]{2,1,0,3:T(2,128)(2,1)}), bf16[4,2,128,1024]{2,1,0,3:T(2,128)(2,1)S(1)}, u32[]{:S(2)}, u32[]{:S(2)}) async-start(bf16[4,2,128,1024]{2,1,0,3:T(2,128)(2,1)} %copy.13), calls=%async_computation | async-start | bytes 4194304 | tf_op jit(solution)/shard_map/all_to_all | solution.py:63
  15.5 0.8 multiply_reduce_fusion
  16.3 1.3 fusion.36
  17.5 0.7 add_divide_fusion
  18.2 25.7 %all-to-all-done = bf16[4,2,128,1024]{2,1,0,3:T(2,128)(2,1)S(1)} async-done(((bf16[4,2,128,1024]{2,1,0,3:T(2,128)(2,1)}), bf16[4,2,128,1024]{2,1,0,3:T(2,128)(2,1)S(1)}, u32[]{:S(2)}, u32[]{:S(2)}) %all-to-all-start) | async-done | bytes 2097184 | tf_op jit(solution)/shard_map/all_to_all | solution.py:63
  43.9 0.3 copy.14
  44.2 1.6 copy.15
  45.8 0.0 copy-done
  45.8 7.5 %fusion.11 = (bf16[2,128,64,256]{3,1,2,0:T(8,128)(2,1)S(1)}, f32[256,2,128,64]{0,2,3,1:T(8,128)}) fusion(f32[256]{0:T(256)S(1)} %get-tuple-element.5, bf16[64,2,128,64]{2,0,3,1:T(8,128)(2,1)S(1)} %bitcast.43, f32[256]{0:T(256)S(1)} %sqrt.7, f32[256]{0:T(256)S(1)} %copy-done, f32[64]{0:T(128)S(1)} %multiply_negate_fusion), kind=kOutput, calls=%fused_computation.24 | convolution fusion | flops 549502976 | bytes 27266304 | tf_op jit(solution)/shard_map/esij,er->sijr/dot_general | solution.py:39
  53.3 0.2 fusion.35
  53.5 2.6 %collective-permute-start = (bf16[2,1,64,256]{3,1,2,0:T(2,128)(2,1)S(1)}, bf16[2,1,64,256]{3,1,2,0:T(2,128)(2,1)S(1)}, u32[]{:S(2)}, u32[]{:S(2)}) collective-permute-start(bf16[2,1,64,256]{3,1,2,0:T(2,128)(2,1)S(1)} %get-tuple-element.13), channel_id=1, source_target_pairs={{0,16},{16,32},{32,48},{48,64},{64,80},{80,96},{96,112},{1,17},{17... | collective-permute-start | bytes 196616 | tf_op jit(solution)/shard_map/ppermute | solution.py:18
  56.2 1.3 collective-permute-start.1
  57.5 0.6 collective-permute-done
  58.1 4.0 %collective-permute-done.1 = bf16[2,1,64,256]{3,1,2,0:T(2,128)(2,1)S(1)} collective-permute-done((bf16[2,1,64,256]{3,1,2,0:T(2,128)(2,1)S(1)}, bf16[2,1,64,256]{3,1,2,0:T(2,128)(2,1)S(1)}, u32[]{:S(2)}, u32[]{:S(2)}) %collective-permute-start.1) | collective-permute-done | bytes 65568 | tf_op jit(solution)/shard_map/ppermute | solution.py:20
  62.1 0.1 pad_maximum_fusion.5
  62.2 7.4 %collective-permute-start.2 = (bf16[2,130,1,256]{3,1,2,0:T(8,128)(2,1)S(1)}, bf16[2,130,1,256]{3,1,2,0:T(8,128)(2,1)S(1)}, u32[]{:S(2)}, u32[]{:S(2)}) collective-permute-start(bf16[2,130,1,256]{3,1,2,0:T(8,128)(2,1)S(1)} %get-tuple-element.9), channel_id=1, source_target_pairs={{0,1},{1,2},{2,3},{3,4},{4,5},{5,6},{6,7},{7,8},{8,9},{9,10},{10,1... | collective-permute-start | bytes 399368 | tf_op jit(solution)/shard_map/ppermute | solution.py:18
  69.5 1.9 collective-permute-start.3
  71.5 0.1 collective-permute-done.2
  71.5 5.9 %collective-permute-done.3 = bf16[2,130,1,256]{3,1,2,0:T(8,128)(2,1)S(1)} collective-permute-done((bf16[2,130,1,256]{3,1,2,0:T(8,128)(2,1)S(1)}, bf16[2,130,1,256]{3,1,2,0:T(8,128)(2,1)S(1)}, u32[]{:S(2)}, u32[]{:S(2)}) %collective-permute-start.3) | collective-permute-done | bytes 133152 | tf_op jit(solution)/shard_map/ppermute | solution.py:20
  77.4 7.9 %maximum_convert_fusion = f32[2,130,66,256]{3,1,2,0:T(8,128)} fusion(bf16[2,130,1,256]{3,1,2,0:T(8,128)(2,1)S(1)} %collective-permute-done.3, bf16[2,1,64,256]{3,1,2,0:T(2,128)(2,1)S(1)} %collective-permute-done.1, bf16[2,128,64,256]{3,1,2,0:T(8,128)(2,1)S(1)} %get-tuple-element.17, bf16[2,1,64,256]{3,1,2,0:T(2,128)(2,1)S(1)} %collective-permute-done, ...), kind=kLoop, calls=%fused_computation.26 | loop fusion | flops 43929600 | bytes 26357760 | tf_op jit(solution)/shard_map/convert_element_type | solution.py:66
  85.4 58.4 %fusion.37 = (bf16[2,128,64,256]{3,1,2,0:T(8,128)(2,1)}, f32[2,128,64,256]{3,1,2,0:T(8,128)}) fusion(f32[2,130,66,256]{3,1,2,0:T(8,128)} %maximum_convert_fusion, f32[256]{0:T(256)S(1)} %get-tuple-element.6, f32[256,256]{0,1:T(8,128)S(1)} %get-tuple-element.16, f32[256,2,128,64]{0,2,3,1:T(8,128)} %get-tuple-element.18, f32[256]{0:T(256)S(1)} %get-tuple-element.5), kind=kOutput, calls=%fused_computation.57 | convolution fusion | flops 12952010752 | bytes 142871552 | tf_op jit(solution)/shard_map/dot_general | solution.py:56
  143.8 1.4 fusion.34
  145.2 3.3 %collective-permute-start.4 = (bf16[2,1,64,256]{3,1,2,0:T(2,128)(2,1)S(1)}, bf16[2,1,64,256]{3,1,2,0:T(2,128)(2,1)S(1)}, u32[]{:S(2)}, u32[]{:S(2)}) collective-permute-start(bf16[2,1,64,256]{3,1,2,0:T(2,128)(2,1)S(1)} %get-tuple-element.11), channel_id=1, source_target_pairs={{0,16},{16,32},{32,48},{48,64},{64,80},{80,96},{96,112},{1,17},{17... | collective-permute-start | bytes 196616 | tf_op jit(solution)/shard_map/ppermute | solution.py:18
  148.4 1.3 collective-permute-start.5
  149.7 2.0 collective-permute-done.4
  151.7 2.5 collective-permute-done.5
  154.2 1.0 pad_maximum_fusion.2
  155.2 4.5 %collective-permute-start.6 = (bf16[2,130,1,256]{3,1,2,0:T(8,128)(2,1)S(1)}, bf16[2,130,1,256]{3,1,2,0:T(8,128)(2,1)S(1)}, u32[]{:S(2)}, u32[]{:S(2)}) collective-permute-start(bf16[2,130,1,256]{3,1,2,0:T(8,128)(2,1)S(1)} %get-tuple-element.7), channel_id=1, source_target_pairs={{0,1},{1,2},{2,3},{3,4},{4,5},{5,6},{6,7},{7,8},{8,9},{9,10},{10,1... | collective-permute-start | bytes 399368 | tf_op jit(solution)/shard_map/ppermute | solution.py:18
  159.8 2.1 collective-permute-start.7
  161.9 0.0 collective-permute-done.6
  161.9 5.8 %collective-permute-done.7 = bf16[2,130,1,256]{3,1,2,0:T(8,128)(2,1)S(1)} collective-permute-done((bf16[2,130,1,256]{3,1,2,0:T(8,128)(2,1)S(1)}, bf16[2,130,1,256]{3,1,2,0:T(8,128)(2,1)S(1)}, u32[]{:S(2)}, u32[]{:S(2)}) %collective-permute-start.7) | collective-permute-done | bytes 133152 | tf_op jit(solution)/shard_map/ppermute | solution.py:20
  167.7 11.4 %maximum_convert_fusion.1 = f32[2,130,66,256]{3,1,2,0:T(8,128)} fusion(bf16[2,130,1,256]{3,1,2,0:T(8,128)(2,1)S(1)} %collective-permute-done.7, bf16[2,1,64,256]{3,1,2,0:T(2,128)(2,1)S(1)} %collective-permute-done.5, bf16[2,128,64,256]{3,1,2,0:T(8,128)(2,1)} %get-tuple-element.19, bf16[2,1,64,256]{3,1,2,0:T(2,128)(2,1)S(1)} %collective-permute-done.4, ...), kind=kLoop, calls=%fused_computation.27 | loop fusion | flops 43929600 | bytes 26357760 | tf_op jit(solution)/shard_map/convert_element_type | solution.py:66
  179.0 54.1 %fusion.4 = f32[2,128,64,256]{3,1,2,0:T(8,128)} fusion(f32[2,128,64,256]{3,1,2,0:T(8,128)} %get-tuple-element.20, f32[2,130,66,256]{3,1,2,0:T(8,128)} %maximum_convert_fusion.1, f32[256,2,128,64]{0,2,3,1:T(8,128)} %get-tuple-element.18, f32[256]{0:T(256)S(1)} %get-tuple-element.6, f32[256]{0:T(256)S(1)} %get-tuple-element.5, ...), kind=kOutput, calls=%fused_computation.5 | convolution fusion | flops 12931039232 | bytes 151259136 | tf_op jit(solution)/shard_map/dot_general | solution.py:56
  233.2 17.8 %copy.18 = f32[2,128,64,256]{3,2,1,0:T(8,128)} copy(f32[2,128,64,256]{3,1,2,0:T(8,128)} %fusion.4) | data formatting | bytes 33554432 | tf_op jit(solution)/shard_map/max | solution.py:68
  (2 shorter events, 0.0 us)
Async XLA Ops:
  0.0 45.8 %copy-start = (f32[256]{0:T(256)S(1)}, f32[256]{0:T(256)}, u32[]{:S(2)}) copy-start(f32[256]{0:T(256)} %param.4) | copy-start | bytes 3076
  6.2 37.7 %all-to-all-start = ((bf16[4,2,128,1024]{2,1,0,3:T(2,128)(2,1)}), bf16[4,2,128,1024]{2,1,0,3:T(2,128)(2,1)S(1)}, u32[]{:S(2)}, u32[]{:S(2)}) async-start(bf16[4,2,128,1024]{2,1,0,3:T(2,128)(2,1)} %copy.13), calls=%async_computation | async-start | bytes 4194304 | tf_op jit(solution)/shard_map/all_to_all | solution.py:63
  53.5 4.6 %collective-permute-start = (bf16[2,1,64,256]{3,1,2,0:T(2,128)(2,1)S(1)}, bf16[2,1,64,256]{3,1,2,0:T(2,128)(2,1)S(1)}, u32[]{:S(2)}, u32[]{:S(2)}) collective-permute-start(bf16[2,1,64,256]{3,1,2,0:T(2,128)(2,1)S(1)} %get-tuple-element.13), channel_id=1, source_target_pairs={{0,16},{16,32},{32,48},{48,64},{64,80},{80,96},{96,112},{1,17},{17... | collective-permute-start | bytes 196616 | tf_op jit(solution)/shard_map/ppermute | solution.py:18
  56.2 5.9 %collective-permute-start.1 = (bf16[2,1,64,256]{3,1,2,0:T(2,128)(2,1)S(1)}, bf16[2,1,64,256]{3,1,2,0:T(2,128)(2,1)S(1)}, u32[]{:S(2)}, u32[]{:S(2)}) collective-permute-start(bf16[2,1,64,256]{3,1,2,0:T(2,128)(2,1)S(1)} %get-tuple-element.14), channel_id=1, source_target_pairs={{16,0},{32,16},{48,32},{64,48},{80,64},{96,80},{112,96},{17,1},{33... | collective-permute-start | bytes 196616 | tf_op jit(solution)/shard_map/ppermute | solution.py:20
  62.2 9.4 %collective-permute-start.2 = (bf16[2,130,1,256]{3,1,2,0:T(8,128)(2,1)S(1)}, bf16[2,130,1,256]{3,1,2,0:T(8,128)(2,1)S(1)}, u32[]{:S(2)}, u32[]{:S(2)}) collective-permute-start(bf16[2,130,1,256]{3,1,2,0:T(8,128)(2,1)S(1)} %get-tuple-element.9), channel_id=1, source_target_pairs={{0,1},{1,2},{2,3},{3,4},{4,5},{5,6},{6,7},{7,8},{8,9},{9,10},{10,1... | collective-permute-start | bytes 399368 | tf_op jit(solution)/shard_map/ppermute | solution.py:18
  69.5 7.9 %collective-permute-start.3 = (bf16[2,130,1,256]{3,1,2,0:T(8,128)(2,1)S(1)}, bf16[2,130,1,256]{3,1,2,0:T(8,128)(2,1)S(1)}, u32[]{:S(2)}, u32[]{:S(2)}) collective-permute-start(bf16[2,130,1,256]{3,1,2,0:T(8,128)(2,1)S(1)} %get-tuple-element.10), channel_id=1, source_target_pairs={{1,0},{2,1},{3,2},{4,3},{5,4},{6,5},{7,6},{8,7},{9,8},{10,9},{11,1... | collective-permute-start | bytes 399368 | tf_op jit(solution)/shard_map/ppermute | solution.py:20
  145.2 6.6 %collective-permute-start.4 = (bf16[2,1,64,256]{3,1,2,0:T(2,128)(2,1)S(1)}, bf16[2,1,64,256]{3,1,2,0:T(2,128)(2,1)S(1)}, u32[]{:S(2)}, u32[]{:S(2)}) collective-permute-start(bf16[2,1,64,256]{3,1,2,0:T(2,128)(2,1)S(1)} %get-tuple-element.11), channel_id=1, source_target_pairs={{0,16},{16,32},{32,48},{48,64},{64,80},{80,96},{96,112},{1,17},{17... | collective-permute-start | bytes 196616 | tf_op jit(solution)/shard_map/ppermute | solution.py:18
  148.4 5.8 %collective-permute-start.5 = (bf16[2,1,64,256]{3,1,2,0:T(2,128)(2,1)S(1)}, bf16[2,1,64,256]{3,1,2,0:T(2,128)(2,1)S(1)}, u32[]{:S(2)}, u32[]{:S(2)}) collective-permute-start(bf16[2,1,64,256]{3,1,2,0:T(2,128)(2,1)S(1)} %get-tuple-element.12), channel_id=1, source_target_pairs={{16,0},{32,16},{48,32},{64,48},{80,64},{96,80},{112,96},{17,1},{33... | collective-permute-start | bytes 196616 | tf_op jit(solution)/shard_map/ppermute | solution.py:20
  155.2 6.6 %collective-permute-start.6 = (bf16[2,130,1,256]{3,1,2,0:T(8,128)(2,1)S(1)}, bf16[2,130,1,256]{3,1,2,0:T(8,128)(2,1)S(1)}, u32[]{:S(2)}, u32[]{:S(2)}) collective-permute-start(bf16[2,130,1,256]{3,1,2,0:T(8,128)(2,1)S(1)} %get-tuple-element.7), channel_id=1, source_target_pairs={{0,1},{1,2},{2,3},{3,4},{4,5},{5,6},{6,7},{7,8},{8,9},{9,10},{10,1... | collective-permute-start | bytes 399368 | tf_op jit(solution)/shard_map/ppermute | solution.py:18
  159.8 7.9 %collective-permute-start.7 = (bf16[2,130,1,256]{3,1,2,0:T(8,128)(2,1)S(1)}, bf16[2,130,1,256]{3,1,2,0:T(8,128)(2,1)S(1)}, u32[]{:S(2)}, u32[]{:S(2)}) collective-permute-start(bf16[2,130,1,256]{3,1,2,0:T(8,128)(2,1)S(1)} %get-tuple-element.8), channel_id=1, source_target_pairs={{1,0},{2,1},{3,2},{4,3},{5,4},{6,5},{7,6},{8,7},{9,8},{10,9},{11,1... | collective-permute-start | bytes 399368 | tf_op jit(solution)/shard_map/ppermute | solution.py:20
where the time goes:
time: 252 us; the launch traced here: 251 us
  matrix products  121 us (48%)
  waiting for transfers between devices  46.5 us (18%)
  starting transfers between devices  33.7 us (13%)
  local copies, waits for them, and re-layouts  27.5 us (11%)
  other arithmetic  21.9 us (9%)
    dot_general x2, matrix products, curvature(): result = jnp.dot(flat, gram, precision=lax.Precision.HIGHEST)  113 us
    all_to_all x1, waiting for transfers between devices, per_device(): lax.all_to_all(images, 'gy', split_axis=3, concat_axis=0, tiled=True)  25.7 us
    convert_element_type x2, other arithmetic, per_device(): padded_2(field.astype(jnp.bfloat16), (('gx', 1), ('gy', 2)), 1)  19.3 us
    ppermute x4, waiting for transfers between devices, padded_2(): lax.ppermute(head, axis, [((i + 1) % count, i) for i in range(ends)])  18.1 us
    max x1, local copies, waits for them, and re-layouts, per_device(): field = jnp.maximum(field - step * grad, 0.0)  17.8 us
    ppermute x4, starting transfers between devices, padded_2(): lax.ppermute(tail, axis, [(i, (i + 1) % count) for i in range(ends)])  17.8 us
    all_to_all x1, starting transfers between devices, per_device(): lax.all_to_all(images, 'gy', split_axis=3, concat_axis=0, tiled=True)  9.3 us
    dot_general x1, matrix products, project(): jnp.einsum('esij,er->sijr', piece, kernel_b, preferred_element_type=jnp.f...  7.49 us
  transfers between devices with their start and end apart: 9, of which 8 were waited for; matrix products, arithmetic and copies ran while one was open for 1% of the time, Pallas kernels for 0%

commit v1 on v0

v1 whole, which is shorter than its diff:
```python
import functools

import jax
import jax.numpy as jnp
from jax import lax
from jax.experimental import pallas as pl
from jax.experimental.pallas import tpu as pltpu
from jax.sharding import PartitionSpec as P

E = 64
ITERS = 3
RH = 2
CH = 4
TR = 16


def kernel_parts(rates, smoothing):
    times = 10.0 * (jnp.arange(E, dtype=jnp.float32) + 1.0)
    raw = jnp.exp(-times[:, None] * rates[None, :])
    kernel = raw / jnp.sqrt(jnp.sum(raw * raw, axis=0))[None, :]
    gram = jnp.dot(kernel.T, kernel, precision=lax.Precision.HIGHEST)
    rowsum = jnp.sum(gram, axis=1)
    lam = smoothing * rowsum
    step = 1.0 / (rowsum + 8.0 * lam)
    return (kernel, gram, lam, step)


def halo(cells, axis, dim, width):
    count = lax.axis_size(axis)
    head = lax.slice_in_dim(cells, 0, width, axis=dim)
    tail = lax.slice_in_dim(cells, cells.shape[dim] - width, cells.shape[dim], axis=dim)
    return jnp.concatenate(
        [
            lax.ppermute(tail, axis, [(i, i + 1) for i in range(count - 1)]),
            cells,
            lax.ppermute(head, axis, [(i + 1, i) for i in range(count - 1)]),
        ],
        axis=dim,
    )


def split3(f):
    hi = f.astype(jnp.bfloat16)
    lo = (f - hi.astype(jnp.float32)).astype(jnp.bfloat16)
    return jnp.concatenate([hi, lo, hi], axis=1)


def fit_kernel(wp, x_ref, kb_ref, g3_ref, step_ref, lam_ref, cm_ref, rm_ref,
               o_ref, b_ref, f0_ref, f1_ref, f3_ref, m_ref):
    t = pl.program_id(1)
    rows = TR + 2 * RH
    n = rows * wp
    base = pl.multiple_of(t * (TR * wp), 16)
    step = step_ref[...]
    lam = lam_ref[...]
    cm = cm_ref[...]

    b = jnp.dot(x_ref[0, pl.ds(base, n), :], kb_ref[...],
                preferred_element_type=jnp.float32)
    b_ref[...] = b
    f0 = jnp.maximum(b * step, 0.0)
    f0_ref[...] = f0
    f3_ref[...] = split3(f0)

    def update(src_ref, q):
        o = pl.multiple_of(q * wp, 8)
        c = src_ref[pl.ds(o, wp), :]
        up = src_ref[pl.ds(o - wp, wp), :]
        dn = src_ref[pl.ds(o + wp, wp), :]
        lf = pltpu.roll(c, 1, 0)
        rt = pltpu.roll(c, wp - 1, 0)
        lap = 4.0 * c - up - dn - lf - rt
        m = m_ref[pl.ds(o - wp, wp), :]
        g = m - b_ref[pl.ds(o, wp), :] + lam * lap
        return jnp.maximum(c - step * g, 0.0)

    m_ref[...] = jnp.dot(f3_ref[pl.ds(wp, (rows - 2) * wp), :], g3_ref[...],
                         preferred_element_type=jnp.float32)

    def body1(q, carry):
        f1 = update(f0_ref, q) * (cm * rm_ref[t * TR + q])
        f1_ref[pl.ds(pl.multiple_of(q * wp, 8), wp), :] = f1
        return carry

    lax.fori_loop(1, rows - 1, body1, 0)
    f1_ref[pl.ds(0, wp), :] = jnp.zeros((wp, f1_ref.shape[1]), jnp.float32)
    f1_ref[pl.ds((rows - 1) * wp, wp), :] = jnp.zeros((wp, f1_ref.shape[1]), jnp.float32)

    f3_ref[...] = split3(f1_ref[...])
    m_ref[...] = jnp.dot(f3_ref[pl.ds(wp, (rows - 2) * wp), :], g3_ref[...],
                         preferred_element_type=jnp.float32)

    def body2(q, carry):
        f2 = update(f1_ref, q)
        f2 = pltpu.roll(f2, wp - CH, 0)
        o_ref[0, q - RH] = f2[: wp - 2 * CH]
        return carry

    lax.fori_loop(RH, rows - RH, body2, 0)


def per_device(images, rates, smoothing):
    kernel, gram, lam, step = kernel_parts(rates, smoothing)
    kb = kernel.astype(jnp.bfloat16)
    gh = gram.astype(jnp.bfloat16)
    gl = (gram - gh.astype(jnp.float32)).astype(jnp.bfloat16)
    g3 = jnp.concatenate([gh, gh, gl], axis=0)
    x = lax.all_to_all(images, "gy", split_axis=3, concat_axis=0, tiled=True)
    e, sl, h, w = x.shape
    x = halo(x, "gy", 3, CH)
    x = halo(x, "gx", 2, RH)
    hp, wp = h + 2 * RH, w + 2 * CH
    x = jnp.transpose(x, (1, 2, 3, 0)).reshape(sl, hp * wp, e)
    r = kernel.shape[1]

    gi = lax.axis_index("gx")
    gj = lax.axis_index("gy")
    grow = gi * h + jnp.arange(hp) - RH
    rm = ((grow >= 0) & (grow < h * lax.axis_size("gx"))).astype(jnp.float32)
    gcol = gj * w + jnp.arange(wp) - CH
    cv = ((gcol >= 0) & (gcol < w * lax.axis_size("gy"))).astype(jnp.float32)
    cm = jnp.broadcast_to(cv[:, None], (wp, r))

    rows = TR + 2 * RH
    nt = h // TR
    flops = 2 * sl * nt * rows * wp * r * (e + 2 * 3 * r)
    out = pl.pallas_call(
        functools.partial(fit_kernel, wp),
        out_shape=jax.ShapeDtypeStruct((sl, h, w, r), jnp.float32),
        grid=(sl, nt),
        in_specs=[
            pl.BlockSpec((1, hp * wp, e), lambda s, t: (s, 0, 0)),
            pl.BlockSpec((e, r), lambda s, t: (0, 0)),
            pl.BlockSpec((3 * r, r), lambda s, t: (0, 0)),
            pl.BlockSpec((1, r), lambda s, t: (0, 0)),
            pl.BlockSpec((1, r), lambda s, t: (0, 0)),
            pl.BlockSpec((wp, r), lambda s, t: (0, 0)),
            pl.BlockSpec(memory_space=pltpu.SMEM),
        ],
        out_specs=pl.BlockSpec((1, TR, w, r), lambda s, t: (s, t, 0, 0)),
        scratch_shapes=[
            pltpu.VMEM((rows * wp, r), jnp.float32),
            pltpu.VMEM((rows * wp, r), jnp.float32),
            pltpu.VMEM((rows * wp, r), jnp.float32),
            pltpu.VMEM((rows * wp, 3 * r), jnp.bfloat16),
            pltpu.VMEM(((rows - 2) * wp, r), jnp.float32),
        ],
        compiler_params=pltpu.CompilerParams(
            dimension_semantics=("arbitrary", "arbitrary"),
            vmem_limit_bytes=48 * 1024 * 1024,
        ),
        cost_estimate=pl.CostEstimate(
            flops=flops, transcendentals=0,
            bytes_accessed=sl * (hp * wp * e * 2 + h * w * r * 4),
        ),
    )(x, kb, g3, step[None, :], lam[None, :], cm, rm)
    return out


def solution(mesh):
    in_specs = (P("gy", None, "gx", None), P(), P())
    out_specs = P(None, "gx", "gy", None)
    return jax.shard_map(
        per_device, mesh=mesh, in_specs=in_specs, out_specs=out_specs, check_vma=False
    )
```

time: 252 us -> 176 us (0.70)
  matrix products: 121 us -> 0.58 us
  Pallas kernels: 0 us -> 73.2 us
  starting transfers between devices: 33.7 us -> 21.6 us
  waiting for transfers between devices: 46.5 us -> 34.7 us
  other arithmetic: 21.9 us -> 11.3 us
  local copies, waits for them, and re-layouts: 27.5 us -> 31.9 us
    dot_general x3 -> x0, matrix products: 120 us -> none  [the longest x2 113 us: curvature(): result = jnp.dot(flat, gram, precision=lax.Precision.HIGHEST)]
    pallas_call x0 -> x1, Pallas kernels: none -> 73.2 us  [per_device(): pl.pallas_call(functools.partial(fit_kernel, wp), out_shape=jax.ShapeDtyp...]
    convert_element_type x2 -> x3, other arithmetic: 19.3 us -> 0.1 us  [the longest x1 0.09 us: per_device(): kb = kernel.astype(jnp.bfloat16)]
    max x1 -> x0, local copies, waits for them, and re-layouts: 17.8 us -> none  [per_device(): field = jnp.maximum(field - step * grad, 0.0)]
    ppermute x8 -> x4, waiting for transfers between devices: 20.8 us -> 7.1 us  [the longest x2 5.8 us: halo(): lax.ppermute(head, axis, [(i + 1, i) for i in range(count - 1)])]
    ppermute x8 -> x4, starting transfers between devices: 24.4 us -> 12.3 us  [the longest x2 9.06 us: halo(): lax.ppermute(tail, axis, [(i, i + 1) for i in range(count - 1)])]
    transpose x0 -> x1, local copies, waits for them, and re-layouts: none -> 11 us  [per_device(): x = jnp.transpose(x, (1, 2, 3, 0)).reshape(sl, hp * wp, e)]
    transpose x0 -> x1, other arithmetic: none -> 9.52 us  [per_device(): x = jnp.transpose(x, (1, 2, 3, 0)).reshape(sl, hp * wp, e)]
  transfers between devices with their start and end apart: 9 -> 5, of which waited for: 8 -> 3; matrix products, arithmetic and copies ran while one was open for 1% -> 2% of each run, Pallas kernels for 0% -> 0%
where the time goes in v1:
time: 176 us; the launch traced here: 173 us
  Pallas kernels  73.2 us (42%)
  waiting for transfers between devices  34.7 us (20%)
  local copies, waits for them, and re-layouts  31.9 us (18%)
  starting transfers between devices  21.6 us (12%)
  other arithmetic  11.3 us (6%)
    pallas_call x1, Pallas kernels, per_device(): pl.pallas_call(functools.partial(fit_kernel, wp), out_shape=jax.ShapeDtyp...  73.2 us
    all_to_all x1, waiting for transfers between devices, per_device(): x = lax.all_to_all(images, 'gy', split_axis=3, concat_axis=0, tiled=True)  27.6 us
    transpose x1, local copies, waits for them, and re-layouts, per_device(): x = jnp.transpose(x, (1, 2, 3, 0)).reshape(sl, hp * wp, e)  11 us
    transpose x1, other arithmetic, per_device(): x = jnp.transpose(x, (1, 2, 3, 0)).reshape(sl, hp * wp, e)  9.52 us
    all_to_all x1, starting transfers between devices, per_device(): x = lax.all_to_all(images, 'gy', split_axis=3, concat_axis=0, tiled=True)  9.3 us
    ppermute x2, starting transfers between devices, halo(): lax.ppermute(tail, axis, [(i, i + 1) for i in range(count - 1)])  9.06 us
    unnamed x7, local copies, waits for them, and re-layouts  8.57 us
    ppermute x2, waiting for transfers between devices, halo(): lax.ppermute(head, axis, [(i + 1, i) for i in range(count - 1)])  5.8 us
  transfers between devices with their start and end apart: 5, of which 3 were waited for; matrix products, arithmetic and copies ran while one was open for 2% of the time, Pallas kernels for 0%

profile of v1, /device:TPU:1, one launch (start us, length us, event | category | flops | bytes accessed | tf_op | source)
XLA Modules:
  0.0 173.5 jit_solution(2801390443608975211)
XLA Ops:
  0.0 0.0 copy-start.1
  0.0 0.0 copy-start.2
  0.0 6.2 %copy.8 = bf16[4,2,128,1024]{2,1,0,3:T(2,128)(2,1)} copy(bf16[4,2,128,1024]{3,2,1,0:T(8,128)(2,1)} %param.3) | data formatting | bytes 4194304 | tf_op args[0]
  6.2 9.3 %all-to-all-start = ((bf16[4,2,128,1024]{2,1,0,3:T(2,128)(2,1)}), bf16[4,2,128,1024]{2,1,0,3:T(2,128)(2,1)S(1)}, u32[]{:S(2)}, u32[]{:S(2)}) async-start(bf16[4,2,128,1024]{2,1,0,3:T(2,128)(2,1)} %copy.8), calls=%async_computation | async-start | bytes 4194304 | tf_op jit(solution)/shard_map/all_to_all | solution.py:108
  15.5 0.0 copy-done.1
  15.5 0.1 multiply_reduce_fusion
  15.6 0.6 subtract_convert_fusion
  16.2 0.0 copy-done.2
  16.2 0.1 fusion.3.kb_ref
  16.3 27.6 %all-to-all-done = bf16[4,2,128,1024]{2,1,0,3:T(2,128)(2,1)S(1)} async-done(((bf16[4,2,128,1024]{2,1,0,3:T(2,128)(2,1)}), bf16[4,2,128,1024]{2,1,0,3:T(2,128)(2,1)S(1)}, u32[]{:S(2)}, u32[]{:S(2)}) %all-to-all-start) | async-done | bytes 2097184 | tf_op jit(solution)/shard_map/all_to_all | solution.py:108
  43.9 0.3 copy.9
  44.2 0.2 copy.10
  44.4 0.1 fusion.8
  44.5 5.1 %collective-permute-start = (bf16[64,2,128,4]{2,3,1,0:T(4,128)(2,1)S(1)}, bf16[64,2,128,4]{2,3,1,0:T(4,128)(2,1)S(1)}, u32[]{:S(2)}, u32[]{:S(2)}) collective-permute-start(bf16[64,2,128,4]{2,3,1,0:T(4,128)(2,1)S(1)} %get-tuple-element.11), channel_id=1, source_target_pairs={{0,1},{1,2},{2,3},{3,4},{4,5},{5,6},{6,7},{7,8},{8,9},{9,10},{10,1... | collective-permute-start | bytes 393224 | tf_op jit(solution)/shard_map/ppermute | solution.py:34
  49.6 1.9 %collective-permute-start.1 = (bf16[64,2,128,4]{2,3,1,0:T(4,128)(2,1)S(1)}, bf16[64,2,128,4]{2,3,1,0:T(4,128)(2,1)S(1)}, u32[]{:S(2)}, u32[]{:S(2)}) collective-permute-start(bf16[64,2,128,4]{2,3,1,0:T(4,128)(2,1)S(1)} %get-tuple-element.12), channel_id=1, source_target_pairs={{1,0},{2,1},{3,2},{4,3},{5,4},{6,5},{7,6},{8,7},{9,8},{10,9},{11,1... | collective-permute-start | bytes 393224 | tf_op jit(solution)/shard_map/ppermute | solution.py:36
  51.6 0.0 collective-permute-done
  51.6 5.8 %collective-permute-done.1 = bf16[64,2,128,4]{2,3,1,0:T(4,128)(2,1)S(1)} collective-permute-done((bf16[64,2,128,4]{2,3,1,0:T(4,128)(2,1)S(1)}, bf16[64,2,128,4]{2,3,1,0:T(4,128)(2,1)S(1)}, u32[]{:S(2)}, u32[]{:S(2)}) %collective-permute-start.1) | collective-permute-done | bytes 131104 | tf_op jit(solution)/shard_map/ppermute | solution.py:36
  57.4 1.6 pad_maximum_fusion
  59.0 3.0 %fusion.7 = (bf16[64,2,2,72]{2,3,1,0:T(8,128)(2,1)}, bf16[64,2,2,72]{2,3,1,0:T(8,128)(2,1)}) fusion(bf16[64,2,128,72]{2,3,1,0:T(8,128)(2,1)S(1)} %pad_maximum_fusion), kind=kLoop, calls=%fused_computation.16 | loop fusion | bytes 147456 | tf_op jit(solution)/shard_map/slice | solution.py:31
  62.0 2.3 %copy.11 = bf16[64,2,2,72]{3,0,2,1:T(8,128)(2,1)S(1)} copy(bf16[64,2,2,72]{2,3,1,0:T(8,128)(2,1)} %get-tuple-element.9) | data formatting | bytes 73728 | tf_op jit(solution)/shard_map/slice | solution.py:31
  64.2 2.3 %copy.12 = bf16[64,2,2,72]{3,0,2,1:T(8,128)(2,1)S(1)} copy(bf16[64,2,2,72]{2,3,1,0:T(8,128)(2,1)} %get-tuple-element.10) | data formatting | bytes 73728 | tf_op jit(solution)/shard_map/slice | solution.py:30
  66.5 1.3 collective-permute-start.3
  67.8 4.0 %collective-permute-start.2 = (bf16[64,2,2,72]{3,0,2,1:T(8,128)(2,1)S(1)}, bf16[64,2,2,72]{3,0,2,1:T(8,128)(2,1)S(1)}, u32[]{:S(2)}, u32[]{:S(2)}) collective-permute-start(bf16[64,2,2,72]{3,0,2,1:T(8,128)(2,1)S(1)} %copy.11), channel_id=1, source_target_pairs={{0,16},{16,32},{32,48},{48,64},{64,80},{80,96},{96,112},{1,17},{17... | collective-permute-start | bytes 110600 | tf_op jit(solution)/shard_map/ppermute | solution.py:34
  71.8 1.3 collective-permute-done.2
  73.1 2.1 %copy.13 = bf16[64,2,2,72]{2,3,1,0:T(8,128)(2,1)} copy(bf16[64,2,2,72]{3,0,2,1:T(8,128)(2,1)S(1)} %collective-permute-done.2) | data formatting | bytes 73728 | tf_op jit(solution)/shard_map/ppermute | solution.py:34
  75.2 0.0 collective-permute-done.3
  75.2 2.1 %copy.14 = bf16[64,2,2,72]{2,3,1,0:T(8,128)(2,1)} copy(bf16[64,2,2,72]{3,0,2,1:T(8,128)(2,1)S(1)} %collective-permute-done.3) | data formatting | bytes 73728 | tf_op jit(solution)/shard_map/ppermute | solution.py:36
  77.3 9.5 %maximum_bitcast_fusion = bf16[2,132,72,64]{1,2,0,3:T(8,128)(2,1)} fusion(bf16[64,2,2,72]{2,3,1,0:T(8,128)(2,1)} %copy.14, bf16[64,2,128,4]{2,3,1,0:T(4,128)(2,1)S(1)} %collective-permute-done.1, bf16[64,2,128,64]{2,3,1,0:T(8,128)(2,1)S(1)} %bitcast.14, bf16[64,2,128,4]{2,3,1,0:T(4,128)(2,1)S(1)} %collective-permute-done, bf16[64,2,2,72]{2,3,1,0:T(8,128)(2,1)} %copy.13), kind=kLoop, calls=%fused_computation | loop fusion | flops 12165120 | bytes 4866048 | tf_op jit(solution)/shard_map/transpose | solution.py:113
  86.8 11.0 %copy.15 = bf16[2,132,72,64]{3,2,1,0:T(8,128)(2,1)} copy(bf16[2,132,72,64]{1,2,0,3:T(8,128)(2,1)} %maximum_bitcast_fusion) | data formatting | bytes 4866048 | tf_op jit(solution)/shard_map/transpose | solution.py:113
  97.8 0.1 broadcast_in_dim.8.cm_ref
  97.9 0.0 copy-start
  97.9 2.4 %copy-done = bf16[2,132,72,64]{3,2,1,0:T(8,128)(2,1)S(1)} copy-done((bf16[2,132,72,64]{3,2,1,0:T(8,128)(2,1)S(1)}, bf16[2,132,72,64]{3,2,1,0:T(8,128)(2,1)}, u32[]{:S(2)}) %copy-start) | copy-done | bytes 2433048
  100.3 73.2 %shard_map.37 = f32[2,128,64,256]{3,2,1,0:T(8,128)} custom-call(bf16[2,9504,64]{2,1,0:T(8,128)(2,1)S(1)} %bitcast.9, bf16[64,256]{1,0:T(8,128)(2,1)S(1)} %fusion.3.kb_ref, bf16[768,256]{1,0:T(8,128)(2,1)S(1)} %pad_maximum_fusion.1.g3_ref, f32[1,256]{1,0:T(1,128)S(1)} %bitcast.10, f32[1,256]{1,0:T(1,128)S(1)} %bitcast.11, ...), custom_call_target="tpu_custom_call" | custom-call | flops 18874368000 | bytes 19210240 | tf_op jit(solution)/shard_map/pallas_call | solution.py:127
  (6 shorter events, 0.1 us)
Async XLA Ops:
  0.0 15.5 %copy-start.1 = (f32[256]{0:T(256)S(1)}, f32[256]{0:T(256)}, u32[]{:S(2)}) copy-start(f32[256]{0:T(256)} %param.4) | copy-start | bytes 3076
  0.0 16.2 %copy-start.2 = (f32[256]{0:T(256)S(1)}, f32[256]{0:T(256)}, u32[]{:S(2)}) copy-start(f32[256]{0:T(256)} %param.5) | copy-start | bytes 3076
  6.2 37.7 %all-to-all-start = ((bf16[4,2,128,1024]{2,1,0,3:T(2,128)(2,1)}), bf16[4,2,128,1024]{2,1,0,3:T(2,128)(2,1)S(1)}, u32[]{:S(2)}, u32[]{:S(2)}) async-start(bf16[4,2,128,1024]{2,1,0,3:T(2,128)(2,1)} %copy.8), calls=%async_computation | async-start | bytes 4194304 | tf_op jit(solution)/shard_map/all_to_all | solution.py:108
  44.5 7.1 %collective-permute-start = (bf16[64,2,128,4]{2,3,1,0:T(4,128)(2,1)S(1)}, bf16[64,2,128,4]{2,3,1,0:T(4,128)(2,1)S(1)}, u32[]{:S(2)}, u32[]{:S(2)}) collective-permute-start(bf16[64,2,128,4]{2,3,1,0:T(4,128)(2,1)S(1)} %get-tuple-element.11), channel_id=1, source_target_pairs={{0,1},{1,2},{2,3},{3,4},{4,5},{5,6},{6,7},{7,8},{8,9},{9,10},{10,1... | collective-permute-start | bytes 393224 | tf_op jit(solution)/shard_map/ppermute | solution.py:34
  49.6 7.8 %collective-permute-start.1 = (bf16[64,2,128,4]{2,3,1,0:T(4,128)(2,1)S(1)}, bf16[64,2,128,4]{2,3,1,0:T(4,128)(2,1)S(1)}, u32[]{:S(2)}, u32[]{:S(2)}) collective-permute-start(bf16[64,2,128,4]{2,3,1,0:T(4,128)(2,1)S(1)} %get-tuple-element.12), channel_id=1, source_target_pairs={{1,0},{2,1},{3,2},{4,3},{5,4},{6,5},{7,6},{8,7},{9,8},{10,9},{11,1... | collective-permute-start | bytes 393224 | tf_op jit(solution)/shard_map/ppermute | solution.py:36
  66.5 8.7 %collective-permute-start.3 = (bf16[64,2,2,72]{3,0,2,1:T(8,128)(2,1)S(1)}, bf16[64,2,2,72]{3,0,2,1:T(8,128)(2,1)S(1)}, u32[]{:S(2)}, u32[]{:S(2)}) collective-permute-start(bf16[64,2,2,72]{3,0,2,1:T(8,128)(2,1)S(1)} %copy.12), channel_id=1, source_target_pairs={{16,0},{32,16},{48,32},{64,48},{80,64},{96,80},{112,96},{17,1},{33... | collective-permute-start | bytes 110600 | tf_op jit(solution)/shard_map/ppermute | solution.py:36
  67.8 5.3 %collective-permute-start.2 = (bf16[64,2,2,72]{3,0,2,1:T(8,128)(2,1)S(1)}, bf16[64,2,2,72]{3,0,2,1:T(8,128)(2,1)S(1)}, u32[]{:S(2)}, u32[]{:S(2)}) collective-permute-start(bf16[64,2,2,72]{3,0,2,1:T(8,128)(2,1)S(1)} %copy.11), channel_id=1, source_target_pairs={{0,16},{16,32},{32,48},{48,64},{64,80},{80,96},{96,112},{1,17},{17... | collective-permute-start | bytes 110600 | tf_op jit(solution)/shard_map/ppermute | solution.py:34
  97.9 2.4 %copy-start = (bf16[2,132,72,64]{3,2,1,0:T(8,128)(2,1)S(1)}, bf16[2,132,72,64]{3,2,1,0:T(8,128)(2,1)}, u32[]{:S(2)}) copy-start(bf16[2,132,72,64]{3,2,1,0:T(8,128)(2,1)} %copy.15) | copy-start | bytes 7299076

commit v2 on v1

--- a/solution.py
+++ b/solution.py
@@ -55,12 +55,19 @@
     lam = lam_ref[...]
     cm = cm_ref[...]
 
-    b = jnp.dot(x_ref[0, pl.ds(base, n), :], kb_ref[...],
-                preferred_element_type=jnp.float32)
-    b_ref[...] = b
-    f0 = jnp.maximum(b * step, 0.0)
-    f0_ref[...] = f0
-    f3_ref[...] = split3(f0)
+    kb = kb_ref[...]
+
+    def body0(q, carry):
+        xp = x_ref[0, t * TR + q]
+        bq = lax.dot_general(xp, kb, (((0,), (0,)), ((), ())),
+                             preferred_element_type=jnp.float32)
+        o = pl.multiple_of(q * wp, 8)
+        b_ref[pl.ds(o, wp), :] = bq
+        f0_ref[pl.ds(o, wp), :] = jnp.maximum(bq * step, 0.0)
+        return carry
+
+    lax.fori_loop(0, rows, body0, 0)
+    f3_ref[...] = split3(f0_ref[...])
 
     def update(src_ref, q):
         o = pl.multiple_of(q * wp, 8)
@@ -110,7 +117,7 @@
     x = halo(x, "gy", 3, CH)
     x = halo(x, "gx", 2, RH)
     hp, wp = h + 2 * RH, w + 2 * CH
-    x = jnp.transpose(x, (1, 2, 3, 0)).reshape(sl, hp * wp, e)
+    x = jnp.transpose(x, (1, 2, 0, 3))
     r = kernel.shape[1]
 
     gi = lax.axis_index("gx")
@@ -129,7 +136,7 @@
         out_shape=jax.ShapeDtypeStruct((sl, h, w, r), jnp.float32),
         grid=(sl, nt),
         in_specs=[
-            pl.BlockSpec((1, hp * wp, e), lambda s, t: (s, 0, 0)),
+            pl.BlockSpec((1, hp, e, wp), lambda s, t: (s, 0, 0, 0)),
             pl.BlockSpec((e, r), lambda s, t: (0, 0)),
             pl.BlockSpec((3 * r, r), lambda s, t: (0, 0)),
             pl.BlockSpec((1, r), lambda s, t: (0, 0)),

time: 176 us -> 242 us (1.38)
  the two profiles are of different devices: /device:TPU:1 before, /device:TPU:42 now
where the time goes in v2:
time: 242 us
  Pallas kernels  128 us (53%)
  local copies, waits for them, and re-layouts  48 us (20%)
  waiting for transfers between devices  38.5 us (16%)
  starting transfers between devices  21.2 us (9%)
  other arithmetic  5.45 us (2%)
    pallas_call x1, Pallas kernels, per_device(): pl.pallas_call(functools.partial(fit_kernel, wp), out_shape=jax.ShapeDtyp...  128 us
    all_to_all x1, waiting for transfers between devices, per_device(): x = lax.all_to_all(images, 'gy', split_axis=3, concat_axis=0, tiled=True)  26.9 us
    slice x2, local copies, waits for them, and re-layouts, halo(): lax.slice_in_dim(cells, cells.shape[dim] - width, cells.shape[dim], axis=...  13.5 us
    ppermute x2, starting transfers between devices, halo(): lax.ppermute(head, axis, [(i + 1, i) for i in range(count - 1)])  7.8 us
    ppermute x1, local copies, waits for them, and re-layouts, halo(): lax.ppermute(tail, axis, [(i, i + 1) for i in range(count - 1)])  7.45 us
    ppermute x1, local copies, waits for them, and re-layouts, halo(): lax.ppermute(head, axis, [(i + 1, i) for i in range(count - 1)])  7.44 us
    all_to_all x1, starting transfers between devices, per_device(): x = lax.all_to_all(images, 'gy', split_axis=3, concat_axis=0, tiled=True)  7.35 us
    all_to_all x2, local copies, waits for them, and re-layouts, per_device(): x = lax.all_to_all(images, 'gy', split_axis=3, concat_axis=0, tiled=True)  7.12 us
  transfers between devices with their start and end apart: 5, of which 4 were waited for; matrix products, arithmetic and copies ran while one was open for 3% of the time, Pallas kernels for 0%

profile of v2, /device:TPU:42, one launch (start us, length us, event | category | flops | bytes accessed | tf_op | source)
XLA Modules:
  0.0 241.6 jit_solution(7382315105973844729)
XLA Ops:
  0.0 0.0 copy-start.3
  0.0 0.0 copy-start.4
  0.0 6.2 %copy.7 = bf16[4,2,128,1024]{2,1,0,3:T(2,128)(2,1)} copy(bf16[4,2,128,1024]{3,2,1,0:T(8,128)(2,1)} %param.3) | data formatting | bytes 4194304 | tf_op args[0]
  6.2 7.3 %all-to-all-start = ((bf16[4,2,128,1024]{2,1,0,3:T(2,128)(2,1)}), bf16[4,2,128,1024]{2,1,0,3:T(2,128)(2,1)}, u32[]{:S(2)}, u32[]{:S(2)}) async-start(bf16[4,2,128,1024]{2,1,0,3:T(2,128)(2,1)} %copy.7), calls=%async_computation | async-start | bytes 4194304 | tf_op jit(solution)/shard_map/all_to_all | solution.py:115
  13.5 0.0 copy-done.3
  13.5 0.1 multiply_reduce_fusion
  13.7 0.6 subtract_convert_fusion
  14.2 0.0 copy-done.4
  14.3 0.1 fusion.3.kb_ref
  14.4 26.9 %all-to-all-done = bf16[4,2,128,1024]{2,1,0,3:T(2,128)(2,1)} async-done(((bf16[4,2,128,1024]{2,1,0,3:T(2,128)(2,1)}), bf16[4,2,128,1024]{2,1,0,3:T(2,128)(2,1)}, u32[]{:S(2)}, u32[]{:S(2)}) %all-to-all-start) | async-done | bytes 2097184 | tf_op jit(solution)/shard_map/all_to_all | solution.py:115
  41.3 1.9 copy.8
  43.1 5.3 %copy.9 = bf16[16,4,2,128,64]{4,1,0,3,2:T(4,128)(2,1)} copy(bf16[16,4,2,128,64]{3,4,0,2,1:T(8,128)(2,1)S(1)} %bitcast.13) | data formatting | bytes 4194304 | tf_op jit(solution)/shard_map/all_to_all | solution.py:115
  48.4 7.3 %fusion.7 = (bf16[64,2,128,4]{3,0,2,1:T(8,128)(2,1)}, bf16[64,2,128,4]{3,0,2,1:T(8,128)(2,1)}) fusion(bf16[64,2,128,64]{3,0,2,1:T(8,128)(2,1)} %bitcast.10), kind=kLoop, calls=%fused_computation.18 | loop fusion | bytes 524288 | tf_op jit(solution)/shard_map/slice | solution.py:31
  55.7 6.2 %copy.10 = bf16[64,2,128,4]{2,0,3,1:T(8,128)(2,1)S(1)} copy(bf16[64,2,128,4]{3,0,2,1:T(8,128)(2,1)} %get-tuple-element.11) | data formatting | bytes 262144 | tf_op jit(solution)/shard_map/slice | solution.py:31
  61.9 6.2 %copy.11 = bf16[64,2,128,4]{2,0,3,1:T(8,128)(2,1)S(1)} copy(bf16[64,2,128,4]{3,0,2,1:T(8,128)(2,1)} %get-tuple-element.12) | data formatting | bytes 262144 | tf_op jit(solution)/shard_map/slice | solution.py:30
  68.1 5.6 %collective-permute-start.1 = (bf16[64,2,128,4]{2,0,3,1:T(8,128)(2,1)S(1)}, bf16[64,2,128,4]{2,0,3,1:T(8,128)(2,1)S(1)}, u32[]{:S(2)}, u32[]{:S(2)}) collective-permute-start(bf16[64,2,128,4]{2,0,3,1:T(8,128)(2,1)S(1)} %copy.11), channel_id=1, source_target_pairs={{1,0},{2,1},{3,2},{4,3},{5,4},{6,5},{7,6},{8,7},{9,8},{10,9},{11,1... | collective-permute-start | bytes 393224 | tf_op jit(solution)/shard_map/ppermute | solution.py:36
  73.7 1.9 collective-permute-start
  75.7 6.7 %collective-permute-done = bf16[64,2,128,4]{2,0,3,1:T(8,128)(2,1)S(1)} collective-permute-done((bf16[64,2,128,4]{2,0,3,1:T(8,128)(2,1)S(1)}, bf16[64,2,128,4]{2,0,3,1:T(8,128)(2,1)S(1)}, u32[]{:S(2)}, u32[]{:S(2)}) %collective-permute-start) | collective-permute-done | bytes 131104 | tf_op jit(solution)/shard_map/ppermute | solution.py:34
  82.4 7.5 %copy.12 = bf16[64,2,128,4]{3,0,2,1:T(8,128)(2,1)} copy(bf16[64,2,128,4]{2,0,3,1:T(8,128)(2,1)S(1)} %collective-permute-done) | data formatting | bytes 262144 | tf_op jit(solution)/shard_map/ppermute | solution.py:34
  89.9 0.0 collective-permute-done.1
  89.9 7.4 %copy.13 = bf16[64,2,128,4]{3,0,2,1:T(8,128)(2,1)} copy(bf16[64,2,128,4]{2,0,3,1:T(8,128)(2,1)S(1)} %collective-permute-done.1) | data formatting | bytes 262144 | tf_op jit(solution)/shard_map/ppermute | solution.py:36
  97.3 0.0 copy-start
  97.3 0.0 copy-start.1
  97.3 0.0 copy-start.2
  97.3 1.3 pad_maximum_fusion.3
  98.6 4.1 %collective-permute-start.2 = (bf16[64,2,2,72]{3,0,2,1:T(8,128)(2,1)S(1)}, bf16[64,2,2,72]{3,0,2,1:T(8,128)(2,1)S(1)}, u32[]{:S(2)}, u32[]{:S(2)}) collective-permute-start(bf16[64,2,2,72]{3,0,2,1:T(8,128)(2,1)S(1)} %get-tuple-element.9), channel_id=1, source_target_pairs={{0,16},{16,32},{32,48},{48,64},{64,80},{80,96},{96,112},{1,17},{17... | collective-permute-start | bytes 110600 | tf_op jit(solution)/shard_map/ppermute | solution.py:34
  102.7 2.2 collective-permute-start.3
  104.9 0.1 collective-permute-done.2
  105.0 4.7 %collective-permute-done.3 = bf16[64,2,2,72]{3,0,2,1:T(8,128)(2,1)S(1)} collective-permute-done((bf16[64,2,2,72]{3,0,2,1:T(8,128)(2,1)S(1)}, bf16[64,2,2,72]{3,0,2,1:T(8,128)(2,1)S(1)}, u32[]{:S(2)}, u32[]{:S(2)}) %collective-permute-start.3) | collective-permute-done | bytes 36896 | tf_op jit(solution)/shard_map/ppermute | solution.py:36
  109.8 0.0 copy-done
  109.8 0.0 copy-done.1
  109.8 0.0 copy-done.2
  109.8 3.9 %maximum_bitcast_fusion.x_ref = bf16[2,132,64,72]{3,2,1,0:T(8,128)(2,1)S(1)} fusion(bf16[64,2,2,72]{3,0,2,1:T(8,128)(2,1)S(1)} %collective-permute-done.3, bf16[64,2,128,4]{3,0,2,1:T(8,128)(2,1)S(1)} %copy-done.2, bf16[64,2,128,64]{3,0,2,1:T(8,128)(2,1)S(1)} %bitcast.12, bf16[64,2,128,4]{3,0,2,1:T(8,128)(2,1)S(1)} %copy-done.1, ...), kind=kLoop, calls=%fused_computation | loop fusion | flops 12165120 | bytes 4866048 | tf_op jit(solution)/shard_map/transpose | solution.py:120
  113.7 0.1 broadcast_in_dim.8.cm_ref
  113.8 127.8 %shard_map.37 = f32[2,128,64,256]{3,2,1,0:T(8,128)} custom-call(bf16[2,132,64,72]{3,2,1,0:T(8,128)(2,1)S(1)} %maximum_bitcast_fusion.x_ref, bf16[64,256]{1,0:T(8,128)(2,1)S(1)} %fusion.3.kb_ref, bf16[768,256]{1,0:T(8,128)(2,1)S(1)} %pad_maximum_fusion.g3_ref, f32[1,256]{1,0:T(1,128)S(1)} %bitcast.8, f32[1,256]{1,0:T(1,128)S(1)} %bitcast.9, ...), custom_call_target="tpu_custom_call" | custom-call | flops 18874368000 | bytes 19210240 | tf_op jit(solution)/shard_map/pallas_call | solution.py:134
  (6 shorter events, 0.1 us)
Async XLA Ops:
  0.0 13.5 %copy-start.3 = (f32[256]{0:T(256)S(1)}, f32[256]{0:T(256)}, u32[]{:S(2)}) copy-start(f32[256]{0:T(256)} %param.4) | copy-start | bytes 3076
  0.0 14.2 %copy-start.4 = (f32[256]{0:T(256)S(1)}, f32[256]{0:T(256)}, u32[]{:S(2)}) copy-start(f32[256]{0:T(256)} %param.5) | copy-start | bytes 3076
  6.2 35.1 %all-to-all-start = ((bf16[4,2,128,1024]{2,1,0,3:T(2,128)(2,1)}), bf16[4,2,128,1024]{2,1,0,3:T(2,128)(2,1)}, u32[]{:S(2)}, u32[]{:S(2)}) async-start(bf16[4,2,128,1024]{2,1,0,3:T(2,128)(2,1)} %copy.7), calls=%async_computation | async-start | bytes 4194304 | tf_op jit(solution)/shard_map/all_to_all | solution.py:115
  68.1 21.8 %collective-permute-start.1 = (bf16[64,2,128,4]{2,0,3,1:T(8,128)(2,1)S(1)}, bf16[64,2,128,4]{2,0,3,1:T(8,128)(2,1)S(1)}, u32[]{:S(2)}, u32[]{:S(2)}) collective-permute-start(bf16[64,2,128,4]{2,0,3,1:T(8,128)(2,1)S(1)} %copy.11), channel_id=1, source_target_pairs={{1,0},{2,1},{3,2},{4,3},{5,4},{6,5},{7,6},{8,7},{9,8},{10,9},{11,1... | collective-permute-start | bytes 393224 | tf_op jit(solution)/shard_map/ppermute | solution.py:36
  73.7 8.7 %collective-permute-start = (bf16[64,2,128,4]{2,0,3,1:T(8,128)(2,1)S(1)}, bf16[64,2,128,4]{2,0,3,1:T(8,128)(2,1)S(1)}, u32[]{:S(2)}, u32[]{:S(2)}) collective-permute-start(bf16[64,2,128,4]{2,0,3,1:T(8,128)(2,1)S(1)} %copy.10), channel_id=1, source_target_pairs={{0,1},{1,2},{2,3},{3,4},{4,5},{5,6},{6,7},{7,8},{8,9},{9,10},{10,1... | collective-permute-start | bytes 393224 | tf_op jit(solution)/shard_map/ppermute | solution.py:34
  97.3 12.5 %copy-start = (bf16[16,4,2,128,64]{4,1,0,3,2:T(4,128)(2,1)S(1)}, bf16[16,4,2,128,64]{4,1,0,3,2:T(4,128)(2,1)}, u32[]{:S(2)}) copy-start(bf16[16,4,2,128,64]{4,1,0,3,2:T(4,128)(2,1)} %copy.9) | copy-start | bytes 6291460
  97.3 12.5 %copy-start.1 = (bf16[64,2,128,4]{3,0,2,1:T(8,128)(2,1)S(1)}, bf16[64,2,128,4]{3,0,2,1:T(8,128)(2,1)}, u32[]{:S(2)}) copy-start(bf16[64,2,128,4]{3,0,2,1:T(8,128)(2,1)} %copy.12) | copy-start | bytes 393220
  97.3 12.5 %copy-start.2 = (bf16[64,2,128,4]{3,0,2,1:T(8,128)(2,1)S(1)}, bf16[64,2,128,4]{3,0,2,1:T(8,128)(2,1)}, u32[]{:S(2)}) copy-start(bf16[64,2,128,4]{3,0,2,1:T(8,128)(2,1)} %copy.13) | copy-start | bytes 393220
  98.6 6.4 %collective-permute-start.2 = (bf16[64,2,2,72]{3,0,2,1:T(8,128)(2,1)S(1)}, bf16[64,2,2,72]{3,0,2,1:T(8,128)(2,1)S(1)}, u32[]{:S(2)}, u32[]{:S(2)}) collective-permute-start(bf16[64,2,2,72]{3,0,2,1:T(8,128)(2,1)S(1)} %get-tuple-element.9), channel_id=1, source_target_pairs={{0,16},{16,32},{32,48},{48,64},{64,80},{80,96},{96,112},{1,17},{17... | collective-permute-start | bytes 110600 | tf_op jit(solution)/shard_map/ppermute | solution.py:34
  102.7 7.1 %collective-permute-start.3 = (bf16[64,2,2,72]{3,0,2,1:T(8,128)(2,1)S(1)}, bf16[64,2,2,72]{3,0,2,1:T(8,128)(2,1)S(1)}, u32[]{:S(2)}, u32[]{:S(2)}) collective-permute-start(bf16[64,2,2,72]{3,0,2,1:T(8,128)(2,1)S(1)} %get-tuple-element.10), channel_id=1, source_target_pairs={{16,0},{32,16},{48,32},{64,48},{80,64},{96,80},{112,96},{17,1},{33... | collective-permute-start | bytes 110600 | tf_op jit(solution)/shard_map/ppermute | solution.py:36

commit v3 on v1

--- a/solution.py
+++ b/solution.py
@@ -40,9 +40,7 @@
 
 
 def split3(f):
-    hi = f.astype(jnp.bfloat16)
-    lo = (f - hi.astype(jnp.float32)).astype(jnp.bfloat16)
-    return jnp.concatenate([hi, lo, hi], axis=1)
+    return f.astype(jnp.bfloat16)
 
 
 def fit_kernel(wp, x_ref, kb_ref, g3_ref, step_ref, lam_ref, cm_ref, rm_ref,
@@ -103,8 +101,7 @@
     kernel, gram, lam, step = kernel_parts(rates, smoothing)
     kb = kernel.astype(jnp.bfloat16)
     gh = gram.astype(jnp.bfloat16)
-    gl = (gram - gh.astype(jnp.float32)).astype(jnp.bfloat16)
-    g3 = jnp.concatenate([gh, gh, gl], axis=0)
+    g3 = gh
     x = lax.all_to_all(images, "gy", split_axis=3, concat_axis=0, tiled=True)
     e, sl, h, w = x.shape
     x = halo(x, "gy", 3, CH)
@@ -123,7 +120,7 @@
 
     rows = TR + 2 * RH
     nt = h // TR
-    flops = 2 * sl * nt * rows * wp * r * (e + 2 * 3 * r)
+    flops = 2 * sl * nt * rows * wp * r * (e + 2 * r)
     out = pl.pallas_call(
         functools.partial(fit_kernel, wp),
         out_shape=jax.ShapeDtypeStruct((sl, h, w, r), jnp.float32),
@@ -131,7 +128,7 @@
         in_specs=[
             pl.BlockSpec((1, hp * wp, e), lambda s, t: (s, 0, 0)),
             pl.BlockSpec((e, r), lambda s, t: (0, 0)),
-            pl.BlockSpec((3 * r, r), lambda s, t: (0, 0)),
+            pl.BlockSpec((r, r), lambda s, t: (0, 0)),
             pl.BlockSpec((1, r), lambda s, t: (0, 0)),
             pl.BlockSpec((1, r), lambda s, t: (0, 0)),
             pl.BlockSpec((wp, r), lambda s, t: (0, 0)),
@@ -142,7 +139,7 @@
             pltpu.VMEM((rows * wp, r), jnp.float32),
             pltpu.VMEM((rows * wp, r), jnp.float32),
             pltpu.VMEM((rows * wp, r), jnp.float32),
-            pltpu.VMEM((rows * wp, 3 * r), jnp.bfloat16),
+            pltpu.VMEM((rows * wp, r), jnp.bfloat16),
             pltpu.VMEM(((rows - 2) * wp, r), jnp.float32),
         ],
         compiler_params=pltpu.CompilerParams(

time: 176 us -> 151 us (0.86)
  Pallas kernels: 73.2 us -> 49.2 us
    pallas_call x1, Pallas kernels: 73.2 us -> 49.2 us  [per_device(): pl.pallas_call(functools.partial(fit_kernel, wp), out_shape=jax.ShapeDtyp...]
where the time goes in v3:
time: 151 us; the launch traced here: 149 us
  Pallas kernels  49.2 us (33%)
  waiting for transfers between devices  34.7 us (23%)
  local copies, waits for them, and re-layouts  32 us (21%)
  starting transfers between devices  21.6 us (14%)
  other arithmetic  11.3 us (7%)
    pallas_call x1, Pallas kernels, per_device(): pl.pallas_call(functools.partial(fit_kernel, wp), out_shape=jax.ShapeDtyp...  49.2 us
    all_to_all x1, waiting for transfers between devices, per_device(): x = lax.all_to_all(images, 'gy', split_axis=3, concat_axis=0, tiled=True)  27.7 us
    transpose x1, local copies, waits for them, and re-layouts, per_device(): x = jnp.transpose(x, (1, 2, 3, 0)).reshape(sl, hp * wp, e)  11 us
    transpose x1, other arithmetic, per_device(): x = jnp.transpose(x, (1, 2, 3, 0)).reshape(sl, hp * wp, e)  9.5 us
    all_to_all x1, starting transfers between devices, per_device(): x = lax.all_to_all(images, 'gy', split_axis=3, concat_axis=0, tiled=True)  9.3 us
    ppermute x2, starting transfers between devices, halo(): lax.ppermute(tail, axis, [(i, i + 1) for i in range(count - 1)])  9.06 us
    unnamed x7, local copies, waits for them, and re-layouts  8.55 us
    ppermute x2, waiting for transfers between devices, halo(): lax.ppermute(head, axis, [(i + 1, i) for i in range(count - 1)])  5.81 us
  transfers between devices with their start and end apart: 5, of which 3 were waited for; matrix products, arithmetic and copies ran while one was open for 2% of the time, Pallas kernels for 0%

profile of v3, /device:TPU:1, one launch (start us, length us, event | category | flops | bytes accessed | tf_op | source)
XLA Modules:
  0.0 149.4 jit_solution(9732819137737600464)
XLA Ops:
  0.0 0.0 copy-start.1
  0.0 6.2 %copy.10 = bf16[4,2,128,1024]{2,1,0,3:T(2,128)(2,1)} copy(bf16[4,2,128,1024]{3,2,1,0:T(8,128)(2,1)} %param.3) | data formatting | bytes 4194304 | tf_op args[0]
  6.2 9.3 %all-to-all-start = ((bf16[4,2,128,1024]{2,1,0,3:T(2,128)(2,1)}), bf16[4,2,128,1024]{2,1,0,3:T(2,128)(2,1)S(1)}, u32[]{:S(2)}, u32[]{:S(2)}) async-start(bf16[4,2,128,1024]{2,1,0,3:T(2,128)(2,1)} %copy.10), calls=%async_computation | async-start | bytes 4194304 | tf_op jit(solution)/shard_map/all_to_all | solution.py:105
  15.5 0.0 copy-start.2
  15.5 0.0 copy-done.1
  15.5 0.1 multiply_reduce_fusion
  15.6 0.1 fusion.3.kb_ref
  15.7 0.5 fusion.9
  16.2 27.7 %all-to-all-done = bf16[4,2,128,1024]{2,1,0,3:T(2,128)(2,1)S(1)} async-done(((bf16[4,2,128,1024]{2,1,0,3:T(2,128)(2,1)}), bf16[4,2,128,1024]{2,1,0,3:T(2,128)(2,1)S(1)}, u32[]{:S(2)}, u32[]{:S(2)}) %all-to-all-start) | async-done | bytes 2097184 | tf_op jit(solution)/shard_map/all_to_all | solution.py:105
  43.9 0.3 copy.11
  44.2 0.2 copy.12
  44.4 0.1 fusion.8
  44.5 5.1 %collective-permute-start = (bf16[64,2,128,4]{2,3,1,0:T(4,128)(2,1)S(1)}, bf16[64,2,128,4]{2,3,1,0:T(4,128)(2,1)S(1)}, u32[]{:S(2)}, u32[]{:S(2)}) collective-permute-start(bf16[64,2,128,4]{2,3,1,0:T(4,128)(2,1)S(1)} %get-tuple-element.9), channel_id=1, source_target_pairs={{0,1},{1,2},{2,3},{3,4},{4,5},{5,6},{6,7},{7,8},{8,9},{9,10},{10,1... | collective-permute-start | bytes 393224 | tf_op jit(solution)/shard_map/ppermute | solution.py:34
  49.6 1.9 %collective-permute-start.1 = (bf16[64,2,128,4]{2,3,1,0:T(4,128)(2,1)S(1)}, bf16[64,2,128,4]{2,3,1,0:T(4,128)(2,1)S(1)}, u32[]{:S(2)}, u32[]{:S(2)}) collective-permute-start(bf16[64,2,128,4]{2,3,1,0:T(4,128)(2,1)S(1)} %get-tuple-element.10), channel_id=1, source_target_pairs={{1,0},{2,1},{3,2},{4,3},{5,4},{6,5},{7,6},{8,7},{9,8},{10,9},{11,1... | collective-permute-start | bytes 393224 | tf_op jit(solution)/shard_map/ppermute | solution.py:36
  51.6 0.0 copy-done.2
  51.6 0.0 collective-permute-done
  51.6 5.8 %collective-permute-done.1 = bf16[64,2,128,4]{2,3,1,0:T(4,128)(2,1)S(1)} collective-permute-done((bf16[64,2,128,4]{2,3,1,0:T(4,128)(2,1)S(1)}, bf16[64,2,128,4]{2,3,1,0:T(4,128)(2,1)S(1)}, u32[]{:S(2)}, u32[]{:S(2)}) %collective-permute-start.1) | collective-permute-done | bytes 131104 | tf_op jit(solution)/shard_map/ppermute | solution.py:36
  57.4 1.6 %pad_maximum_fusion = bf16[64,2,128,72]{2,3,1,0:T(8,128)(2,1)S(1)} fusion(bf16[64,2,128,4]{2,3,1,0:T(4,128)(2,1)S(1)} %collective-permute-done.1, bf16[64,2,128,64]{2,3,1,0:T(8,128)(2,1)S(1)} %bitcast.13, bf16[64,2,128,4]{2,3,1,0:T(4,128)(2,1)S(1)} %collective-permute-done), kind=kLoop, calls=%fused_computation.1 | loop fusion | flops 7077888 | bytes 4718592 | tf_op jit(solution)/shard_map/concatenate | solution.py:32
  59.0 3.0 %fusion.7 = (bf16[64,2,2,72]{2,3,1,0:T(8,128)(2,1)}, bf16[64,2,2,72]{2,3,1,0:T(8,128)(2,1)}) fusion(bf16[64,2,128,72]{2,3,1,0:T(8,128)(2,1)S(1)} %pad_maximum_fusion), kind=kLoop, calls=%fused_computation.14 | loop fusion | bytes 147456 | tf_op jit(solution)/shard_map/slice | solution.py:31
  62.0 2.3 %copy.13 = bf16[64,2,2,72]{3,0,2,1:T(8,128)(2,1)S(1)} copy(bf16[64,2,2,72]{2,3,1,0:T(8,128)(2,1)} %get-tuple-element.7) | data formatting | bytes 73728 | tf_op jit(solution)/shard_map/slice | solution.py:31
  64.3 2.3 %copy.14 = bf16[64,2,2,72]{3,0,2,1:T(8,128)(2,1)S(1)} copy(bf16[64,2,2,72]{2,3,1,0:T(8,128)(2,1)} %get-tuple-element.8) | data formatting | bytes 73728 | tf_op jit(solution)/shard_map/slice | solution.py:30
  66.5 1.3 collective-permute-start.3
  67.8 4.0 %collective-permute-start.2 = (bf16[64,2,2,72]{3,0,2,1:T(8,128)(2,1)S(1)}, bf16[64,2,2,72]{3,0,2,1:T(8,128)(2,1)S(1)}, u32[]{:S(2)}, u32[]{:S(2)}) collective-permute-start(bf16[64,2,2,72]{3,0,2,1:T(8,128)(2,1)S(1)} %copy.13), channel_id=1, source_target_pairs={{0,16},{16,32},{32,48},{48,64},{64,80},{80,96},{96,112},{1,17},{17... | collective-permute-start | bytes 110600 | tf_op jit(solution)/shard_map/ppermute | solution.py:34
  71.9 0.1 copy.18.g3_ref
  72.0 1.2 collective-permute-done.2
  73.2 2.1 %copy.15 = bf16[64,2,2,72]{2,3,1,0:T(8,128)(2,1)} copy(bf16[64,2,2,72]{3,0,2,1:T(8,128)(2,1)S(1)} %collective-permute-done.2) | data formatting | bytes 73728 | tf_op jit(solution)/shard_map/ppermute | solution.py:34
  75.2 0.0 collective-permute-done.3
  75.2 2.1 %copy.16 = bf16[64,2,2,72]{2,3,1,0:T(8,128)(2,1)} copy(bf16[64,2,2,72]{3,0,2,1:T(8,128)(2,1)S(1)} %collective-permute-done.3) | data formatting | bytes 73728 | tf_op jit(solution)/shard_map/ppermute | solution.py:36
  77.3 9.5 %maximum_bitcast_fusion = bf16[2,132,72,64]{1,2,0,3:T(8,128)(2,1)} fusion(bf16[64,2,2,72]{2,3,1,0:T(8,128)(2,1)} %copy.16, bf16[64,2,128,4]{2,3,1,0:T(4,128)(2,1)S(1)} %collective-permute-done.1, bf16[64,2,128,64]{2,3,1,0:T(8,128)(2,1)S(1)} %bitcast.14, bf16[64,2,128,4]{2,3,1,0:T(4,128)(2,1)S(1)} %collective-permute-done, bf16[64,2,2,72]{2,3,1,0:T(8,128)(2,1)} %copy.15), kind=kLoop, calls=%fused_computation | loop fusion | flops 12165120 | bytes 4866048 | tf_op jit(solution)/shard_map/transpose | solution.py:110
  86.8 11.0 %copy.17 = bf16[2,132,72,64]{3,2,1,0:T(8,128)(2,1)} copy(bf16[2,132,72,64]{1,2,0,3:T(8,128)(2,1)} %maximum_bitcast_fusion) | data formatting | bytes 4866048 | tf_op jit(solution)/shard_map/transpose | solution.py:110
  97.8 0.1 broadcast_in_dim.8.cm_ref
  97.9 0.0 copy-start
  97.9 2.4 %copy-done = bf16[2,132,72,64]{3,2,1,0:T(8,128)(2,1)S(1)} copy-done((bf16[2,132,72,64]{3,2,1,0:T(8,128)(2,1)S(1)}, bf16[2,132,72,64]{3,2,1,0:T(8,128)(2,1)}, u32[]{:S(2)}) %copy-start) | copy-done | bytes 2433048
  100.3 49.2 %shard_map.37 = f32[2,128,64,256]{3,2,1,0:T(8,128)} custom-call(bf16[2,9504,64]{2,1,0:T(8,128)(2,1)S(1)} %bitcast.9, bf16[64,256]{1,0:T(8,128)(2,1)S(1)} %fusion.3.kb_ref, bf16[256,256]{1,0:T(8,128)(2,1)S(1)} %copy.18.g3_ref, f32[1,256]{1,0:T(1,128)S(1)} %bitcast.10, f32[1,256]{1,0:T(1,128)S(1)} %bitcast.11, f32[72,256]{1,0:T(8,128)S(1)} %broadcast_in_dim.8.cm_ref, ...), custom_call_target="tpu_custom_call" | custom-call | flops 6794772480 | bytes 19210240 | tf_op jit(solution)/shard_map/pallas_call | solution.py:124
  (5 shorter events, 0.0 us)
Async XLA Ops:
  0.0 15.5 %copy-start.1 = (f32[256]{0:T(256)S(1)}, f32[256]{0:T(256)}, u32[]{:S(2)}) copy-start(f32[256]{0:T(256)} %param.4) | copy-start | bytes 3076
  6.2 37.7 %all-to-all-start = ((bf16[4,2,128,1024]{2,1,0,3:T(2,128)(2,1)}), bf16[4,2,128,1024]{2,1,0,3:T(2,128)(2,1)S(1)}, u32[]{:S(2)}, u32[]{:S(2)}) async-start(bf16[4,2,128,1024]{2,1,0,3:T(2,128)(2,1)} %copy.10), calls=%async_computation | async-start | bytes 4194304 | tf_op jit(solution)/shard_map/all_to_all | solution.py:105
  15.5 36.1 %copy-start.2 = (f32[256]{0:T(256)S(1)}, f32[256]{0:T(256)}, u32[]{:S(2)}) copy-start(f32[256]{0:T(256)} %param.5) | copy-start | bytes 3076
  44.5 7.1 %collective-permute-start = (bf16[64,2,128,4]{2,3,1,0:T(4,128)(2,1)S(1)}, bf16[64,2,128,4]{2,3,1,0:T(4,128)(2,1)S(1)}, u32[]{:S(2)}, u32[]{:S(2)}) collective-permute-start(bf16[64,2,128,4]{2,3,1,0:T(4,128)(2,1)S(1)} %get-tuple-element.9), channel_id=1, source_target_pairs={{0,1},{1,2},{2,3},{3,4},{4,5},{5,6},{6,7},{7,8},{8,9},{9,10},{10,1... | collective-permute-start | bytes 393224 | tf_op jit(solution)/shard_map/ppermute | solution.py:34
  49.6 7.8 %collective-permute-start.1 = (bf16[64,2,128,4]{2,3,1,0:T(4,128)(2,1)S(1)}, bf16[64,2,128,4]{2,3,1,0:T(4,128)(2,1)S(1)}, u32[]{:S(2)}, u32[]{:S(2)}) collective-permute-start(bf16[64,2,128,4]{2,3,1,0:T(4,128)(2,1)S(1)} %get-tuple-element.10), channel_id=1, source_target_pairs={{1,0},{2,1},{3,2},{4,3},{5,4},{6,5},{7,6},{8,7},{9,8},{10,9},{11,1... | collective-permute-start | bytes 393224 | tf_op jit(solution)/shard_map/ppermute | solution.py:36
  66.5 8.7 %collective-permute-start.3 = (bf16[64,2,2,72]{3,0,2,1:T(8,128)(2,1)S(1)}, bf16[64,2,2,72]{3,0,2,1:T(8,128)(2,1)S(1)}, u32[]{:S(2)}, u32[]{:S(2)}) collective-permute-start(bf16[64,2,2,72]{3,0,2,1:T(8,128)(2,1)S(1)} %copy.14), channel_id=1, source_target_pairs={{16,0},{32,16},{48,32},{64,48},{80,64},{96,80},{112,96},{17,1},{33... | collective-permute-start | bytes 110600 | tf_op jit(solution)/shard_map/ppermute | solution.py:36
  67.8 5.3 %collective-permute-start.2 = (bf16[64,2,2,72]{3,0,2,1:T(8,128)(2,1)S(1)}, bf16[64,2,2,72]{3,0,2,1:T(8,128)(2,1)S(1)}, u32[]{:S(2)}, u32[]{:S(2)}) collective-permute-start(bf16[64,2,2,72]{3,0,2,1:T(8,128)(2,1)S(1)} %copy.13), channel_id=1, source_target_pairs={{0,16},{16,32},{32,48},{48,64},{64,80},{80,96},{96,112},{1,17},{17... | collective-permute-start | bytes 110600 | tf_op jit(solution)/shard_map/ppermute | solution.py:34
  97.9 2.4 %copy-start = (bf16[2,132,72,64]{3,2,1,0:T(8,128)(2,1)S(1)}, bf16[2,132,72,64]{3,2,1,0:T(8,128)(2,1)}, u32[]{:S(2)}) copy-start(bf16[2,132,72,64]{3,2,1,0:T(8,128)(2,1)} %copy.17) | copy-start | bytes 7299076

commit v4 on v3

--- a/solution.py
+++ b/solution.py
@@ -43,7 +43,7 @@
     return f.astype(jnp.bfloat16)
 
 
-def fit_kernel(wp, x_ref, kb_ref, g3_ref, step_ref, lam_ref, cm_ref, rm_ref,
+def fit_kernel(wp, bin_ref, g3_ref, step_ref, lam_ref, cm_ref, rm_ref,
                o_ref, b_ref, f0_ref, f1_ref, f3_ref, m_ref):
     t = pl.program_id(1)
     rows = TR + 2 * RH
@@ -53,8 +53,7 @@
     lam = lam_ref[...]
     cm = cm_ref[...]
 
-    b = jnp.dot(x_ref[0, pl.ds(base, n), :], kb_ref[...],
-                preferred_element_type=jnp.float32)
+    b = bin_ref[0, pl.ds(base, n), :]
     b_ref[...] = b
     f0 = jnp.maximum(b * step, 0.0)
     f0_ref[...] = f0
@@ -107,7 +106,8 @@
     x = halo(x, "gy", 3, CH)
     x = halo(x, "gx", 2, RH)
     hp, wp = h + 2 * RH, w + 2 * CH
-    x = jnp.transpose(x, (1, 2, 3, 0)).reshape(sl, hp * wp, e)
+    bfull = jnp.einsum("esij,er->sijr", x, kb, preferred_element_type=jnp.float32)
+    bfull = bfull.reshape(sl, hp * wp, kb.shape[1])
     r = kernel.shape[1]
 
     gi = lax.axis_index("gx")
@@ -120,14 +120,13 @@
 
     rows = TR + 2 * RH
     nt = h // TR
-    flops = 2 * sl * nt * rows * wp * r * (e + 2 * r)
+    flops = 2 * sl * nt * rows * wp * r * 2 * r
     out = pl.pallas_call(
         functools.partial(fit_kernel, wp),
         out_shape=jax.ShapeDtypeStruct((sl, h, w, r), jnp.float32),
         grid=(sl, nt),
         in_specs=[
-            pl.BlockSpec((1, hp * wp, e), lambda s, t: (s, 0, 0)),
-            pl.BlockSpec((e, r), lambda s, t: (0, 0)),
+            pl.BlockSpec((1, hp * wp, r), lambda s, t: (s, 0, 0)),
             pl.BlockSpec((r, r), lambda s, t: (0, 0)),
             pl.BlockSpec((1, r), lambda s, t: (0, 0)),
             pl.BlockSpec((1, r), lambda s, t: (0, 0)),
@@ -144,13 +143,13 @@
         ],
         compiler_params=pltpu.CompilerParams(
             dimension_semantics=("arbitrary", "arbitrary"),
-            vmem_limit_bytes=48 * 1024 * 1024,
+            vmem_limit_bytes=60 * 1024 * 1024,
         ),
         cost_estimate=pl.CostEstimate(
             flops=flops, transcendentals=0,
-            bytes_accessed=sl * (hp * wp * e * 2 + h * w * r * 4),
+            bytes_accessed=sl * (hp * wp * r * 4 + h * w * r * 4),
         ),
-    )(x, kb, g3, step[None, :], lam[None, :], cm, rm)
+    )(bfull, g3, step[None, :], lam[None, :], cm, rm)
     return out
 
 

time: 151 us -> 175 us (1.16)
  the two profiles are of different devices: /device:TPU:1 before, /device:TPU:42 now
where the time goes in v4:
time: 175 us; the launch traced here: 174 us
  Pallas kernels  52 us (30%)
  local copies, waits for them, and re-layouts  49.4 us (28%)
  waiting for transfers between devices  36.9 us (21%)
  starting transfers between devices  20.7 us (12%)
  matrix products  12.6 us (7%)
  other arithmetic  2.44 us (1%)
    pallas_call x1, Pallas kernels, per_device(): pl.pallas_call(functools.partial(fit_kernel, wp), out_shape=jax.ShapeDtyp...  52 us
    all_to_all x1, waiting for transfers between devices, per_device(): x = lax.all_to_all(images, 'gy', split_axis=3, concat_axis=0, tiled=True)  27.1 us
    slice x2, local copies, waits for them, and re-layouts, halo(): lax.slice_in_dim(cells, cells.shape[dim] - width, cells.shape[dim], axis=...  13.6 us
    dot_general x1, matrix products, per_device(): jnp.einsum('esij,er->sijr', x, kb, preferred_element_type=jnp.float32)  12.1 us
    ppermute x2, starting transfers between devices, halo(): lax.ppermute(head, axis, [(i + 1, i) for i in range(count - 1)])  7.62 us
    ppermute x1, local copies, waits for them, and re-layouts, halo(): lax.ppermute(head, axis, [(i + 1, i) for i in range(count - 1)])  7.47 us
    ppermute x1, local copies, waits for them, and re-layouts, halo(): lax.ppermute(tail, axis, [(i, i + 1) for i in range(count - 1)])  7.41 us
    all_to_all x1, starting transfers between devices, per_device(): x = lax.all_to_all(images, 'gy', split_axis=3, concat_axis=0, tiled=True)  7.35 us
  transfers between devices with their start and end apart: 5, of which 3 were waited for; matrix products, arithmetic and copies ran while one was open for 6% of the time, Pallas kernels for 0%

profile of v4, /device:TPU:42, one launch (start us, length us, event | category | flops | bytes accessed | tf_op | source)
XLA Modules:
  0.0 174.2 jit_solution(8440383037022323412)
XLA Ops:
  0.0 0.0 copy-start
  0.0 6.2 %copy.9 = bf16[4,2,128,1024]{2,1,0,3:T(2,128)(2,1)} copy(bf16[4,2,128,1024]{3,2,1,0:T(8,128)(2,1)} %param.3) | data formatting | bytes 4194304 | tf_op args[0]
  6.2 7.3 %all-to-all-start = ((bf16[4,2,128,1024]{2,1,0,3:T(2,128)(2,1)}), bf16[4,2,128,1024]{2,1,0,3:T(2,128)(2,1)}, u32[]{:S(2)}, u32[]{:S(2)}) async-start(bf16[4,2,128,1024]{2,1,0,3:T(2,128)(2,1)} %copy.9), calls=%async_computation | async-start | bytes 4194304 | tf_op jit(solution)/shard_map/all_to_all | solution.py:104
  13.5 0.0 copy-done
  13.5 0.1 multiply_reduce_fusion
  13.6 0.5 fusion.24
  14.2 27.1 %all-to-all-done = bf16[4,2,128,1024]{2,1,0,3:T(2,128)(2,1)} async-done(((bf16[4,2,128,1024]{2,1,0,3:T(2,128)(2,1)}), bf16[4,2,128,1024]{2,1,0,3:T(2,128)(2,1)}, u32[]{:S(2)}, u32[]{:S(2)}) %all-to-all-start) | async-done | bytes 2097184 | tf_op jit(solution)/shard_map/all_to_all | solution.py:104
  41.3 1.9 %copy.10 = bf16[4,2,128,1024]{2,3,1,0:T(8,128)(2,1)S(1)} copy(bf16[4,2,128,1024]{2,1,0,3:T(2,128)(2,1)} %all-to-all-done) | data formatting | bytes 4194304 | tf_op jit(solution)/shard_map/all_to_all | solution.py:104
  43.1 5.3 %copy.11 = bf16[16,4,2,128,64]{4,1,0,3,2:T(4,128)(2,1)} copy(bf16[16,4,2,128,64]{3,4,0,2,1:T(8,128)(2,1)S(1)} %bitcast.16) | data formatting | bytes 4194304 | tf_op jit(solution)/shard_map/all_to_all | solution.py:104
  48.4 7.4 %fusion.23 = (bf16[64,2,128,4]{3,0,2,1:T(8,128)(2,1)}, bf16[64,2,128,4]{3,0,2,1:T(8,128)(2,1)}) fusion(bf16[64,2,128,64]{3,0,2,1:T(8,128)(2,1)} %bitcast.12), kind=kLoop, calls=%fused_computation.30 | loop fusion | bytes 524288 | tf_op jit(solution)/shard_map/slice | solution.py:31
  55.7 0.0 copy-start.1
  55.7 6.2 %copy.12 = bf16[64,2,128,4]{2,0,3,1:T(8,128)(2,1)S(1)} copy(bf16[64,2,128,4]{3,0,2,1:T(8,128)(2,1)} %get-tuple-element.9) | data formatting | bytes 262144 | tf_op jit(solution)/shard_map/slice | solution.py:31
  61.9 6.2 %copy.13 = bf16[64,2,128,4]{2,0,3,1:T(8,128)(2,1)S(1)} copy(bf16[64,2,128,4]{3,0,2,1:T(8,128)(2,1)} %get-tuple-element.10) | data formatting | bytes 262144 | tf_op jit(solution)/shard_map/slice | solution.py:30
  68.2 5.6 %collective-permute-start.1 = (bf16[64,2,128,4]{2,0,3,1:T(8,128)(2,1)S(1)}, bf16[64,2,128,4]{2,0,3,1:T(8,128)(2,1)S(1)}, u32[]{:S(2)}, u32[]{:S(2)}) collective-permute-start(bf16[64,2,128,4]{2,0,3,1:T(8,128)(2,1)S(1)} %copy.13), channel_id=1, source_target_pairs={{1,0},{2,1},{3,2},{4,3},{5,4},{6,5},{7,6},{8,7},{9,8},{10,9},{11,1... | collective-permute-start | bytes 393224 | tf_op jit(solution)/shard_map/ppermute | solution.py:36
  73.8 1.9 %collective-permute-start = (bf16[64,2,128,4]{2,0,3,1:T(8,128)(2,1)S(1)}, bf16[64,2,128,4]{2,0,3,1:T(8,128)(2,1)S(1)}, u32[]{:S(2)}, u32[]{:S(2)}) collective-permute-start(bf16[64,2,128,4]{2,0,3,1:T(8,128)(2,1)S(1)} %copy.12), channel_id=1, source_target_pairs={{0,1},{1,2},{2,3},{3,4},{4,5},{5,6},{6,7},{7,8},{8,9},{9,10},{10,1... | collective-permute-start | bytes 393224 | tf_op jit(solution)/shard_map/ppermute | solution.py:34
  75.7 0.0 copy-done.1
  75.7 0.6 add_divide_fusion
  76.3 0.6 and_convert_fusion.rm_ref
  76.9 5.6 %collective-permute-done = bf16[64,2,128,4]{2,0,3,1:T(8,128)(2,1)S(1)} collective-permute-done((bf16[64,2,128,4]{2,0,3,1:T(8,128)(2,1)S(1)}, bf16[64,2,128,4]{2,0,3,1:T(8,128)(2,1)S(1)}, u32[]{:S(2)}, u32[]{:S(2)}) %collective-permute-start) | collective-permute-done | bytes 131104 | tf_op jit(solution)/shard_map/ppermute | solution.py:34
  82.5 7.4 %copy.14 = bf16[64,2,128,4]{3,0,2,1:T(8,128)(2,1)} copy(bf16[64,2,128,4]{2,0,3,1:T(8,128)(2,1)S(1)} %collective-permute-done) | data formatting | bytes 262144 | tf_op jit(solution)/shard_map/ppermute | solution.py:34
  89.9 0.0 collective-permute-done.1
  89.9 7.5 %copy.15 = bf16[64,2,128,4]{3,0,2,1:T(8,128)(2,1)} copy(bf16[64,2,128,4]{2,0,3,1:T(8,128)(2,1)S(1)} %collective-permute-done.1) | data formatting | bytes 262144 | tf_op jit(solution)/shard_map/ppermute | solution.py:36
  97.4 1.1 pad_maximum_fusion.2
  98.5 3.8 %collective-permute-start.2 = (bf16[64,2,2,72]{3,0,2,1:T(8,128)(2,1)S(1)}, bf16[64,2,2,72]{3,0,2,1:T(8,128)(2,1)S(1)}, u32[]{:S(2)}, u32[]{:S(2)}) collective-permute-start(bf16[64,2,2,72]{3,0,2,1:T(8,128)(2,1)S(1)} %get-tuple-element.7), channel_id=1, source_target_pairs={{0,16},{16,32},{32,48},{48,64},{64,80},{80,96},{96,112},{1,17},{17... | collective-permute-start | bytes 110600 | tf_op jit(solution)/shard_map/ppermute | solution.py:34
  102.4 2.0 %collective-permute-start.3 = (bf16[64,2,2,72]{3,0,2,1:T(8,128)(2,1)S(1)}, bf16[64,2,2,72]{3,0,2,1:T(8,128)(2,1)S(1)}, u32[]{:S(2)}, u32[]{:S(2)}) collective-permute-start(bf16[64,2,2,72]{3,0,2,1:T(8,128)(2,1)S(1)} %get-tuple-element.8), channel_id=1, source_target_pairs={{16,0},{32,16},{48,32},{64,48},{80,64},{96,80},{112,96},{17,1},{33... | collective-permute-start | bytes 110600 | tf_op jit(solution)/shard_map/ppermute | solution.py:36
  104.4 0.8 copy.16.g3_ref
  105.1 0.0 collective-permute-done.2
  105.1 4.3 %collective-permute-done.3 = bf16[64,2,2,72]{3,0,2,1:T(8,128)(2,1)S(1)} collective-permute-done((bf16[64,2,2,72]{3,0,2,1:T(8,128)(2,1)S(1)}, bf16[64,2,2,72]{3,0,2,1:T(8,128)(2,1)S(1)}, u32[]{:S(2)}, u32[]{:S(2)}) %collective-permute-start.3) | collective-permute-done | bytes 36896 | tf_op jit(solution)/shard_map/ppermute | solution.py:36
  109.4 12.1 %fusion = f32[2,132,72,256]{3,2,1,0:T(8,128)} fusion(bf16[64,2,2,72]{3,0,2,1:T(8,128)(2,1)S(1)} %collective-permute-done.3, bf16[64,2,128,4]{3,0,2,1:T(8,128)(2,1)} %copy.15, bf16[64,2,128,64]{3,0,2,1:T(8,128)(2,1)} %bitcast.14, bf16[64,2,128,4]{3,0,2,1:T(8,128)(2,1)} %copy.14, bf16[64,2,2,72]{3,0,2,1:T(8,128)(2,1)S(1)} %collective-permute-done.2, ...), kind=kOutput, calls=%fused_computation | convolution fusion | flops 635068416 | bytes 21899520 | tf_op jit(solution)/shard_map/esij,er->sijr/dot_general | solution.py:109
  121.5 0.7 broadcast_in_dim.8.cm_ref
  122.2 52.0 %shard_map.37 = f32[2,128,64,256]{3,2,1,0:T(8,128)} custom-call(f32[2,9504,256]{2,1,0:T(8,128)} %bitcast.15, bf16[256,256]{1,0:T(8,128)(2,1)} %copy.16.g3_ref, f32[1,256]{1,0:T(1,128)} %bitcast.17, f32[1,256]{1,0:T(1,128)} %bitcast.18, f32[72,256]{1,0:T(8,128)} %broadcast_in_dim.8.cm_ref, f32[132]{0:T(256)} %and_convert_fusion.rm_ref), custom_call_target="tpu_custom_call" | custom-call | flops 6039797760 | bytes 36241408 | tf_op jit(solution)/shard_map/pallas_call | solution.py:124
  (3 shorter events, 0.0 us)
Async XLA Ops:
  0.0 13.5 %copy-start = (f32[256]{0:T(256)S(1)}, f32[256]{0:T(256)}, u32[]{:S(2)}) copy-start(f32[256]{0:T(256)} %param.4) | copy-start | bytes 3076
  6.2 35.1 %all-to-all-start = ((bf16[4,2,128,1024]{2,1,0,3:T(2,128)(2,1)}), bf16[4,2,128,1024]{2,1,0,3:T(2,128)(2,1)}, u32[]{:S(2)}, u32[]{:S(2)}) async-start(bf16[4,2,128,1024]{2,1,0,3:T(2,128)(2,1)} %copy.9), calls=%async_computation | async-start | bytes 4194304 | tf_op jit(solution)/shard_map/all_to_all | solution.py:104
  55.7 20.0 %copy-start.1 = (f32[256]{0:T(256)S(1)}, f32[256]{0:T(256)}, u32[]{:S(2)}) copy-start(f32[256]{0:T(256)} %param.5) | copy-start | bytes 3076
  68.2 21.7 %collective-permute-start.1 = (bf16[64,2,128,4]{2,0,3,1:T(8,128)(2,1)S(1)}, bf16[64,2,128,4]{2,0,3,1:T(8,128)(2,1)S(1)}, u32[]{:S(2)}, u32[]{:S(2)}) collective-permute-start(bf16[64,2,128,4]{2,0,3,1:T(8,128)(2,1)S(1)} %copy.13), channel_id=1, source_target_pairs={{1,0},{2,1},{3,2},{4,3},{5,4},{6,5},{7,6},{8,7},{9,8},{10,9},{11,1... | collective-permute-start | bytes 393224 | tf_op jit(solution)/shard_map/ppermute | solution.py:36
  73.8 8.7 %collective-permute-start = (bf16[64,2,128,4]{2,0,3,1:T(8,128)(2,1)S(1)}, bf16[64,2,128,4]{2,0,3,1:T(8,128)(2,1)S(1)}, u32[]{:S(2)}, u32[]{:S(2)}) collective-permute-start(bf16[64,2,128,4]{2,0,3,1:T(8,128)(2,1)S(1)} %copy.12), channel_id=1, source_target_pairs={{0,1},{1,2},{2,3},{3,4},{4,5},{5,6},{6,7},{7,8},{8,9},{9,10},{10,1... | collective-permute-start | bytes 393224 | tf_op jit(solution)/shard_map/ppermute | solution.py:34
  98.5 6.6 %collective-permute-start.2 = (bf16[64,2,2,72]{3,0,2,1:T(8,128)(2,1)S(1)}, bf16[64,2,2,72]{3,0,2,1:T(8,128)(2,1)S(1)}, u32[]{:S(2)}, u32[]{:S(2)}) collective-permute-start(bf16[64,2,2,72]{3,0,2,1:T(8,128)(2,1)S(1)} %get-tuple-element.7), channel_id=1, source_target_pairs={{0,16},{16,32},{32,48},{48,64},{64,80},{80,96},{96,112},{1,17},{17... | collective-permute-start | bytes 110600 | tf_op jit(solution)/shard_map/ppermute | solution.py:34
  102.4 7.1 %collective-permute-start.3 = (bf16[64,2,2,72]{3,0,2,1:T(8,128)(2,1)S(1)}, bf16[64,2,2,72]{3,0,2,1:T(8,128)(2,1)S(1)}, u32[]{:S(2)}, u32[]{:S(2)}) collective-permute-start(bf16[64,2,2,72]{3,0,2,1:T(8,128)(2,1)S(1)} %get-tuple-element.8), channel_id=1, source_target_pairs={{16,0},{32,16},{48,32},{64,48},{80,64},{96,80},{112,96},{17,1},{33... | collective-permute-start | bytes 110600 | tf_op jit(solution)/shard_map/ppermute | solution.py:36

commit v5 on v3

--- a/solution.py
+++ b/solution.py
@@ -11,7 +11,7 @@
 ITERS = 3
 RH = 2
 CH = 4
-TR = 16
+TR = 32
 
 
 def kernel_parts(rates, smoothing):

time: 151 us -> 148 us (0.980)
  Pallas kernels: 49.2 us -> 45.2 us
    pallas_call x1, Pallas kernels: 49.2 us -> 45.2 us  [per_device(): pl.pallas_call(functools.partial(fit_kernel, wp), out_shape=jax.ShapeDtyp...]
where the time goes in v5:
time: 148 us; the launch traced here: 146 us
  Pallas kernels  45.2 us (31%)
  waiting for transfers between devices  34.7 us (23%)
  local copies, waits for them, and re-layouts  32 us (22%)
  starting transfers between devices  21.6 us (15%)
  other arithmetic  11.3 us (8%)
    pallas_call x1, Pallas kernels, per_device(): pl.pallas_call(functools.partial(fit_kernel, wp), out_shape=jax.ShapeDtyp...  45.2 us
    all_to_all x1, waiting for transfers between devices, per_device(): x = lax.all_to_all(images, 'gy', split_axis=3, concat_axis=0, tiled=True)  27.7 us
    transpose x1, local copies, waits for them, and re-layouts, per_device(): x = jnp.transpose(x, (1, 2, 3, 0)).reshape(sl, hp * wp, e)  11 us
    transpose x1, other arithmetic, per_device(): x = jnp.transpose(x, (1, 2, 3, 0)).reshape(sl, hp * wp, e)  9.5 us
    all_to_all x1, starting transfers between devices, per_device(): x = lax.all_to_all(images, 'gy', split_axis=3, concat_axis=0, tiled=True)  9.3 us
    ppermute x2, starting transfers between devices, halo(): lax.ppermute(tail, axis, [(i, i + 1) for i in range(count - 1)])  9.06 us
    unnamed x7, local copies, waits for them, and re-layouts  8.55 us
    ppermute x2, waiting for transfers between devices, halo(): lax.ppermute(head, axis, [(i + 1, i) for i in range(count - 1)])  5.81 us
  transfers between devices with their start and end apart: 5, of which 3 were waited for; matrix products, arithmetic and copies ran while one was open for 2% of the time, Pallas kernels for 0%

profile of v5, /device:TPU:1, one launch (start us, length us, event | category | flops | bytes accessed | tf_op | source)
XLA Modules:
  0.0 145.5 jit_solution(7451509833289119396)
XLA Ops:
  0.0 0.0 copy-start.1
  0.0 6.2 %copy.10 = bf16[4,2,128,1024]{2,1,0,3:T(2,128)(2,1)} copy(bf16[4,2,128,1024]{3,2,1,0:T(8,128)(2,1)} %param.3) | data formatting | bytes 4194304 | tf_op args[0]
  6.2 9.3 %all-to-all-start = ((bf16[4,2,128,1024]{2,1,0,3:T(2,128)(2,1)}), bf16[4,2,128,1024]{2,1,0,3:T(2,128)(2,1)S(1)}, u32[]{:S(2)}, u32[]{:S(2)}) async-start(bf16[4,2,128,1024]{2,1,0,3:T(2,128)(2,1)} %copy.10), calls=%async_computation | async-start | bytes 4194304 | tf_op jit(solution)/shard_map/all_to_all | solution.py:105
  15.5 0.0 copy-start.2
  15.5 0.0 copy-done.1
  15.5 0.1 multiply_reduce_fusion
  15.6 0.1 fusion.3.kb_ref
  15.7 0.5 fusion.9
  16.2 27.7 %all-to-all-done = bf16[4,2,128,1024]{2,1,0,3:T(2,128)(2,1)S(1)} async-done(((bf16[4,2,128,1024]{2,1,0,3:T(2,128)(2,1)}), bf16[4,2,128,1024]{2,1,0,3:T(2,128)(2,1)S(1)}, u32[]{:S(2)}, u32[]{:S(2)}) %all-to-all-start) | async-done | bytes 2097184 | tf_op jit(solution)/shard_map/all_to_all | solution.py:105
  43.9 0.3 copy.11
  44.2 0.2 copy.12
  44.4 0.1 fusion.8
  44.5 5.1 %collective-permute-start = (bf16[64,2,128,4]{2,3,1,0:T(4,128)(2,1)S(1)}, bf16[64,2,128,4]{2,3,1,0:T(4,128)(2,1)S(1)}, u32[]{:S(2)}, u32[]{:S(2)}) collective-permute-start(bf16[64,2,128,4]{2,3,1,0:T(4,128)(2,1)S(1)} %get-tuple-element.9), channel_id=1, source_target_pairs={{0,1},{1,2},{2,3},{3,4},{4,5},{5,6},{6,7},{7,8},{8,9},{9,10},{10,1... | collective-permute-start | bytes 393224 | tf_op jit(solution)/shard_map/ppermute | solution.py:34
  49.6 1.9 %collective-permute-start.1 = (bf16[64,2,128,4]{2,3,1,0:T(4,128)(2,1)S(1)}, bf16[64,2,128,4]{2,3,1,0:T(4,128)(2,1)S(1)}, u32[]{:S(2)}, u32[]{:S(2)}) collective-permute-start(bf16[64,2,128,4]{2,3,1,0:T(4,128)(2,1)S(1)} %get-tuple-element.10), channel_id=1, source_target_pairs={{1,0},{2,1},{3,2},{4,3},{5,4},{6,5},{7,6},{8,7},{9,8},{10,9},{11,1... | collective-permute-start | bytes 393224 | tf_op jit(solution)/shard_map/ppermute | solution.py:36
  51.6 0.0 copy-done.2
  51.6 0.0 collective-permute-done
  51.6 5.8 %collective-permute-done.1 = bf16[64,2,128,4]{2,3,1,0:T(4,128)(2,1)S(1)} collective-permute-done((bf16[64,2,128,4]{2,3,1,0:T(4,128)(2,1)S(1)}, bf16[64,2,128,4]{2,3,1,0:T(4,128)(2,1)S(1)}, u32[]{:S(2)}, u32[]{:S(2)}) %collective-permute-start.1) | collective-permute-done | bytes 131104 | tf_op jit(solution)/shard_map/ppermute | solution.py:36
  57.4 1.6 %pad_maximum_fusion = bf16[64,2,128,72]{2,3,1,0:T(8,128)(2,1)S(1)} fusion(bf16[64,2,128,4]{2,3,1,0:T(4,128)(2,1)S(1)} %collective-permute-done.1, bf16[64,2,128,64]{2,3,1,0:T(8,128)(2,1)S(1)} %bitcast.13, bf16[64,2,128,4]{2,3,1,0:T(4,128)(2,1)S(1)} %collective-permute-done), kind=kLoop, calls=%fused_computation.1 | loop fusion | flops 7077888 | bytes 4718592 | tf_op jit(solution)/shard_map/concatenate | solution.py:32
  59.0 3.0 %fusion.7 = (bf16[64,2,2,72]{2,3,1,0:T(8,128)(2,1)}, bf16[64,2,2,72]{2,3,1,0:T(8,128)(2,1)}) fusion(bf16[64,2,128,72]{2,3,1,0:T(8,128)(2,1)S(1)} %pad_maximum_fusion), kind=kLoop, calls=%fused_computation.14 | loop fusion | bytes 147456 | tf_op jit(solution)/shard_map/slice | solution.py:31
  62.0 2.3 %copy.13 = bf16[64,2,2,72]{3,0,2,1:T(8,128)(2,1)S(1)} copy(bf16[64,2,2,72]{2,3,1,0:T(8,128)(2,1)} %get-tuple-element.7) | data formatting | bytes 73728 | tf_op jit(solution)/shard_map/slice | solution.py:31
  64.3 2.3 %copy.14 = bf16[64,2,2,72]{3,0,2,1:T(8,128)(2,1)S(1)} copy(bf16[64,2,2,72]{2,3,1,0:T(8,128)(2,1)} %get-tuple-element.8) | data formatting | bytes 73728 | tf_op jit(solution)/shard_map/slice | solution.py:30
  66.5 1.3 collective-permute-start.3
  67.8 4.0 %collective-permute-start.2 = (bf16[64,2,2,72]{3,0,2,1:T(8,128)(2,1)S(1)}, bf16[64,2,2,72]{3,0,2,1:T(8,128)(2,1)S(1)}, u32[]{:S(2)}, u32[]{:S(2)}) collective-permute-start(bf16[64,2,2,72]{3,0,2,1:T(8,128)(2,1)S(1)} %copy.13), channel_id=1, source_target_pairs={{0,16},{16,32},{32,48},{48,64},{64,80},{80,96},{96,112},{1,17},{17... | collective-permute-start | bytes 110600 | tf_op jit(solution)/shard_map/ppermute | solution.py:34
  71.9 0.1 copy.18.g3_ref
  72.0 1.2 collective-permute-done.2
  73.2 2.1 %copy.15 = bf16[64,2,2,72]{2,3,1,0:T(8,128)(2,1)} copy(bf16[64,2,2,72]{3,0,2,1:T(8,128)(2,1)S(1)} %collective-permute-done.2) | data formatting | bytes 73728 | tf_op jit(solution)/shard_map/ppermute | solution.py:34
  75.2 0.0 collective-permute-done.3
  75.2 2.1 %copy.16 = bf16[64,2,2,72]{2,3,1,0:T(8,128)(2,1)} copy(bf16[64,2,2,72]{3,0,2,1:T(8,128)(2,1)S(1)} %collective-permute-done.3) | data formatting | bytes 73728 | tf_op jit(solution)/shard_map/ppermute | solution.py:36
  77.3 9.5 %maximum_bitcast_fusion = bf16[2,132,72,64]{1,2,0,3:T(8,128)(2,1)} fusion(bf16[64,2,2,72]{2,3,1,0:T(8,128)(2,1)} %copy.16, bf16[64,2,128,4]{2,3,1,0:T(4,128)(2,1)S(1)} %collective-permute-done.1, bf16[64,2,128,64]{2,3,1,0:T(8,128)(2,1)S(1)} %bitcast.14, bf16[64,2,128,4]{2,3,1,0:T(4,128)(2,1)S(1)} %collective-permute-done, bf16[64,2,2,72]{2,3,1,0:T(8,128)(2,1)} %copy.15), kind=kLoop, calls=%fused_computation | loop fusion | flops 12165120 | bytes 4866048 | tf_op jit(solution)/shard_map/transpose | solution.py:110
  86.8 11.0 %copy.17 = bf16[2,132,72,64]{3,2,1,0:T(8,128)(2,1)} copy(bf16[2,132,72,64]{1,2,0,3:T(8,128)(2,1)} %maximum_bitcast_fusion) | data formatting | bytes 4866048 | tf_op jit(solution)/shard_map/transpose | solution.py:110
  97.8 0.1 broadcast_in_dim.8.cm_ref
  97.9 0.0 copy-start
  97.9 2.4 %copy-done = bf16[2,132,72,64]{3,2,1,0:T(8,128)(2,1)S(1)} copy-done((bf16[2,132,72,64]{3,2,1,0:T(8,128)(2,1)S(1)}, bf16[2,132,72,64]{3,2,1,0:T(8,128)(2,1)}, u32[]{:S(2)}) %copy-start) | copy-done | bytes 2433048
  100.3 45.2 %shard_map.37 = f32[2,128,64,256]{3,2,1,0:T(8,128)} custom-call(bf16[2,9504,64]{2,1,0:T(8,128)(2,1)S(1)} %bitcast.9, bf16[64,256]{1,0:T(8,128)(2,1)S(1)} %fusion.3.kb_ref, bf16[256,256]{1,0:T(8,128)(2,1)S(1)} %copy.18.g3_ref, f32[1,256]{1,0:T(1,128)S(1)} %bitcast.10, f32[1,256]{1,0:T(1,128)S(1)} %bitcast.11, f32[72,256]{1,0:T(8,128)S(1)} %broadcast_in_dim.8.cm_ref, ...), custom_call_target="tpu_custom_call" | custom-call | flops 6115295232 | bytes 19210240 | tf_op jit(solution)/shard_map/pallas_call | solution.py:124
  (5 shorter events, 0.0 us)
Async XLA Ops:
  0.0 15.5 %copy-start.1 = (f32[256]{0:T(256)S(1)}, f32[256]{0:T(256)}, u32[]{:S(2)}) copy-start(f32[256]{0:T(256)} %param.4) | copy-start | bytes 3076
  6.2 37.7 %all-to-all-start = ((bf16[4,2,128,1024]{2,1,0,3:T(2,128)(2,1)}), bf16[4,2,128,1024]{2,1,0,3:T(2,128)(2,1)S(1)}, u32[]{:S(2)}, u32[]{:S(2)}) async-start(bf16[4,2,128,1024]{2,1,0,3:T(2,128)(2,1)} %copy.10), calls=%async_computation | async-start | bytes 4194304 | tf_op jit(solution)/shard_map/all_to_all | solution.py:105
  15.5 36.1 %copy-start.2 = (f32[256]{0:T(256)S(1)}, f32[256]{0:T(256)}, u32[]{:S(2)}) copy-start(f32[256]{0:T(256)} %param.5) | copy-start | bytes 3076
  44.5 7.1 %collective-permute-start = (bf16[64,2,128,4]{2,3,1,0:T(4,128)(2,1)S(1)}, bf16[64,2,128,4]{2,3,1,0:T(4,128)(2,1)S(1)}, u32[]{:S(2)}, u32[]{:S(2)}) collective-permute-start(bf16[64,2,128,4]{2,3,1,0:T(4,128)(2,1)S(1)} %get-tuple-element.9), channel_id=1, source_target_pairs={{0,1},{1,2},{2,3},{3,4},{4,5},{5,6},{6,7},{7,8},{8,9},{9,10},{10,1... | collective-permute-start | bytes 393224 | tf_op jit(solution)/shard_map/ppermute | solution.py:34
  49.6 7.8 %collective-permute-start.1 = (bf16[64,2,128,4]{2,3,1,0:T(4,128)(2,1)S(1)}, bf16[64,2,128,4]{2,3,1,0:T(4,128)(2,1)S(1)}, u32[]{:S(2)}, u32[]{:S(2)}) collective-permute-start(bf16[64,2,128,4]{2,3,1,0:T(4,128)(2,1)S(1)} %get-tuple-element.10), channel_id=1, source_target_pairs={{1,0},{2,1},{3,2},{4,3},{5,4},{6,5},{7,6},{8,7},{9,8},{10,9},{11,1... | collective-permute-start | bytes 393224 | tf_op jit(solution)/shard_map/ppermute | solution.py:36
  66.5 8.7 %collective-permute-start.3 = (bf16[64,2,2,72]{3,0,2,1:T(8,128)(2,1)S(1)}, bf16[64,2,2,72]{3,0,2,1:T(8,128)(2,1)S(1)}, u32[]{:S(2)}, u32[]{:S(2)}) collective-permute-start(bf16[64,2,2,72]{3,0,2,1:T(8,128)(2,1)S(1)} %copy.14), channel_id=1, source_target_pairs={{16,0},{32,16},{48,32},{64,48},{80,64},{96,80},{112,96},{17,1},{33... | collective-permute-start | bytes 110600 | tf_op jit(solution)/shard_map/ppermute | solution.py:36
  67.8 5.3 %collective-permute-start.2 = (bf16[64,2,2,72]{3,0,2,1:T(8,128)(2,1)S(1)}, bf16[64,2,2,72]{3,0,2,1:T(8,128)(2,1)S(1)}, u32[]{:S(2)}, u32[]{:S(2)}) collective-permute-start(bf16[64,2,2,72]{3,0,2,1:T(8,128)(2,1)S(1)} %copy.13), channel_id=1, source_target_pairs={{0,16},{16,32},{32,48},{48,64},{64,80},{80,96},{96,112},{1,17},{17... | collective-permute-start | bytes 110600 | tf_op jit(solution)/shard_map/ppermute | solution.py:34
  97.9 2.4 %copy-start = (bf16[2,132,72,64]{3,2,1,0:T(8,128)(2,1)S(1)}, bf16[2,132,72,64]{3,2,1,0:T(8,128)(2,1)}, u32[]{:S(2)}) copy-start(bf16[2,132,72,64]{3,2,1,0:T(8,128)(2,1)} %copy.17) | copy-start | bytes 7299076

commit v6 on v5

--- a/solution.py
+++ b/solution.py
@@ -102,11 +102,16 @@
     kb = kernel.astype(jnp.bfloat16)
     gh = gram.astype(jnp.bfloat16)
     g3 = gh
-    x = lax.all_to_all(images, "gy", split_axis=3, concat_axis=0, tiled=True)
-    e, sl, h, w = x.shape
-    x = halo(x, "gy", 3, CH)
-    x = halo(x, "gx", 2, RH)
+    ny = lax.axis_size("gy")
+    e = images.shape[0] * ny
+    sl, h = images.shape[1], images.shape[2]
+    w = images.shape[3] // ny
     hp, wp = h + 2 * RH, w + 2 * CH
+    x = halo(images, "gx", 2, RH)
+    x = jnp.pad(x, ((0, 0), (0, 0), (0, 0), (CH, CH)))
+    x = jnp.stack([x[..., j * w: j * w + wp] for j in range(ny)], axis=3)
+    x = lax.all_to_all(x, "gy", split_axis=3, concat_axis=0, tiled=True)
+    x = x.reshape(e, sl, hp, wp)
     x = jnp.transpose(x, (1, 2, 3, 0)).reshape(sl, hp * wp, e)
     r = kernel.shape[1]
 

time: 148 us -> 156 us (1.054)
  the two profiles are of different devices: /device:TPU:1 before, /device:TPU:83 now
where the time goes in v6:
time: 156 us; the launch traced here: 155 us
  waiting for transfers between devices  59.8 us (38%)
  Pallas kernels  45.2 us (29%)
  local copies, waits for them, and re-layouts  35.2 us (23%)
  starting transfers between devices  14.4 us (9%)
    all_to_all x1, waiting for transfers between devices, per_device(): x = lax.all_to_all(x, 'gy', split_axis=3, concat_axis=0, tiled=True)  59.8 us
    pallas_call x1, Pallas kernels, per_device(): pl.pallas_call(functools.partial(fit_kernel, wp), out_shape=jax.ShapeDtyp...  45.2 us
    unnamed x25, local copies, waits for them, and re-layouts  19.7 us
    all_to_all x1, starting transfers between devices, per_device(): x = lax.all_to_all(x, 'gy', split_axis=3, concat_axis=0, tiled=True)  8.23 us
    all_to_all x1, local copies, waits for them, and re-layouts, per_device(): x = lax.all_to_all(x, 'gy', split_axis=3, concat_axis=0, tiled=True)  6.72 us
    transpose x1, local copies, waits for them, and re-layouts, per_device(): x = jnp.transpose(x, (1, 2, 3, 0)).reshape(sl, hp * wp, e)  6.57 us
    ppermute x1, starting transfers between devices, halo(): lax.ppermute(tail, axis, [(i, i + 1) for i in range(count - 1)])  3.25 us
  transfers between devices with their start and end apart: 3, of which 1 were waited for; matrix products, arithmetic and copies ran while one was open for 3% of the time, Pallas kernels for 0%

profile of v6, /device:TPU:83, one launch (start us, length us, event | category | flops | bytes accessed | tf_op | source)
XLA Modules:
  0.0 155.5 jit_solution(16274165627842816191)
XLA Ops:
  0.0 1.0 fusion.25
  1.1 3.3 %collective-permute-start = (bf16[4,2,2,1024]{3,0,2,1:T(4,128)(2,1)S(1)}, bf16[4,2,2,1024]{3,0,2,1:T(4,128)(2,1)S(1)}, u32[]{:S(2)}, u32[]{:S(2)}) collective-permute-start(bf16[4,2,2,1024]{3,0,2,1:T(4,128)(2,1)S(1)} %copy.17), channel_id=1, source_target_pairs={{0,16},{16,32},{32,48},{48,64},{64,80},{80,96},{96,112},{1,17},{17... | collective-permute-start | bytes 98312 | tf_op jit(solution)/shard_map/ppermute | solution.py:34
  4.3 2.9 %collective-permute-start.1 = (bf16[4,2,2,1024]{3,0,2,1:T(4,128)(2,1)S(1)}, bf16[4,2,2,1024]{3,0,2,1:T(4,128)(2,1)S(1)}, u32[]{:S(2)}, u32[]{:S(2)}) collective-permute-start(bf16[4,2,2,1024]{3,0,2,1:T(4,128)(2,1)S(1)} %copy.18), channel_id=1, source_target_pairs={{16,0},{32,16},{48,32},{64,48},{80,64},{96,80},{112,96},{17,1},{33... | collective-permute-start | bytes 98312 | tf_op jit(solution)/shard_map/ppermute | solution.py:36
  7.3 0.0 collective-permute-done
  7.3 3.3 %constant_dynamic-update-slice_fusion.1 = bf16[4,2,132,1024]{3,0,2,1:T(4,128)(2,1)S(1)} fusion(bf16[4,2,132,1024]{3,0,2,1:T(4,128)(2,1)S(1)} %constant_dynamic-update-slice_fusion.2, bf16[4,2,128,1024]{3,2,1,0:T(8,128)(2,1)} %param.3), kind=kLoop, calls=%fused_computation.40 | loop fusion | bytes 4194304
  10.7 0.0 collective-permute-done.1
  10.7 0.9 fusion.1
  11.6 0.9 fusion.17
  12.6 0.9 fusion.16
  13.5 0.9 fusion.15
  14.4 0.9 fusion.14
  15.3 0.9 fusion.13
  16.3 0.9 fusion.12
  17.2 0.9 fusion.11
  18.1 0.9 fusion.10
  19.1 0.9 fusion.9
  20.0 0.9 fusion.8
  20.9 0.9 fusion.7
  21.8 0.9 fusion.6
  22.8 0.9 fusion.5
  23.7 0.9 fusion.4
  24.6 0.9 fusion.3
  25.6 0.0 copy-start.1
  25.6 0.0 copy-start.2
  25.6 8.2 %all-to-all-start = ((bf16[4,2,132,16,72]{4,0,2,1,3:T(4,128)(2,1)}), bf16[4,2,132,16,72]{4,0,2,1,3:T(4,128)(2,1)}, u32[]{:S(2)}, u32[]{:S(2)}) async-start(bf16[4,2,132,16,72]{4,0,2,1,3:T(4,128)(2,1)} %fusion.3), calls=%async_computation | async-start | bytes 8650752 | tf_op jit(solution)/shard_map/all_to_all | solution.py:113
  33.8 0.0 copy-done.1
  33.8 0.1 multiply_reduce_fusion
  33.9 0.5 fusion.26
  34.4 0.1 copy.15.g3_ref
  34.6 0.0 copy-done.2
  34.6 0.1 fusion.21.kb_ref
  34.7 59.8 %all-to-all-done = bf16[4,2,132,16,72]{4,0,2,1,3:T(4,128)(2,1)} async-done(((bf16[4,2,132,16,72]{4,0,2,1,3:T(4,128)(2,1)}), bf16[4,2,132,16,72]{4,0,2,1,3:T(4,128)(2,1)}, u32[]{:S(2)}, u32[]{:S(2)}) %all-to-all-start) | async-done | bytes 2433056 | tf_op jit(solution)/shard_map/all_to_all | solution.py:113
  94.5 6.7 %copy.13 = bf16[16,4,2,132,1,72]{5,1,0,3,2,4:T(4,128)(2,1)} copy(bf16[16,4,2,132,1,72]{5,1,3,2,0,4:T(4,128)(2,1)} %bitcast.17) | data formatting | bytes 4866048 | tf_op jit(solution)/shard_map/all_to_all | solution.py:113
  101.2 6.6 %copy.14 = bf16[2,132,72,64]{3,2,1,0:T(8,128)(2,1)} copy(bf16[2,132,72,64]{2,3,1,0:T(8,128)(2,1)} %bitcast.76) | data formatting | bytes 4866048 | tf_op jit(solution)/shard_map/transpose | solution.py:115
  107.8 0.1 broadcast_in_dim.8.cm_ref
  107.9 0.0 copy-start
  107.9 2.4 %copy-done = bf16[2,132,72,64]{3,2,1,0:T(8,128)(2,1)S(1)} copy-done((bf16[2,132,72,64]{3,2,1,0:T(8,128)(2,1)S(1)}, bf16[2,132,72,64]{3,2,1,0:T(8,128)(2,1)}, u32[]{:S(2)}) %copy-start) | copy-done | bytes 2433048
  110.3 45.2 %shard_map.37 = f32[2,128,64,256]{3,2,1,0:T(8,128)} custom-call(bf16[2,9504,64]{2,1,0:T(8,128)(2,1)S(1)} %bitcast.73, bf16[64,256]{1,0:T(8,128)(2,1)S(1)} %fusion.21.kb_ref, bf16[256,256]{1,0:T(8,128)(2,1)S(1)} %copy.15.g3_ref, f32[1,256]{1,0:T(1,128)S(1)} %bitcast.74, f32[1,256]{1,0:T(1,128)S(1)} %bitcast.75, f32[72,256]{1,0:T(8,128)S(1)} %broadcast_in_dim.8.cm_ref, ...), custom_call_target="tpu_custom_call" | custom-call | flops 6115295232 | bytes 19210240 | tf_op jit(solution)/shard_map/pallas_call | solution.py:129
  (9 shorter events, 0.1 us)
Async XLA Ops:
  1.1 6.2 %collective-permute-start = (bf16[4,2,2,1024]{3,0,2,1:T(4,128)(2,1)S(1)}, bf16[4,2,2,1024]{3,0,2,1:T(4,128)(2,1)S(1)}, u32[]{:S(2)}, u32[]{:S(2)}) collective-permute-start(bf16[4,2,2,1024]{3,0,2,1:T(4,128)(2,1)S(1)} %copy.17), channel_id=1, source_target_pairs={{0,16},{16,32},{32,48},{48,64},{64,80},{80,96},{96,112},{1,17},{17... | collective-permute-start | bytes 98312 | tf_op jit(solution)/shard_map/ppermute | solution.py:34
  4.3 6.3 %collective-permute-start.1 = (bf16[4,2,2,1024]{3,0,2,1:T(4,128)(2,1)S(1)}, bf16[4,2,2,1024]{3,0,2,1:T(4,128)(2,1)S(1)}, u32[]{:S(2)}, u32[]{:S(2)}) collective-permute-start(bf16[4,2,2,1024]{3,0,2,1:T(4,128)(2,1)S(1)} %copy.18), channel_id=1, source_target_pairs={{16,0},{32,16},{48,32},{64,48},{80,64},{96,80},{112,96},{17,1},{33... | collective-permute-start | bytes 98312 | tf_op jit(solution)/shard_map/ppermute | solution.py:36
  25.6 8.2 %copy-start.1 = (f32[256]{0:T(256)S(1)}, f32[256]{0:T(256)}, u32[]{:S(2)}) copy-start(f32[256]{0:T(256)} %param.4) | copy-start | bytes 3076
  25.6 9.0 %copy-start.2 = (f32[256]{0:T(256)S(1)}, f32[256]{0:T(256)}, u32[]{:S(2)}) copy-start(f32[256]{0:T(256)} %param.5) | copy-start | bytes 3076
  25.6 69.0 %all-to-all-start = ((bf16[4,2,132,16,72]{4,0,2,1,3:T(4,128)(2,1)}), bf16[4,2,132,16,72]{4,0,2,1,3:T(4,128)(2,1)}, u32[]{:S(2)}, u32[]{:S(2)}) async-start(bf16[4,2,132,16,72]{4,0,2,1,3:T(4,128)(2,1)} %fusion.3), calls=%async_computation | async-start | bytes 8650752 | tf_op jit(solution)/shard_map/all_to_all | solution.py:113
  107.9 2.4 %copy-start = (bf16[2,132,72,64]{3,2,1,0:T(8,128)(2,1)S(1)}, bf16[2,132,72,64]{3,2,1,0:T(8,128)(2,1)}, u32[]{:S(2)}) copy-start(bf16[2,132,72,64]{3,2,1,0:T(8,128)(2,1)} %copy.14) | copy-start | bytes 7299076

commit v7 on v6

--- a/solution.py
+++ b/solution.py
@@ -103,16 +103,20 @@
     gh = gram.astype(jnp.bfloat16)
     g3 = gh
     ny = lax.axis_size("gy")
-    e = images.shape[0] * ny
+    ee = images.shape[0]
+    e = ee * ny
     sl, h = images.shape[1], images.shape[2]
     w = images.shape[3] // ny
     hp, wp = h + 2 * RH, w + 2 * CH
     x = halo(images, "gx", 2, RH)
     x = jnp.pad(x, ((0, 0), (0, 0), (0, 0), (CH, CH)))
-    x = jnp.stack([x[..., j * w: j * w + wp] for j in range(ny)], axis=3)
-    x = lax.all_to_all(x, "gy", split_axis=3, concat_axis=0, tiled=True)
-    x = x.reshape(e, sl, hp, wp)
-    x = jnp.transpose(x, (1, 2, 3, 0)).reshape(sl, hp * wp, e)
+    mid = x[..., CH:CH + ny * w].reshape(ee, sl, hp, ny, w)
+    left = x[..., 0:ny * w].reshape(ee, sl, hp, ny, w)[..., :CH]
+    right = x[..., 2 * CH:2 * CH + ny * w].reshape(ee, sl, hp, ny, w)[..., w - CH:]
+    x = jnp.concatenate([left, mid, right], axis=4)
+    x = jnp.transpose(x, (0, 1, 3, 2, 4)).reshape(ee, sl, ny, hp * wp)
+    x = lax.all_to_all(x, "gy", split_axis=2, concat_axis=0, tiled=True)
+    x = jnp.transpose(x.reshape(e, sl, hp * wp), (1, 2, 0))
     r = kernel.shape[1]
 
     gi = lax.axis_index("gx")

time: 156 us -> 151 us (0.968)
  the two profiles are of different devices: /device:TPU:83 before, /device:TPU:1 now
where the time goes in v7:
time: 151 us; the launch traced here: 149 us
  local copies, waits for them, and re-layouts  46.7 us (31%)
  Pallas kernels  45.2 us (30%)
  waiting for transfers between devices  34.8 us (23%)
  starting transfers between devices  15.4 us (10%)
  other arithmetic  6.46 us (4%)
    pallas_call x1, Pallas kernels, per_device(): pl.pallas_call(functools.partial(fit_kernel, wp), out_shape=jax.ShapeDtyp...  45.2 us
    all_to_all x1, waiting for transfers between devices, per_device(): x = lax.all_to_all(x, 'gy', split_axis=2, concat_axis=0, tiled=True)  31.4 us
    reshape x2, local copies, waits for them, and re-layouts, per_device(): x = jnp.transpose(x, (0, 1, 3, 2, 4)).reshape(ee, sl, ny, hp * wp)  14.2 us
    all_to_all x1, starting transfers between devices, per_device(): x = lax.all_to_all(x, 'gy', split_axis=2, concat_axis=0, tiled=True)  9.74 us
    reshape x1, local copies, waits for them, and re-layouts, per_device(): left = x[..., 0:ny * w].reshape(ee, sl, hp, ny, w)[..., :CH]  5.96 us
    reshape x1, local copies, waits for them, and re-layouts, per_device(): x = jnp.transpose(x.reshape(e, sl, hp * wp), (1, 2, 0))  5.59 us
    slice x1, local copies, waits for them, and re-layouts, per_device(): left = x[..., 0:ny * w].reshape(ee, sl, hp, ny, w)[..., :CH]  4.5 us
    ppermute x1, starting transfers between devices, halo(): lax.ppermute(tail, axis, [(i, i + 1) for i in range(count - 1)])  4.37 us
  transfers between devices with their start and end apart: 3, of which 2 were waited for; matrix products, arithmetic and copies ran while one was open for 1% of the time, Pallas kernels for 0%

profile of v7, /device:TPU:1, one launch (start us, length us, event | category | flops | bytes accessed | tf_op | source)
XLA Modules:
  0.0 149.2 jit_solution(14876579572680896117)
XLA Ops:
  0.0 1.0 fusion.7
  1.0 4.4 %collective-permute-start = (bf16[4,2,2,1024]{3,2,1,0:T(2,128)(2,1)S(1)}, bf16[4,2,2,1024]{3,2,1,0:T(2,128)(2,1)S(1)}, u32[]{:S(2)}, u32[]{:S(2)}) collective-permute-start(bf16[4,2,2,1024]{3,2,1,0:T(2,128)(2,1)S(1)} %get-tuple-element.9), channel_id=1, source_target_pairs={{0,16},{16,32},{32,48},{48,64},{64,80},{80,96},{96,112},{1,17},{17... | collective-permute-start | bytes 98312 | tf_op jit(solution)/shard_map/ppermute | solution.py:34
  5.4 1.3 collective-permute-start.1
  6.7 0.0 collective-permute-done
  6.7 3.3 %collective-permute-done.1 = bf16[4,2,2,1024]{3,2,1,0:T(2,128)(2,1)S(1)} collective-permute-done((bf16[4,2,2,1024]{3,2,1,0:T(2,128)(2,1)S(1)}, bf16[4,2,2,1024]{3,2,1,0:T(2,128)(2,1)S(1)}, u32[]{:S(2)}, u32[]{:S(2)}) %collective-permute-start.1) | collective-permute-done | bytes 32800 | tf_op jit(solution)/shard_map/ppermute | solution.py:36
  10.1 2.3 %pad_maximum_fusion = bf16[4,2,132,1024]{3,2,1,0:T(8,128)(2,1)S(1)} fusion(bf16[4,2,2,1024]{3,2,1,0:T(2,128)(2,1)S(1)} %collective-permute-done.1, bf16[4,2,128,1024]{3,2,1,0:T(8,128)(2,1)} %param.3, bf16[4,2,2,1024]{3,2,1,0:T(2,128)(2,1)S(1)} %collective-permute-done), kind=kLoop, calls=%fused_computation.3 | loop fusion | flops 6488064 | bytes 4325376 | tf_op jit(solution)/shard_map/concatenate | solution.py:32
  12.4 4.1 %reshape.37 = bf16[4,2,132,16,64]{4,3,2,1,0:T(8,128)(2,1)} reshape(bf16[4,2,132,1024]{3,2,1,0:T(8,128)(2,1)S(1)} %pad_maximum_fusion) | data formatting | bytes 4325376 | tf_op jit(solution)/shard_map/reshape | solution.py:113
  16.5 4.5 %pad_slice_fusion.1 = (bf16[4,2,132,1024]{3,2,1,0:T(8,128)(2,1)}, bf16[4,2,132,1024]{3,2,1,0:T(8,128)(2,1)}) fusion(bf16[4,2,132,1024]{3,2,1,0:T(8,128)(2,1)S(1)} %pad_maximum_fusion), kind=kLoop, calls=%fused_computation.2 | loop fusion | bytes 6488064 | tf_op jit(solution)/shard_map/slice | solution.py:114
  21.0 0.0 copy-start.2
  21.0 6.0 %reshape.36 = bf16[4,2,132,16,64]{4,3,2,1,0:T(8,128)(2,1)} reshape(bf16[4,2,132,1024]{3,2,1,0:T(8,128)(2,1)} %get-tuple-element.7) | data formatting | bytes 4325376 | tf_op jit(solution)/shard_map/reshape | solution.py:114
  27.0 0.0 copy-done.2
  27.0 0.0 slice-start
  27.0 4.0 %reshape.38 = bf16[4,2,132,16,64]{4,3,2,1,0:T(8,128)(2,1)} reshape(bf16[4,2,132,1024]{3,2,1,0:T(8,128)(2,1)S(1)} %copy-done.2) | data formatting | bytes 4325376 | tf_op jit(solution)/shard_map/reshape | solution.py:115
  31.0 0.0 slice-start.1
  31.0 0.0 copy-start.1
  31.0 3.6 %slice.26 = bf16[4,2,132,16,4]{4,3,2,1,0:T(8,128)(2,1)S(1)} slice(bf16[4,2,132,16,64]{4,3,2,1,0:T(8,128)(2,1)} %reshape.38), slice={[0:4], [0:2], [0:132], [0:16], [60:64]} | slice | bytes 270336 | tf_op jit(solution)/shard_map/slice | solution.py:115
  34.6 0.0 slice-done
  34.6 0.0 slice-done.1
  34.6 1.2 copy-done.1
  35.8 3.9 %maximum_bitcast_fusion = bf16[4,2,16,132,72]{4,2,3,1,0:T(8,128)(2,1)S(1)} fusion(bf16[4,2,132,16,4]{4,3,2,1,0:T(8,128)(2,1)S(1)} %slice.26, bf16[4,2,132,16,64]{4,3,2,1,0:T(8,128)(2,1)S(1)} %bitcast.17, bf16[4,2,132,16,4]{4,3,2,1,0:T(8,128)(2,1)S(1)} %bitcast.18), kind=kLoop, calls=%fused_computation | loop fusion | flops 7299072 | bytes 4866048 | tf_op jit(solution)/shard_map/transpose | solution.py:117
  39.8 3.2 %copy.16 = bf16[4,2,16,132,72]{4,3,1,0,2:T(8,128)(2,1)} copy(bf16[4,2,16,132,72]{4,2,3,1,0:T(8,128)(2,1)S(1)} %maximum_bitcast_fusion) | data formatting | bytes 4866048 | tf_op jit(solution)/shard_map/reshape | solution.py:117
  43.0 0.0 copy-start.3
  43.0 10.9 %reshape.41 = bf16[4,2,16,9504]{3,1,0,2:T(2,128)(2,1)} reshape(bf16[4,2,16,132,72]{4,3,1,0,2:T(8,128)(2,1)} %copy.16) | data formatting | bytes 4866048 | tf_op jit(solution)/shard_map/reshape | solution.py:117
  53.9 0.0 copy-start.4
  53.9 9.7 %all-to-all-start = ((bf16[4,2,16,9504]{3,1,0,2:T(2,128)(2,1)}), bf16[4,2,16,9504]{3,1,0,2:T(2,128)(2,1)S(1)}, u32[]{:S(2)}, u32[]{:S(2)}) async-start(bf16[4,2,16,9504]{3,1,0,2:T(2,128)(2,1)} %reshape.41), calls=%async_computation | async-start | bytes 4915200 | tf_op jit(solution)/shard_map/all_to_all | solution.py:118
  63.7 0.0 copy-done.3
  63.7 0.1 multiply_reduce_fusion
  63.8 0.5 fusion.8
  64.3 0.1 copy.15.g3_ref
  64.5 0.0 copy-done.4
  64.5 0.1 fusion.3.kb_ref
  64.6 31.4 %all-to-all-done = bf16[4,2,16,9504]{3,1,0,2:T(2,128)(2,1)S(1)} async-done(((bf16[4,2,16,9504]{3,1,0,2:T(2,128)(2,1)}), bf16[4,2,16,9504]{3,1,0,2:T(2,128)(2,1)S(1)}, u32[]{:S(2)}, u32[]{:S(2)}) %all-to-all-start) | async-done | bytes 2433056 | tf_op jit(solution)/shard_map/all_to_all | solution.py:118
  96.0 5.6 %copy.14 = bf16[64,2,9504]{0,2,1:T(8,128)(2,1)} copy(bf16[64,2,9504]{2,1,0:T(2,128)(2,1)S(1)} %bitcast.19) | data formatting | bytes 4866048 | tf_op jit(solution)/shard_map/reshape | solution.py:119
  101.6 0.1 broadcast_in_dim.8.cm_ref
  101.6 0.0 copy-start
  101.6 2.4 %copy-done = bf16[64,2,9504]{0,2,1:T(8,128)(2,1)S(1)} copy-done((bf16[64,2,9504]{0,2,1:T(8,128)(2,1)S(1)}, bf16[64,2,9504]{0,2,1:T(8,128)(2,1)}, u32[]{:S(2)}) %copy-start) | copy-done | bytes 2433048
  104.0 45.2 %shard_map.37 = f32[2,128,64,256]{3,2,1,0:T(8,128)} custom-call(bf16[2,9504,64]{2,1,0:T(8,128)(2,1)S(1)} %bitcast.13, bf16[64,256]{1,0:T(8,128)(2,1)S(1)} %fusion.3.kb_ref, bf16[256,256]{1,0:T(8,128)(2,1)S(1)} %copy.15.g3_ref, f32[1,256]{1,0:T(1,128)S(1)} %bitcast.14, f32[1,256]{1,0:T(1,128)S(1)} %bitcast.15, f32[72,256]{1,0:T(8,128)S(1)} %broadcast_in_dim.8.cm_ref, ...), custom_call_target="tpu_custom_call" | custom-call | flops 6115295232 | bytes 19210240 | tf_op jit(solution)/shard_map/pallas_call | solution.py:133
  (6 shorter events, 0.0 us)
Async XLA Ops:
  1.0 5.7 %collective-permute-start = (bf16[4,2,2,1024]{3,2,1,0:T(2,128)(2,1)S(1)}, bf16[4,2,2,1024]{3,2,1,0:T(2,128)(2,1)S(1)}, u32[]{:S(2)}, u32[]{:S(2)}) collective-permute-start(bf16[4,2,2,1024]{3,2,1,0:T(2,128)(2,1)S(1)} %get-tuple-element.9), channel_id=1, source_target_pairs={{0,16},{16,32},{32,48},{48,64},{64,80},{80,96},{96,112},{1,17},{17... | collective-permute-start | bytes 98312 | tf_op jit(solution)/shard_map/ppermute | solution.py:34
  5.4 4.7 %collective-permute-start.1 = (bf16[4,2,2,1024]{3,2,1,0:T(2,128)(2,1)S(1)}, bf16[4,2,2,1024]{3,2,1,0:T(2,128)(2,1)S(1)}, u32[]{:S(2)}, u32[]{:S(2)}) collective-permute-start(bf16[4,2,2,1024]{3,2,1,0:T(2,128)(2,1)S(1)} %get-tuple-element.10), channel_id=1, source_target_pairs={{16,0},{32,16},{48,32},{64,48},{80,64},{96,80},{112,96},{17,1},{33... | collective-permute-start | bytes 98312 | tf_op jit(solution)/shard_map/ppermute | solution.py:36
  21.0 6.0 %copy-start.2 = (bf16[4,2,132,1024]{3,2,1,0:T(8,128)(2,1)S(1)}, bf16[4,2,132,1024]{3,2,1,0:T(8,128)(2,1)}, u32[]{:S(2)}) copy-start(bf16[4,2,132,1024]{3,2,1,0:T(8,128)(2,1)} %get-tuple-element.8) | copy-start | bytes 6488068
  27.0 7.6 %slice-start = ((s8[4325376]{0:T(1024)(128)(4,1)}), s8[131072]{0:T(1024)(128)(4,1)S(1)}, s32[]{:S(2)}) async-start(s8[4325376]{0:T(1024)(128)(4,1)} %bitcast.16), calls=%async_computation.1 | async-start | bytes 262144
  31.0 3.6 %slice-start.1 = ((s8[4325376]{0:T(1024)(128)(4,1)}), s8[4194304]{0:T(1024)(128)(4,1)S(1)}, s32[]{:S(2)}) async-start(s8[4325376]{0:T(1024)(128)(4,1)} %bitcast.16), calls=%async_computation.2 | async-start | bytes 8388608
  31.0 4.8 %copy-start.1 = (bf16[4,2,132,16,64]{4,3,2,1,0:T(8,128)(2,1)S(1)}, bf16[4,2,132,16,64]{4,3,2,1,0:T(8,128)(2,1)}, u32[]{:S(2)}) copy-start(bf16[4,2,132,16,64]{4,3,2,1,0:T(8,128)(2,1)} %reshape.36) | copy-start | bytes 6488068
  43.0 20.7 %copy-start.3 = (f32[256]{0:T(256)S(1)}, f32[256]{0:T(256)}, u32[]{:S(2)}) copy-start(f32[256]{0:T(256)} %param.4) | copy-start | bytes 3076
  53.9 10.5 %copy-start.4 = (f32[256]{0:T(256)S(1)}, f32[256]{0:T(256)}, u32[]{:S(2)}) copy-start(f32[256]{0:T(256)} %param.5) | copy-start | bytes 3076
  53.9 42.0 %all-to-all-start = ((bf16[4,2,16,9504]{3,1,0,2:T(2,128)(2,1)}), bf16[4,2,16,9504]{3,1,0,2:T(2,128)(2,1)S(1)}, u32[]{:S(2)}, u32[]{:S(2)}) async-start(bf16[4,2,16,9504]{3,1,0,2:T(2,128)(2,1)} %reshape.41), calls=%async_computation | async-start | bytes 4915200 | tf_op jit(solution)/shard_map/all_to_all | solution.py:118
  101.6 2.4 %copy-start = (bf16[64,2,9504]{0,2,1:T(8,128)(2,1)S(1)}, bf16[64,2,9504]{0,2,1:T(8,128)(2,1)}, u32[]{:S(2)}) copy-start(bf16[64,2,9504]{0,2,1:T(8,128)(2,1)} %copy.14) | copy-start | bytes 7299076

commit v8 on v5

--- a/solution.py
+++ b/solution.py
@@ -43,9 +43,12 @@
     return f.astype(jnp.bfloat16)
 
 
-def fit_kernel(wp, x_ref, kb_ref, g3_ref, step_ref, lam_ref, cm_ref, rm_ref,
-               o_ref, b_ref, f0_ref, f1_ref, f3_ref, m_ref):
-    t = pl.program_id(1)
+def fit_kernel(wp, aliased, x_ref, kb_ref, g3_ref, step_ref, lam_ref, cm_ref, rm_ref,
+               *rest):
+    if aliased:
+        rest = rest[1:]
+    o_ref, b_ref, f0_ref, f1_ref, f3_ref, m_ref = rest
+    t = pl.program_id(0)
     rows = TR + 2 * RH
     n = rows * wp
     base = pl.multiple_of(t * (TR * wp), 16)
@@ -102,12 +105,10 @@
     kb = kernel.astype(jnp.bfloat16)
     gh = gram.astype(jnp.bfloat16)
     g3 = gh
-    x = lax.all_to_all(images, "gy", split_axis=3, concat_axis=0, tiled=True)
-    e, sl, h, w = x.shape
-    x = halo(x, "gy", 3, CH)
-    x = halo(x, "gx", 2, RH)
+    e = images.shape[0] * lax.axis_size("gy")
+    sl, h = images.shape[1], images.shape[2]
+    w = images.shape[3] // lax.axis_size("gy")
     hp, wp = h + 2 * RH, w + 2 * CH
-    x = jnp.transpose(x, (1, 2, 3, 0)).reshape(sl, hp * wp, e)
     r = kernel.shape[1]
 
     gi = lax.axis_index("gx")
@@ -120,37 +121,58 @@
 
     rows = TR + 2 * RH
     nt = h // TR
-    flops = 2 * sl * nt * rows * wp * r * (e + 2 * r)
-    out = pl.pallas_call(
-        functools.partial(fit_kernel, wp),
-        out_shape=jax.ShapeDtypeStruct((sl, h, w, r), jnp.float32),
-        grid=(sl, nt),
-        in_specs=[
-            pl.BlockSpec((1, hp * wp, e), lambda s, t: (s, 0, 0)),
-            pl.BlockSpec((e, r), lambda s, t: (0, 0)),
-            pl.BlockSpec((r, r), lambda s, t: (0, 0)),
-            pl.BlockSpec((1, r), lambda s, t: (0, 0)),
-            pl.BlockSpec((1, r), lambda s, t: (0, 0)),
-            pl.BlockSpec((wp, r), lambda s, t: (0, 0)),
+    flops = 2 * nt * rows * wp * r * (e + 2 * r)
+    out = None
+    xs = None
+    for s in range(sl):
+        piece = images[:, s]
+        if xs is not None:
+            xs, piece = lax.optimization_barrier((xs, piece))
+        x = lax.all_to_all(piece, "gy", split_axis=2, concat_axis=0, tiled=True)
+        if out is not None:
+            out, x = lax.optimization_barrier((out, x))
+        x = halo(x, "gy", 2, CH)
+        x = halo(x, "gx", 1, RH)
+        x = jnp.transpose(x, (1, 2, 0)).reshape(1, hp * wp, e)
+        xs = x
+        args = [x, kb, g3, step[None, :], lam[None, :], cm, rm]
+        in_specs = [
+            pl.BlockSpec((1, hp * wp, e), lambda t: (0, 0, 0)),
+            pl.BlockSpec((e, r), lambda t: (0, 0)),
+            pl.BlockSpec((r, r), lambda t: (0, 0)),
+            pl.BlockSpec((1, r), lambda t: (0, 0)),
+            pl.BlockSpec((1, r), lambda t: (0, 0)),
+            pl.BlockSpec((wp, r), lambda t: (0, 0)),
             pl.BlockSpec(memory_space=pltpu.SMEM),
-        ],
-        out_specs=pl.BlockSpec((1, TR, w, r), lambda s, t: (s, t, 0, 0)),
-        scratch_shapes=[
-            pltpu.VMEM((rows * wp, r), jnp.float32),
-            pltpu.VMEM((rows * wp, r), jnp.float32),
-            pltpu.VMEM((rows * wp, r), jnp.float32),
-            pltpu.VMEM((rows * wp, r), jnp.bfloat16),
-            pltpu.VMEM(((rows - 2) * wp, r), jnp.float32),
-        ],
-        compiler_params=pltpu.CompilerParams(
-            dimension_semantics=("arbitrary", "arbitrary"),
-            vmem_limit_bytes=48 * 1024 * 1024,
-        ),
-        cost_estimate=pl.CostEstimate(
-            flops=flops, transcendentals=0,
-            bytes_accessed=sl * (hp * wp * e * 2 + h * w * r * 4),
-        ),
-    )(x, kb, g3, step[None, :], lam[None, :], cm, rm)
+        ]
+        aliases = {}
+        if out is not None:
+            args.append(out)
+            in_specs.append(pl.BlockSpec(memory_space=pl.ANY))
+            aliases = {len(args) - 1: 0}
+        out = pl.pallas_call(
+            functools.partial(fit_kernel, wp, out is not None),
+            out_shape=jax.ShapeDtypeStruct((sl, h, w, r), jnp.float32),
+            grid=(nt,),
+            in_specs=in_specs,
+            out_specs=pl.BlockSpec((1, TR, w, r), lambda t, s=s: (s, t, 0, 0)),
+            scratch_shapes=[
+                pltpu.VMEM((rows * wp, r), jnp.float32),
+                pltpu.VMEM((rows * wp, r), jnp.float32),
+                pltpu.VMEM((rows * wp, r), jnp.float32),
+                pltpu.VMEM((rows * wp, r), jnp.bfloat16),
+                pltpu.VMEM(((rows - 2) * wp, r), jnp.float32),
+            ],
+            input_output_aliases=aliases,
+            compiler_params=pltpu.CompilerParams(
+                dimension_semantics=("arbitrary",),
+                vmem_limit_bytes=48 * 1024 * 1024,
+            ),
+            cost_estimate=pl.CostEstimate(
+                flops=flops, transcendentals=0,
+                bytes_accessed=hp * wp * e * 2 + h * w * r * 4,
+            ),
+        )(*args)
     return out
 
 

time: 148 us -> 157 us (1.061); the launches traced: 146 us -> 157 us
  blocking collectives: 0 us -> 25.8 us
  waiting for transfers between devices: 34.7 us -> 13.3 us
  starting transfers between devices: 21.6 us -> 29 us
  other arithmetic: 11.3 us -> 9.32 us
  Pallas kernels: 45.2 us -> 47.1 us
    all_to_all x1, waiting for transfers between devices: 27.7 us -> 0.01 us  [per_device(): x = lax.all_to_all(piece, 'gy', split_axis=2, concat_axis=0, tiled=True)]
    all_to_all x0 -> x1, blocking collectives: none -> 25.8 us  [per_device(): x = lax.all_to_all(piece, 'gy', split_axis=2, concat_axis=0, tiled=True)]
    ppermute x2 -> x4, waiting for transfers between devices: 5.81 us -> 13.3 us  [halo(): lax.ppermute(head, axis, [(i + 1, i) for i in range(count - 1)])]
    ppermute x2 -> x4, starting transfers between devices: 9.06 us -> 15.8 us  [halo(): lax.ppermute(tail, axis, [(i, i + 1) for i in range(count - 1)])]
    unnamed x7 -> x6, local copies, waits for them, and re-layouts: 8.55 us -> 3.15 us
    ppermute x2 -> x4, starting transfers between devices: 3.21 us -> 6.59 us  [halo(): lax.ppermute(head, axis, [(i + 1, i) for i in range(count - 1)])]
    slice x0 -> x1, local copies, waits for them, and re-layouts: none -> 2.75 us  [per_device(): piece = images[:, s]]
    all_to_all x1, starting transfers between devices: 9.3 us -> 6.66 us  [per_device(): x = lax.all_to_all(piece, 'gy', split_axis=2, concat_axis=0, tiled=True)]
  transfers between devices with their start and end apart: 5 -> 9, of which waited for: 3 -> 3; matrix products, arithmetic and copies ran while one was open for 2% -> 3% of each run, Pallas kernels for 0% -> 15%
where the time goes in v8:
time: 157 us
  Pallas kernels  47.1 us (30%)
  local copies, waits for them, and re-layouts  31.1 us (20%)
  starting transfers between devices  29 us (18%)
  blocking collectives  25.8 us (16%)
  waiting for transfers between devices  13.3 us (8%)
  other arithmetic  9.32 us (6%)
    pallas_call x2, Pallas kernels, per_device(): pl.pallas_call(functools.partial(fit_kernel, wp, out is not None), out_sh...  47.1 us
    all_to_all x1, blocking collectives, per_device(): x = lax.all_to_all(piece, 'gy', split_axis=2, concat_axis=0, tiled=True)  25.8 us
    ppermute x4, starting transfers between devices, halo(): lax.ppermute(tail, axis, [(i, i + 1) for i in range(count - 1)])  15.8 us
    transpose x2, local copies, waits for them, and re-layouts, per_device(): x = jnp.transpose(x, (1, 2, 0)).reshape(1, hp * wp, e)  13.4 us
    ppermute x4, waiting for transfers between devices, halo(): lax.ppermute(head, axis, [(i + 1, i) for i in range(count - 1)])  13.3 us
    transpose x2, other arithmetic, per_device(): x = jnp.transpose(x, (1, 2, 0)).reshape(1, hp * wp, e)  7.95 us
    all_to_all x1, starting transfers between devices, per_device(): x = lax.all_to_all(piece, 'gy', split_axis=2, concat_axis=0, tiled=True)  6.66 us
    ppermute x4, starting transfers between devices, halo(): lax.ppermute(head, axis, [(i + 1, i) for i in range(count - 1)])  6.59 us
  transfers between devices with their start and end apart: 9, of which 3 were waited for; matrix products, arithmetic and copies ran while one was open for 3% of the time, Pallas kernels for 15%

profile of v8, /device:TPU:1, one launch (start us, length us, event | category | flops | bytes accessed | tf_op | source)
XLA Modules:
  0.0 156.5 jit_solution(12028050903121245613)
XLA Ops:
  0.0 2.8 %fusion.7 = (bf16[4,1,128,1024]{3,2,1,0:T(8,128)(2,1)}, bf16[4,1,128,1024]{3,2,1,0:T(8,128)(2,1)S(1)}) fusion(bf16[4,2,128,1024]{3,2,1,0:T(8,128)(2,1)} %param.3), kind=kLoop, calls=%fused_computation.16 | loop fusion | bytes 4194304 | tf_op jit(solution)/shard_map/slice | solution.py:128
  2.8 0.7 copy.32
  3.5 25.8 %all_to_all.36 = bf16[4,128,1024]{1,0,2:T(4,128)(2,1)S(1)} all-to-all(bf16[4,128,1024]{1,0,2:T(4,128)(2,1)S(1)} %bitcast.31), channel_id=1, replica_groups=mesh['gx'=8,'gy'=16] {'gy'}, dimensions={2} | all-to-all | bytes 2097152 | tf_op jit(solution)/shard_map/all_to_all | solution.py:131
  29.4 0.1 copy.16
  29.5 0.1 copy.17
  29.6 0.1 fusion.11
  29.7 3.2 %collective-permute-start = (bf16[64,128,4]{1,2,0:T(4,128)(2,1)S(1)}, bf16[64,128,4]{1,2,0:T(4,128)(2,1)S(1)}, u32[]{:S(2)}, u32[]{:S(2)}) collective-permute-start(bf16[64,128,4]{1,2,0:T(4,128)(2,1)S(1)} %get-tuple-element.21), channel_id=1, source_target_pairs={{0,1},{1,2},{2,3},{3,4},{4,5},{5,6},{6,7},{7,8},{8,9},{9,10},{10,1... | collective-permute-start | bytes 196616 | tf_op jit(solution)/shard_map/ppermute | solution.py:34
  32.9 1.9 %collective-permute-start.1 = (bf16[64,128,4]{1,2,0:T(4,128)(2,1)S(1)}, bf16[64,128,4]{1,2,0:T(4,128)(2,1)S(1)}, u32[]{:S(2)}, u32[]{:S(2)}) collective-permute-start(bf16[64,128,4]{1,2,0:T(4,128)(2,1)S(1)} %get-tuple-element.22), channel_id=1, source_target_pairs={{1,0},{2,1},{3,2},{4,3},{5,4},{6,5},{7,6},{8,7},{9,8},{10,9},{11,1... | collective-permute-start | bytes 196616 | tf_op jit(solution)/shard_map/ppermute | solution.py:36
  34.8 0.0 collective-permute-done
  34.8 5.1 %collective-permute-done.1 = bf16[64,128,4]{1,2,0:T(4,128)(2,1)S(1)} collective-permute-done((bf16[64,128,4]{1,2,0:T(4,128)(2,1)S(1)}, bf16[64,128,4]{1,2,0:T(4,128)(2,1)S(1)}, u32[]{:S(2)}, u32[]{:S(2)}) %collective-permute-start.1) | collective-permute-done | bytes 65568 | tf_op jit(solution)/shard_map/ppermute | solution.py:36
  40.0 0.6 pad_maximum_fusion
  40.5 0.4 fusion.9
  41.0 0.0 copy-start
  41.0 1.1 copy.18
  42.1 0.5 copy.19
  42.6 1.3 collective-permute-start.3
  43.9 4.0 %collective-permute-start.2 = (bf16[64,2,72]{2,0,1:T(8,128)(2,1)}, bf16[64,2,72]{2,0,1:T(8,128)(2,1)S(1)}, u32[]{:S(2)}, u32[]{:S(2)}) collective-permute-start(bf16[64,2,72]{2,0,1:T(8,128)(2,1)} %copy.18), channel_id=1, source_target_pairs={{0,16},{16,32},{32,48},{48,64},{64,80},{80,96},{96,112},{1,17},{17... | collective-permute-start | bytes 55304 | tf_op jit(solution)/shard_map/ppermute | solution.py:34
  47.9 0.0 copy-done
  47.9 0.1 multiply_reduce_fusion
  48.0 2.4 %copy.33 = bf16[4,1,128,1024]{2,0,3,1:T(4,128)(2,1)} copy(bf16[4,1,128,1024]{3,2,1,0:T(8,128)(2,1)} %get-tuple-element.13) | data formatting | bytes 2097152
  50.4 0.0 collective-permute-done.2
  50.4 0.6 copy.20
  51.0 0.0 collective-permute-done.3
  51.0 1.3 copy.21
  52.3 3.4 %maximum_bitcast_fusion = bf16[132,72,64]{0,1,2:T(8,128)(2,1)} fusion(bf16[64,2,72]{1,2,0:T(8,128)(2,1)S(1)} %copy.21, bf16[64,128,4]{1,2,0:T(4,128)(2,1)S(1)} %collective-permute-done.1, bf16[64,128,64]{1,2,0:T(8,128)(2,1)S(1)} %bitcast.26, bf16[64,128,4]{1,2,0:T(4,128)(2,1)S(1)} %collective-permute-done, bf16[64,2,72]{1,2,0:T(8,128)(2,1)S(1)} %copy.20), kind=kLoop, calls=%fused_computation | loop fusion | flops 6082560 | bytes 2433024 | tf_op jit(solution)/shard_map/transpose | solution.py:136
  55.7 6.7 %copy.22 = bf16[132,72,64]{2,1,0:T(8,128)(2,1)S(1)} copy(bf16[132,72,64]{0,1,2:T(8,128)(2,1)} %maximum_bitcast_fusion) | data formatting | bytes 2433024 | tf_op jit(solution)/shard_map/transpose | solution.py:136
  62.5 0.0 copy-start.1
  62.5 6.7 %all-to-all-start.1 = ((bf16[4,128,1024]{1,0,2:T(4,128)(2,1)}), bf16[4,128,1024]{1,0,2:T(4,128)(2,1)}, u32[]{:S(2)}, u32[]{:S(2)}) async-start(bf16[4,128,1024]{1,0,2:T(4,128)(2,1)} %bitcast.30), calls=%async_computation.1 | async-start | bytes 2097152 | tf_op jit(solution)/shard_map/all_to_all | solution.py:131
  69.1 0.5 fusion.12
  69.6 0.1 copy.23.g3_ref
  69.8 0.0 copy-done.1
  69.8 0.1 fusion.3.kb_ref
  69.9 0.1 broadcast_in_dim.8.cm_ref
  70.0 23.5 %shard_map.37.rest_0_ = f32[2,128,64,256]{3,2,1,0:T(8,128)} custom-call(bf16[1,9504,64]{2,1,0:T(8,128)(2,1)S(1)} %bitcast.18, bf16[64,256]{1,0:T(8,128)(2,1)S(1)} %fusion.3.kb_ref, bf16[256,256]{1,0:T(8,128)(2,1)S(1)} %copy.23.g3_ref, f32[1,256]{1,0:T(1,128)S(1)} %bitcast.20, f32[1,256]{1,0:T(1,128)S(1)} %bitcast.22, f32[72,256]{1,0:T(8,128)S(1)} %broadcast_in_dim.8.cm_ref, ...), custom_call_target="tpu_custom_call" | custom-call | flops 3057647616 | bytes 9605120 | tf_op jit(solution)/shard_map/pallas_call | solution.py:153
  93.5 0.0 all-to-all-done.1
  93.5 1.4 copy.25
  94.9 0.1 copy.26
  95.0 0.1 fusion.10
  95.0 5.0 %collective-permute-start.4 = (bf16[64,128,4]{1,2,0:T(4,128)(2,1)S(1)}, bf16[64,128,4]{1,2,0:T(4,128)(2,1)S(1)}, u32[]{:S(2)}, u32[]{:S(2)}) collective-permute-start(bf16[64,128,4]{1,2,0:T(4,128)(2,1)S(1)} %get-tuple-element.19), channel_id=1, source_target_pairs={{0,1},{1,2},{2,3},{3,4},{4,5},{5,6},{6,7},{7,8},{8,9},{9,10},{10,1... | collective-permute-start | bytes 196616 | tf_op jit(solution)/shard_map/ppermute | solution.py:34
  100.1 1.9 %collective-permute-start.5 = (bf16[64,128,4]{1,2,0:T(4,128)(2,1)S(1)}, bf16[64,128,4]{1,2,0:T(4,128)(2,1)S(1)}, u32[]{:S(2)}, u32[]{:S(2)}) collective-permute-start(bf16[64,128,4]{1,2,0:T(4,128)(2,1)S(1)} %get-tuple-element.20), channel_id=1, source_target_pairs={{1,0},{2,1},{3,2},{4,3},{5,4},{6,5},{7,6},{8,7},{9,8},{10,9},{11,1... | collective-permute-start | bytes 196616 | tf_op jit(solution)/shard_map/ppermute | solution.py:36
  102.0 0.0 collective-permute-done.4
  102.0 5.2 %collective-permute-done.5 = bf16[64,128,4]{1,2,0:T(4,128)(2,1)S(1)} collective-permute-done((bf16[64,128,4]{1,2,0:T(4,128)(2,1)S(1)}, bf16[64,128,4]{1,2,0:T(4,128)(2,1)S(1)}, u32[]{:S(2)}, u32[]{:S(2)}) %collective-permute-start.5) | collective-permute-done | bytes 65568 | tf_op jit(solution)/shard_map/ppermute | solution.py:36
  107.2 0.6 pad_maximum_fusion.1
  107.8 1.5 fusion.8
  109.2 1.8 %copy.27 = bf16[64,2,72]{2,0,1:T(8,128)(2,1)S(1)} copy(bf16[64,2,72]{1,2,0:T(8,128)(2,1)} %get-tuple-element.15) | data formatting | bytes 36864 | tf_op jit(solution)/shard_map/slice | solution.py:31
  111.0 3.5 %collective-permute-start.6 = (bf16[64,2,72]{2,0,1:T(8,128)(2,1)S(1)}, bf16[64,2,72]{2,0,1:T(8,128)(2,1)S(1)}, u32[]{:S(2)}, u32[]{:S(2)}) collective-permute-start(bf16[64,2,72]{2,0,1:T(8,128)(2,1)S(1)} %copy.27), channel_id=1, source_target_pairs={{0,16},{16,32},{32,48},{48,64},{64,80},{80,96},{96,112},{1,17},{17... | collective-permute-start | bytes 55304 | tf_op jit(solution)/shard_map/ppermute | solution.py:34
  114.5 0.5 copy.28
  115.0 1.5 collective-permute-start.7
  116.5 0.0 collective-permute-done.6
  116.5 0.6 copy.29
  117.1 3.0 %collective-permute-done.7 = bf16[64,2,72]{2,0,1:T(8,128)(2,1)S(1)} collective-permute-done((bf16[64,2,72]{2,0,1:T(8,128)(2,1)S(1)}, bf16[64,2,72]{2,0,1:T(8,128)(2,1)S(1)}, u32[]{:S(2)}, u32[]{:S(2)}) %collective-permute-start.7) | collective-permute-done | bytes 18464 | tf_op jit(solution)/shard_map/ppermute | solution.py:36
  120.2 1.6 copy.30
  121.7 4.5 %maximum_bitcast_fusion.1 = bf16[132,72,64]{0,1,2:T(8,128)(2,1)} fusion(bf16[64,2,72]{1,2,0:T(8,128)(2,1)} %copy.30, bf16[64,128,4]{1,2,0:T(4,128)(2,1)S(1)} %collective-permute-done.5, bf16[64,128,64]{1,2,0:T(8,128)(2,1)S(1)} %bitcast.29, bf16[64,128,4]{1,2,0:T(4,128)(2,1)S(1)} %collective-permute-done.4, bf16[64,2,72]{1,2,0:T(8,128)(2,1)S(1)} %copy.29), kind=kLoop, calls=%fused_computation.1 | loop fusion | flops 6082560 | bytes 2433024 | tf_op jit(solution)/shard_map/transpose | solution.py:136
  126.2 6.7 %copy.31 = bf16[132,72,64]{2,1,0:T(8,128)(2,1)S(1)} copy(bf16[132,72,64]{0,1,2:T(8,128)(2,1)} %maximum_bitcast_fusion.1) | data formatting | bytes 2433024 | tf_op jit(solution)/shard_map/transpose | solution.py:136
  133.0 23.6 %shard_map.38 = f32[2,128,64,256]{3,2,1,0:T(8,128)} custom-call(bf16[1,9504,64]{2,1,0:T(8,128)(2,1)S(1)} %bitcast.19, bf16[64,256]{1,0:T(8,128)(2,1)S(1)} %fusion.3.kb_ref, bf16[256,256]{1,0:T(8,128)(2,1)S(1)} %copy.23.g3_ref, f32[1,256]{1,0:T(1,128)S(1)} %bitcast.21, f32[1,256]{1,0:T(1,128)S(1)} %bitcast.23, ...), custom_call_target="tpu_custom_call", output_to_operand_aliasing={{}: (7, {})} | custom-call | flops 3057647616 | bytes 9605120 | tf_op jit(solution)/shard_map/pallas_call | solution.py:153
  (5 shorter events, 0.0 us)
Async XLA Ops:
  29.7 5.2 %collective-permute-start = (bf16[64,128,4]{1,2,0:T(4,128)(2,1)S(1)}, bf16[64,128,4]{1,2,0:T(4,128)(2,1)S(1)}, u32[]{:S(2)}, u32[]{:S(2)}) collective-permute-start(bf16[64,128,4]{1,2,0:T(4,128)(2,1)S(1)} %get-tuple-element.21), channel_id=1, source_target_pairs={{0,1},{1,2},{2,3},{3,4},{4,5},{5,6},{6,7},{7,8},{8,9},{9,10},{10,1... | collective-permute-start | bytes 196616 | tf_op jit(solution)/shard_map/ppermute | solution.py:34
  32.9 7.1 %collective-permute-start.1 = (bf16[64,128,4]{1,2,0:T(4,128)(2,1)S(1)}, bf16[64,128,4]{1,2,0:T(4,128)(2,1)S(1)}, u32[]{:S(2)}, u32[]{:S(2)}) collective-permute-start(bf16[64,128,4]{1,2,0:T(4,128)(2,1)S(1)} %get-tuple-element.22), channel_id=1, source_target_pairs={{1,0},{2,1},{3,2},{4,3},{5,4},{6,5},{7,6},{8,7},{9,8},{10,9},{11,1... | collective-permute-start | bytes 196616 | tf_op jit(solution)/shard_map/ppermute | solution.py:36
  41.0 6.9 %copy-start = (f32[256]{0:T(256)S(1)}, f32[256]{0:T(256)}, u32[]{:S(2)}) copy-start(f32[256]{0:T(256)} %param.4) | copy-start | bytes 3076
  42.6 8.4 %collective-permute-start.3 = (bf16[64,2,72]{2,0,1:T(8,128)(2,1)S(1)}, bf16[64,2,72]{2,0,1:T(8,128)(2,1)}, u32[]{:S(2)}, u32[]{:S(2)}) collective-permute-start(bf16[64,2,72]{2,0,1:T(8,128)(2,1)S(1)} %copy.19), channel_id=1, source_target_pairs={{16,0},{32,16},{48,32},{64,48},{80,64},{96,80},{112,96},{17,1},{33... | collective-permute-start | bytes 55304 | tf_op jit(solution)/shard_map/ppermute | solution.py:36
  43.9 6.5 %collective-permute-start.2 = (bf16[64,2,72]{2,0,1:T(8,128)(2,1)}, bf16[64,2,72]{2,0,1:T(8,128)(2,1)S(1)}, u32[]{:S(2)}, u32[]{:S(2)}) collective-permute-start(bf16[64,2,72]{2,0,1:T(8,128)(2,1)} %copy.18), channel_id=1, source_target_pairs={{0,16},{16,32},{32,48},{48,64},{64,80},{80,96},{96,112},{1,17},{17... | collective-permute-start | bytes 55304 | tf_op jit(solution)/shard_map/ppermute | solution.py:34
  62.5 7.3 %copy-start.1 = (f32[256]{0:T(256)S(1)}, f32[256]{0:T(256)}, u32[]{:S(2)}) copy-start(f32[256]{0:T(256)} %param.5) | copy-start | bytes 3076
  62.5 31.0 %all-to-all-start.1 = ((bf16[4,128,1024]{1,0,2:T(4,128)(2,1)}), bf16[4,128,1024]{1,0,2:T(4,128)(2,1)}, u32[]{:S(2)}, u32[]{:S(2)}) async-start(bf16[4,128,1024]{1,0,2:T(4,128)(2,1)} %bitcast.30), calls=%async_computation.1 | async-start | bytes 2097152 | tf_op jit(solution)/shard_map/all_to_all | solution.py:131
  95.0 7.0 %collective-permute-start.4 = (bf16[64,128,4]{1,2,0:T(4,128)(2,1)S(1)}, bf16[64,128,4]{1,2,0:T(4,128)(2,1)S(1)}, u32[]{:S(2)}, u32[]{:S(2)}) collective-permute-start(bf16[64,128,4]{1,2,0:T(4,128)(2,1)S(1)} %get-tuple-element.19), channel_id=1, source_target_pairs={{0,1},{1,2},{2,3},{3,4},{4,5},{5,6},{6,7},{7,8},{8,9},{9,10},{10,1... | collective-permute-start | bytes 196616 | tf_op jit(solution)/shard_map/ppermute | solution.py:34
  100.1 7.1 %collective-permute-start.5 = (bf16[64,128,4]{1,2,0:T(4,128)(2,1)S(1)}, bf16[64,128,4]{1,2,0:T(4,128)(2,1)S(1)}, u32[]{:S(2)}, u32[]{:S(2)}) collective-permute-start(bf16[64,128,4]{1,2,0:T(4,128)(2,1)S(1)} %get-tuple-element.20), channel_id=1, source_target_pairs={{1,0},{2,1},{3,2},{4,3},{5,4},{6,5},{7,6},{8,7},{9,8},{10,9},{11,1... | collective-permute-start | bytes 196616 | tf_op jit(solution)/shard_map/ppermute | solution.py:36
  111.0 5.5 %collective-permute-start.6 = (bf16[64,2,72]{2,0,1:T(8,128)(2,1)S(1)}, bf16[64,2,72]{2,0,1:T(8,128)(2,1)S(1)}, u32[]{:S(2)}, u32[]{:S(2)}) collective-permute-start(bf16[64,2,72]{2,0,1:T(8,128)(2,1)S(1)} %copy.27), channel_id=1, source_target_pairs={{0,16},{16,32},{32,48},{48,64},{64,80},{80,96},{96,112},{1,17},{17... | collective-permute-start | bytes 55304 | tf_op jit(solution)/shard_map/ppermute | solution.py:34
  115.0 5.1 %collective-permute-start.7 = (bf16[64,2,72]{2,0,1:T(8,128)(2,1)S(1)}, bf16[64,2,72]{2,0,1:T(8,128)(2,1)S(1)}, u32[]{:S(2)}, u32[]{:S(2)}) collective-permute-start(bf16[64,2,72]{2,0,1:T(8,128)(2,1)S(1)} %copy.28), channel_id=1, source_target_pairs={{16,0},{32,16},{48,32},{64,48},{80,64},{96,80},{112,96},{17,1},{33... | collective-permute-start | bytes 55304 | tf_op jit(solution)/shard_map/ppermute | solution.py:36

commit v9 on v5

--- a/solution.py
+++ b/solution.py
@@ -39,57 +39,63 @@
     )
 
 
-def split3(f):
-    return f.astype(jnp.bfloat16)
-
-
-def fit_kernel(wp, x_ref, kb_ref, g3_ref, step_ref, lam_ref, cm_ref, rm_ref,
-               o_ref, b_ref, f0_ref, f1_ref, f3_ref, m_ref):
+def fit_kernel(wp, x_ref, kb_ref, g_ref, step_ref, lam_ref, cm_ref, rm_ref,
+               o_ref, b_ref, f1_ref, fb_ref, m_ref):
     t = pl.program_id(1)
     rows = TR + 2 * RH
     n = rows * wp
+    r = b_ref.shape[1]
     base = pl.multiple_of(t * (TR * wp), 16)
     step = step_ref[...]
     lam = lam_ref[...]
     cm = cm_ref[...]
 
-    b = jnp.dot(x_ref[0, pl.ds(base, n), :], kb_ref[...],
-                preferred_element_type=jnp.float32)
-    b_ref[...] = b
-    f0 = jnp.maximum(b * step, 0.0)
-    f0_ref[...] = f0
-    f3_ref[...] = split3(f0)
+    b_ref[...] = jnp.dot(x_ref[0, pl.ds(base, n), :], kb_ref[...],
+                         preferred_element_type=jnp.float32)
+    inner = (rows - 2) * wp
+    fb_ref[pl.ds(2 * wp, inner), :] = jnp.maximum(
+        b_ref[pl.ds(wp, inner), :] * step, 0.0).astype(jnp.bfloat16)
 
-    def update(src_ref, q):
-        o = pl.multiple_of(q * wp, 8)
-        c = src_ref[pl.ds(o, wp), :]
-        up = src_ref[pl.ds(o - wp, wp), :]
-        dn = src_ref[pl.ds(o + wp, wp), :]
+    def lap_of(c, up, dn):
         lf = pltpu.roll(c, 1, 0)
         rt = pltpu.roll(c, wp - 1, 0)
-        lap = 4.0 * c - up - dn - lf - rt
-        m = m_ref[pl.ds(o - wp, wp), :]
-        g = m - b_ref[pl.ds(o, wp), :] + lam * lap
-        return jnp.maximum(c - step * g, 0.0)
+        return 4.0 * c - up - dn - lf - rt
 
-    m_ref[...] = jnp.dot(f3_ref[pl.ds(wp, (rows - 2) * wp), :], g3_ref[...],
+    def row1(q):
+        o = q * wp
+        bu = b_ref[pl.ds(o - wp, wp), :]
+        bc = b_ref[pl.ds(o, wp), :]
+        bd = b_ref[pl.ds(o + wp, wp), :]
+        c = jnp.maximum(bc * step, 0.0)
+        up = jnp.maximum(bu * step, 0.0)
+        dn = jnp.maximum(bd * step, 0.0)
+        g = m_ref[pl.ds(o - wp, wp), :] - bc + lam * lap_of(c, up, dn)
+        return jnp.maximum(c - step * g, 0.0) * (cm * rm_ref[t * TR + q])
+
+    m_ref[...] = jnp.dot(fb_ref[pl.ds(2 * wp, inner), :], g_ref[...],
                          preferred_element_type=jnp.float32)
 
-    def body1(q, carry):
-        f1 = update(f0_ref, q) * (cm * rm_ref[t * TR + q])
-        f1_ref[pl.ds(pl.multiple_of(q * wp, 8), wp), :] = f1
+    def body1(k, carry):
+        q = 2 * k + 1
+        pair = jnp.concatenate([row1(q), row1(q + 1)], axis=0)
+        o = pl.multiple_of((q + 1) * wp, 16)
+        f1_ref[pl.ds(o, 2 * wp), :] = pair
+        fb_ref[pl.ds(o, 2 * wp), :] = pair.astype(jnp.bfloat16)
         return carry
 
-    lax.fori_loop(1, rows - 1, body1, 0)
-    f1_ref[pl.ds(0, wp), :] = jnp.zeros((wp, f1_ref.shape[1]), jnp.float32)
-    f1_ref[pl.ds((rows - 1) * wp, wp), :] = jnp.zeros((wp, f1_ref.shape[1]), jnp.float32)
+    lax.fori_loop(0, (rows - 2) // 2, body1, 0)
 
-    f3_ref[...] = split3(f1_ref[...])
-    m_ref[...] = jnp.dot(f3_ref[pl.ds(wp, (rows - 2) * wp), :], g3_ref[...],
+    m_ref[...] = jnp.dot(fb_ref[pl.ds(2 * wp, inner), :], g_ref[...],
                          preferred_element_type=jnp.float32)
 
     def body2(q, carry):
-        f2 = update(f1_ref, q)
+        o = q * wp
+        c = f1_ref[pl.ds(o + wp, wp), :]
+        up = f1_ref[pl.ds(o, wp), :]
+        dn = f1_ref[pl.ds(o + 2 * wp, wp), :]
+        g = (m_ref[pl.ds(o - wp, wp), :] - b_ref[pl.ds(o, wp), :]
+             + lam * lap_of(c, up, dn))
+        f2 = jnp.maximum(c - step * g, 0.0)
         f2 = pltpu.roll(f2, wp - CH, 0)
         o_ref[0, q - RH] = f2[: wp - 2 * CH]
         return carry
@@ -137,9 +143,8 @@
         out_specs=pl.BlockSpec((1, TR, w, r), lambda s, t: (s, t, 0, 0)),
         scratch_shapes=[
             pltpu.VMEM((rows * wp, r), jnp.float32),
-            pltpu.VMEM((rows * wp, r), jnp.float32),
-            pltpu.VMEM((rows * wp, r), jnp.float32),
-            pltpu.VMEM((rows * wp, r), jnp.bfloat16),
+            pltpu.VMEM(((rows + 2) * wp, r), jnp.float32),
+            pltpu.VMEM(((rows + 2) * wp, r), jnp.bfloat16),
             pltpu.VMEM(((rows - 2) * wp, r), jnp.float32),
         ],
         compiler_params=pltpu.CompilerParams(

time: 148 us -> 150 us (1.014)
  Pallas kernels: 45.2 us -> 48.1 us
    pallas_call x1, Pallas kernels: 45.2 us -> 48.1 us  [per_device(): pl.pallas_call(functools.partial(fit_kernel, wp), out_shape=jax.ShapeDtyp...]
where the time goes in v9:
time: 150 us; the launch traced here: 148 us
  Pallas kernels  48.1 us (32%)
  waiting for transfers between devices  34.7 us (23%)
  local copies, waits for them, and re-layouts  32 us (21%)
  starting transfers between devices  21.6 us (14%)
  other arithmetic  11.3 us (8%)
    pallas_call x1, Pallas kernels, per_device(): pl.pallas_call(functools.partial(fit_kernel, wp), out_shape=jax.ShapeDtyp...  48.1 us
    all_to_all x1, waiting for transfers between devices, per_device(): x = lax.all_to_all(images, 'gy', split_axis=3, concat_axis=0, tiled=True)  27.7 us
    transpose x1, local copies, waits for them, and re-layouts, per_device(): x = jnp.transpose(x, (1, 2, 3, 0)).reshape(sl, hp * wp, e)  11 us
    transpose x1, other arithmetic, per_device(): x = jnp.transpose(x, (1, 2, 3, 0)).reshape(sl, hp * wp, e)  9.5 us
    all_to_all x1, starting transfers between devices, per_device(): x = lax.all_to_all(images, 'gy', split_axis=3, concat_axis=0, tiled=True)  9.3 us
    ppermute x2, starting transfers between devices, halo(): lax.ppermute(tail, axis, [(i, i + 1) for i in range(count - 1)])  9.06 us
    unnamed x7, local copies, waits for them, and re-layouts  8.55 us
    ppermute x2, waiting for transfers between devices, halo(): lax.ppermute(head, axis, [(i + 1, i) for i in range(count - 1)])  5.81 us
  transfers between devices with their start and end apart: 5, of which 3 were waited for; matrix products, arithmetic and copies ran while one was open for 2% of the time, Pallas kernels for 0%

profile of v9, /device:TPU:1, one launch (start us, length us, event | category | flops | bytes accessed | tf_op | source)
XLA Modules:
  0.0 148.3 jit_solution(3216523088368042358)
XLA Ops:
  0.0 0.0 copy-start.1
  0.0 6.2 %copy.10 = bf16[4,2,128,1024]{2,1,0,3:T(2,128)(2,1)} copy(bf16[4,2,128,1024]{3,2,1,0:T(8,128)(2,1)} %param.3) | data formatting | bytes 4194304 | tf_op args[0]
  6.2 9.3 %all-to-all-start = ((bf16[4,2,128,1024]{2,1,0,3:T(2,128)(2,1)}), bf16[4,2,128,1024]{2,1,0,3:T(2,128)(2,1)S(1)}, u32[]{:S(2)}, u32[]{:S(2)}) async-start(bf16[4,2,128,1024]{2,1,0,3:T(2,128)(2,1)} %copy.10), calls=%async_computation | async-start | bytes 4194304 | tf_op jit(solution)/shard_map/all_to_all | solution.py:111
  15.5 0.0 copy-start.2
  15.5 0.0 copy-done.1
  15.5 0.1 multiply_reduce_fusion
  15.6 0.1 fusion.3.kb_ref
  15.7 0.5 fusion.9
  16.2 27.7 %all-to-all-done = bf16[4,2,128,1024]{2,1,0,3:T(2,128)(2,1)S(1)} async-done(((bf16[4,2,128,1024]{2,1,0,3:T(2,128)(2,1)}), bf16[4,2,128,1024]{2,1,0,3:T(2,128)(2,1)S(1)}, u32[]{:S(2)}, u32[]{:S(2)}) %all-to-all-start) | async-done | bytes 2097184 | tf_op jit(solution)/shard_map/all_to_all | solution.py:111
  43.9 0.3 copy.11
  44.2 0.2 copy.12
  44.4 0.1 fusion.8
  44.5 5.1 %collective-permute-start = (bf16[64,2,128,4]{2,3,1,0:T(4,128)(2,1)S(1)}, bf16[64,2,128,4]{2,3,1,0:T(4,128)(2,1)S(1)}, u32[]{:S(2)}, u32[]{:S(2)}) collective-permute-start(bf16[64,2,128,4]{2,3,1,0:T(4,128)(2,1)S(1)} %get-tuple-element.9), channel_id=1, source_target_pairs={{0,1},{1,2},{2,3},{3,4},{4,5},{5,6},{6,7},{7,8},{8,9},{9,10},{10,1... | collective-permute-start | bytes 393224 | tf_op jit(solution)/shard_map/ppermute | solution.py:34
  49.6 1.9 %collective-permute-start.1 = (bf16[64,2,128,4]{2,3,1,0:T(4,128)(2,1)S(1)}, bf16[64,2,128,4]{2,3,1,0:T(4,128)(2,1)S(1)}, u32[]{:S(2)}, u32[]{:S(2)}) collective-permute-start(bf16[64,2,128,4]{2,3,1,0:T(4,128)(2,1)S(1)} %get-tuple-element.10), channel_id=1, source_target_pairs={{1,0},{2,1},{3,2},{4,3},{5,4},{6,5},{7,6},{8,7},{9,8},{10,9},{11,1... | collective-permute-start | bytes 393224 | tf_op jit(solution)/shard_map/ppermute | solution.py:36
  51.6 0.0 copy-done.2
  51.6 0.0 collective-permute-done
  51.6 5.8 %collective-permute-done.1 = bf16[64,2,128,4]{2,3,1,0:T(4,128)(2,1)S(1)} collective-permute-done((bf16[64,2,128,4]{2,3,1,0:T(4,128)(2,1)S(1)}, bf16[64,2,128,4]{2,3,1,0:T(4,128)(2,1)S(1)}, u32[]{:S(2)}, u32[]{:S(2)}) %collective-permute-start.1) | collective-permute-done | bytes 131104 | tf_op jit(solution)/shard_map/ppermute | solution.py:36
  57.4 1.6 %pad_maximum_fusion = bf16[64,2,128,72]{2,3,1,0:T(8,128)(2,1)S(1)} fusion(bf16[64,2,128,4]{2,3,1,0:T(4,128)(2,1)S(1)} %collective-permute-done.1, bf16[64,2,128,64]{2,3,1,0:T(8,128)(2,1)S(1)} %bitcast.13, bf16[64,2,128,4]{2,3,1,0:T(4,128)(2,1)S(1)} %collective-permute-done), kind=kLoop, calls=%fused_computation.1 | loop fusion | flops 7077888 | bytes 4718592 | tf_op jit(solution)/shard_map/concatenate | solution.py:32
  59.0 3.0 %fusion.7 = (bf16[64,2,2,72]{2,3,1,0:T(8,128)(2,1)}, bf16[64,2,2,72]{2,3,1,0:T(8,128)(2,1)}) fusion(bf16[64,2,128,72]{2,3,1,0:T(8,128)(2,1)S(1)} %pad_maximum_fusion), kind=kLoop, calls=%fused_computation.14 | loop fusion | bytes 147456 | tf_op jit(solution)/shard_map/slice | solution.py:31
  62.0 2.3 %copy.13 = bf16[64,2,2,72]{3,0,2,1:T(8,128)(2,1)S(1)} copy(bf16[64,2,2,72]{2,3,1,0:T(8,128)(2,1)} %get-tuple-element.7) | data formatting | bytes 73728 | tf_op jit(solution)/shard_map/slice | solution.py:31
  64.3 2.3 %copy.14 = bf16[64,2,2,72]{3,0,2,1:T(8,128)(2,1)S(1)} copy(bf16[64,2,2,72]{2,3,1,0:T(8,128)(2,1)} %get-tuple-element.8) | data formatting | bytes 73728 | tf_op jit(solution)/shard_map/slice | solution.py:30
  66.5 1.3 collective-permute-start.3
  67.8 4.0 %collective-permute-start.2 = (bf16[64,2,2,72]{3,0,2,1:T(8,128)(2,1)S(1)}, bf16[64,2,2,72]{3,0,2,1:T(8,128)(2,1)S(1)}, u32[]{:S(2)}, u32[]{:S(2)}) collective-permute-start(bf16[64,2,2,72]{3,0,2,1:T(8,128)(2,1)S(1)} %copy.13), channel_id=1, source_target_pairs={{0,16},{16,32},{32,48},{48,64},{64,80},{80,96},{96,112},{1,17},{17... | collective-permute-start | bytes 110600 | tf_op jit(solution)/shard_map/ppermute | solution.py:34
  71.9 0.1 copy.18.g_ref
  72.0 1.2 collective-permute-done.2
  73.2 2.1 %copy.15 = bf16[64,2,2,72]{2,3,1,0:T(8,128)(2,1)} copy(bf16[64,2,2,72]{3,0,2,1:T(8,128)(2,1)S(1)} %collective-permute-done.2) | data formatting | bytes 73728 | tf_op jit(solution)/shard_map/ppermute | solution.py:34
  75.2 0.0 collective-permute-done.3
  75.2 2.1 %copy.16 = bf16[64,2,2,72]{2,3,1,0:T(8,128)(2,1)} copy(bf16[64,2,2,72]{3,0,2,1:T(8,128)(2,1)S(1)} %collective-permute-done.3) | data formatting | bytes 73728 | tf_op jit(solution)/shard_map/ppermute | solution.py:36
  77.3 9.5 %maximum_bitcast_fusion = bf16[2,132,72,64]{1,2,0,3:T(8,128)(2,1)} fusion(bf16[64,2,2,72]{2,3,1,0:T(8,128)(2,1)} %copy.16, bf16[64,2,128,4]{2,3,1,0:T(4,128)(2,1)S(1)} %collective-permute-done.1, bf16[64,2,128,64]{2,3,1,0:T(8,128)(2,1)S(1)} %bitcast.14, bf16[64,2,128,4]{2,3,1,0:T(4,128)(2,1)S(1)} %collective-permute-done, bf16[64,2,2,72]{2,3,1,0:T(8,128)(2,1)} %copy.15), kind=kLoop, calls=%fused_computation | loop fusion | flops 12165120 | bytes 4866048 | tf_op jit(solution)/shard_map/transpose | solution.py:116
  86.8 11.0 %copy.17 = bf16[2,132,72,64]{3,2,1,0:T(8,128)(2,1)} copy(bf16[2,132,72,64]{1,2,0,3:T(8,128)(2,1)} %maximum_bitcast_fusion) | data formatting | bytes 4866048 | tf_op jit(solution)/shard_map/transpose | solution.py:116
  97.8 0.1 broadcast_in_dim.8.cm_ref
  97.9 0.0 copy-start
  97.9 2.4 %copy-done = bf16[2,132,72,64]{3,2,1,0:T(8,128)(2,1)S(1)} copy-done((bf16[2,132,72,64]{3,2,1,0:T(8,128)(2,1)S(1)}, bf16[2,132,72,64]{3,2,1,0:T(8,128)(2,1)}, u32[]{:S(2)}) %copy-start) | copy-done | bytes 2433048
  100.3 48.1 %shard_map.37 = f32[2,128,64,256]{3,2,1,0:T(8,128)} custom-call(bf16[2,9504,64]{2,1,0:T(8,128)(2,1)S(1)} %bitcast.9, bf16[64,256]{1,0:T(8,128)(2,1)S(1)} %fusion.3.kb_ref, bf16[256,256]{1,0:T(8,128)(2,1)S(1)} %copy.18.g_ref, f32[1,256]{1,0:T(1,128)S(1)} %bitcast.10, f32[1,256]{1,0:T(1,128)S(1)} %bitcast.11, f32[72,256]{1,0:T(8,128)S(1)} %broadcast_in_dim.8.cm_ref, ...), custom_call_target="tpu_custom_call" | custom-call | flops 6115295232 | bytes 19210240 | tf_op jit(solution)/shard_map/pallas_call | solution.py:130
  (5 shorter events, 0.0 us)
Async XLA Ops:
  0.0 15.5 %copy-start.1 = (f32[256]{0:T(256)S(1)}, f32[256]{0:T(256)}, u32[]{:S(2)}) copy-start(f32[256]{0:T(256)} %param.4) | copy-start | bytes 3076
  6.2 37.7 %all-to-all-start = ((bf16[4,2,128,1024]{2,1,0,3:T(2,128)(2,1)}), bf16[4,2,128,1024]{2,1,0,3:T(2,128)(2,1)S(1)}, u32[]{:S(2)}, u32[]{:S(2)}) async-start(bf16[4,2,128,1024]{2,1,0,3:T(2,128)(2,1)} %copy.10), calls=%async_computation | async-start | bytes 4194304 | tf_op jit(solution)/shard_map/all_to_all | solution.py:111
  15.5 36.1 %copy-start.2 = (f32[256]{0:T(256)S(1)}, f32[256]{0:T(256)}, u32[]{:S(2)}) copy-start(f32[256]{0:T(256)} %param.5) | copy-start | bytes 3076
  44.5 7.1 %collective-permute-start = (bf16[64,2,128,4]{2,3,1,0:T(4,128)(2,1)S(1)}, bf16[64,2,128,4]{2,3,1,0:T(4,128)(2,1)S(1)}, u32[]{:S(2)}, u32[]{:S(2)}) collective-permute-start(bf16[64,2,128,4]{2,3,1,0:T(4,128)(2,1)S(1)} %get-tuple-element.9), channel_id=1, source_target_pairs={{0,1},{1,2},{2,3},{3,4},{4,5},{5,6},{6,7},{7,8},{8,9},{9,10},{10,1... | collective-permute-start | bytes 393224 | tf_op jit(solution)/shard_map/ppermute | solution.py:34
  49.6 7.8 %collective-permute-start.1 = (bf16[64,2,128,4]{2,3,1,0:T(4,128)(2,1)S(1)}, bf16[64,2,128,4]{2,3,1,0:T(4,128)(2,1)S(1)}, u32[]{:S(2)}, u32[]{:S(2)}) collective-permute-start(bf16[64,2,128,4]{2,3,1,0:T(4,128)(2,1)S(1)} %get-tuple-element.10), channel_id=1, source_target_pairs={{1,0},{2,1},{3,2},{4,3},{5,4},{6,5},{7,6},{8,7},{9,8},{10,9},{11,1... | collective-permute-start | bytes 393224 | tf_op jit(solution)/shard_map/ppermute | solution.py:36
  66.5 8.7 %collective-permute-start.3 = (bf16[64,2,2,72]{3,0,2,1:T(8,128)(2,1)S(1)}, bf16[64,2,2,72]{3,0,2,1:T(8,128)(2,1)S(1)}, u32[]{:S(2)}, u32[]{:S(2)}) collective-permute-start(bf16[64,2,2,72]{3,0,2,1:T(8,128)(2,1)S(1)} %copy.14), channel_id=1, source_target_pairs={{16,0},{32,16},{48,32},{64,48},{80,64},{96,80},{112,96},{17,1},{33... | collective-permute-start | bytes 110600 | tf_op jit(solution)/shard_map/ppermute | solution.py:36
  67.8 5.3 %collective-permute-start.2 = (bf16[64,2,2,72]{3,0,2,1:T(8,128)(2,1)S(1)}, bf16[64,2,2,72]{3,0,2,1:T(8,128)(2,1)S(1)}, u32[]{:S(2)}, u32[]{:S(2)}) collective-permute-start(bf16[64,2,2,72]{3,0,2,1:T(8,128)(2,1)S(1)} %copy.13), channel_id=1, source_target_pairs={{0,16},{16,32},{32,48},{48,64},{64,80},{80,96},{96,112},{1,17},{17... | collective-permute-start | bytes 110600 | tf_op jit(solution)/shard_map/ppermute | solution.py:34
  97.9 2.4 %copy-start = (bf16[2,132,72,64]{3,2,1,0:T(8,128)(2,1)S(1)}, bf16[2,132,72,64]{3,2,1,0:T(8,128)(2,1)}, u32[]{:S(2)}) copy-start(bf16[2,132,72,64]{3,2,1,0:T(8,128)(2,1)} %copy.17) | copy-start | bytes 7299076

commit v10 on v5

--- a/solution.py
+++ b/solution.py
@@ -39,26 +39,23 @@
     )
 
 
-def split3(f):
-    return f.astype(jnp.bfloat16)
-
-
-def fit_kernel(wp, x_ref, kb_ref, g3_ref, step_ref, lam_ref, cm_ref, rm_ref,
+def fit_kernel(wp, x_ref, kb_ref, g3_ref, step_ref, alpha_ref, beta_ref, cm_ref, rm_ref,
                o_ref, b_ref, f0_ref, f1_ref, f3_ref, m_ref):
     t = pl.program_id(1)
     rows = TR + 2 * RH
     n = rows * wp
     base = pl.multiple_of(t * (TR * wp), 16)
     step = step_ref[...]
-    lam = lam_ref[...]
+    alpha = alpha_ref[...]
+    beta = beta_ref[...]
     cm = cm_ref[...]
 
-    b = jnp.dot(x_ref[0, pl.ds(base, n), :], kb_ref[...],
-                preferred_element_type=jnp.float32)
-    b_ref[...] = b
-    f0 = jnp.maximum(b * step, 0.0)
+    sb = jnp.dot(x_ref[0, pl.ds(base, n), :], kb_ref[...],
+                 preferred_element_type=jnp.float32) * step
+    b_ref[...] = sb
+    f0 = jnp.maximum(sb, 0.0)
     f0_ref[...] = f0
-    f3_ref[...] = split3(f0)
+    f3_ref[...] = f0.astype(jnp.bfloat16)
 
     def update(src_ref, q):
         o = pl.multiple_of(q * wp, 8)
@@ -67,10 +64,9 @@
         dn = src_ref[pl.ds(o + wp, wp), :]
         lf = pltpu.roll(c, 1, 0)
         rt = pltpu.roll(c, wp - 1, 0)
-        lap = 4.0 * c - up - dn - lf - rt
-        m = m_ref[pl.ds(o - wp, wp), :]
-        g = m - b_ref[pl.ds(o, wp), :] + lam * lap
-        return jnp.maximum(c - step * g, 0.0)
+        nb = (up + dn) + (lf + rt)
+        v = (alpha * c + beta * nb) + (b_ref[pl.ds(o, wp), :] - m_ref[pl.ds(o - wp, wp), :])
+        return jnp.maximum(v, 0.0)
 
     m_ref[...] = jnp.dot(f3_ref[pl.ds(wp, (rows - 2) * wp), :], g3_ref[...],
                          preferred_element_type=jnp.float32)
@@ -84,7 +80,7 @@
     f1_ref[pl.ds(0, wp), :] = jnp.zeros((wp, f1_ref.shape[1]), jnp.float32)
     f1_ref[pl.ds((rows - 1) * wp, wp), :] = jnp.zeros((wp, f1_ref.shape[1]), jnp.float32)
 
-    f3_ref[...] = split3(f1_ref[...])
+    f3_ref[...] = f1_ref[...].astype(jnp.bfloat16)
     m_ref[...] = jnp.dot(f3_ref[pl.ds(wp, (rows - 2) * wp), :], g3_ref[...],
                          preferred_element_type=jnp.float32)
 
@@ -100,8 +96,9 @@
 def per_device(images, rates, smoothing):
     kernel, gram, lam, step = kernel_parts(rates, smoothing)
     kb = kernel.astype(jnp.bfloat16)
-    gh = gram.astype(jnp.bfloat16)
-    g3 = gh
+    g3 = (gram * step[None, :]).astype(jnp.bfloat16)
+    beta = step * lam
+    alpha = 1.0 - 4.0 * beta
     x = lax.all_to_all(images, "gy", split_axis=3, concat_axis=0, tiled=True)
     e, sl, h, w = x.shape
     x = halo(x, "gy", 3, CH)
@@ -131,6 +128,7 @@
             pl.BlockSpec((r, r), lambda s, t: (0, 0)),
             pl.BlockSpec((1, r), lambda s, t: (0, 0)),
             pl.BlockSpec((1, r), lambda s, t: (0, 0)),
+            pl.BlockSpec((1, r), lambda s, t: (0, 0)),
             pl.BlockSpec((wp, r), lambda s, t: (0, 0)),
             pl.BlockSpec(memory_space=pltpu.SMEM),
         ],
@@ -150,7 +148,7 @@
             flops=flops, transcendentals=0,
             bytes_accessed=sl * (hp * wp * e * 2 + h * w * r * 4),
         ),
-    )(x, kb, g3, step[None, :], lam[None, :], cm, rm)
+    )(x, kb, g3, step[None, :], alpha[None, :], beta[None, :], cm, rm)
     return out
 
 

time: 148 us -> 145 us (0.980)
  Pallas kernels: 45.2 us -> 42.8 us
    pallas_call x1, Pallas kernels: 45.2 us -> 42.8 us  [per_device(): pl.pallas_call(functools.partial(fit_kernel, wp), out_shape=jax.ShapeDtyp...]
where the time goes in v10:
time: 145 us; the launch traced here: 143 us
  Pallas kernels  42.8 us (30%)
  waiting for transfers between devices  34.6 us (24%)
  local copies, waits for them, and re-layouts  32.1 us (22%)
  starting transfers between devices  21.6 us (15%)
  other arithmetic  11.3 us (8%)
    pallas_call x1, Pallas kernels, per_device(): pl.pallas_call(functools.partial(fit_kernel, wp), out_shape=jax.ShapeDtyp...  42.8 us
    all_to_all x1, waiting for transfers between devices, per_device(): x = lax.all_to_all(images, 'gy', split_axis=3, concat_axis=0, tiled=True)  27.6 us
    transpose x1, local copies, waits for them, and re-layouts, per_device(): x = jnp.transpose(x, (1, 2, 3, 0)).reshape(sl, hp * wp, e)  11 us
    transpose x1, other arithmetic, per_device(): x = jnp.transpose(x, (1, 2, 3, 0)).reshape(sl, hp * wp, e)  9.52 us
    all_to_all x1, starting transfers between devices, per_device(): x = lax.all_to_all(images, 'gy', split_axis=3, concat_axis=0, tiled=True)  9.3 us
    ppermute x2, starting transfers between devices, halo(): lax.ppermute(tail, axis, [(i, i + 1) for i in range(count - 1)])  9.06 us
    unnamed x7, local copies, waits for them, and re-layouts  8.57 us
    ppermute x2, waiting for transfers between devices, halo(): lax.ppermute(head, axis, [(i + 1, i) for i in range(count - 1)])  5.74 us
  transfers between devices with their start and end apart: 5, of which 3 were waited for; matrix products, arithmetic and copies ran while one was open for 2% of the time, Pallas kernels for 0%

profile of v10, /device:TPU:1, one launch (start us, length us, event | category | flops | bytes accessed | tf_op | source)
XLA Modules:
  0.0 143.1 jit_solution(17460606738867730461)
XLA Ops:
  0.0 0.0 copy-start.2
  0.0 0.0 copy-start.1
  0.0 6.2 %copy.10 = bf16[4,2,128,1024]{2,1,0,3:T(2,128)(2,1)} copy(bf16[4,2,128,1024]{3,2,1,0:T(8,128)(2,1)} %param.3) | data formatting | bytes 4194304 | tf_op args[0]
  6.2 9.3 %all-to-all-start = ((bf16[4,2,128,1024]{2,1,0,3:T(2,128)(2,1)}), bf16[4,2,128,1024]{2,1,0,3:T(2,128)(2,1)S(1)}, u32[]{:S(2)}, u32[]{:S(2)}) async-start(bf16[4,2,128,1024]{2,1,0,3:T(2,128)(2,1)} %copy.10), calls=%async_computation | async-start | bytes 4194304 | tf_op jit(solution)/shard_map/all_to_all | solution.py:102
  15.5 0.0 copy-done.2
  15.5 0.1 multiply_reduce_fusion
  15.6 0.5 fusion.9
  16.1 0.1 copy.18
  16.3 0.0 copy-done.1
  16.3 27.6 %all-to-all-done = bf16[4,2,128,1024]{2,1,0,3:T(2,128)(2,1)S(1)} async-done(((bf16[4,2,128,1024]{2,1,0,3:T(2,128)(2,1)}), bf16[4,2,128,1024]{2,1,0,3:T(2,128)(2,1)S(1)}, u32[]{:S(2)}, u32[]{:S(2)}) %all-to-all-start) | async-done | bytes 2097184 | tf_op jit(solution)/shard_map/all_to_all | solution.py:102
  43.9 0.3 copy.11
  44.2 0.2 copy.12
  44.4 0.1 fusion.8
  44.5 5.1 %collective-permute-start = (bf16[64,2,128,4]{2,3,1,0:T(4,128)(2,1)S(1)}, bf16[64,2,128,4]{2,3,1,0:T(4,128)(2,1)S(1)}, u32[]{:S(2)}, u32[]{:S(2)}) collective-permute-start(bf16[64,2,128,4]{2,3,1,0:T(4,128)(2,1)S(1)} %get-tuple-element.10), channel_id=1, source_target_pairs={{0,1},{1,2},{2,3},{3,4},{4,5},{5,6},{6,7},{7,8},{8,9},{9,10},{10,1... | collective-permute-start | bytes 393224 | tf_op jit(solution)/shard_map/ppermute | solution.py:34
  49.6 1.9 %collective-permute-start.1 = (bf16[64,2,128,4]{2,3,1,0:T(4,128)(2,1)S(1)}, bf16[64,2,128,4]{2,3,1,0:T(4,128)(2,1)S(1)}, u32[]{:S(2)}, u32[]{:S(2)}) collective-permute-start(bf16[64,2,128,4]{2,3,1,0:T(4,128)(2,1)S(1)} %get-tuple-element.11), channel_id=1, source_target_pairs={{1,0},{2,1},{3,2},{4,3},{5,4},{6,5},{7,6},{8,7},{9,8},{10,9},{11,1... | collective-permute-start | bytes 393224 | tf_op jit(solution)/shard_map/ppermute | solution.py:36
  51.5 0.1 fusion.3.kb_ref
  51.7 0.0 collective-permute-done
  51.7 5.7 %collective-permute-done.1 = bf16[64,2,128,4]{2,3,1,0:T(4,128)(2,1)S(1)} collective-permute-done((bf16[64,2,128,4]{2,3,1,0:T(4,128)(2,1)S(1)}, bf16[64,2,128,4]{2,3,1,0:T(4,128)(2,1)S(1)}, u32[]{:S(2)}, u32[]{:S(2)}) %collective-permute-start.1) | collective-permute-done | bytes 131104 | tf_op jit(solution)/shard_map/ppermute | solution.py:36
  57.4 1.6 %pad_maximum_fusion = bf16[64,2,128,72]{2,3,1,0:T(8,128)(2,1)S(1)} fusion(bf16[64,2,128,4]{2,3,1,0:T(4,128)(2,1)S(1)} %collective-permute-done.1, bf16[64,2,128,64]{2,3,1,0:T(8,128)(2,1)S(1)} %bitcast.15, bf16[64,2,128,4]{2,3,1,0:T(4,128)(2,1)S(1)} %collective-permute-done), kind=kLoop, calls=%fused_computation.1 | loop fusion | flops 7077888 | bytes 4718592 | tf_op jit(solution)/shard_map/concatenate | solution.py:32
  59.0 3.0 %fusion.7 = (bf16[64,2,2,72]{2,3,1,0:T(8,128)(2,1)}, bf16[64,2,2,72]{2,3,1,0:T(8,128)(2,1)}) fusion(bf16[64,2,128,72]{2,3,1,0:T(8,128)(2,1)S(1)} %pad_maximum_fusion), kind=kLoop, calls=%fused_computation.17 | loop fusion | bytes 147456 | tf_op jit(solution)/shard_map/slice | solution.py:31
  62.0 2.3 %copy.13 = bf16[64,2,2,72]{3,0,2,1:T(8,128)(2,1)S(1)} copy(bf16[64,2,2,72]{2,3,1,0:T(8,128)(2,1)} %get-tuple-element.8) | data formatting | bytes 73728 | tf_op jit(solution)/shard_map/slice | solution.py:31
  64.3 2.3 %copy.14 = bf16[64,2,2,72]{3,0,2,1:T(8,128)(2,1)S(1)} copy(bf16[64,2,2,72]{2,3,1,0:T(8,128)(2,1)} %get-tuple-element.9) | data formatting | bytes 73728 | tf_op jit(solution)/shard_map/slice | solution.py:30
  66.5 1.3 collective-permute-start.3
  67.8 4.0 %collective-permute-start.2 = (bf16[64,2,2,72]{3,0,2,1:T(8,128)(2,1)S(1)}, bf16[64,2,2,72]{3,0,2,1:T(8,128)(2,1)S(1)}, u32[]{:S(2)}, u32[]{:S(2)}) collective-permute-start(bf16[64,2,2,72]{3,0,2,1:T(8,128)(2,1)S(1)} %copy.13), channel_id=1, source_target_pairs={{0,16},{16,32},{32,48},{48,64},{64,80},{80,96},{96,112},{1,17},{17... | collective-permute-start | bytes 110600 | tf_op jit(solution)/shard_map/ppermute | solution.py:34
  71.9 1.3 collective-permute-done.2
  73.1 2.1 %copy.15 = bf16[64,2,2,72]{2,3,1,0:T(8,128)(2,1)} copy(bf16[64,2,2,72]{3,0,2,1:T(8,128)(2,1)S(1)} %collective-permute-done.2) | data formatting | bytes 73728 | tf_op jit(solution)/shard_map/ppermute | solution.py:34
  75.2 0.0 collective-permute-done.3
  75.2 2.1 %copy.16 = bf16[64,2,2,72]{2,3,1,0:T(8,128)(2,1)} copy(bf16[64,2,2,72]{3,0,2,1:T(8,128)(2,1)S(1)} %collective-permute-done.3) | data formatting | bytes 73728 | tf_op jit(solution)/shard_map/ppermute | solution.py:36
  77.3 9.5 %maximum_bitcast_fusion = bf16[2,132,72,64]{1,2,0,3:T(8,128)(2,1)} fusion(bf16[64,2,2,72]{2,3,1,0:T(8,128)(2,1)} %copy.16, bf16[64,2,128,4]{2,3,1,0:T(4,128)(2,1)S(1)} %collective-permute-done.1, bf16[64,2,128,64]{2,3,1,0:T(8,128)(2,1)S(1)} %bitcast.16, bf16[64,2,128,4]{2,3,1,0:T(4,128)(2,1)S(1)} %collective-permute-done, bf16[64,2,2,72]{2,3,1,0:T(8,128)(2,1)} %copy.15), kind=kLoop, calls=%fused_computation | loop fusion | flops 12165120 | bytes 4866048 | tf_op jit(solution)/shard_map/transpose | solution.py:107
  86.8 11.0 %copy.17 = bf16[2,132,72,64]{3,2,1,0:T(8,128)(2,1)} copy(bf16[2,132,72,64]{1,2,0,3:T(8,128)(2,1)} %maximum_bitcast_fusion) | data formatting | bytes 4866048 | tf_op jit(solution)/shard_map/transpose | solution.py:107
  97.8 0.1 broadcast_in_dim.22.cm_ref
  97.9 0.0 copy-start
  97.9 2.4 %copy-done = bf16[2,132,72,64]{3,2,1,0:T(8,128)(2,1)S(1)} copy-done((bf16[2,132,72,64]{3,2,1,0:T(8,128)(2,1)S(1)}, bf16[2,132,72,64]{3,2,1,0:T(8,128)(2,1)}, u32[]{:S(2)}) %copy-start) | copy-done | bytes 2433048
  100.3 42.8 %shard_map.37 = f32[2,128,64,256]{3,2,1,0:T(8,128)} custom-call(bf16[2,9504,64]{2,1,0:T(8,128)(2,1)S(1)} %bitcast.10, bf16[64,256]{1,0:T(8,128)(2,1)S(1)} %fusion.3.kb_ref, bf16[256,256]{1,0:T(8,128)(2,1)S(1)} %multiply_convert_fusion.g3_ref, f32[1,256]{1,0:T(1,128)S(1)} %bitcast.11, f32[1,256]{1,0:T(1,128)S(1)} %bitcast.12, f32[1,256]{1,0:T(1,128)S(1)} %bitcast.13, ...), custom_call_target="tpu_custom_call" | custom-call | flops 6115295232 | bytes 19210240 | tf_op jit(solution)/shard_map/pallas_call | solution.py:121
  (6 shorter events, 0.1 us)
Async XLA Ops:
  0.0 15.5 %copy-start.2 = (f32[256]{0:T(256)S(1)}, f32[256]{0:T(256)}, u32[]{:S(2)}) copy-start(f32[256]{0:T(256)} %param.4) | copy-start | bytes 3076
  0.0 16.3 %copy-start.1 = (f32[256]{0:T(256)S(1)}, f32[256]{0:T(256)}, u32[]{:S(2)}) copy-start(f32[256]{0:T(256)} %param.5) | copy-start | bytes 3076
  6.2 37.7 %all-to-all-start = ((bf16[4,2,128,1024]{2,1,0,3:T(2,128)(2,1)}), bf16[4,2,128,1024]{2,1,0,3:T(2,128)(2,1)S(1)}, u32[]{:S(2)}, u32[]{:S(2)}) async-start(bf16[4,2,128,1024]{2,1,0,3:T(2,128)(2,1)} %copy.10), calls=%async_computation | async-start | bytes 4194304 | tf_op jit(solution)/shard_map/all_to_all | solution.py:102
  44.5 7.1 %collective-permute-start = (bf16[64,2,128,4]{2,3,1,0:T(4,128)(2,1)S(1)}, bf16[64,2,128,4]{2,3,1,0:T(4,128)(2,1)S(1)}, u32[]{:S(2)}, u32[]{:S(2)}) collective-permute-start(bf16[64,2,128,4]{2,3,1,0:T(4,128)(2,1)S(1)} %get-tuple-element.10), channel_id=1, source_target_pairs={{0,1},{1,2},{2,3},{3,4},{4,5},{5,6},{6,7},{7,8},{8,9},{9,10},{10,1... | collective-permute-start | bytes 393224 | tf_op jit(solution)/shard_map/ppermute | solution.py:34
  49.6 7.8 %collective-permute-start.1 = (bf16[64,2,128,4]{2,3,1,0:T(4,128)(2,1)S(1)}, bf16[64,2,128,4]{2,3,1,0:T(4,128)(2,1)S(1)}, u32[]{:S(2)}, u32[]{:S(2)}) collective-permute-start(bf16[64,2,128,4]{2,3,1,0:T(4,128)(2,1)S(1)} %get-tuple-element.11), channel_id=1, source_target_pairs={{1,0},{2,1},{3,2},{4,3},{5,4},{6,5},{7,6},{8,7},{9,8},{10,9},{11,1... | collective-permute-start | bytes 393224 | tf_op jit(solution)/shard_map/ppermute | solution.py:36
  66.5 8.7 %collective-permute-start.3 = (bf16[64,2,2,72]{3,0,2,1:T(8,128)(2,1)S(1)}, bf16[64,2,2,72]{3,0,2,1:T(8,128)(2,1)S(1)}, u32[]{:S(2)}, u32[]{:S(2)}) collective-permute-start(bf16[64,2,2,72]{3,0,2,1:T(8,128)(2,1)S(1)} %copy.14), channel_id=1, source_target_pairs={{16,0},{32,16},{48,32},{64,48},{80,64},{96,80},{112,96},{17,1},{33... | collective-permute-start | bytes 110600 | tf_op jit(solution)/shard_map/ppermute | solution.py:36
  67.8 5.3 %collective-permute-start.2 = (bf16[64,2,2,72]{3,0,2,1:T(8,128)(2,1)S(1)}, bf16[64,2,2,72]{3,0,2,1:T(8,128)(2,1)S(1)}, u32[]{:S(2)}, u32[]{:S(2)}) collective-permute-start(bf16[64,2,2,72]{3,0,2,1:T(8,128)(2,1)S(1)} %copy.13), channel_id=1, source_target_pairs={{0,16},{16,32},{32,48},{48,64},{64,80},{80,96},{96,112},{1,17},{17... | collective-permute-start | bytes 110600 | tf_op jit(solution)/shard_map/ppermute | solution.py:34
  97.9 2.4 %copy-start = (bf16[2,132,72,64]{3,2,1,0:T(8,128)(2,1)S(1)}, bf16[2,132,72,64]{3,2,1,0:T(8,128)(2,1)}, u32[]{:S(2)}) copy-start(bf16[2,132,72,64]{3,2,1,0:T(8,128)(2,1)} %copy.17) | copy-start | bytes 7299076

commit v11 on v10

--- a/solution.py
+++ b/solution.py
@@ -11,7 +11,7 @@
 ITERS = 3
 RH = 2
 CH = 4
-TR = 32
+TR = 64
 
 
 def kernel_parts(rates, smoothing):

time: 145 us -> 144 us (level)
  no operation moved by 1% of the time
where the time goes in v11:
time: 144 us; the launch traced here: 142 us
  Pallas kernels  41.4 us (29%)
  waiting for transfers between devices  34.5 us (24%)
  local copies, waits for them, and re-layouts  32.1 us (22%)
  starting transfers between devices  21.8 us (15%)
  other arithmetic  11.3 us (8%)
    pallas_call x1, Pallas kernels, per_device(): pl.pallas_call(functools.partial(fit_kernel, wp), out_shape=jax.ShapeDtyp...  41.4 us
    all_to_all x1, waiting for transfers between devices, per_device(): x = lax.all_to_all(images, 'gy', split_axis=3, concat_axis=0, tiled=True)  27.6 us
    transpose x1, local copies, waits for them, and re-layouts, per_device(): x = jnp.transpose(x, (1, 2, 3, 0)).reshape(sl, hp * wp, e)  11 us
    transpose x1, other arithmetic, per_device(): x = jnp.transpose(x, (1, 2, 3, 0)).reshape(sl, hp * wp, e)  9.52 us
    all_to_all x1, starting transfers between devices, per_device(): x = lax.all_to_all(images, 'gy', split_axis=3, concat_axis=0, tiled=True)  9.3 us
    ppermute x2, starting transfers between devices, halo(): lax.ppermute(tail, axis, [(i, i + 1) for i in range(count - 1)])  9.24 us
    unnamed x7, local copies, waits for them, and re-layouts  8.57 us
    ppermute x2, waiting for transfers between devices, halo(): lax.ppermute(head, axis, [(i + 1, i) for i in range(count - 1)])  5.74 us
  transfers between devices with their start and end apart: 5, of which 3 were waited for; matrix products, arithmetic and copies ran while one was open for 2% of the time, Pallas kernels for 0%

profile of v11, /device:TPU:1, one launch (start us, length us, event | category | flops | bytes accessed | tf_op | source)
XLA Modules:
  0.0 141.7 jit_solution(12135851997329410010)
XLA Ops:
  0.0 0.0 copy-start.2
  0.0 0.0 copy-start.1
  0.0 6.2 %copy.10 = bf16[4,2,128,1024]{2,1,0,3:T(2,128)(2,1)} copy(bf16[4,2,128,1024]{3,2,1,0:T(8,128)(2,1)} %param.3) | data formatting | bytes 4194304 | tf_op args[0]
  6.2 9.3 %all-to-all-start = ((bf16[4,2,128,1024]{2,1,0,3:T(2,128)(2,1)}), bf16[4,2,128,1024]{2,1,0,3:T(2,128)(2,1)S(1)}, u32[]{:S(2)}, u32[]{:S(2)}) async-start(bf16[4,2,128,1024]{2,1,0,3:T(2,128)(2,1)} %copy.10), calls=%async_computation | async-start | bytes 4194304 | tf_op jit(solution)/shard_map/all_to_all | solution.py:102
  15.5 0.0 copy-done.2
  15.5 0.1 multiply_reduce_fusion
  15.6 0.5 fusion.9
  16.1 0.1 copy.18
  16.3 0.0 copy-done.1
  16.3 27.6 %all-to-all-done = bf16[4,2,128,1024]{2,1,0,3:T(2,128)(2,1)S(1)} async-done(((bf16[4,2,128,1024]{2,1,0,3:T(2,128)(2,1)}), bf16[4,2,128,1024]{2,1,0,3:T(2,128)(2,1)S(1)}, u32[]{:S(2)}, u32[]{:S(2)}) %all-to-all-start) | async-done | bytes 2097184 | tf_op jit(solution)/shard_map/all_to_all | solution.py:102
  43.9 0.3 copy.11
  44.2 0.2 copy.12
  44.4 0.1 fusion.8
  44.5 5.1 %collective-permute-start = (bf16[64,2,128,4]{2,3,1,0:T(4,128)(2,1)S(1)}, bf16[64,2,128,4]{2,3,1,0:T(4,128)(2,1)S(1)}, u32[]{:S(2)}, u32[]{:S(2)}) collective-permute-start(bf16[64,2,128,4]{2,3,1,0:T(4,128)(2,1)S(1)} %get-tuple-element.10), channel_id=1, source_target_pairs={{0,1},{1,2},{2,3},{3,4},{4,5},{5,6},{6,7},{7,8},{8,9},{9,10},{10,1... | collective-permute-start | bytes 393224 | tf_op jit(solution)/shard_map/ppermute | solution.py:34
  49.6 1.9 %collective-permute-start.1 = (bf16[64,2,128,4]{2,3,1,0:T(4,128)(2,1)S(1)}, bf16[64,2,128,4]{2,3,1,0:T(4,128)(2,1)S(1)}, u32[]{:S(2)}, u32[]{:S(2)}) collective-permute-start(bf16[64,2,128,4]{2,3,1,0:T(4,128)(2,1)S(1)} %get-tuple-element.11), channel_id=1, source_target_pairs={{1,0},{2,1},{3,2},{4,3},{5,4},{6,5},{7,6},{8,7},{9,8},{10,9},{11,1... | collective-permute-start | bytes 393224 | tf_op jit(solution)/shard_map/ppermute | solution.py:36
  51.5 0.1 fusion.3.kb_ref
  51.7 0.0 collective-permute-done
  51.7 5.7 %collective-permute-done.1 = bf16[64,2,128,4]{2,3,1,0:T(4,128)(2,1)S(1)} collective-permute-done((bf16[64,2,128,4]{2,3,1,0:T(4,128)(2,1)S(1)}, bf16[64,2,128,4]{2,3,1,0:T(4,128)(2,1)S(1)}, u32[]{:S(2)}, u32[]{:S(2)}) %collective-permute-start.1) | collective-permute-done | bytes 131104 | tf_op jit(solution)/shard_map/ppermute | solution.py:36
  57.4 1.6 %pad_maximum_fusion = bf16[64,2,128,72]{2,3,1,0:T(8,128)(2,1)S(1)} fusion(bf16[64,2,128,4]{2,3,1,0:T(4,128)(2,1)S(1)} %collective-permute-done.1, bf16[64,2,128,64]{2,3,1,0:T(8,128)(2,1)S(1)} %bitcast.15, bf16[64,2,128,4]{2,3,1,0:T(4,128)(2,1)S(1)} %collective-permute-done), kind=kLoop, calls=%fused_computation.1 | loop fusion | flops 7077888 | bytes 4718592 | tf_op jit(solution)/shard_map/concatenate | solution.py:32
  59.0 3.0 %fusion.7 = (bf16[64,2,2,72]{2,3,1,0:T(8,128)(2,1)}, bf16[64,2,2,72]{2,3,1,0:T(8,128)(2,1)}) fusion(bf16[64,2,128,72]{2,3,1,0:T(8,128)(2,1)S(1)} %pad_maximum_fusion), kind=kLoop, calls=%fused_computation.17 | loop fusion | bytes 147456 | tf_op jit(solution)/shard_map/slice | solution.py:31
  62.0 2.3 %copy.13 = bf16[64,2,2,72]{3,0,2,1:T(8,128)(2,1)S(1)} copy(bf16[64,2,2,72]{2,3,1,0:T(8,128)(2,1)} %get-tuple-element.8) | data formatting | bytes 73728 | tf_op jit(solution)/shard_map/slice | solution.py:31
  64.3 2.3 %copy.14 = bf16[64,2,2,72]{3,0,2,1:T(8,128)(2,1)S(1)} copy(bf16[64,2,2,72]{2,3,1,0:T(8,128)(2,1)} %get-tuple-element.9) | data formatting | bytes 73728 | tf_op jit(solution)/shard_map/slice | solution.py:30
  66.5 1.3 collective-permute-start.3
  67.8 4.2 %collective-permute-start.2 = (bf16[64,2,2,72]{3,0,2,1:T(8,128)(2,1)S(1)}, bf16[64,2,2,72]{3,0,2,1:T(8,128)(2,1)S(1)}, u32[]{:S(2)}, u32[]{:S(2)}) collective-permute-start(bf16[64,2,2,72]{3,0,2,1:T(8,128)(2,1)S(1)} %copy.13), channel_id=1, source_target_pairs={{0,16},{16,32},{32,48},{48,64},{64,80},{80,96},{96,112},{1,17},{17... | collective-permute-start | bytes 110600 | tf_op jit(solution)/shard_map/ppermute | solution.py:34
  72.0 1.1 collective-permute-done.2
  73.1 2.1 %copy.15 = bf16[64,2,2,72]{2,3,1,0:T(8,128)(2,1)} copy(bf16[64,2,2,72]{3,0,2,1:T(8,128)(2,1)S(1)} %collective-permute-done.2) | data formatting | bytes 73728 | tf_op jit(solution)/shard_map/ppermute | solution.py:34
  75.2 0.0 collective-permute-done.3
  75.2 2.1 %copy.16 = bf16[64,2,2,72]{2,3,1,0:T(8,128)(2,1)} copy(bf16[64,2,2,72]{3,0,2,1:T(8,128)(2,1)S(1)} %collective-permute-done.3) | data formatting | bytes 73728 | tf_op jit(solution)/shard_map/ppermute | solution.py:36
  77.3 9.5 %maximum_bitcast_fusion = bf16[2,132,72,64]{1,2,0,3:T(8,128)(2,1)} fusion(bf16[64,2,2,72]{2,3,1,0:T(8,128)(2,1)} %copy.16, bf16[64,2,128,4]{2,3,1,0:T(4,128)(2,1)S(1)} %collective-permute-done.1, bf16[64,2,128,64]{2,3,1,0:T(8,128)(2,1)S(1)} %bitcast.16, bf16[64,2,128,4]{2,3,1,0:T(4,128)(2,1)S(1)} %collective-permute-done, bf16[64,2,2,72]{2,3,1,0:T(8,128)(2,1)} %copy.15), kind=kLoop, calls=%fused_computation | loop fusion | flops 12165120 | bytes 4866048 | tf_op jit(solution)/shard_map/transpose | solution.py:107
  86.8 11.0 %copy.17 = bf16[2,132,72,64]{3,2,1,0:T(8,128)(2,1)} copy(bf16[2,132,72,64]{1,2,0,3:T(8,128)(2,1)} %maximum_bitcast_fusion) | data formatting | bytes 4866048 | tf_op jit(solution)/shard_map/transpose | solution.py:107
  97.8 0.1 broadcast_in_dim.22.cm_ref
  97.9 0.0 copy-start
  97.9 2.4 %copy-done = bf16[2,132,72,64]{3,2,1,0:T(8,128)(2,1)S(1)} copy-done((bf16[2,132,72,64]{3,2,1,0:T(8,128)(2,1)S(1)}, bf16[2,132,72,64]{3,2,1,0:T(8,128)(2,1)}, u32[]{:S(2)}) %copy-start) | copy-done | bytes 2433048
  100.3 41.4 %shard_map.37 = f32[2,128,64,256]{3,2,1,0:T(8,128)} custom-call(bf16[2,9504,64]{2,1,0:T(8,128)(2,1)S(1)} %bitcast.10, bf16[64,256]{1,0:T(8,128)(2,1)S(1)} %fusion.3.kb_ref, bf16[256,256]{1,0:T(8,128)(2,1)S(1)} %multiply_convert_fusion.g3_ref, f32[1,256]{1,0:T(1,128)S(1)} %bitcast.11, f32[1,256]{1,0:T(1,128)S(1)} %bitcast.12, f32[1,256]{1,0:T(1,128)S(1)} %bitcast.13, ...), custom_call_target="tpu_custom_call" | custom-call | flops 5775556608 | bytes 19210240 | tf_op jit(solution)/shard_map/pallas_call | solution.py:121
  (6 shorter events, 0.1 us)
Async XLA Ops:
  0.0 15.5 %copy-start.2 = (f32[256]{0:T(256)S(1)}, f32[256]{0:T(256)}, u32[]{:S(2)}) copy-start(f32[256]{0:T(256)} %param.4) | copy-start | bytes 3076
  0.0 16.3 %copy-start.1 = (f32[256]{0:T(256)S(1)}, f32[256]{0:T(256)}, u32[]{:S(2)}) copy-start(f32[256]{0:T(256)} %param.5) | copy-start | bytes 3076
  6.2 37.7 %all-to-all-start = ((bf16[4,2,128,1024]{2,1,0,3:T(2,128)(2,1)}), bf16[4,2,128,1024]{2,1,0,3:T(2,128)(2,1)S(1)}, u32[]{:S(2)}, u32[]{:S(2)}) async-start(bf16[4,2,128,1024]{2,1,0,3:T(2,128)(2,1)} %copy.10), calls=%async_computation | async-start | bytes 4194304 | tf_op jit(solution)/shard_map/all_to_all | solution.py:102
  44.5 7.1 %collective-permute-start = (bf16[64,2,128,4]{2,3,1,0:T(4,128)(2,1)S(1)}, bf16[64,2,128,4]{2,3,1,0:T(4,128)(2,1)S(1)}, u32[]{:S(2)}, u32[]{:S(2)}) collective-permute-start(bf16[64,2,128,4]{2,3,1,0:T(4,128)(2,1)S(1)} %get-tuple-element.10), channel_id=1, source_target_pairs={{0,1},{1,2},{2,3},{3,4},{4,5},{5,6},{6,7},{7,8},{8,9},{9,10},{10,1... | collective-permute-start | bytes 393224 | tf_op jit(solution)/shard_map/ppermute | solution.py:34
  49.6 7.8 %collective-permute-start.1 = (bf16[64,2,128,4]{2,3,1,0:T(4,128)(2,1)S(1)}, bf16[64,2,128,4]{2,3,1,0:T(4,128)(2,1)S(1)}, u32[]{:S(2)}, u32[]{:S(2)}) collective-permute-start(bf16[64,2,128,4]{2,3,1,0:T(4,128)(2,1)S(1)} %get-tuple-element.11), channel_id=1, source_target_pairs={{1,0},{2,1},{3,2},{4,3},{5,4},{6,5},{7,6},{8,7},{9,8},{10,9},{11,1... | collective-permute-start | bytes 393224 | tf_op jit(solution)/shard_map/ppermute | solution.py:36
  66.5 8.7 %collective-permute-start.3 = (bf16[64,2,2,72]{3,0,2,1:T(8,128)(2,1)S(1)}, bf16[64,2,2,72]{3,0,2,1:T(8,128)(2,1)S(1)}, u32[]{:S(2)}, u32[]{:S(2)}) collective-permute-start(bf16[64,2,2,72]{3,0,2,1:T(8,128)(2,1)S(1)} %copy.14), channel_id=1, source_target_pairs={{16,0},{32,16},{48,32},{64,48},{80,64},{96,80},{112,96},{17,1},{33... | collective-permute-start | bytes 110600 | tf_op jit(solution)/shard_map/ppermute | solution.py:36
  67.8 5.3 %collective-permute-start.2 = (bf16[64,2,2,72]{3,0,2,1:T(8,128)(2,1)S(1)}, bf16[64,2,2,72]{3,0,2,1:T(8,128)(2,1)S(1)}, u32[]{:S(2)}, u32[]{:S(2)}) collective-permute-start(bf16[64,2,2,72]{3,0,2,1:T(8,128)(2,1)S(1)} %copy.13), channel_id=1, source_target_pairs={{0,16},{16,32},{32,48},{48,64},{64,80},{80,96},{96,112},{1,17},{17... | collective-permute-start | bytes 110600 | tf_op jit(solution)/shard_map/ppermute | solution.py:34
  97.9 2.4 %copy-start = (bf16[2,132,72,64]{3,2,1,0:T(8,128)(2,1)S(1)}, bf16[2,132,72,64]{3,2,1,0:T(8,128)(2,1)}, u32[]{:S(2)}) copy-start(bf16[2,132,72,64]{3,2,1,0:T(8,128)(2,1)} %copy.17) | copy-start | bytes 7299076

commit v12 on v11

--- a/solution.py
+++ b/solution.py
@@ -50,7 +50,7 @@
     beta = beta_ref[...]
     cm = cm_ref[...]
 
-    sb = jnp.dot(x_ref[0, pl.ds(base, n), :], kb_ref[...],
+    sb = jnp.dot(x_ref[0, pl.ds(base, n), :].astype(jnp.bfloat16), kb_ref[...],
                  preferred_element_type=jnp.float32) * step
     b_ref[...] = sb
     f0 = jnp.maximum(sb, 0.0)
@@ -104,7 +104,9 @@
     x = halo(x, "gy", 3, CH)
     x = halo(x, "gx", 2, RH)
     hp, wp = h + 2 * RH, w + 2 * CH
-    x = jnp.transpose(x, (1, 2, 3, 0)).reshape(sl, hp * wp, e)
+    eye = jnp.eye(e, dtype=jnp.bfloat16)
+    x = jnp.einsum("esij,ef->sijf", x, eye, preferred_element_type=jnp.float32)
+    x = x.reshape(sl, hp * wp, e)
     r = kernel.shape[1]
 
     gi = lax.axis_index("gx")
@@ -146,7 +148,7 @@
         ),
         cost_estimate=pl.CostEstimate(
             flops=flops, transcendentals=0,
-            bytes_accessed=sl * (hp * wp * e * 2 + h * w * r * 4),
+            bytes_accessed=sl * (hp * wp * e * 4 + h * w * r * 4),
         ),
     )(x, kb, g3, step[None, :], alpha[None, :], beta[None, :], cm, rm)
     return out

time: 144 us -> 161 us (1.12)
  the two profiles are of different devices: /device:TPU:1 before, /device:TPU:42 now
where the time goes in v12:
time: 161 us
  local copies, waits for them, and re-layouts  48.1 us (30%)
  Pallas kernels  43.3 us (27%)
  waiting for transfers between devices  38.4 us (24%)
  starting transfers between devices  21.2 us (13%)
  matrix products  7.97 us (5%)
    pallas_call x1, Pallas kernels, per_device(): pl.pallas_call(functools.partial(fit_kernel, wp), out_shape=jax.ShapeDtyp...  43.3 us
    all_to_all x1, waiting for transfers between devices, per_device(): x = lax.all_to_all(images, 'gy', split_axis=3, concat_axis=0, tiled=True)  26.9 us
    slice x2, local copies, waits for them, and re-layouts, halo(): lax.slice_in_dim(cells, cells.shape[dim] - width, cells.shape[dim], axis=...  13.5 us
    ppermute x2, starting transfers between devices, halo(): lax.ppermute(head, axis, [(i + 1, i) for i in range(count - 1)])  7.8 us
    dot_general x1, matrix products, per_device(): x = jnp.einsum('esij,ef->sijf', x, eye, preferred_element_type=jnp.float32)  7.46 us
    ppermute x1, local copies, waits for them, and re-layouts, halo(): lax.ppermute(tail, axis, [(i, i + 1) for i in range(count - 1)])  7.45 us
    ppermute x1, local copies, waits for them, and re-layouts, halo(): lax.ppermute(head, axis, [(i + 1, i) for i in range(count - 1)])  7.44 us
    all_to_all x1, starting transfers between devices, per_device(): x = lax.all_to_all(images, 'gy', split_axis=3, concat_axis=0, tiled=True)  7.35 us
  transfers between devices with their start and end apart: 5, of which 4 were waited for; matrix products, arithmetic and copies ran while one was open for 5% of the time, Pallas kernels for 0%

profile of v12, /device:TPU:42, one launch (start us, length us, event | category | flops | bytes accessed | tf_op | source)
XLA Modules:
  0.0 160.7 jit_solution(2223791134911065717)
XLA Ops:
  0.0 0.0 copy-start.4
  0.0 0.0 copy-start.3
  0.0 6.2 %copy.11 = bf16[4,2,128,1024]{2,1,0,3:T(2,128)(2,1)} copy(bf16[4,2,128,1024]{3,2,1,0:T(8,128)(2,1)} %param.3) | data formatting | bytes 4194304 | tf_op args[0]
  6.2 7.3 %all-to-all-start = ((bf16[4,2,128,1024]{2,1,0,3:T(2,128)(2,1)}), bf16[4,2,128,1024]{2,1,0,3:T(2,128)(2,1)}, u32[]{:S(2)}, u32[]{:S(2)}) async-start(bf16[4,2,128,1024]{2,1,0,3:T(2,128)(2,1)} %copy.11), calls=%async_computation | async-start | bytes 4194304 | tf_op jit(solution)/shard_map/all_to_all | solution.py:102
  13.5 0.0 copy-done.4
  13.5 0.1 multiply_reduce_fusion
  13.7 0.5 fusion.21
  14.2 0.1 copy.19
  14.3 0.0 copy-done.3
  14.4 26.9 %all-to-all-done = bf16[4,2,128,1024]{2,1,0,3:T(2,128)(2,1)} async-done(((bf16[4,2,128,1024]{2,1,0,3:T(2,128)(2,1)}), bf16[4,2,128,1024]{2,1,0,3:T(2,128)(2,1)}, u32[]{:S(2)}, u32[]{:S(2)}) %all-to-all-start) | async-done | bytes 2097184 | tf_op jit(solution)/shard_map/all_to_all | solution.py:102
  41.3 1.9 %copy.12 = bf16[4,2,128,1024]{2,3,1,0:T(8,128)(2,1)S(1)} copy(bf16[4,2,128,1024]{2,1,0,3:T(2,128)(2,1)} %all-to-all-done) | data formatting | bytes 4194304 | tf_op jit(solution)/shard_map/all_to_all | solution.py:102
  43.1 5.3 %copy.13 = bf16[16,4,2,128,64]{4,1,0,3,2:T(4,128)(2,1)} copy(bf16[16,4,2,128,64]{3,4,0,2,1:T(8,128)(2,1)S(1)} %bitcast.20) | data formatting | bytes 4194304 | tf_op jit(solution)/shard_map/all_to_all | solution.py:102
  48.4 7.3 %fusion.20 = (bf16[64,2,128,4]{3,0,2,1:T(8,128)(2,1)}, bf16[64,2,128,4]{3,0,2,1:T(8,128)(2,1)}) fusion(bf16[64,2,128,64]{3,0,2,1:T(8,128)(2,1)} %bitcast.16), kind=kLoop, calls=%fused_computation.31 | loop fusion | bytes 524288 | tf_op jit(solution)/shard_map/slice | solution.py:31
  55.7 6.2 %copy.14 = bf16[64,2,128,4]{2,0,3,1:T(8,128)(2,1)S(1)} copy(bf16[64,2,128,4]{3,0,2,1:T(8,128)(2,1)} %get-tuple-element.10) | data formatting | bytes 262144 | tf_op jit(solution)/shard_map/slice | solution.py:31
  61.9 6.2 %copy.15 = bf16[64,2,128,4]{2,0,3,1:T(8,128)(2,1)S(1)} copy(bf16[64,2,128,4]{3,0,2,1:T(8,128)(2,1)} %get-tuple-element.11) | data formatting | bytes 262144 | tf_op jit(solution)/shard_map/slice | solution.py:30
  68.1 5.6 %collective-permute-start.1 = (bf16[64,2,128,4]{2,0,3,1:T(8,128)(2,1)S(1)}, bf16[64,2,128,4]{2,0,3,1:T(8,128)(2,1)S(1)}, u32[]{:S(2)}, u32[]{:S(2)}) collective-permute-start(bf16[64,2,128,4]{2,0,3,1:T(8,128)(2,1)S(1)} %copy.15), channel_id=1, source_target_pairs={{1,0},{2,1},{3,2},{4,3},{5,4},{6,5},{7,6},{8,7},{9,8},{10,9},{11,1... | collective-permute-start | bytes 393224 | tf_op jit(solution)/shard_map/ppermute | solution.py:36
  73.7 1.9 %collective-permute-start = (bf16[64,2,128,4]{2,0,3,1:T(8,128)(2,1)S(1)}, bf16[64,2,128,4]{2,0,3,1:T(8,128)(2,1)S(1)}, u32[]{:S(2)}, u32[]{:S(2)}) collective-permute-start(bf16[64,2,128,4]{2,0,3,1:T(8,128)(2,1)S(1)} %copy.14), channel_id=1, source_target_pairs={{0,1},{1,2},{2,3},{3,4},{4,5},{5,6},{6,7},{7,8},{8,9},{9,10},{10,1... | collective-permute-start | bytes 393224 | tf_op jit(solution)/shard_map/ppermute | solution.py:34
  75.6 0.1 fusion.13.kb_ref
  75.8 6.7 %collective-permute-done = bf16[64,2,128,4]{2,0,3,1:T(8,128)(2,1)S(1)} collective-permute-done((bf16[64,2,128,4]{2,0,3,1:T(8,128)(2,1)S(1)}, bf16[64,2,128,4]{2,0,3,1:T(8,128)(2,1)S(1)}, u32[]{:S(2)}, u32[]{:S(2)}) %collective-permute-start) | collective-permute-done | bytes 131104 | tf_op jit(solution)/shard_map/ppermute | solution.py:34
  82.4 7.5 %copy.16 = bf16[64,2,128,4]{3,0,2,1:T(8,128)(2,1)} copy(bf16[64,2,128,4]{2,0,3,1:T(8,128)(2,1)S(1)} %collective-permute-done) | data formatting | bytes 262144 | tf_op jit(solution)/shard_map/ppermute | solution.py:34
  89.9 0.0 collective-permute-done.1
  89.9 7.4 %copy.17 = bf16[64,2,128,4]{3,0,2,1:T(8,128)(2,1)} copy(bf16[64,2,128,4]{2,0,3,1:T(8,128)(2,1)S(1)} %collective-permute-done.1) | data formatting | bytes 262144 | tf_op jit(solution)/shard_map/ppermute | solution.py:36
  97.3 0.0 copy-start
  97.3 0.0 copy-start.1
  97.3 0.0 copy-start.2
  97.3 1.3 pad_maximum_fusion.2
  98.6 4.1 %collective-permute-start.2 = (bf16[64,2,2,72]{3,0,2,1:T(8,128)(2,1)S(1)}, bf16[64,2,2,72]{3,0,2,1:T(8,128)(2,1)S(1)}, u32[]{:S(2)}, u32[]{:S(2)}) collective-permute-start(bf16[64,2,2,72]{3,0,2,1:T(8,128)(2,1)S(1)} %get-tuple-element.8), channel_id=1, source_target_pairs={{0,16},{16,32},{32,48},{48,64},{64,80},{80,96},{96,112},{1,17},{17... | collective-permute-start | bytes 110600 | tf_op jit(solution)/shard_map/ppermute | solution.py:34
  102.7 2.2 %collective-permute-start.3 = (bf16[64,2,2,72]{3,0,2,1:T(8,128)(2,1)S(1)}, bf16[64,2,2,72]{3,0,2,1:T(8,128)(2,1)S(1)}, u32[]{:S(2)}, u32[]{:S(2)}) collective-permute-start(bf16[64,2,2,72]{3,0,2,1:T(8,128)(2,1)S(1)} %get-tuple-element.9), channel_id=1, source_target_pairs={{16,0},{32,16},{48,32},{64,48},{80,64},{96,80},{112,96},{17,1},{33... | collective-permute-start | bytes 110600 | tf_op jit(solution)/shard_map/ppermute | solution.py:36
  104.9 0.1 collective-permute-done.2
  105.0 4.7 %collective-permute-done.3 = bf16[64,2,2,72]{3,0,2,1:T(8,128)(2,1)S(1)} collective-permute-done((bf16[64,2,2,72]{3,0,2,1:T(8,128)(2,1)S(1)}, bf16[64,2,2,72]{3,0,2,1:T(8,128)(2,1)S(1)}, u32[]{:S(2)}, u32[]{:S(2)}) %collective-permute-start.3) | collective-permute-done | bytes 36896 | tf_op jit(solution)/shard_map/ppermute | solution.py:36
  109.8 0.0 copy-done
  109.8 0.0 copy-done.1
  109.8 0.0 copy-done.2
  109.8 7.5 %fusion = f32[2,132,72,64]{3,2,1,0:T(8,128)} fusion(bf16[64,2,2,72]{3,0,2,1:T(8,128)(2,1)S(1)} %collective-permute-done.3, bf16[64,2,128,4]{3,0,2,1:T(8,128)(2,1)S(1)} %copy-done.2, bf16[64,2,128,64]{3,0,2,1:T(8,128)(2,1)S(1)} %bitcast.18, bf16[64,2,128,4]{3,0,2,1:T(8,128)(2,1)S(1)} %copy-done.1, bf16[64,2,2,72]{3,0,2,1:T(8,128)(2,1)S(1)} %collective-permute-done.2), kind=kOutput, calls=%fused_computation | convolution fusion | flops 167882752 | bytes 7299072 | tf_op jit(solution)/shard_map/esij,ef->sijf/dot_general | solution.py:108
  117.3 0.1 broadcast_in_dim.22.cm_ref
  117.3 43.3 %shard_map.37 = f32[2,128,64,256]{3,2,1,0:T(8,128)} custom-call(f32[2,9504,64]{2,1,0:T(8,128)} %bitcast.19, bf16[64,256]{1,0:T(8,128)(2,1)S(1)} %fusion.13.kb_ref, bf16[256,256]{1,0:T(8,128)(2,1)S(1)} %multiply_convert_fusion.g3_ref, f32[1,256]{1,0:T(1,128)S(1)} %bitcast.13, f32[1,256]{1,0:T(1,128)S(1)} %bitcast.14, f32[1,256]{1,0:T(1,128)S(1)} %bitcast.15, ...), custom_call_target="tpu_custom_call" | custom-call | flops 5775556608 | bytes 21643264 | tf_op jit(solution)/shard_map/pallas_call | solution.py:123
  (6 shorter events, 0.1 us)
Async XLA Ops:
  0.0 13.5 %copy-start.4 = (f32[256]{0:T(256)S(1)}, f32[256]{0:T(256)}, u32[]{:S(2)}) copy-start(f32[256]{0:T(256)} %param.4) | copy-start | bytes 3076
  0.0 14.3 %copy-start.3 = (f32[256]{0:T(256)S(1)}, f32[256]{0:T(256)}, u32[]{:S(2)}) copy-start(f32[256]{0:T(256)} %param.5) | copy-start | bytes 3076
  6.2 35.1 %all-to-all-start = ((bf16[4,2,128,1024]{2,1,0,3:T(2,128)(2,1)}), bf16[4,2,128,1024]{2,1,0,3:T(2,128)(2,1)}, u32[]{:S(2)}, u32[]{:S(2)}) async-start(bf16[4,2,128,1024]{2,1,0,3:T(2,128)(2,1)} %copy.11), calls=%async_computation | async-start | bytes 4194304 | tf_op jit(solution)/shard_map/all_to_all | solution.py:102
  68.1 21.8 %collective-permute-start.1 = (bf16[64,2,128,4]{2,0,3,1:T(8,128)(2,1)S(1)}, bf16[64,2,128,4]{2,0,3,1:T(8,128)(2,1)S(1)}, u32[]{:S(2)}, u32[]{:S(2)}) collective-permute-start(bf16[64,2,128,4]{2,0,3,1:T(8,128)(2,1)S(1)} %copy.15), channel_id=1, source_target_pairs={{1,0},{2,1},{3,2},{4,3},{5,4},{6,5},{7,6},{8,7},{9,8},{10,9},{11,1... | collective-permute-start | bytes 393224 | tf_op jit(solution)/shard_map/ppermute | solution.py:36
  73.7 8.7 %collective-permute-start = (bf16[64,2,128,4]{2,0,3,1:T(8,128)(2,1)S(1)}, bf16[64,2,128,4]{2,0,3,1:T(8,128)(2,1)S(1)}, u32[]{:S(2)}, u32[]{:S(2)}) collective-permute-start(bf16[64,2,128,4]{2,0,3,1:T(8,128)(2,1)S(1)} %copy.14), channel_id=1, source_target_pairs={{0,1},{1,2},{2,3},{3,4},{4,5},{5,6},{6,7},{7,8},{8,9},{9,10},{10,1... | collective-permute-start | bytes 393224 | tf_op jit(solution)/shard_map/ppermute | solution.py:34
  97.3 12.5 %copy-start = (bf16[16,4,2,128,64]{4,1,0,3,2:T(4,128)(2,1)S(1)}, bf16[16,4,2,128,64]{4,1,0,3,2:T(4,128)(2,1)}, u32[]{:S(2)}) copy-start(bf16[16,4,2,128,64]{4,1,0,3,2:T(4,128)(2,1)} %copy.13) | copy-start | bytes 6291460
  97.3 12.5 %copy-start.1 = (bf16[64,2,128,4]{3,0,2,1:T(8,128)(2,1)S(1)}, bf16[64,2,128,4]{3,0,2,1:T(8,128)(2,1)}, u32[]{:S(2)}) copy-start(bf16[64,2,128,4]{3,0,2,1:T(8,128)(2,1)} %copy.16) | copy-start | bytes 393220
  97.3 12.5 %copy-start.2 = (bf16[64,2,128,4]{3,0,2,1:T(8,128)(2,1)S(1)}, bf16[64,2,128,4]{3,0,2,1:T(8,128)(2,1)}, u32[]{:S(2)}) copy-start(bf16[64,2,128,4]{3,0,2,1:T(8,128)(2,1)} %copy.17) | copy-start | bytes 393220
  98.6 6.4 %collective-permute-start.2 = (bf16[64,2,2,72]{3,0,2,1:T(8,128)(2,1)S(1)}, bf16[64,2,2,72]{3,0,2,1:T(8,128)(2,1)S(1)}, u32[]{:S(2)}, u32[]{:S(2)}) collective-permute-start(bf16[64,2,2,72]{3,0,2,1:T(8,128)(2,1)S(1)} %get-tuple-element.8), channel_id=1, source_target_pairs={{0,16},{16,32},{32,48},{48,64},{64,80},{80,96},{96,112},{1,17},{17... | collective-permute-start | bytes 110600 | tf_op jit(solution)/shard_map/ppermute | solution.py:34
  102.7 7.1 %collective-permute-start.3 = (bf16[64,2,2,72]{3,0,2,1:T(8,128)(2,1)S(1)}, bf16[64,2,2,72]{3,0,2,1:T(8,128)(2,1)S(1)}, u32[]{:S(2)}, u32[]{:S(2)}) collective-permute-start(bf16[64,2,2,72]{3,0,2,1:T(8,128)(2,1)S(1)} %get-tuple-element.9), channel_id=1, source_target_pairs={{16,0},{32,16},{48,32},{64,48},{80,64},{96,80},{112,96},{17,1},{33... | collective-permute-start | bytes 110600 | tf_op jit(solution)/shard_map/ppermute | solution.py:36

commit v13 on v12

--- a/solution.py
+++ b/solution.py
@@ -5,6 +5,7 @@
 from jax import lax
 from jax.experimental import pallas as pl
 from jax.experimental.pallas import tpu as pltpu
+from jax.experimental.layout import Layout, with_layout_constraint
 from jax.sharding import PartitionSpec as P
 
 E = 64
@@ -93,6 +94,10 @@
     lax.fori_loop(RH, rows - RH, body2, 0)
 
 
+def pin(x):
+    return with_layout_constraint(x, Layout(tuple(range(x.ndim))))
+
+
 def per_device(images, rates, smoothing):
     kernel, gram, lam, step = kernel_parts(rates, smoothing)
     kb = kernel.astype(jnp.bfloat16)
@@ -101,11 +106,12 @@
     alpha = 1.0 - 4.0 * beta
     x = lax.all_to_all(images, "gy", split_axis=3, concat_axis=0, tiled=True)
     e, sl, h, w = x.shape
-    x = halo(x, "gy", 3, CH)
-    x = halo(x, "gx", 2, RH)
     hp, wp = h + 2 * RH, w + 2 * CH
     eye = jnp.eye(e, dtype=jnp.bfloat16)
     x = jnp.einsum("esij,ef->sijf", x, eye, preferred_element_type=jnp.float32)
+    x = pin(x)
+    x = pin(halo(x, "gy", 2, CH))
+    x = pin(halo(x, "gx", 1, RH))
     x = x.reshape(sl, hp * wp, e)
     r = kernel.shape[1]
 

time: 161 us -> 136 us (0.84)
  the two profiles are of different devices: /device:TPU:42 before, /device:TPU:70 now
where the time goes in v13:
time: 136 us; the launch traced here: 135 us
  waiting for transfers between devices  43.8 us (32%)
  Pallas kernels  43.3 us (32%)
  starting transfers between devices  20.8 us (15%)
  local copies, waits for them, and re-layouts  15.9 us (12%)
  other arithmetic  7.49 us (6%)
  matrix products  3.92 us (3%)
    pallas_call x1, Pallas kernels, per_device(): pl.pallas_call(functools.partial(fit_kernel, wp), out_shape=jax.ShapeDtyp...  43.3 us
    all_to_all x1, waiting for transfers between devices, per_device(): x = lax.all_to_all(images, 'gy', split_axis=3, concat_axis=0, tiled=True)  27.7 us
    ppermute x2, waiting for transfers between devices, halo(): lax.ppermute(tail, axis, [(i, i + 1) for i in range(count - 1)])  12.5 us
    all_to_all x3, local copies, waits for them, and re-layouts, per_device(): x = lax.all_to_all(images, 'gy', split_axis=3, concat_axis=0, tiled=True)  8.31 us
    all_to_all x1, starting transfers between devices, per_device(): x = lax.all_to_all(images, 'gy', split_axis=3, concat_axis=0, tiled=True)  7.45 us
    ppermute x2, starting transfers between devices, halo(): lax.ppermute(tail, axis, [(i, i + 1) for i in range(count - 1)])  7.32 us
    unnamed x9, local copies, waits for them, and re-layouts  7.18 us
    concatenate x1, other arithmetic, halo(): jnp.concatenate([lax.ppermute(tail, axis, [(i, i + 1) for i in range(coun...  6.24 us
  transfers between devices with their start and end apart: 5, of which 4 were waited for; matrix products, arithmetic and copies ran while one was open for 1% of the time, Pallas kernels for 0%

profile of v13, /device:TPU:70, one launch (start us, length us, event | category | flops | bytes accessed | tf_op | source)
XLA Modules:
  0.0 135.4 jit_solution(12832037889040843349)
XLA Ops:
  0.0 0.0 copy-start.3
  0.0 0.0 copy-start.2
  0.0 6.2 %copy.15 = bf16[4,2,128,1024]{2,1,0,3:T(2,128)(2,1)} copy(bf16[4,2,128,1024]{3,2,1,0:T(8,128)(2,1)} %param.3) | data formatting | bytes 4194304 | tf_op args[0]
  6.2 7.4 %all-to-all-start = ((bf16[4,2,128,1024]{2,1,0,3:T(2,128)(2,1)}), bf16[4,2,128,1024]{2,1,0,3:T(2,128)(2,1)S(1)}, u32[]{:S(2)}, u32[]{:S(2)}) async-start(bf16[4,2,128,1024]{2,1,0,3:T(2,128)(2,1)} %copy.15), calls=%async_computation | async-start | bytes 4194304 | tf_op jit(solution)/shard_map/all_to_all | solution.py:107
  13.6 0.0 copy-done.3
  13.6 0.1 multiply_reduce_fusion
  13.8 0.5 fusion.9
  14.3 0.0 copy-done.2
  14.3 0.1 fusion.3.kb_ref
  14.4 27.7 %all-to-all-done = bf16[4,2,128,1024]{2,1,0,3:T(2,128)(2,1)S(1)} async-done(((bf16[4,2,128,1024]{2,1,0,3:T(2,128)(2,1)}), bf16[4,2,128,1024]{2,1,0,3:T(2,128)(2,1)S(1)}, u32[]{:S(2)}, u32[]{:S(2)}) %all-to-all-start) | async-done | bytes 2097184 | tf_op jit(solution)/shard_map/all_to_all | solution.py:107
  42.1 0.3 copy.16
  42.4 0.2 copy.17
  42.6 7.8 %copy.18 = bf16[64,2,128,64]{0,3,2,1:T(8,128)(2,1)} copy(bf16[64,2,128,64]{2,3,1,0:T(8,128)(2,1)S(1)} %bitcast.21) | data formatting | bytes 4194304 | tf_op jit(solution)/shard_map/all_to_all | solution.py:107
  50.4 3.4 %fusion.7 = f32[64,16384]{0,1:S(1)} fusion(bf16[64,16384]{0,1:T(8,128)(2,1)} %bitcast.20), kind=kOutput, calls=%fused_computation.14 | convolution fusion | flops 134221824 | bytes 6291456
  53.9 0.0 copy-start
  53.9 0.2 fusion.8
  54.1 2.2 %collective-permute-start = (f32[2,128,4,64]{3,2,1,0:T(4,128)S(1)}, f32[2,128,4,64]{3,2,1,0:T(4,128)S(1)}, u32[]{:S(2)}, u32[]{:S(2)}) collective-permute-start(f32[2,128,4,64]{3,2,1,0:T(4,128)S(1)} %get-tuple-element.10), channel_id=1, source_target_pairs={{0,1},{1,2},{2,3},{3,4},{4,5},{5,6},{6,7},{7,8},{8,9},{9,10},{10,1... | collective-permute-start | bytes 786440 | tf_op jit(solution)/shard_map/ppermute | solution.py:35
  56.3 1.0 copy-done
  57.3 3.9 %collective-permute-start.1 = (f32[2,128,4,64]{3,2,1,0:T(4,128)S(1)}, f32[2,128,4,64]{3,2,1,0:T(4,128)S(1)}, u32[]{:S(2)}, u32[]{:S(2)}) collective-permute-start(f32[2,128,4,64]{3,2,1,0:T(4,128)S(1)} %get-tuple-element.11), channel_id=1, source_target_pairs={{1,0},{2,1},{3,2},{4,3},{5,4},{6,5},{7,6},{8,7},{9,8},{10,9},{11,1... | collective-permute-start | bytes 786440 | tf_op jit(solution)/shard_map/ppermute | solution.py:37
  61.2 0.1 copy.19
  61.3 0.0 copy-start.1
  61.3 11.2 %collective-permute-done = f32[2,128,4,64]{3,2,1,0:T(4,128)S(1)} collective-permute-done((f32[2,128,4,64]{3,2,1,0:T(4,128)S(1)}, f32[2,128,4,64]{3,2,1,0:T(4,128)S(1)}, u32[]{:S(2)}, u32[]{:S(2)}) %collective-permute-start) | collective-permute-done | bytes 262176 | tf_op jit(solution)/shard_map/ppermute | solution.py:35
  72.6 0.0 collective-permute-done.1
  72.6 1.0 pad_maximum_fusion.3
  73.6 5.1 %collective-permute-start.2 = (f32[2,2,72,64]{3,2,1,0:T(8,128)S(1)}, f32[2,2,72,64]{3,2,1,0:T(8,128)S(1)}, u32[]{:S(2)}, u32[]{:S(2)}) collective-permute-start(f32[2,2,72,64]{3,2,1,0:T(8,128)S(1)} %get-tuple-element.8), channel_id=1, source_target_pairs={{0,16},{16,32},{32,48},{48,64},{64,80},{80,96},{96,112},{1,17},{17... | collective-permute-start | bytes 221192 | tf_op jit(solution)/shard_map/ppermute | solution.py:35
  78.7 2.2 %collective-permute-start.3 = (f32[2,2,72,64]{3,2,1,0:T(8,128)S(1)}, f32[2,2,72,64]{3,2,1,0:T(8,128)S(1)}, u32[]{:S(2)}, u32[]{:S(2)}) collective-permute-start(f32[2,2,72,64]{3,2,1,0:T(8,128)S(1)} %get-tuple-element.9), channel_id=1, source_target_pairs={{16,0},{32,16},{48,32},{64,48},{80,64},{96,80},{112,96},{17,1},{33... | collective-permute-start | bytes 221192 | tf_op jit(solution)/shard_map/ppermute | solution.py:37
  80.9 1.3 collective-permute-done.2
  82.2 3.6 %collective-permute-done.3 = f32[2,2,72,64]{3,2,1,0:T(8,128)S(1)} collective-permute-done((f32[2,2,72,64]{3,2,1,0:T(8,128)S(1)}, f32[2,2,72,64]{3,2,1,0:T(8,128)S(1)}, u32[]{:S(2)}, u32[]{:S(2)}) %collective-permute-start.3) | collective-permute-done | bytes 73760 | tf_op jit(solution)/shard_map/ppermute | solution.py:37
  85.7 0.0 copy-done.1
  85.7 6.2 %pad_maximum_fusion = f32[2,132,72,64]{3,2,1,0:T(8,128)} fusion(f32[2,2,72,64]{3,2,1,0:T(8,128)S(1)} %collective-permute-done.3, f32[2,128,4,64]{3,2,1,0:T(4,128)S(1)} %collective-permute-done.1, f32[2,128,64,64]{3,2,1,0:T(8,128)S(1)} %bitcast.18, f32[2,128,4,64]{3,2,1,0:T(4,128)S(1)} %collective-permute-done, f32[2,2,72,64]{3,2,1,0:T(8,128)S(1)} %collective-permute-done.2), kind=kLoop, calls=%fused_computation | loop fusion | flops 4866048 | bytes 9732096 | tf_op jit(solution)/shard_map/concatenate | solution.py:33
  92.0 0.1 broadcast_in_dim.22.cm_ref
  92.1 43.3 %shard_map.37 = f32[2,128,64,256]{3,2,1,0:T(8,128)} custom-call(f32[2,9504,64]{2,1,0:T(8,128)} %bitcast.19, bf16[64,256]{1,0:T(8,128)(2,1)S(1)} %fusion.3.kb_ref, bf16[256,256]{1,0:T(8,128)(2,1)S(1)} %multiply_convert_fusion.g3_ref, f32[1,256]{1,0:T(1,128)S(1)} %bitcast.13, f32[1,256]{1,0:T(1,128)S(1)} %bitcast.14, f32[1,256]{1,0:T(1,128)S(1)} %bitcast.15, ...), custom_call_target="tpu_custom_call" | custom-call | flops 5775556608 | bytes 21643264 | tf_op jit(solution)/shard_map/pallas_call | solution.py:129
  (6 shorter events, 0.1 us)
Async XLA Ops:
  0.0 13.6 %copy-start.3 = (f32[256]{0:T(256)S(1)}, f32[256]{0:T(256)}, u32[]{:S(2)}) copy-start(f32[256]{0:T(256)} %param.4) | copy-start | bytes 3076
  0.0 14.3 %copy-start.2 = (f32[256]{0:T(256)S(1)}, f32[256]{0:T(256)}, u32[]{:S(2)}) copy-start(f32[256]{0:T(256)} %param.5) | copy-start | bytes 3076
  6.2 35.9 %all-to-all-start = ((bf16[4,2,128,1024]{2,1,0,3:T(2,128)(2,1)}), bf16[4,2,128,1024]{2,1,0,3:T(2,128)(2,1)S(1)}, u32[]{:S(2)}, u32[]{:S(2)}) async-start(bf16[4,2,128,1024]{2,1,0,3:T(2,128)(2,1)} %copy.15), calls=%async_computation | async-start | bytes 4194304 | tf_op jit(solution)/shard_map/all_to_all | solution.py:107
  53.9 3.4 %copy-start = (f32[64,16384]{0,1}, f32[64,16384]{0,1:S(1)}, u32[]{:S(2)}) copy-start(f32[64,16384]{0,1:S(1)} %fusion.7) | copy-start | bytes 12582916
  54.1 18.5 %collective-permute-start = (f32[2,128,4,64]{3,2,1,0:T(4,128)S(1)}, f32[2,128,4,64]{3,2,1,0:T(4,128)S(1)}, u32[]{:S(2)}, u32[]{:S(2)}) collective-permute-start(f32[2,128,4,64]{3,2,1,0:T(4,128)S(1)} %get-tuple-element.10), channel_id=1, source_target_pairs={{0,1},{1,2},{2,3},{3,4},{4,5},{5,6},{6,7},{7,8},{8,9},{9,10},{10,1... | collective-permute-start | bytes 786440 | tf_op jit(solution)/shard_map/ppermute | solution.py:35
  57.3 15.3 %collective-permute-start.1 = (f32[2,128,4,64]{3,2,1,0:T(4,128)S(1)}, f32[2,128,4,64]{3,2,1,0:T(4,128)S(1)}, u32[]{:S(2)}, u32[]{:S(2)}) collective-permute-start(f32[2,128,4,64]{3,2,1,0:T(4,128)S(1)} %get-tuple-element.11), channel_id=1, source_target_pairs={{1,0},{2,1},{3,2},{4,3},{5,4},{6,5},{7,6},{8,7},{9,8},{10,9},{11,1... | collective-permute-start | bytes 786440 | tf_op jit(solution)/shard_map/ppermute | solution.py:37
  61.3 24.4 %copy-start.1 = (f32[64,16384]{0,1:S(1)}, f32[64,16384]{0,1}, u32[]{:S(2)}) copy-start(f32[64,16384]{0,1} %copy-done) | copy-start | bytes 12582916
  73.6 8.6 %collective-permute-start.2 = (f32[2,2,72,64]{3,2,1,0:T(8,128)S(1)}, f32[2,2,72,64]{3,2,1,0:T(8,128)S(1)}, u32[]{:S(2)}, u32[]{:S(2)}) collective-permute-start(f32[2,2,72,64]{3,2,1,0:T(8,128)S(1)} %get-tuple-element.8), channel_id=1, source_target_pairs={{0,16},{16,32},{32,48},{48,64},{64,80},{80,96},{96,112},{1,17},{17... | collective-permute-start | bytes 221192 | tf_op jit(solution)/shard_map/ppermute | solution.py:35
  78.7 7.0 %collective-permute-start.3 = (f32[2,2,72,64]{3,2,1,0:T(8,128)S(1)}, f32[2,2,72,64]{3,2,1,0:T(8,128)S(1)}, u32[]{:S(2)}, u32[]{:S(2)}) collective-permute-start(f32[2,2,72,64]{3,2,1,0:T(8,128)S(1)} %get-tuple-element.9), channel_id=1, source_target_pairs={{16,0},{32,16},{48,32},{64,48},{80,64},{96,80},{112,96},{17,1},{33... | collective-permute-start | bytes 221192 | tf_op jit(solution)/shard_map/ppermute | solution.py:37

commit v14 on v13

--- a/solution.py
+++ b/solution.py
@@ -51,7 +51,8 @@
     beta = beta_ref[...]
     cm = cm_ref[...]
 
-    sb = jnp.dot(x_ref[0, pl.ds(base, n), :].astype(jnp.bfloat16), kb_ref[...],
+    xt = x_ref[0, pl.ds(t * TR, rows)].astype(jnp.float32).reshape(n, x_ref.shape[3])
+    sb = jnp.dot(xt.astype(jnp.bfloat16), kb_ref[...],
                  preferred_element_type=jnp.float32) * step
     b_ref[...] = sb
     f0 = jnp.maximum(sb, 0.0)
@@ -107,12 +108,9 @@
     x = lax.all_to_all(images, "gy", split_axis=3, concat_axis=0, tiled=True)
     e, sl, h, w = x.shape
     hp, wp = h + 2 * RH, w + 2 * CH
-    eye = jnp.eye(e, dtype=jnp.bfloat16)
-    x = jnp.einsum("esij,ef->sijf", x, eye, preferred_element_type=jnp.float32)
-    x = pin(x)
+    x = pin(jnp.transpose(x, (1, 2, 3, 0)))
     x = pin(halo(x, "gy", 2, CH))
     x = pin(halo(x, "gx", 1, RH))
-    x = x.reshape(sl, hp * wp, e)
     r = kernel.shape[1]
 
     gi = lax.axis_index("gx")
@@ -131,7 +129,7 @@
         out_shape=jax.ShapeDtypeStruct((sl, h, w, r), jnp.float32),
         grid=(sl, nt),
         in_specs=[
-            pl.BlockSpec((1, hp * wp, e), lambda s, t: (s, 0, 0)),
+            pl.BlockSpec((1, hp, wp, e), lambda s, t: (s, 0, 0, 0)),
             pl.BlockSpec((e, r), lambda s, t: (0, 0)),
             pl.BlockSpec((r, r), lambda s, t: (0, 0)),
             pl.BlockSpec((1, r), lambda s, t: (0, 0)),
@@ -154,7 +152,7 @@
         ),
         cost_estimate=pl.CostEstimate(
             flops=flops, transcendentals=0,
-            bytes_accessed=sl * (hp * wp * e * 4 + h * w * r * 4),
+            bytes_accessed=sl * (hp * wp * e * 2 + h * w * r * 4),
         ),
     )(x, kb, g3, step[None, :], alpha[None, :], beta[None, :], cm, rm)
     return out

time: 136 us -> 124 us (0.912)
  the two profiles are of different devices: /device:TPU:70 before, /device:TPU:1 now
where the time goes in v14:
time: 124 us; the launch traced here: 123 us
  Pallas kernels  41.4 us (33%)
  waiting for transfers between devices  38.7 us (31%)
  starting transfers between devices  20.2 us (16%)
  local copies, waits for them, and re-layouts  16.1 us (13%)
  other arithmetic  6.25 us (5%)
    pallas_call x1, Pallas kernels, per_device(): pl.pallas_call(functools.partial(fit_kernel, wp), out_shape=jax.ShapeDtyp...  41.4 us
    all_to_all x1, waiting for transfers between devices, per_device(): x = lax.all_to_all(images, 'gy', split_axis=3, concat_axis=0, tiled=True)  27.6 us
    ppermute x2, waiting for transfers between devices, halo(): lax.ppermute(head, axis, [(i + 1, i) for i in range(count - 1)])  9.68 us
    all_to_all x1, starting transfers between devices, per_device(): x = lax.all_to_all(images, 'gy', split_axis=3, concat_axis=0, tiled=True)  9.3 us
    all_to_all x3, local copies, waits for them, and re-layouts, per_device(): x = lax.all_to_all(images, 'gy', split_axis=3, concat_axis=0, tiled=True)  8.27 us
    ppermute x2, starting transfers between devices, halo(): lax.ppermute(tail, axis, [(i, i + 1) for i in range(count - 1)])  7.72 us
    unnamed x7, local copies, waits for them, and re-layouts  6.19 us
    concatenate x1, other arithmetic, halo(): jnp.concatenate([lax.ppermute(tail, axis, [(i, i + 1) for i in range(coun...  5.07 us
  transfers between devices with their start and end apart: 5, of which 5 were waited for; matrix products, arithmetic and copies ran while one was open for 1% of the time, Pallas kernels for 0%

profile of v14, /device:TPU:1, one launch (start us, length us, event | category | flops | bytes accessed | tf_op | source)
XLA Modules:
  0.0 123.4 jit_solution(4967173198924089996)
XLA Ops:
  0.0 0.0 copy-start.2
  0.0 0.0 copy-start.1
  0.0 6.2 %copy.10 = bf16[4,2,128,1024]{2,1,0,3:T(2,128)(2,1)} copy(bf16[4,2,128,1024]{3,2,1,0:T(8,128)(2,1)} %param.3) | data formatting | bytes 4194304 | tf_op args[0]
  6.2 9.3 %all-to-all-start = ((bf16[4,2,128,1024]{2,1,0,3:T(2,128)(2,1)}), bf16[4,2,128,1024]{2,1,0,3:T(2,128)(2,1)S(1)}, u32[]{:S(2)}, u32[]{:S(2)}) async-start(bf16[4,2,128,1024]{2,1,0,3:T(2,128)(2,1)} %copy.10), calls=%async_computation | async-start | bytes 4194304 | tf_op jit(solution)/shard_map/all_to_all | solution.py:108
  15.5 0.0 copy-done.2
  15.5 0.1 multiply_reduce_fusion
  15.6 0.5 fusion.8
  16.1 0.1 copy.14
  16.3 0.0 copy-done.1
  16.3 27.6 %all-to-all-done = bf16[4,2,128,1024]{2,1,0,3:T(2,128)(2,1)S(1)} async-done(((bf16[4,2,128,1024]{2,1,0,3:T(2,128)(2,1)}), bf16[4,2,128,1024]{2,1,0,3:T(2,128)(2,1)S(1)}, u32[]{:S(2)}, u32[]{:S(2)}) %all-to-all-start) | async-done | bytes 2097184 | tf_op jit(solution)/shard_map/all_to_all | solution.py:108
  43.9 0.3 copy.11
  44.2 0.2 copy.12
  44.4 7.8 %copy.13 = bf16[64,2,128,64]{0,3,2,1:T(8,128)(2,1)} copy(bf16[64,2,128,64]{2,3,1,0:T(8,128)(2,1)S(1)} %bitcast.14) | data formatting | bytes 4194304 | tf_op jit(solution)/shard_map/all_to_all | solution.py:108
  52.2 1.4 %fusion.7 = (bf16[2,128,4,64]{3,2,1,0:T(4,128)(2,1)S(1)}, bf16[2,128,4,64]{3,2,1,0:T(4,128)(2,1)S(1)}) fusion(bf16[2,128,64,64]{3,2,1,0:T(8,128)(2,1)} %bitcast.11), kind=kLoop, calls=%fused_computation.19 | loop fusion | bytes 524288 | tf_op jit(solution)/shard_map/slice | solution.py:32
  53.6 5.1 %collective-permute-start = (bf16[2,128,4,64]{3,2,1,0:T(4,128)(2,1)S(1)}, bf16[2,128,4,64]{3,2,1,0:T(4,128)(2,1)S(1)}, u32[]{:S(2)}, u32[]{:S(2)}) collective-permute-start(bf16[2,128,4,64]{3,2,1,0:T(4,128)(2,1)S(1)} %get-tuple-element.10), channel_id=1, source_target_pairs={{0,1},{1,2},{2,3},{3,4},{4,5},{5,6},{6,7},{7,8},{8,9},{9,10},{10,1... | collective-permute-start | bytes 393224 | tf_op jit(solution)/shard_map/ppermute | solution.py:35
  58.7 1.9 %collective-permute-start.1 = (bf16[2,128,4,64]{3,2,1,0:T(4,128)(2,1)S(1)}, bf16[2,128,4,64]{3,2,1,0:T(4,128)(2,1)S(1)}, u32[]{:S(2)}, u32[]{:S(2)}) collective-permute-start(bf16[2,128,4,64]{3,2,1,0:T(4,128)(2,1)S(1)} %get-tuple-element.11), channel_id=1, source_target_pairs={{1,0},{2,1},{3,2},{4,3},{5,4},{6,5},{7,6},{8,7},{9,8},{10,9},{11,1... | collective-permute-start | bytes 393224 | tf_op jit(solution)/shard_map/ppermute | solution.py:37
  60.6 0.1 fusion.3.kb_ref
  60.7 0.0 copy-start
  60.8 1.2 %collective-permute-done = bf16[2,128,4,64]{3,2,1,0:T(4,128)(2,1)S(1)} collective-permute-done((bf16[2,128,4,64]{3,2,1,0:T(4,128)(2,1)S(1)}, bf16[2,128,4,64]{3,2,1,0:T(4,128)(2,1)S(1)}, u32[]{:S(2)}, u32[]{:S(2)}) %collective-permute-start) | collective-permute-done | bytes 131104 | tf_op jit(solution)/shard_map/ppermute | solution.py:35
  62.0 5.9 %collective-permute-done.1 = bf16[2,128,4,64]{3,2,1,0:T(4,128)(2,1)S(1)} collective-permute-done((bf16[2,128,4,64]{3,2,1,0:T(4,128)(2,1)S(1)}, bf16[2,128,4,64]{3,2,1,0:T(4,128)(2,1)S(1)}, u32[]{:S(2)}, u32[]{:S(2)}) %collective-permute-start.1) | collective-permute-done | bytes 131104 | tf_op jit(solution)/shard_map/ppermute | solution.py:37
  67.9 0.9 pad_maximum_fusion.3
  68.9 2.6 %collective-permute-start.2 = (bf16[2,2,72,64]{3,2,1,0:T(8,128)(2,1)S(1)}, bf16[2,2,72,64]{3,2,1,0:T(8,128)(2,1)S(1)}, u32[]{:S(2)}, u32[]{:S(2)}) collective-permute-start(bf16[2,2,72,64]{3,2,1,0:T(8,128)(2,1)S(1)} %get-tuple-element.8), channel_id=1, source_target_pairs={{0,16},{16,32},{32,48},{48,64},{64,80},{80,96},{96,112},{1,17},{17... | collective-permute-start | bytes 110600 | tf_op jit(solution)/shard_map/ppermute | solution.py:35
  71.5 1.3 %collective-permute-start.3 = (bf16[2,2,72,64]{3,2,1,0:T(8,128)(2,1)S(1)}, bf16[2,2,72,64]{3,2,1,0:T(8,128)(2,1)S(1)}, u32[]{:S(2)}, u32[]{:S(2)}) collective-permute-start(bf16[2,2,72,64]{3,2,1,0:T(8,128)(2,1)S(1)} %get-tuple-element.9), channel_id=1, source_target_pairs={{16,0},{32,16},{48,32},{64,48},{80,64},{96,80},{112,96},{17,1},{33... | collective-permute-start | bytes 110600 | tf_op jit(solution)/shard_map/ppermute | solution.py:37
  72.8 0.2 collective-permute-done.2
  73.0 3.8 %collective-permute-done.3 = bf16[2,2,72,64]{3,2,1,0:T(8,128)(2,1)S(1)} collective-permute-done((bf16[2,2,72,64]{3,2,1,0:T(8,128)(2,1)S(1)}, bf16[2,2,72,64]{3,2,1,0:T(8,128)(2,1)S(1)}, u32[]{:S(2)}, u32[]{:S(2)}) %collective-permute-start.3) | collective-permute-done | bytes 36896 | tf_op jit(solution)/shard_map/ppermute | solution.py:37
  76.8 0.0 copy-done
  76.8 5.1 %pad_maximum_fusion.x_ref = bf16[2,132,72,64]{3,2,1,0:T(8,128)(2,1)S(1)} fusion(bf16[2,2,72,64]{3,2,1,0:T(8,128)(2,1)S(1)} %collective-permute-done.3, bf16[2,128,4,64]{3,2,1,0:T(4,128)(2,1)S(1)} %collective-permute-done.1, bf16[2,128,64,64]{3,2,1,0:T(8,128)(2,1)S(1)} %bitcast.13, bf16[2,128,4,64]{3,2,1,0:T(4,128)(2,1)S(1)} %collective-permute-done, ...), kind=kLoop, calls=%fused_computation | loop fusion | flops 12165120 | bytes 4866048 | tf_op jit(solution)/shard_map/concatenate | solution.py:33
  81.9 0.1 broadcast_in_dim.22.cm_ref
  82.0 41.4 %shard_map.37 = f32[2,128,64,256]{3,2,1,0:T(8,128)} custom-call(bf16[2,132,72,64]{3,2,1,0:T(8,128)(2,1)S(1)} %pad_maximum_fusion.x_ref, bf16[64,256]{1,0:T(8,128)(2,1)S(1)} %fusion.3.kb_ref, bf16[256,256]{1,0:T(8,128)(2,1)S(1)} %multiply_convert_fusion.g3_ref, f32[1,256]{1,0:T(1,128)S(1)} %bitcast.8, f32[1,256]{1,0:T(1,128)S(1)} %bitcast.9, ...), custom_call_target="tpu_custom_call" | custom-call | flops 5775556608 | bytes 19210240 | tf_op jit(solution)/shard_map/pallas_call | solution.py:127
  (6 shorter events, 0.1 us)
Async XLA Ops:
  0.0 15.5 %copy-start.2 = (f32[256]{0:T(256)S(1)}, f32[256]{0:T(256)}, u32[]{:S(2)}) copy-start(f32[256]{0:T(256)} %param.4) | copy-start | bytes 3076
  0.0 16.3 %copy-start.1 = (f32[256]{0:T(256)S(1)}, f32[256]{0:T(256)}, u32[]{:S(2)}) copy-start(f32[256]{0:T(256)} %param.5) | copy-start | bytes 3076
  6.2 37.7 %all-to-all-start = ((bf16[4,2,128,1024]{2,1,0,3:T(2,128)(2,1)}), bf16[4,2,128,1024]{2,1,0,3:T(2,128)(2,1)S(1)}, u32[]{:S(2)}, u32[]{:S(2)}) async-start(bf16[4,2,128,1024]{2,1,0,3:T(2,128)(2,1)} %copy.10), calls=%async_computation | async-start | bytes 4194304 | tf_op jit(solution)/shard_map/all_to_all | solution.py:108
  53.6 8.4 %collective-permute-start = (bf16[2,128,4,64]{3,2,1,0:T(4,128)(2,1)S(1)}, bf16[2,128,4,64]{3,2,1,0:T(4,128)(2,1)S(1)}, u32[]{:S(2)}, u32[]{:S(2)}) collective-permute-start(bf16[2,128,4,64]{3,2,1,0:T(4,128)(2,1)S(1)} %get-tuple-element.10), channel_id=1, source_target_pairs={{0,1},{1,2},{2,3},{3,4},{4,5},{5,6},{6,7},{7,8},{8,9},{9,10},{10,1... | collective-permute-start | bytes 393224 | tf_op jit(solution)/shard_map/ppermute | solution.py:35
  58.7 9.2 %collective-permute-start.1 = (bf16[2,128,4,64]{3,2,1,0:T(4,128)(2,1)S(1)}, bf16[2,128,4,64]{3,2,1,0:T(4,128)(2,1)S(1)}, u32[]{:S(2)}, u32[]{:S(2)}) collective-permute-start(bf16[2,128,4,64]{3,2,1,0:T(4,128)(2,1)S(1)} %get-tuple-element.11), channel_id=1, source_target_pairs={{1,0},{2,1},{3,2},{4,3},{5,4},{6,5},{7,6},{8,7},{9,8},{10,9},{11,1... | collective-permute-start | bytes 393224 | tf_op jit(solution)/shard_map/ppermute | solution.py:37
  60.7 16.1 %copy-start = (bf16[64,2,128,64]{0,3,2,1:T(8,128)(2,1)S(1)}, bf16[64,2,128,64]{0,3,2,1:T(8,128)(2,1)}, u32[]{:S(2)}) copy-start(bf16[64,2,128,64]{0,3,2,1:T(8,128)(2,1)} %copy.13) | copy-start | bytes 6291460
  68.9 4.2 %collective-permute-start.2 = (bf16[2,2,72,64]{3,2,1,0:T(8,128)(2,1)S(1)}, bf16[2,2,72,64]{3,2,1,0:T(8,128)(2,1)S(1)}, u32[]{:S(2)}, u32[]{:S(2)}) collective-permute-start(bf16[2,2,72,64]{3,2,1,0:T(8,128)(2,1)S(1)} %get-tuple-element.8), channel_id=1, source_target_pairs={{0,16},{16,32},{32,48},{48,64},{64,80},{80,96},{96,112},{1,17},{17... | collective-permute-start | bytes 110600 | tf_op jit(solution)/shard_map/ppermute | solution.py:35
  71.5 5.3 %collective-permute-start.3 = (bf16[2,2,72,64]{3,2,1,0:T(8,128)(2,1)S(1)}, bf16[2,2,72,64]{3,2,1,0:T(8,128)(2,1)S(1)}, u32[]{:S(2)}, u32[]{:S(2)}) collective-permute-start(bf16[2,2,72,64]{3,2,1,0:T(8,128)(2,1)S(1)} %get-tuple-element.9), channel_id=1, source_target_pairs={{16,0},{32,16},{48,32},{64,48},{80,64},{96,80},{112,96},{17,1},{33... | collective-permute-start | bytes 110600 | tf_op jit(solution)/shard_map/ppermute | solution.py:37

commit v15 on v14

--- a/solution.py
+++ b/solution.py
@@ -95,6 +95,29 @@
     lax.fori_loop(RH, rows - RH, body2, 0)
 
 
+def halo2d(x, rh, ch):
+    nx, ny = lax.axis_size("gx"), lax.axis_size("gy")
+    h, w = x.shape[1], x.shape[2]
+    rows = {-1: (h - rh, h), 0: (0, h), 1: (0, rh)}
+    cols = {-1: (w - ch, w), 0: (0, w), 1: (0, ch)}
+
+    def piece(di, dj):
+        p = x[:, rows[di][0]:rows[di][1], cols[dj][0]:cols[dj][1]]
+        if di == 0 and dj == 0:
+            return p
+        pairs = []
+        for i in range(nx):
+            for j in range(ny):
+                si, sj = i + di, j + dj
+                if 0 <= si < nx and 0 <= sj < ny:
+                    pairs.append((si * ny + sj, i * ny + j))
+        return lax.ppermute(p, ("gx", "gy"), pairs)
+
+    band = [jnp.concatenate([piece(di, -1), piece(di, 0), piece(di, 1)], axis=2)
+            for di in (-1, 0, 1)]
+    return jnp.concatenate(band, axis=1)
+
+
 def pin(x):
     return with_layout_constraint(x, Layout(tuple(range(x.ndim))))
 
@@ -109,8 +132,7 @@
     e, sl, h, w = x.shape
     hp, wp = h + 2 * RH, w + 2 * CH
     x = pin(jnp.transpose(x, (1, 2, 3, 0)))
-    x = pin(halo(x, "gy", 2, CH))
-    x = pin(halo(x, "gx", 1, RH))
+    x = pin(halo2d(x, RH, CH))
     r = kernel.shape[1]
 
     gi = lax.axis_index("gx")

time: 124 us -> 138 us (1.11); the launches traced: 123 us -> 136 us
  starting transfers between devices: 20.2 us -> 33 us
  waiting for transfers between devices: 38.7 us -> 31.2 us
  other arithmetic: 6.25 us -> 11.8 us
  local copies, waits for them, and re-layouts: 16.1 us -> 17.7 us
    ppermute x4 -> x8, starting transfers between devices: 10.9 us -> 23.7 us  [piece(): return lax.ppermute(p, ('gx', 'gy'), pairs)]
    ppermute x4 -> x8, waiting for transfers between devices: 11.1 us -> 3.71 us  [piece(): return lax.ppermute(p, ('gx', 'gy'), pairs)]
    concatenate x1, other arithmetic: 5.07 us -> 11.6 us  [halo2d(): return jnp.concatenate(band, axis=1)]
    slice x1 -> x3, local copies, waits for them, and re-layouts: 1.42 us -> 3.07 us  [piece(): p = x[:, rows[di][0]:rows[di][1], cols[dj][0]:cols[dj][1]]]
    unnamed x7 -> x5, local copies, waits for them, and re-layouts: 6.19 us -> 6.18 us
  transfers between devices with their start and end apart: 5 -> 9, of which waited for: 5 -> 3; matrix products, arithmetic and copies ran while one was open for 1% -> 1% of each run, Pallas kernels for 0% -> 0%
where the time goes in v15:
time: 138 us; the launch traced here: 136 us
  Pallas kernels  41.4 us (30%)
  starting transfers between devices  33 us (24%)
  waiting for transfers between devices  31.2 us (23%)
  local copies, waits for them, and re-layouts  17.7 us (13%)
  other arithmetic  11.8 us (9%)
    pallas_call x1, Pallas kernels, per_device(): pl.pallas_call(functools.partial(fit_kernel, wp), out_shape=jax.ShapeDtyp...  41.4 us
    all_to_all x1, waiting for transfers between devices, per_device(): x = lax.all_to_all(images, 'gy', split_axis=3, concat_axis=0, tiled=True)  27.5 us
    ppermute x8, starting transfers between devices, piece(): return lax.ppermute(p, ('gx', 'gy'), pairs)  23.7 us
    concatenate x1, other arithmetic, halo2d(): return jnp.concatenate(band, axis=1)  11.6 us
    all_to_all x1, starting transfers between devices, per_device(): x = lax.all_to_all(images, 'gy', split_axis=3, concat_axis=0, tiled=True)  9.3 us
    all_to_all x3, local copies, waits for them, and re-layouts, per_device(): x = lax.all_to_all(images, 'gy', split_axis=3, concat_axis=0, tiled=True)  8.27 us
    unnamed x5, local copies, waits for them, and re-layouts  6.18 us
    ppermute x8, waiting for transfers between devices, piece(): return lax.ppermute(p, ('gx', 'gy'), pairs)  3.71 us
  transfers between devices with their start and end apart: 9, of which 3 were waited for; matrix products, arithmetic and copies ran while one was open for 1% of the time, Pallas kernels for 0%

profile of v15, /device:TPU:1, one launch (start us, length us, event | category | flops | bytes accessed | tf_op | source)
XLA Modules:
  0.0 135.9 jit_solution(972160739487107063)
XLA Ops:
  0.0 0.0 copy-start.1
  0.0 0.0 copy-start
  0.0 6.2 %copy.10 = bf16[4,2,128,1024]{2,1,0,3:T(2,128)(2,1)} copy(bf16[4,2,128,1024]{3,2,1,0:T(8,128)(2,1)} %param.3) | data formatting | bytes 4194304 | tf_op args[0]
  6.2 9.3 %all-to-all-start = ((bf16[4,2,128,1024]{2,1,0,3:T(2,128)(2,1)}), bf16[4,2,128,1024]{2,1,0,3:T(2,128)(2,1)S(1)}, u32[]{:S(2)}, u32[]{:S(2)}) async-start(bf16[4,2,128,1024]{2,1,0,3:T(2,128)(2,1)} %copy.10), calls=%async_computation | async-start | bytes 4194304 | tf_op jit(solution)/shard_map/all_to_all | solution.py:131
  15.5 0.0 copy-done.1
  15.5 0.1 multiply_reduce_fusion
  15.6 0.5 fusion.10
  16.1 0.1 copy.14
  16.3 0.0 copy-done
  16.3 0.1 fusion.3.kb_ref
  16.4 27.5 %all-to-all-done = bf16[4,2,128,1024]{2,1,0,3:T(2,128)(2,1)S(1)} async-done(((bf16[4,2,128,1024]{2,1,0,3:T(2,128)(2,1)}), bf16[4,2,128,1024]{2,1,0,3:T(2,128)(2,1)S(1)}, u32[]{:S(2)}, u32[]{:S(2)}) %all-to-all-start) | async-done | bytes 2097184 | tf_op jit(solution)/shard_map/all_to_all | solution.py:131
  43.9 0.3 copy.11
  44.2 0.2 copy.12
  44.4 7.8 %copy.13 = bf16[64,2,128,64]{0,3,2,1:T(8,128)(2,1)} copy(bf16[64,2,128,64]{2,3,1,0:T(8,128)(2,1)S(1)} %bitcast.15) | data formatting | bytes 4194304 | tf_op jit(solution)/shard_map/all_to_all | solution.py:131
  52.2 0.8 fusion.7
  53.0 1.4 %fusion.9 = (bf16[2,128,4,64]{3,2,1,0:T(4,128)(2,1)S(1)}, bf16[2,128,4,64]{3,2,1,0:T(4,128)(2,1)S(1)}) fusion(bf16[2,128,64,64]{3,2,1,0:T(8,128)(2,1)} %bitcast.12), kind=kLoop, calls=%fused_computation.18 | loop fusion | bytes 524288 | tf_op jit(solution)/shard_map/slice | solution.py:105
  54.4 5.2 %collective-permute-start = (bf16[2,2,4,64]{3,2,1,0:T(4,128)(2,1)S(1)}, bf16[2,2,4,64]{3,2,1,0:T(4,128)(2,1)S(1)}, u32[]{:S(2)}, u32[]{:S(2)}) collective-permute-start(bf16[2,2,4,64]{3,2,1,0:T(4,128)(2,1)S(1)} %get-tuple-element.8), channel_id=1, source_target_pairs={{0,17},{1,18},{2,19},{3,20},{4,21},{5,22},{6,23},{7,24},{8,25},{9,... | collective-permute-start | bytes 6152 | tf_op jit(solution)/shard_map/ppermute | solution.py:114
  59.6 1.3 collective-permute-start.5
  60.9 4.3 %collective-permute-start.2 = (bf16[2,2,4,64]{3,2,1,0:T(4,128)(2,1)S(1)}, bf16[2,2,4,64]{3,2,1,0:T(4,128)(2,1)S(1)}, u32[]{:S(2)}, u32[]{:S(2)}) collective-permute-start(bf16[2,2,4,64]{3,2,1,0:T(4,128)(2,1)S(1)} %get-tuple-element.10), channel_id=1, source_target_pairs={{1,16},{2,17},{3,18},{4,19},{5,20},{6,21},{7,22},{8,23},{9,24},{10... | collective-permute-start | bytes 6152 | tf_op jit(solution)/shard_map/ppermute | solution.py:114
  65.2 3.3 %collective-permute-start.3 = (bf16[2,128,4,64]{3,2,1,0:T(4,128)(2,1)S(1)}, bf16[2,128,4,64]{3,2,1,0:T(4,128)(2,1)S(1)}, u32[]{:S(2)}, u32[]{:S(2)}) collective-permute-start(bf16[2,128,4,64]{3,2,1,0:T(4,128)(2,1)S(1)} %get-tuple-element.14), channel_id=1, source_target_pairs={{0,1},{1,2},{2,3},{3,4},{4,5},{5,6},{6,7},{7,8},{8,9},{9,10},{10,1... | collective-permute-start | bytes 393224 | tf_op jit(solution)/shard_map/ppermute | solution.py:114
  68.5 1.9 %collective-permute-start.4 = (bf16[2,128,4,64]{3,2,1,0:T(4,128)(2,1)S(1)}, bf16[2,128,4,64]{3,2,1,0:T(4,128)(2,1)S(1)}, u32[]{:S(2)}, u32[]{:S(2)}) collective-permute-start(bf16[2,128,4,64]{3,2,1,0:T(4,128)(2,1)S(1)} %get-tuple-element.15), channel_id=1, source_target_pairs={{1,0},{2,1},{3,2},{4,3},{5,4},{6,5},{7,6},{8,7},{9,8},{10,9},{11,1... | collective-permute-start | bytes 393224 | tf_op jit(solution)/shard_map/ppermute | solution.py:114
  70.4 0.9 fusion.8
  71.3 0.0 collective-permute-done
  71.3 1.3 collective-permute-start.7
  72.6 0.0 collective-permute-done.5
  72.6 5.1 %collective-permute-start.1 = (bf16[2,2,64,64]{3,2,1,0:T(8,128)(2,1)S(1)}, bf16[2,2,64,64]{3,2,1,0:T(8,128)(2,1)S(1)}, u32[]{:S(2)}, u32[]{:S(2)}) collective-permute-start(bf16[2,2,64,64]{3,2,1,0:T(8,128)(2,1)S(1)} %get-tuple-element.12), channel_id=1, source_target_pairs={{0,16},{1,17},{2,18},{3,19},{4,20},{5,21},{6,22},{7,23},{8,24},{9,... | collective-permute-start | bytes 98312 | tf_op jit(solution)/shard_map/ppermute | solution.py:114
  77.7 0.0 collective-permute-done.2
  77.8 1.3 collective-permute-start.6
  79.1 0.7 collective-permute-done.7
  79.7 0.0 collective-permute-done.1
  79.7 3.0 %collective-permute-done.6 = bf16[2,2,64,64]{3,2,1,0:T(8,128)(2,1)S(1)} collective-permute-done((bf16[2,2,64,64]{3,2,1,0:T(8,128)(2,1)S(1)}, bf16[2,2,64,64]{3,2,1,0:T(8,128)(2,1)S(1)}, u32[]{:S(2)}, u32[]{:S(2)}) %collective-permute-start.6) | collective-permute-done | bytes 32800 | tf_op jit(solution)/shard_map/ppermute | solution.py:114
  82.8 0.0 collective-permute-done.3
  82.8 0.0 collective-permute-done.4
  82.8 11.6 %maximum_maximum_fusion.x_ref = bf16[2,132,72,64]{3,2,1,0:T(8,128)(2,1)S(1)} fusion(bf16[2,2,4,64]{3,2,1,0:T(4,128)(2,1)S(1)} %collective-permute-done.7, bf16[2,2,64,64]{3,2,1,0:T(8,128)(2,1)S(1)} %collective-permute-done.6, bf16[2,2,4,64]{3,2,1,0:T(4,128)(2,1)S(1)} %collective-permute-done.5, bf16[2,128,4,64]{3,2,1,0:T(4,128)(2,1)S(1)} %collective-permute-done.4, ...), kind=kLoop, calls=%fused_computation | loop fusion | flops 21897216 | bytes 4866048 | tf_op jit(solution)/shard_map/concatenate | solution.py:118
  94.3 0.1 broadcast_in_dim.22.cm_ref
  94.4 41.4 %shard_map.37 = f32[2,128,64,256]{3,2,1,0:T(8,128)} custom-call(bf16[2,132,72,64]{3,2,1,0:T(8,128)(2,1)S(1)} %maximum_maximum_fusion.x_ref, bf16[64,256]{1,0:T(8,128)(2,1)S(1)} %fusion.3.kb_ref, bf16[256,256]{1,0:T(8,128)(2,1)S(1)} %multiply_convert_fusion.g3_ref, f32[1,256]{1,0:T(1,128)S(1)} %bitcast.8, f32[1,256]{1,0:T(1,128)S(1)} %bitcast.9, ...), custom_call_target="tpu_custom_call" | custom-call | flops 5775556608 | bytes 19210240 | tf_op jit(solution)/shard_map/pallas_call | solution.py:149
  (6 shorter events, 0.1 us)
Async XLA Ops:
  0.0 15.5 %copy-start.1 = (f32[256]{0:T(256)S(1)}, f32[256]{0:T(256)}, u32[]{:S(2)}) copy-start(f32[256]{0:T(256)} %param.4) | copy-start | bytes 3076
  0.0 16.3 %copy-start = (f32[256]{0:T(256)S(1)}, f32[256]{0:T(256)}, u32[]{:S(2)}) copy-start(f32[256]{0:T(256)} %param.5) | copy-start | bytes 3076
  6.2 37.7 %all-to-all-start = ((bf16[4,2,128,1024]{2,1,0,3:T(2,128)(2,1)}), bf16[4,2,128,1024]{2,1,0,3:T(2,128)(2,1)S(1)}, u32[]{:S(2)}, u32[]{:S(2)}) async-start(bf16[4,2,128,1024]{2,1,0,3:T(2,128)(2,1)} %copy.10), calls=%async_computation | async-start | bytes 4194304 | tf_op jit(solution)/shard_map/all_to_all | solution.py:131
  54.4 16.9 %collective-permute-start = (bf16[2,2,4,64]{3,2,1,0:T(4,128)(2,1)S(1)}, bf16[2,2,4,64]{3,2,1,0:T(4,128)(2,1)S(1)}, u32[]{:S(2)}, u32[]{:S(2)}) collective-permute-start(bf16[2,2,4,64]{3,2,1,0:T(4,128)(2,1)S(1)} %get-tuple-element.8), channel_id=1, source_target_pairs={{0,17},{1,18},{2,19},{3,20},{4,21},{5,22},{6,23},{7,24},{8,25},{9,... | collective-permute-start | bytes 6152 | tf_op jit(solution)/shard_map/ppermute | solution.py:114
  59.6 13.0 %collective-permute-start.5 = (bf16[2,2,4,64]{3,2,1,0:T(4,128)(2,1)S(1)}, bf16[2,2,4,64]{3,2,1,0:T(4,128)(2,1)S(1)}, u32[]{:S(2)}, u32[]{:S(2)}) collective-permute-start(bf16[2,2,4,64]{3,2,1,0:T(4,128)(2,1)S(1)} %get-tuple-element.9), channel_id=1, source_target_pairs={{16,1},{17,2},{18,3},{19,4},{20,5},{21,6},{22,7},{23,8},{24,9},{25... | collective-permute-start | bytes 6152 | tf_op jit(solution)/shard_map/ppermute | solution.py:114
  60.9 16.8 %collective-permute-start.2 = (bf16[2,2,4,64]{3,2,1,0:T(4,128)(2,1)S(1)}, bf16[2,2,4,64]{3,2,1,0:T(4,128)(2,1)S(1)}, u32[]{:S(2)}, u32[]{:S(2)}) collective-permute-start(bf16[2,2,4,64]{3,2,1,0:T(4,128)(2,1)S(1)} %get-tuple-element.10), channel_id=1, source_target_pairs={{1,16},{2,17},{3,18},{4,19},{5,20},{6,21},{7,22},{8,23},{9,24},{10... | collective-permute-start | bytes 6152 | tf_op jit(solution)/shard_map/ppermute | solution.py:114
  65.2 17.6 %collective-permute-start.3 = (bf16[2,128,4,64]{3,2,1,0:T(4,128)(2,1)S(1)}, bf16[2,128,4,64]{3,2,1,0:T(4,128)(2,1)S(1)}, u32[]{:S(2)}, u32[]{:S(2)}) collective-permute-start(bf16[2,128,4,64]{3,2,1,0:T(4,128)(2,1)S(1)} %get-tuple-element.14), channel_id=1, source_target_pairs={{0,1},{1,2},{2,3},{3,4},{4,5},{5,6},{6,7},{7,8},{8,9},{9,10},{10,1... | collective-permute-start | bytes 393224 | tf_op jit(solution)/shard_map/ppermute | solution.py:114
  68.5 14.3 %collective-permute-start.4 = (bf16[2,128,4,64]{3,2,1,0:T(4,128)(2,1)S(1)}, bf16[2,128,4,64]{3,2,1,0:T(4,128)(2,1)S(1)}, u32[]{:S(2)}, u32[]{:S(2)}) collective-permute-start(bf16[2,128,4,64]{3,2,1,0:T(4,128)(2,1)S(1)} %get-tuple-element.15), channel_id=1, source_target_pairs={{1,0},{2,1},{3,2},{4,3},{5,4},{6,5},{7,6},{8,7},{9,8},{10,9},{11,1... | collective-permute-start | bytes 393224 | tf_op jit(solution)/shard_map/ppermute | solution.py:114
  71.3 8.4 %collective-permute-start.7 = (bf16[2,2,4,64]{3,2,1,0:T(4,128)(2,1)S(1)}, bf16[2,2,4,64]{3,2,1,0:T(4,128)(2,1)S(1)}, u32[]{:S(2)}, u32[]{:S(2)}) collective-permute-start(bf16[2,2,4,64]{3,2,1,0:T(4,128)(2,1)S(1)} %get-tuple-element.11), channel_id=1, source_target_pairs={{17,0},{18,1},{19,2},{20,3},{21,4},{22,5},{23,6},{24,7},{25,8},{26... | collective-permute-start | bytes 6152 | tf_op jit(solution)/shard_map/ppermute | solution.py:114
  72.6 7.1 %collective-permute-start.1 = (bf16[2,2,64,64]{3,2,1,0:T(8,128)(2,1)S(1)}, bf16[2,2,64,64]{3,2,1,0:T(8,128)(2,1)S(1)}, u32[]{:S(2)}, u32[]{:S(2)}) collective-permute-start(bf16[2,2,64,64]{3,2,1,0:T(8,128)(2,1)S(1)} %get-tuple-element.12), channel_id=1, source_target_pairs={{0,16},{1,17},{2,18},{3,19},{4,20},{5,21},{6,22},{7,23},{8,24},{9,... | collective-permute-start | bytes 98312 | tf_op jit(solution)/shard_map/ppermute | solution.py:114
  77.8 5.0 %collective-permute-start.6 = (bf16[2,2,64,64]{3,2,1,0:T(8,128)(2,1)S(1)}, bf16[2,2,64,64]{3,2,1,0:T(8,128)(2,1)S(1)}, u32[]{:S(2)}, u32[]{:S(2)}) collective-permute-start(bf16[2,2,64,64]{3,2,1,0:T(8,128)(2,1)S(1)} %get-tuple-element.13), channel_id=1, source_target_pairs={{16,0},{17,1},{18,2},{19,3},{20,4},{21,5},{22,6},{23,7},{24,8},{25... | collective-permute-start | bytes 98312 | tf_op jit(solution)/shard_map/ppermute | solution.py:114

commit v16 on v14

--- a/solution.py
+++ b/solution.py
@@ -78,7 +78,7 @@
         f1_ref[pl.ds(pl.multiple_of(q * wp, 8), wp), :] = f1
         return carry
 
-    lax.fori_loop(1, rows - 1, body1, 0)
+    lax.fori_loop(1, rows - 1, body1, 0, unroll=2)
     f1_ref[pl.ds(0, wp), :] = jnp.zeros((wp, f1_ref.shape[1]), jnp.float32)
     f1_ref[pl.ds((rows - 1) * wp, wp), :] = jnp.zeros((wp, f1_ref.shape[1]), jnp.float32)
 
@@ -92,7 +92,7 @@
         o_ref[0, q - RH] = f2[: wp - 2 * CH]
         return carry
 
-    lax.fori_loop(RH, rows - RH, body2, 0)
+    lax.fori_loop(RH, rows - RH, body2, 0, unroll=2)
 
 
 def pin(x):

time: 124 us -> 123 us (level)
  no operation moved by 1% of the time
where the time goes in v16:
time: 123 us; the launch traced here: 122 us
  Pallas kernels  40.3 us (33%)
  waiting for transfers between devices  38.7 us (31%)
  starting transfers between devices  20.2 us (16%)
  local copies, waits for them, and re-layouts  16.1 us (13%)
  other arithmetic  6.25 us (5%)
    pallas_call x1, Pallas kernels, per_device(): pl.pallas_call(functools.partial(fit_kernel, wp), out_shape=jax.ShapeDtyp...  40.3 us
    all_to_all x1, waiting for transfers between devices, per_device(): x = lax.all_to_all(images, 'gy', split_axis=3, concat_axis=0, tiled=True)  27.6 us
    ppermute x2, waiting for transfers between devices, halo(): lax.ppermute(head, axis, [(i + 1, i) for i in range(count - 1)])  9.68 us
    all_to_all x1, starting transfers between devices, per_device(): x = lax.all_to_all(images, 'gy', split_axis=3, concat_axis=0, tiled=True)  9.3 us
    all_to_all x3, local copies, waits for them, and re-layouts, per_device(): x = lax.all_to_all(images, 'gy', split_axis=3, concat_axis=0, tiled=True)  8.27 us
    ppermute x2, starting transfers between devices, halo(): lax.ppermute(tail, axis, [(i, i + 1) for i in range(count - 1)])  7.72 us
    unnamed x7, local copies, waits for them, and re-layouts  6.19 us
    concatenate x1, other arithmetic, halo(): jnp.concatenate([lax.ppermute(tail, axis, [(i, i + 1) for i in range(coun...  5.07 us
  transfers between devices with their start and end apart: 5, of which 5 were waited for; matrix products, arithmetic and copies ran while one was open for 1% of the time, Pallas kernels for 0%

profile of v16, /device:TPU:1, one launch (start us, length us, event | category | flops | bytes accessed | tf_op | source)
XLA Modules:
  0.0 122.2 jit_solution(15592493667254080036)
XLA Ops:
  0.0 0.0 copy-start.2
  0.0 0.0 copy-start.1
  0.0 6.2 %copy.10 = bf16[4,2,128,1024]{2,1,0,3:T(2,128)(2,1)} copy(bf16[4,2,128,1024]{3,2,1,0:T(8,128)(2,1)} %param.3) | data formatting | bytes 4194304 | tf_op args[0]
  6.2 9.3 %all-to-all-start = ((bf16[4,2,128,1024]{2,1,0,3:T(2,128)(2,1)}), bf16[4,2,128,1024]{2,1,0,3:T(2,128)(2,1)S(1)}, u32[]{:S(2)}, u32[]{:S(2)}) async-start(bf16[4,2,128,1024]{2,1,0,3:T(2,128)(2,1)} %copy.10), calls=%async_computation | async-start | bytes 4194304 | tf_op jit(solution)/shard_map/all_to_all | solution.py:108
  15.5 0.0 copy-done.2
  15.5 0.1 multiply_reduce_fusion
  15.6 0.5 fusion.8
  16.1 0.1 copy.14
  16.3 0.0 copy-done.1
  16.3 27.6 %all-to-all-done = bf16[4,2,128,1024]{2,1,0,3:T(2,128)(2,1)S(1)} async-done(((bf16[4,2,128,1024]{2,1,0,3:T(2,128)(2,1)}), bf16[4,2,128,1024]{2,1,0,3:T(2,128)(2,1)S(1)}, u32[]{:S(2)}, u32[]{:S(2)}) %all-to-all-start) | async-done | bytes 2097184 | tf_op jit(solution)/shard_map/all_to_all | solution.py:108
  43.9 0.3 copy.11
  44.2 0.2 copy.12
  44.4 7.8 %copy.13 = bf16[64,2,128,64]{0,3,2,1:T(8,128)(2,1)} copy(bf16[64,2,128,64]{2,3,1,0:T(8,128)(2,1)S(1)} %bitcast.14) | data formatting | bytes 4194304 | tf_op jit(solution)/shard_map/all_to_all | solution.py:108
  52.2 1.4 %fusion.7 = (bf16[2,128,4,64]{3,2,1,0:T(4,128)(2,1)S(1)}, bf16[2,128,4,64]{3,2,1,0:T(4,128)(2,1)S(1)}) fusion(bf16[2,128,64,64]{3,2,1,0:T(8,128)(2,1)} %bitcast.11), kind=kLoop, calls=%fused_computation.19 | loop fusion | bytes 524288 | tf_op jit(solution)/shard_map/slice | solution.py:32
  53.6 5.1 %collective-permute-start = (bf16[2,128,4,64]{3,2,1,0:T(4,128)(2,1)S(1)}, bf16[2,128,4,64]{3,2,1,0:T(4,128)(2,1)S(1)}, u32[]{:S(2)}, u32[]{:S(2)}) collective-permute-start(bf16[2,128,4,64]{3,2,1,0:T(4,128)(2,1)S(1)} %get-tuple-element.10), channel_id=1, source_target_pairs={{0,1},{1,2},{2,3},{3,4},{4,5},{5,6},{6,7},{7,8},{8,9},{9,10},{10,1... | collective-permute-start | bytes 393224 | tf_op jit(solution)/shard_map/ppermute | solution.py:35
  58.7 1.9 %collective-permute-start.1 = (bf16[2,128,4,64]{3,2,1,0:T(4,128)(2,1)S(1)}, bf16[2,128,4,64]{3,2,1,0:T(4,128)(2,1)S(1)}, u32[]{:S(2)}, u32[]{:S(2)}) collective-permute-start(bf16[2,128,4,64]{3,2,1,0:T(4,128)(2,1)S(1)} %get-tuple-element.11), channel_id=1, source_target_pairs={{1,0},{2,1},{3,2},{4,3},{5,4},{6,5},{7,6},{8,7},{9,8},{10,9},{11,1... | collective-permute-start | bytes 393224 | tf_op jit(solution)/shard_map/ppermute | solution.py:37
  60.6 0.1 fusion.3.kb_ref
  60.7 0.0 copy-start
  60.8 1.2 %collective-permute-done = bf16[2,128,4,64]{3,2,1,0:T(4,128)(2,1)S(1)} collective-permute-done((bf16[2,128,4,64]{3,2,1,0:T(4,128)(2,1)S(1)}, bf16[2,128,4,64]{3,2,1,0:T(4,128)(2,1)S(1)}, u32[]{:S(2)}, u32[]{:S(2)}) %collective-permute-start) | collective-permute-done | bytes 131104 | tf_op jit(solution)/shard_map/ppermute | solution.py:35
  62.0 5.9 %collective-permute-done.1 = bf16[2,128,4,64]{3,2,1,0:T(4,128)(2,1)S(1)} collective-permute-done((bf16[2,128,4,64]{3,2,1,0:T(4,128)(2,1)S(1)}, bf16[2,128,4,64]{3,2,1,0:T(4,128)(2,1)S(1)}, u32[]{:S(2)}, u32[]{:S(2)}) %collective-permute-start.1) | collective-permute-done | bytes 131104 | tf_op jit(solution)/shard_map/ppermute | solution.py:37
  67.9 0.9 pad_maximum_fusion.3
  68.9 2.6 %collective-permute-start.2 = (bf16[2,2,72,64]{3,2,1,0:T(8,128)(2,1)S(1)}, bf16[2,2,72,64]{3,2,1,0:T(8,128)(2,1)S(1)}, u32[]{:S(2)}, u32[]{:S(2)}) collective-permute-start(bf16[2,2,72,64]{3,2,1,0:T(8,128)(2,1)S(1)} %get-tuple-element.8), channel_id=1, source_target_pairs={{0,16},{16,32},{32,48},{48,64},{64,80},{80,96},{96,112},{1,17},{17... | collective-permute-start | bytes 110600 | tf_op jit(solution)/shard_map/ppermute | solution.py:35
  71.5 1.3 %collective-permute-start.3 = (bf16[2,2,72,64]{3,2,1,0:T(8,128)(2,1)S(1)}, bf16[2,2,72,64]{3,2,1,0:T(8,128)(2,1)S(1)}, u32[]{:S(2)}, u32[]{:S(2)}) collective-permute-start(bf16[2,2,72,64]{3,2,1,0:T(8,128)(2,1)S(1)} %get-tuple-element.9), channel_id=1, source_target_pairs={{16,0},{32,16},{48,32},{64,48},{80,64},{96,80},{112,96},{17,1},{33... | collective-permute-start | bytes 110600 | tf_op jit(solution)/shard_map/ppermute | solution.py:37
  72.8 0.2 collective-permute-done.2
  73.0 3.8 %collective-permute-done.3 = bf16[2,2,72,64]{3,2,1,0:T(8,128)(2,1)S(1)} collective-permute-done((bf16[2,2,72,64]{3,2,1,0:T(8,128)(2,1)S(1)}, bf16[2,2,72,64]{3,2,1,0:T(8,128)(2,1)S(1)}, u32[]{:S(2)}, u32[]{:S(2)}) %collective-permute-start.3) | collective-permute-done | bytes 36896 | tf_op jit(solution)/shard_map/ppermute | solution.py:37
  76.8 0.0 copy-done
  76.8 5.1 %pad_maximum_fusion.x_ref = bf16[2,132,72,64]{3,2,1,0:T(8,128)(2,1)S(1)} fusion(bf16[2,2,72,64]{3,2,1,0:T(8,128)(2,1)S(1)} %collective-permute-done.3, bf16[2,128,4,64]{3,2,1,0:T(4,128)(2,1)S(1)} %collective-permute-done.1, bf16[2,128,64,64]{3,2,1,0:T(8,128)(2,1)S(1)} %bitcast.13, bf16[2,128,4,64]{3,2,1,0:T(4,128)(2,1)S(1)} %collective-permute-done, ...), kind=kLoop, calls=%fused_computation | loop fusion | flops 12165120 | bytes 4866048 | tf_op jit(solution)/shard_map/concatenate | solution.py:33
  81.9 0.1 broadcast_in_dim.22.cm_ref
  82.0 40.3 %shard_map.37 = f32[2,128,64,256]{3,2,1,0:T(8,128)} custom-call(bf16[2,132,72,64]{3,2,1,0:T(8,128)(2,1)S(1)} %pad_maximum_fusion.x_ref, bf16[64,256]{1,0:T(8,128)(2,1)S(1)} %fusion.3.kb_ref, bf16[256,256]{1,0:T(8,128)(2,1)S(1)} %multiply_convert_fusion.g3_ref, f32[1,256]{1,0:T(1,128)S(1)} %bitcast.8, f32[1,256]{1,0:T(1,128)S(1)} %bitcast.9, ...), custom_call_target="tpu_custom_call" | custom-call | flops 5775556608 | bytes 19210240 | tf_op jit(solution)/shard_map/pallas_call | solution.py:127
  (6 shorter events, 0.1 us)
Async XLA Ops:
  0.0 15.5 %copy-start.2 = (f32[256]{0:T(256)S(1)}, f32[256]{0:T(256)}, u32[]{:S(2)}) copy-start(f32[256]{0:T(256)} %param.4) | copy-start | bytes 3076
  0.0 16.3 %copy-start.1 = (f32[256]{0:T(256)S(1)}, f32[256]{0:T(256)}, u32[]{:S(2)}) copy-start(f32[256]{0:T(256)} %param.5) | copy-start | bytes 3076
  6.2 37.7 %all-to-all-start = ((bf16[4,2,128,1024]{2,1,0,3:T(2,128)(2,1)}), bf16[4,2,128,1024]{2,1,0,3:T(2,128)(2,1)S(1)}, u32[]{:S(2)}, u32[]{:S(2)}) async-start(bf16[4,2,128,1024]{2,1,0,3:T(2,128)(2,1)} %copy.10), calls=%async_computation | async-start | bytes 4194304 | tf_op jit(solution)/shard_map/all_to_all | solution.py:108
  53.6 8.4 %collective-permute-start = (bf16[2,128,4,64]{3,2,1,0:T(4,128)(2,1)S(1)}, bf16[2,128,4,64]{3,2,1,0:T(4,128)(2,1)S(1)}, u32[]{:S(2)}, u32[]{:S(2)}) collective-permute-start(bf16[2,128,4,64]{3,2,1,0:T(4,128)(2,1)S(1)} %get-tuple-element.10), channel_id=1, source_target_pairs={{0,1},{1,2},{2,3},{3,4},{4,5},{5,6},{6,7},{7,8},{8,9},{9,10},{10,1... | collective-permute-start | bytes 393224 | tf_op jit(solution)/shard_map/ppermute | solution.py:35
  58.7 9.2 %collective-permute-start.1 = (bf16[2,128,4,64]{3,2,1,0:T(4,128)(2,1)S(1)}, bf16[2,128,4,64]{3,2,1,0:T(4,128)(2,1)S(1)}, u32[]{:S(2)}, u32[]{:S(2)}) collective-permute-start(bf16[2,128,4,64]{3,2,1,0:T(4,128)(2,1)S(1)} %get-tuple-element.11), channel_id=1, source_target_pairs={{1,0},{2,1},{3,2},{4,3},{5,4},{6,5},{7,6},{8,7},{9,8},{10,9},{11,1... | collective-permute-start | bytes 393224 | tf_op jit(solution)/shard_map/ppermute | solution.py:37
  60.7 16.1 %copy-start = (bf16[64,2,128,64]{0,3,2,1:T(8,128)(2,1)S(1)}, bf16[64,2,128,64]{0,3,2,1:T(8,128)(2,1)}, u32[]{:S(2)}) copy-start(bf16[64,2,128,64]{0,3,2,1:T(8,128)(2,1)} %copy.13) | copy-start | bytes 6291460
  68.9 4.2 %collective-permute-start.2 = (bf16[2,2,72,64]{3,2,1,0:T(8,128)(2,1)S(1)}, bf16[2,2,72,64]{3,2,1,0:T(8,128)(2,1)S(1)}, u32[]{:S(2)}, u32[]{:S(2)}) collective-permute-start(bf16[2,2,72,64]{3,2,1,0:T(8,128)(2,1)S(1)} %get-tuple-element.8), channel_id=1, source_target_pairs={{0,16},{16,32},{32,48},{48,64},{64,80},{80,96},{96,112},{1,17},{17... | collective-permute-start | bytes 110600 | tf_op jit(solution)/shard_map/ppermute | solution.py:35
  71.5 5.3 %collective-permute-start.3 = (bf16[2,2,72,64]{3,2,1,0:T(8,128)(2,1)S(1)}, bf16[2,2,72,64]{3,2,1,0:T(8,128)(2,1)S(1)}, u32[]{:S(2)}, u32[]{:S(2)}) collective-permute-start(bf16[2,2,72,64]{3,2,1,0:T(8,128)(2,1)S(1)} %get-tuple-element.9), channel_id=1, source_target_pairs={{16,0},{32,16},{48,32},{64,48},{80,64},{96,80},{112,96},{17,1},{33... | collective-permute-start | bytes 110600 | tf_op jit(solution)/shard_map/ppermute | solution.py:37

commit v17 on v16

--- a/solution.py
+++ b/solution.py
@@ -57,7 +57,8 @@
     b_ref[...] = sb
     f0 = jnp.maximum(sb, 0.0)
     f0_ref[...] = f0
-    f3_ref[...] = f0.astype(jnp.bfloat16)
+    inner = (rows - 2) * wp
+    f3_ref[pl.ds(2 * wp, inner), :] = f0[wp:(rows - 1) * wp].astype(jnp.bfloat16)
 
     def update(src_ref, q):
         o = pl.multiple_of(q * wp, 8)
@@ -70,20 +71,20 @@
         v = (alpha * c + beta * nb) + (b_ref[pl.ds(o, wp), :] - m_ref[pl.ds(o - wp, wp), :])
         return jnp.maximum(v, 0.0)
 
-    m_ref[...] = jnp.dot(f3_ref[pl.ds(wp, (rows - 2) * wp), :], g3_ref[...],
+    m_ref[...] = jnp.dot(f3_ref[pl.ds(2 * wp, inner), :], g3_ref[...],
                          preferred_element_type=jnp.float32)
 
     def body1(q, carry):
-        f1 = update(f0_ref, q) * (cm * rm_ref[t * TR + q])
+        f1 = update(f0_ref, q) * cm
         f1_ref[pl.ds(pl.multiple_of(q * wp, 8), wp), :] = f1
         return carry
 
     lax.fori_loop(1, rows - 1, body1, 0, unroll=2)
-    f1_ref[pl.ds(0, wp), :] = jnp.zeros((wp, f1_ref.shape[1]), jnp.float32)
-    f1_ref[pl.ds((rows - 1) * wp, wp), :] = jnp.zeros((wp, f1_ref.shape[1]), jnp.float32)
+    for q in (1, rows - 2):
+        f1_ref[pl.ds(q * wp, wp), :] = f1_ref[pl.ds(q * wp, wp), :] * rm_ref[t * TR + q]
 
-    f3_ref[...] = f1_ref[...].astype(jnp.bfloat16)
-    m_ref[...] = jnp.dot(f3_ref[pl.ds(wp, (rows - 2) * wp), :], g3_ref[...],
+    f3_ref[pl.ds(2 * wp, inner), :] = f1_ref[pl.ds(wp, inner), :].astype(jnp.bfloat16)
+    m_ref[...] = jnp.dot(f3_ref[pl.ds(2 * wp, inner), :], g3_ref[...],
                          preferred_element_type=jnp.float32)
 
     def body2(q, carry):

time: 123 us -> 121 us (0.984)
  Pallas kernels: 40.3 us -> 38.9 us
    pallas_call x1, Pallas kernels: 40.3 us -> 38.9 us  [per_device(): pl.pallas_call(functools.partial(fit_kernel, wp), out_shape=jax.ShapeDtyp...]
where the time goes in v17:
time: 121 us
  Pallas kernels  38.9 us (32%)
  waiting for transfers between devices  38.7 us (32%)
  starting transfers between devices  20.2 us (17%)
  local copies, waits for them, and re-layouts  16.1 us (13%)
  other arithmetic  6.25 us (5%)
    pallas_call x1, Pallas kernels, per_device(): pl.pallas_call(functools.partial(fit_kernel, wp), out_shape=jax.ShapeDtyp...  38.9 us
    all_to_all x1, waiting for transfers between devices, per_device(): x = lax.all_to_all(images, 'gy', split_axis=3, concat_axis=0, tiled=True)  27.6 us
    ppermute x2, waiting for transfers between devices, halo(): lax.ppermute(head, axis, [(i + 1, i) for i in range(count - 1)])  9.68 us
    all_to_all x1, starting transfers between devices, per_device(): x = lax.all_to_all(images, 'gy', split_axis=3, concat_axis=0, tiled=True)  9.3 us
    all_to_all x3, local copies, waits for them, and re-layouts, per_device(): x = lax.all_to_all(images, 'gy', split_axis=3, concat_axis=0, tiled=True)  8.27 us
    ppermute x2, starting transfers between devices, halo(): lax.ppermute(tail, axis, [(i, i + 1) for i in range(count - 1)])  7.72 us
    unnamed x7, local copies, waits for them, and re-layouts  6.19 us
    concatenate x1, other arithmetic, halo(): jnp.concatenate([lax.ppermute(tail, axis, [(i, i + 1) for i in range(coun...  5.07 us
  transfers between devices with their start and end apart: 5, of which 5 were waited for; matrix products, arithmetic and copies ran while one was open for 1% of the time, Pallas kernels for 0%

profile of v17, /device:TPU:1, one launch (start us, length us, event | category | flops | bytes accessed | tf_op | source)
XLA Modules:
  0.0 120.9 jit_solution(2595729117133887199)
XLA Ops:
  0.0 0.0 copy-start.2
  0.0 0.0 copy-start.1
  0.0 6.2 %copy.10 = bf16[4,2,128,1024]{2,1,0,3:T(2,128)(2,1)} copy(bf16[4,2,128,1024]{3,2,1,0:T(8,128)(2,1)} %param.3) | data formatting | bytes 4194304 | tf_op args[0]
  6.2 9.3 %all-to-all-start = ((bf16[4,2,128,1024]{2,1,0,3:T(2,128)(2,1)}), bf16[4,2,128,1024]{2,1,0,3:T(2,128)(2,1)S(1)}, u32[]{:S(2)}, u32[]{:S(2)}) async-start(bf16[4,2,128,1024]{2,1,0,3:T(2,128)(2,1)} %copy.10), calls=%async_computation | async-start | bytes 4194304 | tf_op jit(solution)/shard_map/all_to_all | solution.py:109
  15.5 0.0 copy-done.2
  15.5 0.1 multiply_reduce_fusion
  15.6 0.5 fusion.8
  16.1 0.1 copy.14
  16.3 0.0 copy-done.1
  16.3 27.6 %all-to-all-done = bf16[4,2,128,1024]{2,1,0,3:T(2,128)(2,1)S(1)} async-done(((bf16[4,2,128,1024]{2,1,0,3:T(2,128)(2,1)}), bf16[4,2,128,1024]{2,1,0,3:T(2,128)(2,1)S(1)}, u32[]{:S(2)}, u32[]{:S(2)}) %all-to-all-start) | async-done | bytes 2097184 | tf_op jit(solution)/shard_map/all_to_all | solution.py:109
  43.9 0.3 copy.11
  44.2 0.2 copy.12
  44.4 7.8 %copy.13 = bf16[64,2,128,64]{0,3,2,1:T(8,128)(2,1)} copy(bf16[64,2,128,64]{2,3,1,0:T(8,128)(2,1)S(1)} %bitcast.14) | data formatting | bytes 4194304 | tf_op jit(solution)/shard_map/all_to_all | solution.py:109
  52.2 1.4 %fusion.7 = (bf16[2,128,4,64]{3,2,1,0:T(4,128)(2,1)S(1)}, bf16[2,128,4,64]{3,2,1,0:T(4,128)(2,1)S(1)}) fusion(bf16[2,128,64,64]{3,2,1,0:T(8,128)(2,1)} %bitcast.11), kind=kLoop, calls=%fused_computation.19 | loop fusion | bytes 524288 | tf_op jit(solution)/shard_map/slice | solution.py:32
  53.6 5.1 %collective-permute-start = (bf16[2,128,4,64]{3,2,1,0:T(4,128)(2,1)S(1)}, bf16[2,128,4,64]{3,2,1,0:T(4,128)(2,1)S(1)}, u32[]{:S(2)}, u32[]{:S(2)}) collective-permute-start(bf16[2,128,4,64]{3,2,1,0:T(4,128)(2,1)S(1)} %get-tuple-element.10), channel_id=1, source_target_pairs={{0,1},{1,2},{2,3},{3,4},{4,5},{5,6},{6,7},{7,8},{8,9},{9,10},{10,1... | collective-permute-start | bytes 393224 | tf_op jit(solution)/shard_map/ppermute | solution.py:35
  58.7 1.9 %collective-permute-start.1 = (bf16[2,128,4,64]{3,2,1,0:T(4,128)(2,1)S(1)}, bf16[2,128,4,64]{3,2,1,0:T(4,128)(2,1)S(1)}, u32[]{:S(2)}, u32[]{:S(2)}) collective-permute-start(bf16[2,128,4,64]{3,2,1,0:T(4,128)(2,1)S(1)} %get-tuple-element.11), channel_id=1, source_target_pairs={{1,0},{2,1},{3,2},{4,3},{5,4},{6,5},{7,6},{8,7},{9,8},{10,9},{11,1... | collective-permute-start | bytes 393224 | tf_op jit(solution)/shard_map/ppermute | solution.py:37
  60.6 0.1 fusion.3.kb_ref
  60.7 0.0 copy-start
  60.8 1.2 %collective-permute-done = bf16[2,128,4,64]{3,2,1,0:T(4,128)(2,1)S(1)} collective-permute-done((bf16[2,128,4,64]{3,2,1,0:T(4,128)(2,1)S(1)}, bf16[2,128,4,64]{3,2,1,0:T(4,128)(2,1)S(1)}, u32[]{:S(2)}, u32[]{:S(2)}) %collective-permute-start) | collective-permute-done | bytes 131104 | tf_op jit(solution)/shard_map/ppermute | solution.py:35
  62.0 5.9 %collective-permute-done.1 = bf16[2,128,4,64]{3,2,1,0:T(4,128)(2,1)S(1)} collective-permute-done((bf16[2,128,4,64]{3,2,1,0:T(4,128)(2,1)S(1)}, bf16[2,128,4,64]{3,2,1,0:T(4,128)(2,1)S(1)}, u32[]{:S(2)}, u32[]{:S(2)}) %collective-permute-start.1) | collective-permute-done | bytes 131104 | tf_op jit(solution)/shard_map/ppermute | solution.py:37
  67.9 0.9 pad_maximum_fusion.3
  68.9 2.6 %collective-permute-start.2 = (bf16[2,2,72,64]{3,2,1,0:T(8,128)(2,1)S(1)}, bf16[2,2,72,64]{3,2,1,0:T(8,128)(2,1)S(1)}, u32[]{:S(2)}, u32[]{:S(2)}) collective-permute-start(bf16[2,2,72,64]{3,2,1,0:T(8,128)(2,1)S(1)} %get-tuple-element.8), channel_id=1, source_target_pairs={{0,16},{16,32},{32,48},{48,64},{64,80},{80,96},{96,112},{1,17},{17... | collective-permute-start | bytes 110600 | tf_op jit(solution)/shard_map/ppermute | solution.py:35
  71.5 1.3 %collective-permute-start.3 = (bf16[2,2,72,64]{3,2,1,0:T(8,128)(2,1)S(1)}, bf16[2,2,72,64]{3,2,1,0:T(8,128)(2,1)S(1)}, u32[]{:S(2)}, u32[]{:S(2)}) collective-permute-start(bf16[2,2,72,64]{3,2,1,0:T(8,128)(2,1)S(1)} %get-tuple-element.9), channel_id=1, source_target_pairs={{16,0},{32,16},{48,32},{64,48},{80,64},{96,80},{112,96},{17,1},{33... | collective-permute-start | bytes 110600 | tf_op jit(solution)/shard_map/ppermute | solution.py:37
  72.8 0.2 collective-permute-done.2
  73.0 3.8 %collective-permute-done.3 = bf16[2,2,72,64]{3,2,1,0:T(8,128)(2,1)S(1)} collective-permute-done((bf16[2,2,72,64]{3,2,1,0:T(8,128)(2,1)S(1)}, bf16[2,2,72,64]{3,2,1,0:T(8,128)(2,1)S(1)}, u32[]{:S(2)}, u32[]{:S(2)}) %collective-permute-start.3) | collective-permute-done | bytes 36896 | tf_op jit(solution)/shard_map/ppermute | solution.py:37
  76.8 0.0 copy-done
  76.8 5.1 %pad_maximum_fusion.x_ref = bf16[2,132,72,64]{3,2,1,0:T(8,128)(2,1)S(1)} fusion(bf16[2,2,72,64]{3,2,1,0:T(8,128)(2,1)S(1)} %collective-permute-done.3, bf16[2,128,4,64]{3,2,1,0:T(4,128)(2,1)S(1)} %collective-permute-done.1, bf16[2,128,64,64]{3,2,1,0:T(8,128)(2,1)S(1)} %bitcast.13, bf16[2,128,4,64]{3,2,1,0:T(4,128)(2,1)S(1)} %collective-permute-done, ...), kind=kLoop, calls=%fused_computation | loop fusion | flops 12165120 | bytes 4866048 | tf_op jit(solution)/shard_map/concatenate | solution.py:33
  81.9 0.1 broadcast_in_dim.22.cm_ref
  82.0 38.9 %shard_map.37 = f32[2,128,64,256]{3,2,1,0:T(8,128)} custom-call(bf16[2,132,72,64]{3,2,1,0:T(8,128)(2,1)S(1)} %pad_maximum_fusion.x_ref, bf16[64,256]{1,0:T(8,128)(2,1)S(1)} %fusion.3.kb_ref, bf16[256,256]{1,0:T(8,128)(2,1)S(1)} %multiply_convert_fusion.g3_ref, f32[1,256]{1,0:T(1,128)S(1)} %bitcast.8, f32[1,256]{1,0:T(1,128)S(1)} %bitcast.9, ...), custom_call_target="tpu_custom_call" | custom-call | flops 5775556608 | bytes 19210240 | tf_op jit(solution)/shard_map/pallas_call | solution.py:128
  (6 shorter events, 0.1 us)
Async XLA Ops:
  0.0 15.5 %copy-start.2 = (f32[256]{0:T(256)S(1)}, f32[256]{0:T(256)}, u32[]{:S(2)}) copy-start(f32[256]{0:T(256)} %param.4) | copy-start | bytes 3076
  0.0 16.3 %copy-start.1 = (f32[256]{0:T(256)S(1)}, f32[256]{0:T(256)}, u32[]{:S(2)}) copy-start(f32[256]{0:T(256)} %param.5) | copy-start | bytes 3076
  6.2 37.7 %all-to-all-start = ((bf16[4,2,128,1024]{2,1,0,3:T(2,128)(2,1)}), bf16[4,2,128,1024]{2,1,0,3:T(2,128)(2,1)S(1)}, u32[]{:S(2)}, u32[]{:S(2)}) async-start(bf16[4,2,128,1024]{2,1,0,3:T(2,128)(2,1)} %copy.10), calls=%async_computation | async-start | bytes 4194304 | tf_op jit(solution)/shard_map/all_to_all | solution.py:109
  53.6 8.4 %collective-permute-start = (bf16[2,128,4,64]{3,2,1,0:T(4,128)(2,1)S(1)}, bf16[2,128,4,64]{3,2,1,0:T(4,128)(2,1)S(1)}, u32[]{:S(2)}, u32[]{:S(2)}) collective-permute-start(bf16[2,128,4,64]{3,2,1,0:T(4,128)(2,1)S(1)} %get-tuple-element.10), channel_id=1, source_target_pairs={{0,1},{1,2},{2,3},{3,4},{4,5},{5,6},{6,7},{7,8},{8,9},{9,10},{10,1... | collective-permute-start | bytes 393224 | tf_op jit(solution)/shard_map/ppermute | solution.py:35
  58.7 9.2 %collective-permute-start.1 = (bf16[2,128,4,64]{3,2,1,0:T(4,128)(2,1)S(1)}, bf16[2,128,4,64]{3,2,1,0:T(4,128)(2,1)S(1)}, u32[]{:S(2)}, u32[]{:S(2)}) collective-permute-start(bf16[2,128,4,64]{3,2,1,0:T(4,128)(2,1)S(1)} %get-tuple-element.11), channel_id=1, source_target_pairs={{1,0},{2,1},{3,2},{4,3},{5,4},{6,5},{7,6},{8,7},{9,8},{10,9},{11,1... | collective-permute-start | bytes 393224 | tf_op jit(solution)/shard_map/ppermute | solution.py:37
  60.7 16.1 %copy-start = (bf16[64,2,128,64]{0,3,2,1:T(8,128)(2,1)S(1)}, bf16[64,2,128,64]{0,3,2,1:T(8,128)(2,1)}, u32[]{:S(2)}) copy-start(bf16[64,2,128,64]{0,3,2,1:T(8,128)(2,1)} %copy.13) | copy-start | bytes 6291460
  68.9 4.2 %collective-permute-start.2 = (bf16[2,2,72,64]{3,2,1,0:T(8,128)(2,1)S(1)}, bf16[2,2,72,64]{3,2,1,0:T(8,128)(2,1)S(1)}, u32[]{:S(2)}, u32[]{:S(2)}) collective-permute-start(bf16[2,2,72,64]{3,2,1,0:T(8,128)(2,1)S(1)} %get-tuple-element.8), channel_id=1, source_target_pairs={{0,16},{16,32},{32,48},{48,64},{64,80},{80,96},{96,112},{1,17},{17... | collective-permute-start | bytes 110600 | tf_op jit(solution)/shard_map/ppermute | solution.py:35
  71.5 5.3 %collective-permute-start.3 = (bf16[2,2,72,64]{3,2,1,0:T(8,128)(2,1)S(1)}, bf16[2,2,72,64]{3,2,1,0:T(8,128)(2,1)S(1)}, u32[]{:S(2)}, u32[]{:S(2)}) collective-permute-start(bf16[2,2,72,64]{3,2,1,0:T(8,128)(2,1)S(1)} %get-tuple-element.9), channel_id=1, source_target_pairs={{16,0},{32,16},{48,32},{64,48},{80,64},{96,80},{112,96},{17,1},{33... | collective-permute-start | bytes 110600 | tf_op jit(solution)/shard_map/ppermute | solution.py:37

commit v18 on v17

--- a/solution.py
+++ b/solution.py
@@ -79,7 +79,7 @@
         f1_ref[pl.ds(pl.multiple_of(q * wp, 8), wp), :] = f1
         return carry
 
-    lax.fori_loop(1, rows - 1, body1, 0, unroll=2)
+    lax.fori_loop(1, rows - 1, body1, 0, unroll=4)
     for q in (1, rows - 2):
         f1_ref[pl.ds(q * wp, wp), :] = f1_ref[pl.ds(q * wp, wp), :] * rm_ref[t * TR + q]
 
@@ -93,7 +93,7 @@
         o_ref[0, q - RH] = f2[: wp - 2 * CH]
         return carry
 
-    lax.fori_loop(RH, rows - RH, body2, 0, unroll=2)
+    lax.fori_loop(RH, rows - RH, body2, 0, unroll=4)
 
 
 def pin(x):

time: 121 us -> 123 us (1.017)
  Pallas kernels: 38.9 us -> 41 us
    pallas_call x1, Pallas kernels: 38.9 us -> 41 us  [per_device(): pl.pallas_call(functools.partial(fit_kernel, wp), out_shape=jax.ShapeDtyp...]
where the time goes in v18:
time: 123 us
  Pallas kernels  41 us (33%)
  waiting for transfers between devices  38.7 us (31%)
  starting transfers between devices  20.2 us (16%)
  local copies, waits for them, and re-layouts  16.1 us (13%)
  other arithmetic  6.25 us (5%)
    pallas_call x1, Pallas kernels, per_device(): pl.pallas_call(functools.partial(fit_kernel, wp), out_shape=jax.ShapeDtyp...  41 us
    all_to_all x1, waiting for transfers between devices, per_device(): x = lax.all_to_all(images, 'gy', split_axis=3, concat_axis=0, tiled=True)  27.6 us
    ppermute x2, waiting for transfers between devices, halo(): lax.ppermute(head, axis, [(i + 1, i) for i in range(count - 1)])  9.68 us
    all_to_all x1, starting transfers between devices, per_device(): x = lax.all_to_all(images, 'gy', split_axis=3, concat_axis=0, tiled=True)  9.3 us
    all_to_all x3, local copies, waits for them, and re-layouts, per_device(): x = lax.all_to_all(images, 'gy', split_axis=3, concat_axis=0, tiled=True)  8.27 us
    ppermute x2, starting transfers between devices, halo(): lax.ppermute(tail, axis, [(i, i + 1) for i in range(count - 1)])  7.72 us
    unnamed x7, local copies, waits for them, and re-layouts  6.19 us
    concatenate x1, other arithmetic, halo(): jnp.concatenate([lax.ppermute(tail, axis, [(i, i + 1) for i in range(coun...  5.07 us
  transfers between devices with their start and end apart: 5, of which 5 were waited for; matrix products, arithmetic and copies ran while one was open for 1% of the time, Pallas kernels for 0%

profile of v18, /device:TPU:1, one launch (start us, length us, event | category | flops | bytes accessed | tf_op | source)
XLA Modules:
  0.0 123.0 jit_solution(4501224558023324446)
XLA Ops:
  0.0 0.0 copy-start.2
  0.0 0.0 copy-start.1
  0.0 6.2 %copy.10 = bf16[4,2,128,1024]{2,1,0,3:T(2,128)(2,1)} copy(bf16[4,2,128,1024]{3,2,1,0:T(8,128)(2,1)} %param.3) | data formatting | bytes 4194304 | tf_op args[0]
  6.2 9.3 %all-to-all-start = ((bf16[4,2,128,1024]{2,1,0,3:T(2,128)(2,1)}), bf16[4,2,128,1024]{2,1,0,3:T(2,128)(2,1)S(1)}, u32[]{:S(2)}, u32[]{:S(2)}) async-start(bf16[4,2,128,1024]{2,1,0,3:T(2,128)(2,1)} %copy.10), calls=%async_computation | async-start | bytes 4194304 | tf_op jit(solution)/shard_map/all_to_all | solution.py:109
  15.5 0.0 copy-done.2
  15.5 0.1 multiply_reduce_fusion
  15.6 0.5 fusion.8
  16.1 0.1 copy.14
  16.3 0.0 copy-done.1
  16.3 27.6 %all-to-all-done = bf16[4,2,128,1024]{2,1,0,3:T(2,128)(2,1)S(1)} async-done(((bf16[4,2,128,1024]{2,1,0,3:T(2,128)(2,1)}), bf16[4,2,128,1024]{2,1,0,3:T(2,128)(2,1)S(1)}, u32[]{:S(2)}, u32[]{:S(2)}) %all-to-all-start) | async-done | bytes 2097184 | tf_op jit(solution)/shard_map/all_to_all | solution.py:109
  43.9 0.3 copy.11
  44.2 0.2 copy.12
  44.4 7.8 %copy.13 = bf16[64,2,128,64]{0,3,2,1:T(8,128)(2,1)} copy(bf16[64,2,128,64]{2,3,1,0:T(8,128)(2,1)S(1)} %bitcast.14) | data formatting | bytes 4194304 | tf_op jit(solution)/shard_map/all_to_all | solution.py:109
  52.2 1.4 %fusion.7 = (bf16[2,128,4,64]{3,2,1,0:T(4,128)(2,1)S(1)}, bf16[2,128,4,64]{3,2,1,0:T(4,128)(2,1)S(1)}) fusion(bf16[2,128,64,64]{3,2,1,0:T(8,128)(2,1)} %bitcast.11), kind=kLoop, calls=%fused_computation.19 | loop fusion | bytes 524288 | tf_op jit(solution)/shard_map/slice | solution.py:32
  53.6 5.1 %collective-permute-start = (bf16[2,128,4,64]{3,2,1,0:T(4,128)(2,1)S(1)}, bf16[2,128,4,64]{3,2,1,0:T(4,128)(2,1)S(1)}, u32[]{:S(2)}, u32[]{:S(2)}) collective-permute-start(bf16[2,128,4,64]{3,2,1,0:T(4,128)(2,1)S(1)} %get-tuple-element.10), channel_id=1, source_target_pairs={{0,1},{1,2},{2,3},{3,4},{4,5},{5,6},{6,7},{7,8},{8,9},{9,10},{10,1... | collective-permute-start | bytes 393224 | tf_op jit(solution)/shard_map/ppermute | solution.py:35
  58.7 1.9 %collective-permute-start.1 = (bf16[2,128,4,64]{3,2,1,0:T(4,128)(2,1)S(1)}, bf16[2,128,4,64]{3,2,1,0:T(4,128)(2,1)S(1)}, u32[]{:S(2)}, u32[]{:S(2)}) collective-permute-start(bf16[2,128,4,64]{3,2,1,0:T(4,128)(2,1)S(1)} %get-tuple-element.11), channel_id=1, source_target_pairs={{1,0},{2,1},{3,2},{4,3},{5,4},{6,5},{7,6},{8,7},{9,8},{10,9},{11,1... | collective-permute-start | bytes 393224 | tf_op jit(solution)/shard_map/ppermute | solution.py:37
  60.6 0.1 fusion.3.kb_ref
  60.7 0.0 copy-start
  60.8 1.2 %collective-permute-done = bf16[2,128,4,64]{3,2,1,0:T(4,128)(2,1)S(1)} collective-permute-done((bf16[2,128,4,64]{3,2,1,0:T(4,128)(2,1)S(1)}, bf16[2,128,4,64]{3,2,1,0:T(4,128)(2,1)S(1)}, u32[]{:S(2)}, u32[]{:S(2)}) %collective-permute-start) | collective-permute-done | bytes 131104 | tf_op jit(solution)/shard_map/ppermute | solution.py:35
  62.0 5.9 %collective-permute-done.1 = bf16[2,128,4,64]{3,2,1,0:T(4,128)(2,1)S(1)} collective-permute-done((bf16[2,128,4,64]{3,2,1,0:T(4,128)(2,1)S(1)}, bf16[2,128,4,64]{3,2,1,0:T(4,128)(2,1)S(1)}, u32[]{:S(2)}, u32[]{:S(2)}) %collective-permute-start.1) | collective-permute-done | bytes 131104 | tf_op jit(solution)/shard_map/ppermute | solution.py:37
  67.9 0.9 pad_maximum_fusion.3
  68.9 2.6 %collective-permute-start.2 = (bf16[2,2,72,64]{3,2,1,0:T(8,128)(2,1)S(1)}, bf16[2,2,72,64]{3,2,1,0:T(8,128)(2,1)S(1)}, u32[]{:S(2)}, u32[]{:S(2)}) collective-permute-start(bf16[2,2,72,64]{3,2,1,0:T(8,128)(2,1)S(1)} %get-tuple-element.8), channel_id=1, source_target_pairs={{0,16},{16,32},{32,48},{48,64},{64,80},{80,96},{96,112},{1,17},{17... | collective-permute-start | bytes 110600 | tf_op jit(solution)/shard_map/ppermute | solution.py:35
  71.5 1.3 %collective-permute-start.3 = (bf16[2,2,72,64]{3,2,1,0:T(8,128)(2,1)S(1)}, bf16[2,2,72,64]{3,2,1,0:T(8,128)(2,1)S(1)}, u32[]{:S(2)}, u32[]{:S(2)}) collective-permute-start(bf16[2,2,72,64]{3,2,1,0:T(8,128)(2,1)S(1)} %get-tuple-element.9), channel_id=1, source_target_pairs={{16,0},{32,16},{48,32},{64,48},{80,64},{96,80},{112,96},{17,1},{33... | collective-permute-start | bytes 110600 | tf_op jit(solution)/shard_map/ppermute | solution.py:37
  72.8 0.2 collective-permute-done.2
  73.0 3.8 %collective-permute-done.3 = bf16[2,2,72,64]{3,2,1,0:T(8,128)(2,1)S(1)} collective-permute-done((bf16[2,2,72,64]{3,2,1,0:T(8,128)(2,1)S(1)}, bf16[2,2,72,64]{3,2,1,0:T(8,128)(2,1)S(1)}, u32[]{:S(2)}, u32[]{:S(2)}) %collective-permute-start.3) | collective-permute-done | bytes 36896 | tf_op jit(solution)/shard_map/ppermute | solution.py:37
  76.8 0.0 copy-done
  76.8 5.1 %pad_maximum_fusion.x_ref = bf16[2,132,72,64]{3,2,1,0:T(8,128)(2,1)S(1)} fusion(bf16[2,2,72,64]{3,2,1,0:T(8,128)(2,1)S(1)} %collective-permute-done.3, bf16[2,128,4,64]{3,2,1,0:T(4,128)(2,1)S(1)} %collective-permute-done.1, bf16[2,128,64,64]{3,2,1,0:T(8,128)(2,1)S(1)} %bitcast.13, bf16[2,128,4,64]{3,2,1,0:T(4,128)(2,1)S(1)} %collective-permute-done, ...), kind=kLoop, calls=%fused_computation | loop fusion | flops 12165120 | bytes 4866048 | tf_op jit(solution)/shard_map/concatenate | solution.py:33
  81.9 0.1 broadcast_in_dim.22.cm_ref
  82.0 41.0 %shard_map.37 = f32[2,128,64,256]{3,2,1,0:T(8,128)} custom-call(bf16[2,132,72,64]{3,2,1,0:T(8,128)(2,1)S(1)} %pad_maximum_fusion.x_ref, bf16[64,256]{1,0:T(8,128)(2,1)S(1)} %fusion.3.kb_ref, bf16[256,256]{1,0:T(8,128)(2,1)S(1)} %multiply_convert_fusion.g3_ref, f32[1,256]{1,0:T(1,128)S(1)} %bitcast.8, f32[1,256]{1,0:T(1,128)S(1)} %bitcast.9, ...), custom_call_target="tpu_custom_call" | custom-call | flops 5775556608 | bytes 19210240 | tf_op jit(solution)/shard_map/pallas_call | solution.py:128
  (6 shorter events, 0.1 us)
Async XLA Ops:
  0.0 15.5 %copy-start.2 = (f32[256]{0:T(256)S(1)}, f32[256]{0:T(256)}, u32[]{:S(2)}) copy-start(f32[256]{0:T(256)} %param.4) | copy-start | bytes 3076
  0.0 16.3 %copy-start.1 = (f32[256]{0:T(256)S(1)}, f32[256]{0:T(256)}, u32[]{:S(2)}) copy-start(f32[256]{0:T(256)} %param.5) | copy-start | bytes 3076
  6.2 37.7 %all-to-all-start = ((bf16[4,2,128,1024]{2,1,0,3:T(2,128)(2,1)}), bf16[4,2,128,1024]{2,1,0,3:T(2,128)(2,1)S(1)}, u32[]{:S(2)}, u32[]{:S(2)}) async-start(bf16[4,2,128,1024]{2,1,0,3:T(2,128)(2,1)} %copy.10), calls=%async_computation | async-start | bytes 4194304 | tf_op jit(solution)/shard_map/all_to_all | solution.py:109
  53.6 8.4 %collective-permute-start = (bf16[2,128,4,64]{3,2,1,0:T(4,128)(2,1)S(1)}, bf16[2,128,4,64]{3,2,1,0:T(4,128)(2,1)S(1)}, u32[]{:S(2)}, u32[]{:S(2)}) collective-permute-start(bf16[2,128,4,64]{3,2,1,0:T(4,128)(2,1)S(1)} %get-tuple-element.10), channel_id=1, source_target_pairs={{0,1},{1,2},{2,3},{3,4},{4,5},{5,6},{6,7},{7,8},{8,9},{9,10},{10,1... | collective-permute-start | bytes 393224 | tf_op jit(solution)/shard_map/ppermute | solution.py:35
  58.7 9.2 %collective-permute-start.1 = (bf16[2,128,4,64]{3,2,1,0:T(4,128)(2,1)S(1)}, bf16[2,128,4,64]{3,2,1,0:T(4,128)(2,1)S(1)}, u32[]{:S(2)}, u32[]{:S(2)}) collective-permute-start(bf16[2,128,4,64]{3,2,1,0:T(4,128)(2,1)S(1)} %get-tuple-element.11), channel_id=1, source_target_pairs={{1,0},{2,1},{3,2},{4,3},{5,4},{6,5},{7,6},{8,7},{9,8},{10,9},{11,1... | collective-permute-start | bytes 393224 | tf_op jit(solution)/shard_map/ppermute | solution.py:37
  60.7 16.1 %copy-start = (bf16[64,2,128,64]{0,3,2,1:T(8,128)(2,1)S(1)}, bf16[64,2,128,64]{0,3,2,1:T(8,128)(2,1)}, u32[]{:S(2)}) copy-start(bf16[64,2,128,64]{0,3,2,1:T(8,128)(2,1)} %copy.13) | copy-start | bytes 6291460
  68.9 4.2 %collective-permute-start.2 = (bf16[2,2,72,64]{3,2,1,0:T(8,128)(2,1)S(1)}, bf16[2,2,72,64]{3,2,1,0:T(8,128)(2,1)S(1)}, u32[]{:S(2)}, u32[]{:S(2)}) collective-permute-start(bf16[2,2,72,64]{3,2,1,0:T(8,128)(2,1)S(1)} %get-tuple-element.8), channel_id=1, source_target_pairs={{0,16},{16,32},{32,48},{48,64},{64,80},{80,96},{96,112},{1,17},{17... | collective-permute-start | bytes 110600 | tf_op jit(solution)/shard_map/ppermute | solution.py:35
  71.5 5.3 %collective-permute-start.3 = (bf16[2,2,72,64]{3,2,1,0:T(8,128)(2,1)S(1)}, bf16[2,2,72,64]{3,2,1,0:T(8,128)(2,1)S(1)}, u32[]{:S(2)}, u32[]{:S(2)}) collective-permute-start(bf16[2,2,72,64]{3,2,1,0:T(8,128)(2,1)S(1)} %get-tuple-element.9), channel_id=1, source_target_pairs={{16,0},{32,16},{48,32},{64,48},{80,64},{96,80},{112,96},{17,1},{33... | collective-permute-start | bytes 110600 | tf_op jit(solution)/shard_map/ppermute | solution.py:37

commit v19 on v17

--- a/solution.py
+++ b/solution.py
@@ -109,8 +109,16 @@
     x = lax.all_to_all(images, "gy", split_axis=3, concat_axis=0, tiled=True)
     e, sl, h, w = x.shape
     hp, wp = h + 2 * RH, w + 2 * CH
-    x = pin(jnp.transpose(x, (1, 2, 3, 0)))
-    x = pin(halo(x, "gy", 2, CH))
+    ny = lax.axis_size("gy")
+    dense = Layout((3, 1, 0, 2))
+    head = with_layout_constraint(x[..., :CH], dense)
+    tail = with_layout_constraint(x[..., w - CH:], dense)
+    left = lax.ppermute(tail, "gy", [(i, i + 1) for i in range(ny - 1)])
+    right = lax.ppermute(head, "gy", [(i + 1, i) for i in range(ny - 1)])
+    x = jnp.concatenate([pin(jnp.transpose(left, (1, 2, 3, 0))),
+                         pin(jnp.transpose(x, (1, 2, 3, 0))),
+                         pin(jnp.transpose(right, (1, 2, 3, 0)))], axis=2)
+    x = pin(x)
     x = pin(halo(x, "gx", 1, RH))
     r = kernel.shape[1]
 

time: 121 us -> 116 us (0.959)
  the two profiles are of different devices: /device:TPU:1 before, /device:TPU:42 now
where the time goes in v19:
time: 116 us; the launch traced here: 115 us
  Pallas kernels  38.9 us (34%)
  waiting for transfers between devices  33.6 us (29%)
  starting transfers between devices  20.7 us (18%)
  local copies, waits for them, and re-layouts  15.1 us (13%)
  other arithmetic  6.25 us (5%)
    pallas_call x1, Pallas kernels, per_device(): pl.pallas_call(functools.partial(fit_kernel, wp), out_shape=jax.ShapeDtyp...  38.9 us
    all_to_all x1, waiting for transfers between devices, per_device(): x = lax.all_to_all(images, 'gy', split_axis=3, concat_axis=0, tiled=True)  26.8 us
    all_to_all x1, starting transfers between devices, per_device(): x = lax.all_to_all(images, 'gy', split_axis=3, concat_axis=0, tiled=True)  7.35 us
    transpose x1, local copies, waits for them, and re-layouts, per_device(): jnp.transpose(x, (1, 2, 3, 0))  6.41 us
    unnamed x7, local copies, waits for them, and re-layouts  6.19 us
    ppermute x1, starting transfers between devices, per_device(): right = lax.ppermute(head, 'gy', [(i + 1, i) for i in range(ny - 1)])  5.62 us
    concatenate x1, other arithmetic, halo(): jnp.concatenate([lax.ppermute(tail, axis, [(i, i + 1) for i in range(coun...  5.07 us
    ppermute x1, waiting for transfers between devices, halo(): lax.ppermute(head, axis, [(i + 1, i) for i in range(count - 1)])  4.75 us
  transfers between devices with their start and end apart: 5, of which 4 were waited for; matrix products, arithmetic and copies ran while one was open for 6% of the time, Pallas kernels for 0%

profile of v19, /device:TPU:42, one launch (start us, length us, event | category | flops | bytes accessed | tf_op | source)
XLA Modules:
  0.0 115.2 jit_solution(5401568441181830043)
XLA Ops:
  0.0 0.0 copy-start.2
  0.0 0.0 copy-start.1
  0.0 6.2 %copy.15 = bf16[4,2,128,1024]{2,1,0,3:T(2,128)(2,1)} copy(bf16[4,2,128,1024]{3,2,1,0:T(8,128)(2,1)} %param.3) | data formatting | bytes 4194304 | tf_op args[0]
  6.2 7.3 %all-to-all-start = ((bf16[4,2,128,1024]{2,1,0,3:T(2,128)(2,1)}), bf16[4,2,128,1024]{2,1,0,3:T(2,128)(2,1)S(1)}, u32[]{:S(2)}, u32[]{:S(2)}) async-start(bf16[4,2,128,1024]{2,1,0,3:T(2,128)(2,1)} %copy.15), calls=%async_computation | async-start | bytes 4194304 | tf_op jit(solution)/shard_map/all_to_all | solution.py:109
  13.5 0.0 copy-done.2
  13.5 0.1 multiply_reduce_fusion
  13.7 0.5 fusion.8
  14.2 0.1 copy.21
  14.3 0.0 copy-done.1
  14.4 26.8 %all-to-all-done = bf16[4,2,128,1024]{2,1,0,3:T(2,128)(2,1)S(1)} async-done(((bf16[4,2,128,1024]{2,1,0,3:T(2,128)(2,1)}), bf16[4,2,128,1024]{2,1,0,3:T(2,128)(2,1)S(1)}, u32[]{:S(2)}, u32[]{:S(2)}) %all-to-all-start) | async-done | bytes 2097184 | tf_op jit(solution)/shard_map/all_to_all | solution.py:109
  41.2 0.3 copy.16
  41.4 1.6 %copy.17 = bf16[16,4,2,128,64]{3,1,0,2,4:T(4,128)(2,1)S(1)} copy(bf16[16,4,2,128,64]{3,4,0,2,1:T(8,128)(2,1)S(1)} %bitcast.16) | data formatting | bytes 4194304 | tf_op jit(solution)/shard_map/all_to_all | solution.py:109
  43.1 0.2 copy.18
  43.3 0.2 copy.20
  43.5 5.6 %collective-permute-start.1 = (bf16[64,2,128,4]{0,3,2,1:T(4,128)(2,1)S(1)}, bf16[64,2,128,4]{0,3,2,1:T(4,128)(2,1)S(1)}, u32[]{:S(2)}, u32[]{:S(2)}) collective-permute-start(bf16[64,2,128,4]{0,3,2,1:T(4,128)(2,1)S(1)} %copy.20), channel_id=1, source_target_pairs={{1,0},{2,1},{3,2},{4,3},{5,4},{6,5},{7,6},{8,7},{9,8},{10,9},{11,1... | collective-permute-start | bytes 393224 | tf_op jit(solution)/shard_map/ppermute | solution.py:117
  49.1 1.9 %collective-permute-start = (bf16[64,2,128,4]{0,3,2,1:T(4,128)(2,1)S(1)}, bf16[64,2,128,4]{0,3,2,1:T(4,128)(2,1)S(1)}, u32[]{:S(2)}, u32[]{:S(2)}) collective-permute-start(bf16[64,2,128,4]{0,3,2,1:T(4,128)(2,1)S(1)} %copy.18), channel_id=1, source_target_pairs={{0,1},{1,2},{2,3},{3,4},{4,5},{5,6},{6,7},{7,8},{8,9},{9,10},{10,1... | collective-permute-start | bytes 393224 | tf_op jit(solution)/shard_map/ppermute | solution.py:116
  51.1 0.1 fusion.3.kb_ref
  51.2 6.4 %copy.19 = bf16[2,128,64,64]{3,2,1,0:T(8,128)(2,1)} copy(bf16[2,128,64,64]{1,3,0,2:T(8,128)(2,1)S(1)} %bitcast.15) | data formatting | bytes 4194304 | tf_op jit(solution)/shard_map/transpose | solution.py:119
  57.6 0.0 copy-start
  57.6 0.0 collective-permute-done.1
  57.6 1.6 %collective-permute-done = bf16[64,2,128,4]{0,3,2,1:T(4,128)(2,1)S(1)} collective-permute-done((bf16[64,2,128,4]{0,3,2,1:T(4,128)(2,1)S(1)}, bf16[64,2,128,4]{0,3,2,1:T(4,128)(2,1)S(1)}, u32[]{:S(2)}, u32[]{:S(2)}) %collective-permute-start) | collective-permute-done | bytes 131104 | tf_op jit(solution)/shard_map/ppermute | solution.py:116
  59.2 0.9 pad_maximum_fusion.3
  60.2 3.8 %collective-permute-start.2 = (bf16[2,2,72,64]{3,2,1,0:T(8,128)(2,1)S(1)}, bf16[2,2,72,64]{3,2,1,0:T(8,128)(2,1)S(1)}, u32[]{:S(2)}, u32[]{:S(2)}) collective-permute-start(bf16[2,2,72,64]{3,2,1,0:T(8,128)(2,1)S(1)} %get-tuple-element.8), channel_id=1, source_target_pairs={{0,16},{16,32},{32,48},{48,64},{64,80},{80,96},{96,112},{1,17},{17... | collective-permute-start | bytes 110600 | tf_op jit(solution)/shard_map/ppermute | solution.py:35
  64.0 2.0 %collective-permute-start.3 = (bf16[2,2,72,64]{3,2,1,0:T(8,128)(2,1)S(1)}, bf16[2,2,72,64]{3,2,1,0:T(8,128)(2,1)S(1)}, u32[]{:S(2)}, u32[]{:S(2)}) collective-permute-start(bf16[2,2,72,64]{3,2,1,0:T(8,128)(2,1)S(1)} %get-tuple-element.9), channel_id=1, source_target_pairs={{16,0},{32,16},{48,32},{64,48},{80,64},{96,80},{112,96},{17,1},{33... | collective-permute-start | bytes 110600 | tf_op jit(solution)/shard_map/ppermute | solution.py:37
  66.0 0.4 collective-permute-done.2
  66.4 4.7 %collective-permute-done.3 = bf16[2,2,72,64]{3,2,1,0:T(8,128)(2,1)S(1)} collective-permute-done((bf16[2,2,72,64]{3,2,1,0:T(8,128)(2,1)S(1)}, bf16[2,2,72,64]{3,2,1,0:T(8,128)(2,1)S(1)}, u32[]{:S(2)}, u32[]{:S(2)}) %collective-permute-start.3) | collective-permute-done | bytes 36896 | tf_op jit(solution)/shard_map/ppermute | solution.py:37
  71.2 0.0 copy-done
  71.2 5.1 %pad_maximum_fusion.x_ref = bf16[2,132,72,64]{3,2,1,0:T(8,128)(2,1)S(1)} fusion(bf16[2,2,72,64]{3,2,1,0:T(8,128)(2,1)S(1)} %collective-permute-done.3, bf16[2,128,4,64]{3,2,1,0:T(4,128)(2,1)S(1)} %bitcast.18, bf16[2,128,64,64]{3,2,1,0:T(8,128)(2,1)S(1)} %copy-done, bf16[2,128,4,64]{3,2,1,0:T(4,128)(2,1)S(1)} %bitcast.20, ...), kind=kLoop, calls=%fused_computation | loop fusion | flops 12165120 | bytes 4866048 | tf_op jit(solution)/shard_map/concatenate | solution.py:33
  76.2 0.1 broadcast_in_dim.22.cm_ref
  76.3 38.9 %shard_map.37 = f32[2,128,64,256]{3,2,1,0:T(8,128)} custom-call(bf16[2,132,72,64]{3,2,1,0:T(8,128)(2,1)S(1)} %pad_maximum_fusion.x_ref, bf16[64,256]{1,0:T(8,128)(2,1)S(1)} %fusion.3.kb_ref, bf16[256,256]{1,0:T(8,128)(2,1)S(1)} %multiply_convert_fusion.g3_ref, f32[1,256]{1,0:T(1,128)S(1)} %bitcast.11, f32[1,256]{1,0:T(1,128)S(1)} %bitcast.12, ...), custom_call_target="tpu_custom_call" | custom-call | flops 5775556608 | bytes 19210240 | tf_op jit(solution)/shard_map/pallas_call | solution.py:136
  (7 shorter events, 0.1 us)
Async XLA Ops:
  0.0 13.5 %copy-start.2 = (f32[256]{0:T(256)S(1)}, f32[256]{0:T(256)}, u32[]{:S(2)}) copy-start(f32[256]{0:T(256)} %param.4) | copy-start | bytes 3076
  0.0 14.3 %copy-start.1 = (f32[256]{0:T(256)S(1)}, f32[256]{0:T(256)}, u32[]{:S(2)}) copy-start(f32[256]{0:T(256)} %param.5) | copy-start | bytes 3076
  6.2 35.0 %all-to-all-start = ((bf16[4,2,128,1024]{2,1,0,3:T(2,128)(2,1)}), bf16[4,2,128,1024]{2,1,0,3:T(2,128)(2,1)S(1)}, u32[]{:S(2)}, u32[]{:S(2)}) async-start(bf16[4,2,128,1024]{2,1,0,3:T(2,128)(2,1)} %copy.15), calls=%async_computation | async-start | bytes 4194304 | tf_op jit(solution)/shard_map/all_to_all | solution.py:109
  43.5 14.1 %collective-permute-start.1 = (bf16[64,2,128,4]{0,3,2,1:T(4,128)(2,1)S(1)}, bf16[64,2,128,4]{0,3,2,1:T(4,128)(2,1)S(1)}, u32[]{:S(2)}, u32[]{:S(2)}) collective-permute-start(bf16[64,2,128,4]{0,3,2,1:T(4,128)(2,1)S(1)} %copy.20), channel_id=1, source_target_pairs={{1,0},{2,1},{3,2},{4,3},{5,4},{6,5},{7,6},{8,7},{9,8},{10,9},{11,1... | collective-permute-start | bytes 393224 | tf_op jit(solution)/shard_map/ppermute | solution.py:117
  49.1 10.1 %collective-permute-start = (bf16[64,2,128,4]{0,3,2,1:T(4,128)(2,1)S(1)}, bf16[64,2,128,4]{0,3,2,1:T(4,128)(2,1)S(1)}, u32[]{:S(2)}, u32[]{:S(2)}) collective-permute-start(bf16[64,2,128,4]{0,3,2,1:T(4,128)(2,1)S(1)} %copy.18), channel_id=1, source_target_pairs={{0,1},{1,2},{2,3},{3,4},{4,5},{5,6},{6,7},{7,8},{8,9},{9,10},{10,1... | collective-permute-start | bytes 393224 | tf_op jit(solution)/shard_map/ppermute | solution.py:116
  57.6 13.6 %copy-start = (bf16[2,128,64,64]{3,2,1,0:T(8,128)(2,1)S(1)}, bf16[2,128,64,64]{3,2,1,0:T(8,128)(2,1)}, u32[]{:S(2)}) copy-start(bf16[2,128,64,64]{3,2,1,0:T(8,128)(2,1)} %copy.19) | copy-start | bytes 6291460
  60.2 6.2 %collective-permute-start.2 = (bf16[2,2,72,64]{3,2,1,0:T(8,128)(2,1)S(1)}, bf16[2,2,72,64]{3,2,1,0:T(8,128)(2,1)S(1)}, u32[]{:S(2)}, u32[]{:S(2)}) collective-permute-start(bf16[2,2,72,64]{3,2,1,0:T(8,128)(2,1)S(1)} %get-tuple-element.8), channel_id=1, source_target_pairs={{0,16},{16,32},{32,48},{48,64},{64,80},{80,96},{96,112},{1,17},{17... | collective-permute-start | bytes 110600 | tf_op jit(solution)/shard_map/ppermute | solution.py:35
  64.0 7.1 %collective-permute-start.3 = (bf16[2,2,72,64]{3,2,1,0:T(8,128)(2,1)S(1)}, bf16[2,2,72,64]{3,2,1,0:T(8,128)(2,1)S(1)}, u32[]{:S(2)}, u32[]{:S(2)}) collective-permute-start(bf16[2,2,72,64]{3,2,1,0:T(8,128)(2,1)S(1)} %get-tuple-element.9), channel_id=1, source_target_pairs={{16,0},{32,16},{48,32},{64,48},{80,64},{96,80},{112,96},{17,1},{33... | collective-permute-start | bytes 110600 | tf_op jit(solution)/shard_map/ppermute | solution.py:37

commit v20 on v19

--- a/solution.py
+++ b/solution.py
@@ -115,11 +115,15 @@
     tail = with_layout_constraint(x[..., w - CH:], dense)
     left = lax.ppermute(tail, "gy", [(i, i + 1) for i in range(ny - 1)])
     right = lax.ppermute(head, "gy", [(i + 1, i) for i in range(ny - 1)])
-    x = jnp.concatenate([pin(jnp.transpose(left, (1, 2, 3, 0))),
-                         pin(jnp.transpose(x, (1, 2, 3, 0))),
-                         pin(jnp.transpose(right, (1, 2, 3, 0)))], axis=2)
-    x = pin(x)
-    x = pin(halo(x, "gx", 1, RH))
+    nx = lax.axis_size("gx")
+    edge = lambda a, b: jnp.concatenate([left[:, :, a:b], x[:, :, a:b], right[:, :, a:b]], axis=3)
+    top = lax.ppermute(edge(h - RH, h), "gx", [(i, i + 1) for i in range(nx - 1)])
+    bot = lax.ppermute(edge(0, RH), "gx", [(i + 1, i) for i in range(nx - 1)])
+    em = lambda a: pin(jnp.transpose(a, (1, 2, 3, 0)))
+    centre = jnp.concatenate([pin(jnp.transpose(x[:, k:k + 1], (1, 2, 3, 0)))
+                              for k in range(sl)], axis=0)
+    mid = jnp.concatenate([em(left), centre, em(right)], axis=2)
+    x = pin(jnp.concatenate([em(top), mid, em(bot)], axis=1))
     r = kernel.shape[1]
 
     gi = lax.axis_index("gx")

time: 116 us -> 125 us (1.078)
  the two profiles are of different devices: /device:TPU:42 before, /device:TPU:1 now
where the time goes in v20:
time: 125 us; the launch traced here: 124 us
  Pallas kernels  39 us (31%)
  local copies, waits for them, and re-layouts  27.8 us (22%)
  waiting for transfers between devices  27.5 us (22%)
  starting transfers between devices  21.8 us (17%)
  other arithmetic  6.98 us (6%)
    pallas_call x1, Pallas kernels, per_device(): pl.pallas_call(functools.partial(fit_kernel, wp), out_shape=jax.ShapeDtyp...  39 us
    all_to_all x1, waiting for transfers between devices, per_device(): x = lax.all_to_all(images, 'gy', split_axis=3, concat_axis=0, tiled=True)  27.5 us
    unnamed x13, local copies, waits for them, and re-layouts  22.5 us
    all_to_all x1, starting transfers between devices, per_device(): x = lax.all_to_all(images, 'gy', split_axis=3, concat_axis=0, tiled=True)  9.3 us
    concatenate x1, other arithmetic, per_device(): x = pin(jnp.concatenate([em(top), mid, em(bot)], axis=1))  6.05 us
    ppermute x1, starting transfers between devices, per_device(): left = lax.ppermute(tail, 'gy', [(i, i + 1) for i in range(ny - 1)])  4.27 us
    ppermute x1, starting transfers between devices, per_device(): lax.ppermute(edge(h - RH, h), 'gx', [(i, i + 1) for i in range(nx - 1)])  4.16 us
    slice x1, local copies, waits for them, and re-layouts, per_device(): x[:, :, a:b]  2.89 us
  transfers between devices with their start and end apart: 5, of which 1 were waited for; matrix products, arithmetic and copies ran while one was open for 18% of the time, Pallas kernels for 0%

profile of v20, /device:TPU:1, one launch (start us, length us, event | category | flops | bytes accessed | tf_op | source)
XLA Modules:
  0.0 123.8 jit_solution(15683638101952183994)
XLA Ops:
  0.0 0.0 copy-start.3
  0.0 0.0 copy-start.2
  0.0 6.2 %copy.21 = bf16[4,2,128,1024]{2,1,0,3:T(2,128)(2,1)} copy(bf16[4,2,128,1024]{3,2,1,0:T(8,128)(2,1)} %param.3) | data formatting | bytes 4194304 | tf_op args[0]
  6.2 9.3 %all-to-all-start = ((bf16[4,2,128,1024]{2,1,0,3:T(2,128)(2,1)}), bf16[4,2,128,1024]{2,1,0,3:T(2,128)(2,1)S(1)}, u32[]{:S(2)}, u32[]{:S(2)}) async-start(bf16[4,2,128,1024]{2,1,0,3:T(2,128)(2,1)} %copy.21), calls=%async_computation | async-start | bytes 4194304 | tf_op jit(solution)/shard_map/all_to_all | solution.py:109
  15.5 0.0 copy-done.3
  15.5 0.1 multiply_reduce_fusion
  15.6 0.5 fusion.12
  16.1 0.1 copy.32
  16.3 0.0 copy-done.2
  16.3 0.1 fusion.3.kb_ref
  16.4 27.5 %all-to-all-done = bf16[4,2,128,1024]{2,1,0,3:T(2,128)(2,1)S(1)} async-done(((bf16[4,2,128,1024]{2,1,0,3:T(2,128)(2,1)}), bf16[4,2,128,1024]{2,1,0,3:T(2,128)(2,1)S(1)}, u32[]{:S(2)}, u32[]{:S(2)}) %all-to-all-start) | async-done | bytes 2097184 | tf_op jit(solution)/shard_map/all_to_all | solution.py:109
  43.9 0.3 copy.22
  44.2 0.2 copy.23
  44.4 0.1 fusion.9
  44.5 0.2 copy.28
  44.7 2.8 %collective-permute-start.1 = (bf16[64,2,128,4]{0,3,2,1:T(4,128)(2,1)S(1)}, bf16[64,2,128,4]{0,3,2,1:T(4,128)(2,1)S(1)}, u32[]{:S(2)}, u32[]{:S(2)}) collective-permute-start(bf16[64,2,128,4]{0,3,2,1:T(4,128)(2,1)S(1)} %copy.28), channel_id=1, source_target_pairs={{1,0},{2,1},{3,2},{4,3},{5,4},{6,5},{7,6},{8,7},{9,8},{10,9},{11,1... | collective-permute-start | bytes 393224 | tf_op jit(solution)/shard_map/ppermute | solution.py:117
  47.5 2.9 %fusion.7 = (bf16[64,2,2,64]{2,3,1,0:T(8,128)(2,1)}, bf16[64,2,2,64]{2,3,1,0:T(8,128)(2,1)}) fusion(bf16[64,2,128,64]{2,3,1,0:T(8,128)(2,1)S(1)} %bitcast.17), kind=kLoop, calls=%fused_computation.18 | loop fusion | bytes 131072 | tf_op jit(solution)/shard_map/slice | solution.py:119
  50.4 0.2 copy.25
  50.6 4.3 %collective-permute-start = (bf16[64,2,128,4]{0,3,2,1:T(4,128)(2,1)S(1)}, bf16[64,2,128,4]{0,3,2,1:T(4,128)(2,1)S(1)}, u32[]{:S(2)}, u32[]{:S(2)}) collective-permute-start(bf16[64,2,128,4]{0,3,2,1:T(4,128)(2,1)S(1)} %copy.25), channel_id=1, source_target_pairs={{0,1},{1,2},{2,3},{3,4},{4,5},{5,6},{6,7},{7,8},{8,9},{9,10},{10,1... | collective-permute-start | bytes 393224 | tf_op jit(solution)/shard_map/ppermute | solution.py:116
  54.9 3.6 %copy.34 = bf16[64,2,2,64]{0,3,2,1:T(8,128)(2,1)S(1)} copy(bf16[64,2,2,64]{2,3,1,0:T(8,128)(2,1)} %get-tuple-element.8) | data formatting | bytes 65536
  58.5 3.6 %copy.38 = bf16[64,2,2,64]{0,3,2,1:T(8,128)(2,1)S(1)} copy(bf16[64,2,2,64]{2,3,1,0:T(8,128)(2,1)} %get-tuple-element.9) | data formatting | bytes 65536
  62.1 0.0 collective-permute-done.1
  62.1 0.0 copy-start
  62.2 0.0 collective-permute-done
  62.2 0.0 copy-start.1
  62.2 1.3 %collective-permute-start.3 = (bf16[64,2,2,72]{0,3,2,1:T(8,128)(2,1)S(1)}, bf16[64,2,2,72]{0,3,2,1:T(8,128)(2,1)S(1)}, u32[]{:S(2)}, u32[]{:S(2)}) collective-permute-start(bf16[64,2,2,72]{0,3,2,1:T(8,128)(2,1)S(1)} %pad_maximum_fusion.2), channel_id=1, source_target_pairs={{16,0},{32,16},{48,32},{64,48},{80,64},{96,80},{112,96},{17,1},{33... | collective-permute-start | bytes 110600 | tf_op jit(solution)/shard_map/ppermute | solution.py:121
  63.5 0.7 pad_maximum_fusion.1
  64.2 0.0 copy-done
  64.2 0.0 copy-done.1
  64.2 4.2 %collective-permute-start.2 = (bf16[64,2,2,72]{0,3,2,1:T(8,128)(2,1)}, bf16[64,2,2,72]{0,3,2,1:T(8,128)(2,1)S(1)}, u32[]{:S(2)}, u32[]{:S(2)}) collective-permute-start(bf16[64,2,2,72]{0,3,2,1:T(8,128)(2,1)} %pad_maximum_fusion.1), channel_id=1, source_target_pairs={{0,16},{16,32},{32,48},{48,64},{64,80},{80,96},{96,112},{1,17},{17... | collective-permute-start | bytes 110600 | tf_op jit(solution)/shard_map/ppermute | solution.py:120
  68.4 1.2 fusion.8
  69.6 4.7 %copy.36 = bf16[64,1,128,64]{0,3,2,1:T(8,128)(2,1)S(1)} copy(bf16[64,1,128,64]{2,3,1,0:T(8,128)(2,1)} %get-tuple-element.10) | data formatting | bytes 2097152
  74.3 4.4 %copy.37 = bf16[64,1,128,64]{0,3,2,1:T(8,128)(2,1)} copy(bf16[64,1,128,64]{2,3,1,0:T(8,128)(2,1)S(1)} %get-tuple-element.11) | data formatting | bytes 2097152
  78.7 0.0 collective-permute-done.3
  78.7 0.0 collective-permute-done.2
  78.7 6.0 %pad_maximum_fusion.x_ref = bf16[2,132,72,64]{3,2,1,0:T(8,128)(2,1)S(1)} fusion(bf16[2,2,72,64]{3,2,1,0:T(8,128)(2,1)S(1)} %bitcast.24, bf16[2,128,4,64]{3,2,1,0:T(4,128)(2,1)} %bitcast.22, bf16[1,128,64,64]{3,2,1,0:T(8,128)(2,1)} %bitcast.20, bf16[1,128,64,64]{3,2,1,0:T(8,128)(2,1)S(1)} %bitcast.19, bf16[2,128,4,64]{3,2,1,0:T(4,128)(2,1)} %bitcast.23, ...), kind=kLoop, calls=%fused_computation | loop fusion | flops 14598144 | bytes 4866048 | tf_op jit(solution)/shard_map/concatenate | solution.py:126
  84.7 0.1 broadcast_in_dim.22.cm_ref
  84.8 39.0 %shard_map.37 = f32[2,128,64,256]{3,2,1,0:T(8,128)} custom-call(bf16[2,132,72,64]{3,2,1,0:T(8,128)(2,1)S(1)} %pad_maximum_fusion.x_ref, bf16[64,256]{1,0:T(8,128)(2,1)S(1)} %fusion.3.kb_ref, bf16[256,256]{1,0:T(8,128)(2,1)S(1)} %multiply_convert_fusion.g3_ref, f32[1,256]{1,0:T(1,128)S(1)} %bitcast.13, f32[1,256]{1,0:T(1,128)S(1)} %bitcast.14, ...), custom_call_target="tpu_custom_call" | custom-call | flops 5775556608 | bytes 19210240 | tf_op jit(solution)/shard_map/pallas_call | solution.py:140
  (9 shorter events, 0.1 us)
Async XLA Ops:
  0.0 15.5 %copy-start.3 = (f32[256]{0:T(256)S(1)}, f32[256]{0:T(256)}, u32[]{:S(2)}) copy-start(f32[256]{0:T(256)} %param.4) | copy-start | bytes 3076
  0.0 16.3 %copy-start.2 = (f32[256]{0:T(256)S(1)}, f32[256]{0:T(256)}, u32[]{:S(2)}) copy-start(f32[256]{0:T(256)} %param.5) | copy-start | bytes 3076
  6.2 37.7 %all-to-all-start = ((bf16[4,2,128,1024]{2,1,0,3:T(2,128)(2,1)}), bf16[4,2,128,1024]{2,1,0,3:T(2,128)(2,1)S(1)}, u32[]{:S(2)}, u32[]{:S(2)}) async-start(bf16[4,2,128,1024]{2,1,0,3:T(2,128)(2,1)} %copy.21), calls=%async_computation | async-start | bytes 4194304 | tf_op jit(solution)/shard_map/all_to_all | solution.py:109
  44.7 17.4 %collective-permute-start.1 = (bf16[64,2,128,4]{0,3,2,1:T(4,128)(2,1)S(1)}, bf16[64,2,128,4]{0,3,2,1:T(4,128)(2,1)S(1)}, u32[]{:S(2)}, u32[]{:S(2)}) collective-permute-start(bf16[64,2,128,4]{0,3,2,1:T(4,128)(2,1)S(1)} %copy.28), channel_id=1, source_target_pairs={{1,0},{2,1},{3,2},{4,3},{5,4},{6,5},{7,6},{8,7},{9,8},{10,9},{11,1... | collective-permute-start | bytes 393224 | tf_op jit(solution)/shard_map/ppermute | solution.py:117
  50.6 11.5 %collective-permute-start = (bf16[64,2,128,4]{0,3,2,1:T(4,128)(2,1)S(1)}, bf16[64,2,128,4]{0,3,2,1:T(4,128)(2,1)S(1)}, u32[]{:S(2)}, u32[]{:S(2)}) collective-permute-start(bf16[64,2,128,4]{0,3,2,1:T(4,128)(2,1)S(1)} %copy.25), channel_id=1, source_target_pairs={{0,1},{1,2},{2,3},{3,4},{4,5},{5,6},{6,7},{7,8},{8,9},{9,10},{10,1... | collective-permute-start | bytes 393224 | tf_op jit(solution)/shard_map/ppermute | solution.py:116
  62.1 2.1 %copy-start = (bf16[64,2,128,4]{0,3,2,1:T(4,128)(2,1)}, bf16[64,2,128,4]{0,3,2,1:T(4,128)(2,1)S(1)}, u32[]{:S(2)}) copy-start(bf16[64,2,128,4]{0,3,2,1:T(4,128)(2,1)S(1)} %collective-permute-done.1) | copy-start | bytes 393220
  62.2 2.0 %copy-start.1 = (bf16[64,2,128,4]{0,3,2,1:T(4,128)(2,1)}, bf16[64,2,128,4]{0,3,2,1:T(4,128)(2,1)S(1)}, u32[]{:S(2)}) copy-start(bf16[64,2,128,4]{0,3,2,1:T(4,128)(2,1)S(1)} %collective-permute-done) | copy-start | bytes 393220
  62.2 16.4 %collective-permute-start.3 = (bf16[64,2,2,72]{0,3,2,1:T(8,128)(2,1)S(1)}, bf16[64,2,2,72]{0,3,2,1:T(8,128)(2,1)S(1)}, u32[]{:S(2)}, u32[]{:S(2)}) collective-permute-start(bf16[64,2,2,72]{0,3,2,1:T(8,128)(2,1)S(1)} %pad_maximum_fusion.2), channel_id=1, source_target_pairs={{16,0},{32,16},{48,32},{64,48},{80,64},{96,80},{112,96},{17,1},{33... | collective-permute-start | bytes 110600 | tf_op jit(solution)/shard_map/ppermute | solution.py:121
  64.2 14.5 %collective-permute-start.2 = (bf16[64,2,2,72]{0,3,2,1:T(8,128)(2,1)}, bf16[64,2,2,72]{0,3,2,1:T(8,128)(2,1)S(1)}, u32[]{:S(2)}, u32[]{:S(2)}) collective-permute-start(bf16[64,2,2,72]{0,3,2,1:T(8,128)(2,1)} %pad_maximum_fusion.1), channel_id=1, source_target_pairs={{0,16},{16,32},{32,48},{48,64},{64,80},{80,96},{96,112},{1,17},{17... | collective-permute-start | bytes 110600 | tf_op jit(solution)/shard_map/ppermute | solution.py:120

commit v21 on v19

--- a/solution.py
+++ b/solution.py
@@ -60,7 +60,7 @@
     inner = (rows - 2) * wp
     f3_ref[pl.ds(2 * wp, inner), :] = f0[wp:(rows - 1) * wp].astype(jnp.bfloat16)
 
-    def update(src_ref, q):
+    def update(src_ref, q, mo):
         o = pl.multiple_of(q * wp, 8)
         c = src_ref[pl.ds(o, wp), :]
         up = src_ref[pl.ds(o - wp, wp), :]
@@ -68,14 +68,14 @@
         lf = pltpu.roll(c, 1, 0)
         rt = pltpu.roll(c, wp - 1, 0)
         nb = (up + dn) + (lf + rt)
-        v = (alpha * c + beta * nb) + (b_ref[pl.ds(o, wp), :] - m_ref[pl.ds(o - wp, wp), :])
+        v = (alpha * c + beta * nb) + (b_ref[pl.ds(o, wp), :] - m_ref[pl.ds(o - mo * wp, wp), :])
         return jnp.maximum(v, 0.0)
 
     m_ref[...] = jnp.dot(f3_ref[pl.ds(2 * wp, inner), :], g3_ref[...],
                          preferred_element_type=jnp.float32)
 
     def body1(q, carry):
-        f1 = update(f0_ref, q) * cm
+        f1 = update(f0_ref, q, 1) * cm
         f1_ref[pl.ds(pl.multiple_of(q * wp, 8), wp), :] = f1
         return carry
 
@@ -83,12 +83,13 @@
     for q in (1, rows - 2):
         f1_ref[pl.ds(q * wp, wp), :] = f1_ref[pl.ds(q * wp, wp), :] * rm_ref[t * TR + q]
 
-    f3_ref[pl.ds(2 * wp, inner), :] = f1_ref[pl.ds(wp, inner), :].astype(jnp.bfloat16)
-    m_ref[...] = jnp.dot(f3_ref[pl.ds(2 * wp, inner), :], g3_ref[...],
-                         preferred_element_type=jnp.float32)
+    inner2 = (rows - 4) * wp
+    f3_ref[pl.ds(2 * wp, inner2), :] = f1_ref[pl.ds(2 * wp, inner2), :].astype(jnp.bfloat16)
+    m_ref[pl.ds(0, inner2), :] = jnp.dot(f3_ref[pl.ds(2 * wp, inner2), :], g3_ref[...],
+                                         preferred_element_type=jnp.float32)
 
     def body2(q, carry):
-        f2 = update(f1_ref, q)
+        f2 = update(f1_ref, q, 2)
         f2 = pltpu.roll(f2, wp - CH, 0)
         o_ref[0, q - RH] = f2[: wp - 2 * CH]
         return carry

time: 116 us -> 116 us (level)
  the two profiles are of different devices: /device:TPU:42 before, /device:TPU:40 now
where the time goes in v21:
time: 116 us; the launch traced here: 115 us
  Pallas kernels  39.1 us (34%)
  waiting for transfers between devices  33.6 us (29%)
  starting transfers between devices  20.7 us (18%)
  local copies, waits for them, and re-layouts  15.1 us (13%)
  other arithmetic  6.25 us (5%)
    pallas_call x1, Pallas kernels, per_device(): pl.pallas_call(functools.partial(fit_kernel, wp), out_shape=jax.ShapeDtyp...  39.1 us
    all_to_all x1, waiting for transfers between devices, per_device(): x = lax.all_to_all(images, 'gy', split_axis=3, concat_axis=0, tiled=True)  26.8 us
    all_to_all x1, starting transfers between devices, per_device(): x = lax.all_to_all(images, 'gy', split_axis=3, concat_axis=0, tiled=True)  7.35 us
    transpose x1, local copies, waits for them, and re-layouts, per_device(): jnp.transpose(x, (1, 2, 3, 0))  6.41 us
    unnamed x7, local copies, waits for them, and re-layouts  6.19 us
    ppermute x1, starting transfers between devices, per_device(): right = lax.ppermute(head, 'gy', [(i + 1, i) for i in range(ny - 1)])  5.62 us
    concatenate x1, other arithmetic, halo(): jnp.concatenate([lax.ppermute(tail, axis, [(i, i + 1) for i in range(coun...  5.07 us
    ppermute x1, waiting for transfers between devices, halo(): lax.ppermute(head, axis, [(i + 1, i) for i in range(count - 1)])  4.75 us
  transfers between devices with their start and end apart: 5, of which 4 were waited for; matrix products, arithmetic and copies ran while one was open for 6% of the time, Pallas kernels for 0%

profile of v21, /device:TPU:40, one launch (start us, length us, event | category | flops | bytes accessed | tf_op | source)
XLA Modules:
  0.0 115.4 jit_solution(8844382118114836068)
XLA Ops:
  0.0 0.0 copy-start.2
  0.0 0.0 copy-start.1
  0.0 6.2 %copy.15 = bf16[4,2,128,1024]{2,1,0,3:T(2,128)(2,1)} copy(bf16[4,2,128,1024]{3,2,1,0:T(8,128)(2,1)} %param.3) | data formatting | bytes 4194304 | tf_op args[0]
  6.2 7.3 %all-to-all-start = ((bf16[4,2,128,1024]{2,1,0,3:T(2,128)(2,1)}), bf16[4,2,128,1024]{2,1,0,3:T(2,128)(2,1)S(1)}, u32[]{:S(2)}, u32[]{:S(2)}) async-start(bf16[4,2,128,1024]{2,1,0,3:T(2,128)(2,1)} %copy.15), calls=%async_computation | async-start | bytes 4194304 | tf_op jit(solution)/shard_map/all_to_all | solution.py:110
  13.5 0.0 copy-done.2
  13.5 0.1 multiply_reduce_fusion
  13.7 0.5 fusion.8
  14.2 0.1 copy.21
  14.3 0.0 copy-done.1
  14.4 26.8 %all-to-all-done = bf16[4,2,128,1024]{2,1,0,3:T(2,128)(2,1)S(1)} async-done(((bf16[4,2,128,1024]{2,1,0,3:T(2,128)(2,1)}), bf16[4,2,128,1024]{2,1,0,3:T(2,128)(2,1)S(1)}, u32[]{:S(2)}, u32[]{:S(2)}) %all-to-all-start) | async-done | bytes 2097184 | tf_op jit(solution)/shard_map/all_to_all | solution.py:110
  41.2 0.3 copy.16
  41.4 1.6 %copy.17 = bf16[16,4,2,128,64]{3,1,0,2,4:T(4,128)(2,1)S(1)} copy(bf16[16,4,2,128,64]{3,4,0,2,1:T(8,128)(2,1)S(1)} %bitcast.16) | data formatting | bytes 4194304 | tf_op jit(solution)/shard_map/all_to_all | solution.py:110
  43.1 0.2 copy.18
  43.3 0.2 copy.20
  43.5 5.6 %collective-permute-start.1 = (bf16[64,2,128,4]{0,3,2,1:T(4,128)(2,1)S(1)}, bf16[64,2,128,4]{0,3,2,1:T(4,128)(2,1)S(1)}, u32[]{:S(2)}, u32[]{:S(2)}) collective-permute-start(bf16[64,2,128,4]{0,3,2,1:T(4,128)(2,1)S(1)} %copy.20), channel_id=1, source_target_pairs={{1,0},{2,1},{3,2},{4,3},{5,4},{6,5},{7,6},{8,7},{9,8},{10,9},{11,1... | collective-permute-start | bytes 393224 | tf_op jit(solution)/shard_map/ppermute | solution.py:118
  49.1 1.9 %collective-permute-start = (bf16[64,2,128,4]{0,3,2,1:T(4,128)(2,1)S(1)}, bf16[64,2,128,4]{0,3,2,1:T(4,128)(2,1)S(1)}, u32[]{:S(2)}, u32[]{:S(2)}) collective-permute-start(bf16[64,2,128,4]{0,3,2,1:T(4,128)(2,1)S(1)} %copy.18), channel_id=1, source_target_pairs={{0,1},{1,2},{2,3},{3,4},{4,5},{5,6},{6,7},{7,8},{8,9},{9,10},{10,1... | collective-permute-start | bytes 393224 | tf_op jit(solution)/shard_map/ppermute | solution.py:117
  51.1 0.1 fusion.3.kb_ref
  51.2 6.4 %copy.19 = bf16[2,128,64,64]{3,2,1,0:T(8,128)(2,1)} copy(bf16[2,128,64,64]{1,3,0,2:T(8,128)(2,1)S(1)} %bitcast.15) | data formatting | bytes 4194304 | tf_op jit(solution)/shard_map/transpose | solution.py:120
  57.6 0.0 copy-start
  57.6 0.0 collective-permute-done.1
  57.6 1.6 %collective-permute-done = bf16[64,2,128,4]{0,3,2,1:T(4,128)(2,1)S(1)} collective-permute-done((bf16[64,2,128,4]{0,3,2,1:T(4,128)(2,1)S(1)}, bf16[64,2,128,4]{0,3,2,1:T(4,128)(2,1)S(1)}, u32[]{:S(2)}, u32[]{:S(2)}) %collective-permute-start) | collective-permute-done | bytes 131104 | tf_op jit(solution)/shard_map/ppermute | solution.py:117
  59.2 0.9 pad_maximum_fusion.3
  60.2 3.8 %collective-permute-start.2 = (bf16[2,2,72,64]{3,2,1,0:T(8,128)(2,1)S(1)}, bf16[2,2,72,64]{3,2,1,0:T(8,128)(2,1)S(1)}, u32[]{:S(2)}, u32[]{:S(2)}) collective-permute-start(bf16[2,2,72,64]{3,2,1,0:T(8,128)(2,1)S(1)} %get-tuple-element.8), channel_id=1, source_target_pairs={{0,16},{16,32},{32,48},{48,64},{64,80},{80,96},{96,112},{1,17},{17... | collective-permute-start | bytes 110600 | tf_op jit(solution)/shard_map/ppermute | solution.py:35
  64.0 2.0 %collective-permute-start.3 = (bf16[2,2,72,64]{3,2,1,0:T(8,128)(2,1)S(1)}, bf16[2,2,72,64]{3,2,1,0:T(8,128)(2,1)S(1)}, u32[]{:S(2)}, u32[]{:S(2)}) collective-permute-start(bf16[2,2,72,64]{3,2,1,0:T(8,128)(2,1)S(1)} %get-tuple-element.9), channel_id=1, source_target_pairs={{16,0},{32,16},{48,32},{64,48},{80,64},{96,80},{112,96},{17,1},{33... | collective-permute-start | bytes 110600 | tf_op jit(solution)/shard_map/ppermute | solution.py:37
  66.0 0.4 collective-permute-done.2
  66.4 4.7 %collective-permute-done.3 = bf16[2,2,72,64]{3,2,1,0:T(8,128)(2,1)S(1)} collective-permute-done((bf16[2,2,72,64]{3,2,1,0:T(8,128)(2,1)S(1)}, bf16[2,2,72,64]{3,2,1,0:T(8,128)(2,1)S(1)}, u32[]{:S(2)}, u32[]{:S(2)}) %collective-permute-start.3) | collective-permute-done | bytes 36896 | tf_op jit(solution)/shard_map/ppermute | solution.py:37
  71.2 0.0 copy-done
  71.2 5.1 %pad_maximum_fusion.x_ref = bf16[2,132,72,64]{3,2,1,0:T(8,128)(2,1)S(1)} fusion(bf16[2,2,72,64]{3,2,1,0:T(8,128)(2,1)S(1)} %collective-permute-done.3, bf16[2,128,4,64]{3,2,1,0:T(4,128)(2,1)S(1)} %bitcast.18, bf16[2,128,64,64]{3,2,1,0:T(8,128)(2,1)S(1)} %copy-done, bf16[2,128,4,64]{3,2,1,0:T(4,128)(2,1)S(1)} %bitcast.20, ...), kind=kLoop, calls=%fused_computation | loop fusion | flops 12165120 | bytes 4866048 | tf_op jit(solution)/shard_map/concatenate | solution.py:33
  76.2 0.1 broadcast_in_dim.22.cm_ref
  76.3 39.1 %shard_map.37 = f32[2,128,64,256]{3,2,1,0:T(8,128)} custom-call(bf16[2,132,72,64]{3,2,1,0:T(8,128)(2,1)S(1)} %pad_maximum_fusion.x_ref, bf16[64,256]{1,0:T(8,128)(2,1)S(1)} %fusion.3.kb_ref, bf16[256,256]{1,0:T(8,128)(2,1)S(1)} %multiply_convert_fusion.g3_ref, f32[1,256]{1,0:T(1,128)S(1)} %bitcast.11, f32[1,256]{1,0:T(1,128)S(1)} %bitcast.12, ...), custom_call_target="tpu_custom_call" | custom-call | flops 5775556608 | bytes 19210240 | tf_op jit(solution)/shard_map/pallas_call | solution.py:137
  (7 shorter events, 0.1 us)
Async XLA Ops:
  0.0 13.5 %copy-start.2 = (f32[256]{0:T(256)S(1)}, f32[256]{0:T(256)}, u32[]{:S(2)}) copy-start(f32[256]{0:T(256)} %param.4) | copy-start | bytes 3076
  0.0 14.3 %copy-start.1 = (f32[256]{0:T(256)S(1)}, f32[256]{0:T(256)}, u32[]{:S(2)}) copy-start(f32[256]{0:T(256)} %param.5) | copy-start | bytes 3076
  6.2 35.0 %all-to-all-start = ((bf16[4,2,128,1024]{2,1,0,3:T(2,128)(2,1)}), bf16[4,2,128,1024]{2,1,0,3:T(2,128)(2,1)S(1)}, u32[]{:S(2)}, u32[]{:S(2)}) async-start(bf16[4,2,128,1024]{2,1,0,3:T(2,128)(2,1)} %copy.15), calls=%async_computation | async-start | bytes 4194304 | tf_op jit(solution)/shard_map/all_to_all | solution.py:110
  43.5 14.1 %collective-permute-start.1 = (bf16[64,2,128,4]{0,3,2,1:T(4,128)(2,1)S(1)}, bf16[64,2,128,4]{0,3,2,1:T(4,128)(2,1)S(1)}, u32[]{:S(2)}, u32[]{:S(2)}) collective-permute-start(bf16[64,2,128,4]{0,3,2,1:T(4,128)(2,1)S(1)} %copy.20), channel_id=1, source_target_pairs={{1,0},{2,1},{3,2},{4,3},{5,4},{6,5},{7,6},{8,7},{9,8},{10,9},{11,1... | collective-permute-start | bytes 393224 | tf_op jit(solution)/shard_map/ppermute | solution.py:118
  49.1 10.1 %collective-permute-start = (bf16[64,2,128,4]{0,3,2,1:T(4,128)(2,1)S(1)}, bf16[64,2,128,4]{0,3,2,1:T(4,128)(2,1)S(1)}, u32[]{:S(2)}, u32[]{:S(2)}) collective-permute-start(bf16[64,2,128,4]{0,3,2,1:T(4,128)(2,1)S(1)} %copy.18), channel_id=1, source_target_pairs={{0,1},{1,2},{2,3},{3,4},{4,5},{5,6},{6,7},{7,8},{8,9},{9,10},{10,1... | collective-permute-start | bytes 393224 | tf_op jit(solution)/shard_map/ppermute | solution.py:117
  57.6 13.6 %copy-start = (bf16[2,128,64,64]{3,2,1,0:T(8,128)(2,1)S(1)}, bf16[2,128,64,64]{3,2,1,0:T(8,128)(2,1)}, u32[]{:S(2)}) copy-start(bf16[2,128,64,64]{3,2,1,0:T(8,128)(2,1)} %copy.19) | copy-start | bytes 6291460
  60.2 6.2 %collective-permute-start.2 = (bf16[2,2,72,64]{3,2,1,0:T(8,128)(2,1)S(1)}, bf16[2,2,72,64]{3,2,1,0:T(8,128)(2,1)S(1)}, u32[]{:S(2)}, u32[]{:S(2)}) collective-permute-start(bf16[2,2,72,64]{3,2,1,0:T(8,128)(2,1)S(1)} %get-tuple-element.8), channel_id=1, source_target_pairs={{0,16},{16,32},{32,48},{48,64},{64,80},{80,96},{96,112},{1,17},{17... | collective-permute-start | bytes 110600 | tf_op jit(solution)/shard_map/ppermute | solution.py:35
  64.0 7.1 %collective-permute-start.3 = (bf16[2,2,72,64]{3,2,1,0:T(8,128)(2,1)S(1)}, bf16[2,2,72,64]{3,2,1,0:T(8,128)(2,1)S(1)}, u32[]{:S(2)}, u32[]{:S(2)}) collective-permute-start(bf16[2,2,72,64]{3,2,1,0:T(8,128)(2,1)S(1)} %get-tuple-element.9), channel_id=1, source_target_pairs={{16,0},{32,16},{48,32},{64,48},{80,64},{96,80},{112,96},{17,1},{33... | collective-permute-start | bytes 110600 | tf_op jit(solution)/shard_map/ppermute | solution.py:37

commit v22 on v19

--- a/solution.py
+++ b/solution.py
@@ -12,7 +12,7 @@
 ITERS = 3
 RH = 2
 CH = 4
-TR = 64
+TR = 32
 
 
 def kernel_parts(rates, smoothing):

time: 116 us -> 117 us (level)
  Pallas kernels: 38.9 us -> 40.3 us
    pallas_call x1, Pallas kernels: 38.9 us -> 40.3 us  [per_device(): pl.pallas_call(functools.partial(fit_kernel, wp), out_shape=jax.ShapeDtyp...]
where the time goes in v22:
time: 117 us
  Pallas kernels  40.3 us (34%)
  waiting for transfers between devices  33.6 us (29%)
  starting transfers between devices  20.7 us (18%)
  local copies, waits for them, and re-layouts  15.1 us (13%)
  other arithmetic  6.25 us (5%)
    pallas_call x1, Pallas kernels, per_device(): pl.pallas_call(functools.partial(fit_kernel, wp), out_shape=jax.ShapeDtyp...  40.3 us
    all_to_all x1, waiting for transfers between devices, per_device(): x = lax.all_to_all(images, 'gy', split_axis=3, concat_axis=0, tiled=True)  26.8 us
    all_to_all x1, starting transfers between devices, per_device(): x = lax.all_to_all(images, 'gy', split_axis=3, concat_axis=0, tiled=True)  7.35 us
    transpose x1, local copies, waits for them, and re-layouts, per_device(): jnp.transpose(x, (1, 2, 3, 0))  6.41 us
    unnamed x7, local copies, waits for them, and re-layouts  6.19 us
    ppermute x1, starting transfers between devices, per_device(): right = lax.ppermute(head, 'gy', [(i + 1, i) for i in range(ny - 1)])  5.62 us
    concatenate x1, other arithmetic, halo(): jnp.concatenate([lax.ppermute(tail, axis, [(i, i + 1) for i in range(coun...  5.07 us
    ppermute x1, waiting for transfers between devices, halo(): lax.ppermute(head, axis, [(i + 1, i) for i in range(count - 1)])  4.75 us
  transfers between devices with their start and end apart: 5, of which 4 were waited for; matrix products, arithmetic and copies ran while one was open for 6% of the time, Pallas kernels for 0%

profile of v22, /device:TPU:42, one launch (start us, length us, event | category | flops | bytes accessed | tf_op | source)
XLA Modules:
  0.0 116.6 jit_solution(15072103287337394790)
XLA Ops:
  0.0 0.0 copy-start.2
  0.0 0.0 copy-start.1
  0.0 6.2 %copy.15 = bf16[4,2,128,1024]{2,1,0,3:T(2,128)(2,1)} copy(bf16[4,2,128,1024]{3,2,1,0:T(8,128)(2,1)} %param.3) | data formatting | bytes 4194304 | tf_op args[0]
  6.2 7.3 %all-to-all-start = ((bf16[4,2,128,1024]{2,1,0,3:T(2,128)(2,1)}), bf16[4,2,128,1024]{2,1,0,3:T(2,128)(2,1)S(1)}, u32[]{:S(2)}, u32[]{:S(2)}) async-start(bf16[4,2,128,1024]{2,1,0,3:T(2,128)(2,1)} %copy.15), calls=%async_computation | async-start | bytes 4194304 | tf_op jit(solution)/shard_map/all_to_all | solution.py:109
  13.5 0.0 copy-done.2
  13.5 0.1 multiply_reduce_fusion
  13.7 0.5 fusion.8
  14.2 0.1 copy.21
  14.3 0.0 copy-done.1
  14.4 26.8 %all-to-all-done = bf16[4,2,128,1024]{2,1,0,3:T(2,128)(2,1)S(1)} async-done(((bf16[4,2,128,1024]{2,1,0,3:T(2,128)(2,1)}), bf16[4,2,128,1024]{2,1,0,3:T(2,128)(2,1)S(1)}, u32[]{:S(2)}, u32[]{:S(2)}) %all-to-all-start) | async-done | bytes 2097184 | tf_op jit(solution)/shard_map/all_to_all | solution.py:109
  41.2 0.3 copy.16
  41.4 1.6 %copy.17 = bf16[16,4,2,128,64]{3,1,0,2,4:T(4,128)(2,1)S(1)} copy(bf16[16,4,2,128,64]{3,4,0,2,1:T(8,128)(2,1)S(1)} %bitcast.16) | data formatting | bytes 4194304 | tf_op jit(solution)/shard_map/all_to_all | solution.py:109
  43.1 0.2 copy.18
  43.3 0.2 copy.20
  43.5 5.6 %collective-permute-start.1 = (bf16[64,2,128,4]{0,3,2,1:T(4,128)(2,1)S(1)}, bf16[64,2,128,4]{0,3,2,1:T(4,128)(2,1)S(1)}, u32[]{:S(2)}, u32[]{:S(2)}) collective-permute-start(bf16[64,2,128,4]{0,3,2,1:T(4,128)(2,1)S(1)} %copy.20), channel_id=1, source_target_pairs={{1,0},{2,1},{3,2},{4,3},{5,4},{6,5},{7,6},{8,7},{9,8},{10,9},{11,1... | collective-permute-start | bytes 393224 | tf_op jit(solution)/shard_map/ppermute | solution.py:117
  49.1 1.9 %collective-permute-start = (bf16[64,2,128,4]{0,3,2,1:T(4,128)(2,1)S(1)}, bf16[64,2,128,4]{0,3,2,1:T(4,128)(2,1)S(1)}, u32[]{:S(2)}, u32[]{:S(2)}) collective-permute-start(bf16[64,2,128,4]{0,3,2,1:T(4,128)(2,1)S(1)} %copy.18), channel_id=1, source_target_pairs={{0,1},{1,2},{2,3},{3,4},{4,5},{5,6},{6,7},{7,8},{8,9},{9,10},{10,1... | collective-permute-start | bytes 393224 | tf_op jit(solution)/shard_map/ppermute | solution.py:116
  51.1 0.1 fusion.3.kb_ref
  51.2 6.4 %copy.19 = bf16[2,128,64,64]{3,2,1,0:T(8,128)(2,1)} copy(bf16[2,128,64,64]{1,3,0,2:T(8,128)(2,1)S(1)} %bitcast.15) | data formatting | bytes 4194304 | tf_op jit(solution)/shard_map/transpose | solution.py:119
  57.6 0.0 copy-start
  57.6 0.0 collective-permute-done.1
  57.6 1.6 %collective-permute-done = bf16[64,2,128,4]{0,3,2,1:T(4,128)(2,1)S(1)} collective-permute-done((bf16[64,2,128,4]{0,3,2,1:T(4,128)(2,1)S(1)}, bf16[64,2,128,4]{0,3,2,1:T(4,128)(2,1)S(1)}, u32[]{:S(2)}, u32[]{:S(2)}) %collective-permute-start) | collective-permute-done | bytes 131104 | tf_op jit(solution)/shard_map/ppermute | solution.py:116
  59.2 0.9 pad_maximum_fusion.3
  60.2 3.8 %collective-permute-start.2 = (bf16[2,2,72,64]{3,2,1,0:T(8,128)(2,1)S(1)}, bf16[2,2,72,64]{3,2,1,0:T(8,128)(2,1)S(1)}, u32[]{:S(2)}, u32[]{:S(2)}) collective-permute-start(bf16[2,2,72,64]{3,2,1,0:T(8,128)(2,1)S(1)} %get-tuple-element.8), channel_id=1, source_target_pairs={{0,16},{16,32},{32,48},{48,64},{64,80},{80,96},{96,112},{1,17},{17... | collective-permute-start | bytes 110600 | tf_op jit(solution)/shard_map/ppermute | solution.py:35
  64.0 2.0 %collective-permute-start.3 = (bf16[2,2,72,64]{3,2,1,0:T(8,128)(2,1)S(1)}, bf16[2,2,72,64]{3,2,1,0:T(8,128)(2,1)S(1)}, u32[]{:S(2)}, u32[]{:S(2)}) collective-permute-start(bf16[2,2,72,64]{3,2,1,0:T(8,128)(2,1)S(1)} %get-tuple-element.9), channel_id=1, source_target_pairs={{16,0},{32,16},{48,32},{64,48},{80,64},{96,80},{112,96},{17,1},{33... | collective-permute-start | bytes 110600 | tf_op jit(solution)/shard_map/ppermute | solution.py:37
  66.0 0.4 collective-permute-done.2
  66.4 4.7 %collective-permute-done.3 = bf16[2,2,72,64]{3,2,1,0:T(8,128)(2,1)S(1)} collective-permute-done((bf16[2,2,72,64]{3,2,1,0:T(8,128)(2,1)S(1)}, bf16[2,2,72,64]{3,2,1,0:T(8,128)(2,1)S(1)}, u32[]{:S(2)}, u32[]{:S(2)}) %collective-permute-start.3) | collective-permute-done | bytes 36896 | tf_op jit(solution)/shard_map/ppermute | solution.py:37
  71.2 0.0 copy-done
  71.2 5.1 %pad_maximum_fusion.x_ref = bf16[2,132,72,64]{3,2,1,0:T(8,128)(2,1)S(1)} fusion(bf16[2,2,72,64]{3,2,1,0:T(8,128)(2,1)S(1)} %collective-permute-done.3, bf16[2,128,4,64]{3,2,1,0:T(4,128)(2,1)S(1)} %bitcast.18, bf16[2,128,64,64]{3,2,1,0:T(8,128)(2,1)S(1)} %copy-done, bf16[2,128,4,64]{3,2,1,0:T(4,128)(2,1)S(1)} %bitcast.20, ...), kind=kLoop, calls=%fused_computation | loop fusion | flops 12165120 | bytes 4866048 | tf_op jit(solution)/shard_map/concatenate | solution.py:33
  76.2 0.1 broadcast_in_dim.22.cm_ref
  76.3 40.3 %shard_map.37 = f32[2,128,64,256]{3,2,1,0:T(8,128)} custom-call(bf16[2,132,72,64]{3,2,1,0:T(8,128)(2,1)S(1)} %pad_maximum_fusion.x_ref, bf16[64,256]{1,0:T(8,128)(2,1)S(1)} %fusion.3.kb_ref, bf16[256,256]{1,0:T(8,128)(2,1)S(1)} %multiply_convert_fusion.g3_ref, f32[1,256]{1,0:T(1,128)S(1)} %bitcast.11, f32[1,256]{1,0:T(1,128)S(1)} %bitcast.12, ...), custom_call_target="tpu_custom_call" | custom-call | flops 6115295232 | bytes 19210240 | tf_op jit(solution)/shard_map/pallas_call | solution.py:136
  (7 shorter events, 0.1 us)
Async XLA Ops:
  0.0 13.5 %copy-start.2 = (f32[256]{0:T(256)S(1)}, f32[256]{0:T(256)}, u32[]{:S(2)}) copy-start(f32[256]{0:T(256)} %param.4) | copy-start | bytes 3076
  0.0 14.3 %copy-start.1 = (f32[256]{0:T(256)S(1)}, f32[256]{0:T(256)}, u32[]{:S(2)}) copy-start(f32[256]{0:T(256)} %param.5) | copy-start | bytes 3076
  6.2 35.0 %all-to-all-start = ((bf16[4,2,128,1024]{2,1,0,3:T(2,128)(2,1)}), bf16[4,2,128,1024]{2,1,0,3:T(2,128)(2,1)S(1)}, u32[]{:S(2)}, u32[]{:S(2)}) async-start(bf16[4,2,128,1024]{2,1,0,3:T(2,128)(2,1)} %copy.15), calls=%async_computation | async-start | bytes 4194304 | tf_op jit(solution)/shard_map/all_to_all | solution.py:109
  43.5 14.1 %collective-permute-start.1 = (bf16[64,2,128,4]{0,3,2,1:T(4,128)(2,1)S(1)}, bf16[64,2,128,4]{0,3,2,1:T(4,128)(2,1)S(1)}, u32[]{:S(2)}, u32[]{:S(2)}) collective-permute-start(bf16[64,2,128,4]{0,3,2,1:T(4,128)(2,1)S(1)} %copy.20), channel_id=1, source_target_pairs={{1,0},{2,1},{3,2},{4,3},{5,4},{6,5},{7,6},{8,7},{9,8},{10,9},{11,1... | collective-permute-start | bytes 393224 | tf_op jit(solution)/shard_map/ppermute | solution.py:117
  49.1 10.1 %collective-permute-start = (bf16[64,2,128,4]{0,3,2,1:T(4,128)(2,1)S(1)}, bf16[64,2,128,4]{0,3,2,1:T(4,128)(2,1)S(1)}, u32[]{:S(2)}, u32[]{:S(2)}) collective-permute-start(bf16[64,2,128,4]{0,3,2,1:T(4,128)(2,1)S(1)} %copy.18), channel_id=1, source_target_pairs={{0,1},{1,2},{2,3},{3,4},{4,5},{5,6},{6,7},{7,8},{8,9},{9,10},{10,1... | collective-permute-start | bytes 393224 | tf_op jit(solution)/shard_map/ppermute | solution.py:116
  57.6 13.6 %copy-start = (bf16[2,128,64,64]{3,2,1,0:T(8,128)(2,1)S(1)}, bf16[2,128,64,64]{3,2,1,0:T(8,128)(2,1)}, u32[]{:S(2)}) copy-start(bf16[2,128,64,64]{3,2,1,0:T(8,128)(2,1)} %copy.19) | copy-start | bytes 6291460
  60.2 6.2 %collective-permute-start.2 = (bf16[2,2,72,64]{3,2,1,0:T(8,128)(2,1)S(1)}, bf16[2,2,72,64]{3,2,1,0:T(8,128)(2,1)S(1)}, u32[]{:S(2)}, u32[]{:S(2)}) collective-permute-start(bf16[2,2,72,64]{3,2,1,0:T(8,128)(2,1)S(1)} %get-tuple-element.8), channel_id=1, source_target_pairs={{0,16},{16,32},{32,48},{48,64},{64,80},{80,96},{96,112},{1,17},{17... | collective-permute-start | bytes 110600 | tf_op jit(solution)/shard_map/ppermute | solution.py:35
  64.0 7.1 %collective-permute-start.3 = (bf16[2,2,72,64]{3,2,1,0:T(8,128)(2,1)S(1)}, bf16[2,2,72,64]{3,2,1,0:T(8,128)(2,1)S(1)}, u32[]{:S(2)}, u32[]{:S(2)}) collective-permute-start(bf16[2,2,72,64]{3,2,1,0:T(8,128)(2,1)S(1)} %get-tuple-element.9), channel_id=1, source_target_pairs={{16,0},{32,16},{48,32},{64,48},{80,64},{96,80},{112,96},{17,1},{33... | collective-permute-start | bytes 110600 | tf_op jit(solution)/shard_map/ppermute | solution.py:37

commit v23 on v19

--- a/solution.py
+++ b/solution.py
@@ -52,13 +52,24 @@
     cm = cm_ref[...]
 
     xt = x_ref[0, pl.ds(t * TR, rows)].astype(jnp.float32).reshape(n, x_ref.shape[3])
-    sb = jnp.dot(xt.astype(jnp.bfloat16), kb_ref[...],
-                 preferred_element_type=jnp.float32) * step
-    b_ref[...] = sb
-    f0 = jnp.maximum(sb, 0.0)
-    f0_ref[...] = f0
+    b_ref[...] = jnp.dot(xt.astype(jnp.bfloat16), kb_ref[...],
+                         preferred_element_type=jnp.float32)
     inner = (rows - 2) * wp
-    f3_ref[pl.ds(2 * wp, inner), :] = f0[wp:(rows - 1) * wp].astype(jnp.bfloat16)
+    for q in (0, rows - 1):
+        sb = b_ref[pl.ds(q * wp, wp), :] * step
+        b_ref[pl.ds(q * wp, wp), :] = sb
+        f0_ref[pl.ds(q * wp, wp), :] = jnp.maximum(sb, 0.0)
+
+    def body0(k, carry):
+        o = pl.multiple_of((2 * k + 1) * wp, 8)
+        sb = b_ref[pl.ds(o, 2 * wp), :] * step
+        b_ref[pl.ds(o, 2 * wp), :] = sb
+        f0 = jnp.maximum(sb, 0.0)
+        f0_ref[pl.ds(o, 2 * wp), :] = f0
+        f3_ref[pl.ds(pl.multiple_of(o + wp, 16), 2 * wp), :] = f0.astype(jnp.bfloat16)
+        return carry
+
+    lax.fori_loop(0, (rows - 2) // 2, body0, 0)
 
     def update(src_ref, q):
         o = pl.multiple_of(q * wp, 8)

time: 116 us -> 120 us (1.034)
  the two profiles are of different devices: /device:TPU:42 before, /device:TPU:40 now
where the time goes in v23:
time: 120 us
  Pallas kernels  43.6 us (36%)
  waiting for transfers between devices  33.6 us (28%)
  starting transfers between devices  20.7 us (17%)
  local copies, waits for them, and re-layouts  15.1 us (13%)
  other arithmetic  6.25 us (5%)
    pallas_call x1, Pallas kernels, per_device(): pl.pallas_call(functools.partial(fit_kernel, wp), out_shape=jax.ShapeDtyp...  43.6 us
    all_to_all x1, waiting for transfers between devices, per_device(): x = lax.all_to_all(images, 'gy', split_axis=3, concat_axis=0, tiled=True)  26.8 us
    all_to_all x1, starting transfers between devices, per_device(): x = lax.all_to_all(images, 'gy', split_axis=3, concat_axis=0, tiled=True)  7.35 us
    transpose x1, local copies, waits for them, and re-layouts, per_device(): jnp.transpose(x, (1, 2, 3, 0))  6.41 us
    unnamed x7, local copies, waits for them, and re-layouts  6.19 us
    ppermute x1, starting transfers between devices, per_device(): right = lax.ppermute(head, 'gy', [(i + 1, i) for i in range(ny - 1)])  5.62 us
    concatenate x1, other arithmetic, halo(): jnp.concatenate([lax.ppermute(tail, axis, [(i, i + 1) for i in range(coun...  5.07 us
    ppermute x1, waiting for transfers between devices, halo(): lax.ppermute(head, axis, [(i + 1, i) for i in range(count - 1)])  4.75 us
  transfers between devices with their start and end apart: 5, of which 4 were waited for; matrix products, arithmetic and copies ran while one was open for 6% of the time, Pallas kernels for 0%

profile of v23, /device:TPU:40, one launch (start us, length us, event | category | flops | bytes accessed | tf_op | source)
XLA Modules:
  0.0 119.9 jit_solution(17966645700694576044)
XLA Ops:
  0.0 0.0 copy-start.2
  0.0 0.0 copy-start.1
  0.0 6.2 %copy.15 = bf16[4,2,128,1024]{2,1,0,3:T(2,128)(2,1)} copy(bf16[4,2,128,1024]{3,2,1,0:T(8,128)(2,1)} %param.3) | data formatting | bytes 4194304 | tf_op args[0]
  6.2 7.3 %all-to-all-start = ((bf16[4,2,128,1024]{2,1,0,3:T(2,128)(2,1)}), bf16[4,2,128,1024]{2,1,0,3:T(2,128)(2,1)S(1)}, u32[]{:S(2)}, u32[]{:S(2)}) async-start(bf16[4,2,128,1024]{2,1,0,3:T(2,128)(2,1)} %copy.15), calls=%async_computation | async-start | bytes 4194304 | tf_op jit(solution)/shard_map/all_to_all | solution.py:120
  13.5 0.0 copy-done.2
  13.5 0.1 multiply_reduce_fusion
  13.7 0.5 fusion.8
  14.2 0.1 copy.21
  14.3 0.0 copy-done.1
  14.4 26.8 %all-to-all-done = bf16[4,2,128,1024]{2,1,0,3:T(2,128)(2,1)S(1)} async-done(((bf16[4,2,128,1024]{2,1,0,3:T(2,128)(2,1)}), bf16[4,2,128,1024]{2,1,0,3:T(2,128)(2,1)S(1)}, u32[]{:S(2)}, u32[]{:S(2)}) %all-to-all-start) | async-done | bytes 2097184 | tf_op jit(solution)/shard_map/all_to_all | solution.py:120
  41.2 0.3 copy.16
  41.4 1.6 %copy.17 = bf16[16,4,2,128,64]{3,1,0,2,4:T(4,128)(2,1)S(1)} copy(bf16[16,4,2,128,64]{3,4,0,2,1:T(8,128)(2,1)S(1)} %bitcast.16) | data formatting | bytes 4194304 | tf_op jit(solution)/shard_map/all_to_all | solution.py:120
  43.1 0.2 copy.18
  43.3 0.2 copy.20
  43.5 5.6 %collective-permute-start.1 = (bf16[64,2,128,4]{0,3,2,1:T(4,128)(2,1)S(1)}, bf16[64,2,128,4]{0,3,2,1:T(4,128)(2,1)S(1)}, u32[]{:S(2)}, u32[]{:S(2)}) collective-permute-start(bf16[64,2,128,4]{0,3,2,1:T(4,128)(2,1)S(1)} %copy.20), channel_id=1, source_target_pairs={{1,0},{2,1},{3,2},{4,3},{5,4},{6,5},{7,6},{8,7},{9,8},{10,9},{11,1... | collective-permute-start | bytes 393224 | tf_op jit(solution)/shard_map/ppermute | solution.py:128
  49.1 1.9 %collective-permute-start = (bf16[64,2,128,4]{0,3,2,1:T(4,128)(2,1)S(1)}, bf16[64,2,128,4]{0,3,2,1:T(4,128)(2,1)S(1)}, u32[]{:S(2)}, u32[]{:S(2)}) collective-permute-start(bf16[64,2,128,4]{0,3,2,1:T(4,128)(2,1)S(1)} %copy.18), channel_id=1, source_target_pairs={{0,1},{1,2},{2,3},{3,4},{4,5},{5,6},{6,7},{7,8},{8,9},{9,10},{10,1... | collective-permute-start | bytes 393224 | tf_op jit(solution)/shard_map/ppermute | solution.py:127
  51.1 0.1 fusion.3.kb_ref
  51.2 6.4 %copy.19 = bf16[2,128,64,64]{3,2,1,0:T(8,128)(2,1)} copy(bf16[2,128,64,64]{1,3,0,2:T(8,128)(2,1)S(1)} %bitcast.15) | data formatting | bytes 4194304 | tf_op jit(solution)/shard_map/transpose | solution.py:130
  57.6 0.0 copy-start
  57.6 0.0 collective-permute-done.1
  57.6 1.6 %collective-permute-done = bf16[64,2,128,4]{0,3,2,1:T(4,128)(2,1)S(1)} collective-permute-done((bf16[64,2,128,4]{0,3,2,1:T(4,128)(2,1)S(1)}, bf16[64,2,128,4]{0,3,2,1:T(4,128)(2,1)S(1)}, u32[]{:S(2)}, u32[]{:S(2)}) %collective-permute-start) | collective-permute-done | bytes 131104 | tf_op jit(solution)/shard_map/ppermute | solution.py:127
  59.2 0.9 pad_maximum_fusion.3
  60.2 3.8 %collective-permute-start.2 = (bf16[2,2,72,64]{3,2,1,0:T(8,128)(2,1)S(1)}, bf16[2,2,72,64]{3,2,1,0:T(8,128)(2,1)S(1)}, u32[]{:S(2)}, u32[]{:S(2)}) collective-permute-start(bf16[2,2,72,64]{3,2,1,0:T(8,128)(2,1)S(1)} %get-tuple-element.8), channel_id=1, source_target_pairs={{0,16},{16,32},{32,48},{48,64},{64,80},{80,96},{96,112},{1,17},{17... | collective-permute-start | bytes 110600 | tf_op jit(solution)/shard_map/ppermute | solution.py:35
  64.0 2.0 %collective-permute-start.3 = (bf16[2,2,72,64]{3,2,1,0:T(8,128)(2,1)S(1)}, bf16[2,2,72,64]{3,2,1,0:T(8,128)(2,1)S(1)}, u32[]{:S(2)}, u32[]{:S(2)}) collective-permute-start(bf16[2,2,72,64]{3,2,1,0:T(8,128)(2,1)S(1)} %get-tuple-element.9), channel_id=1, source_target_pairs={{16,0},{32,16},{48,32},{64,48},{80,64},{96,80},{112,96},{17,1},{33... | collective-permute-start | bytes 110600 | tf_op jit(solution)/shard_map/ppermute | solution.py:37
  66.0 0.4 collective-permute-done.2
  66.4 4.7 %collective-permute-done.3 = bf16[2,2,72,64]{3,2,1,0:T(8,128)(2,1)S(1)} collective-permute-done((bf16[2,2,72,64]{3,2,1,0:T(8,128)(2,1)S(1)}, bf16[2,2,72,64]{3,2,1,0:T(8,128)(2,1)S(1)}, u32[]{:S(2)}, u32[]{:S(2)}) %collective-permute-start.3) | collective-permute-done | bytes 36896 | tf_op jit(solution)/shard_map/ppermute | solution.py:37
  71.2 0.0 copy-done
  71.2 5.1 %pad_maximum_fusion.x_ref = bf16[2,132,72,64]{3,2,1,0:T(8,128)(2,1)S(1)} fusion(bf16[2,2,72,64]{3,2,1,0:T(8,128)(2,1)S(1)} %collective-permute-done.3, bf16[2,128,4,64]{3,2,1,0:T(4,128)(2,1)S(1)} %bitcast.18, bf16[2,128,64,64]{3,2,1,0:T(8,128)(2,1)S(1)} %copy-done, bf16[2,128,4,64]{3,2,1,0:T(4,128)(2,1)S(1)} %bitcast.20, ...), kind=kLoop, calls=%fused_computation | loop fusion | flops 12165120 | bytes 4866048 | tf_op jit(solution)/shard_map/concatenate | solution.py:33
  76.2 0.1 broadcast_in_dim.22.cm_ref
  76.3 43.6 %shard_map.37 = f32[2,128,64,256]{3,2,1,0:T(8,128)} custom-call(bf16[2,132,72,64]{3,2,1,0:T(8,128)(2,1)S(1)} %pad_maximum_fusion.x_ref, bf16[64,256]{1,0:T(8,128)(2,1)S(1)} %fusion.3.kb_ref, bf16[256,256]{1,0:T(8,128)(2,1)S(1)} %multiply_convert_fusion.g3_ref, f32[1,256]{1,0:T(1,128)S(1)} %bitcast.11, f32[1,256]{1,0:T(1,128)S(1)} %bitcast.12, ...), custom_call_target="tpu_custom_call" | custom-call | flops 5775556608 | bytes 19210240 | tf_op jit(solution)/shard_map/pallas_call | solution.py:147
  (7 shorter events, 0.1 us)
Async XLA Ops:
  0.0 13.5 %copy-start.2 = (f32[256]{0:T(256)S(1)}, f32[256]{0:T(256)}, u32[]{:S(2)}) copy-start(f32[256]{0:T(256)} %param.4) | copy-start | bytes 3076
  0.0 14.3 %copy-start.1 = (f32[256]{0:T(256)S(1)}, f32[256]{0:T(256)}, u32[]{:S(2)}) copy-start(f32[256]{0:T(256)} %param.5) | copy-start | bytes 3076
  6.2 35.0 %all-to-all-start = ((bf16[4,2,128,1024]{2,1,0,3:T(2,128)(2,1)}), bf16[4,2,128,1024]{2,1,0,3:T(2,128)(2,1)S(1)}, u32[]{:S(2)}, u32[]{:S(2)}) async-start(bf16[4,2,128,1024]{2,1,0,3:T(2,128)(2,1)} %copy.15), calls=%async_computation | async-start | bytes 4194304 | tf_op jit(solution)/shard_map/all_to_all | solution.py:120
  43.5 14.1 %collective-permute-start.1 = (bf16[64,2,128,4]{0,3,2,1:T(4,128)(2,1)S(1)}, bf16[64,2,128,4]{0,3,2,1:T(4,128)(2,1)S(1)}, u32[]{:S(2)}, u32[]{:S(2)}) collective-permute-start(bf16[64,2,128,4]{0,3,2,1:T(4,128)(2,1)S(1)} %copy.20), channel_id=1, source_target_pairs={{1,0},{2,1},{3,2},{4,3},{5,4},{6,5},{7,6},{8,7},{9,8},{10,9},{11,1... | collective-permute-start | bytes 393224 | tf_op jit(solution)/shard_map/ppermute | solution.py:128
  49.1 10.1 %collective-permute-start = (bf16[64,2,128,4]{0,3,2,1:T(4,128)(2,1)S(1)}, bf16[64,2,128,4]{0,3,2,1:T(4,128)(2,1)S(1)}, u32[]{:S(2)}, u32[]{:S(2)}) collective-permute-start(bf16[64,2,128,4]{0,3,2,1:T(4,128)(2,1)S(1)} %copy.18), channel_id=1, source_target_pairs={{0,1},{1,2},{2,3},{3,4},{4,5},{5,6},{6,7},{7,8},{8,9},{9,10},{10,1... | collective-permute-start | bytes 393224 | tf_op jit(solution)/shard_map/ppermute | solution.py:127
  57.6 13.6 %copy-start = (bf16[2,128,64,64]{3,2,1,0:T(8,128)(2,1)S(1)}, bf16[2,128,64,64]{3,2,1,0:T(8,128)(2,1)}, u32[]{:S(2)}) copy-start(bf16[2,128,64,64]{3,2,1,0:T(8,128)(2,1)} %copy.19) | copy-start | bytes 6291460
  60.2 6.2 %collective-permute-start.2 = (bf16[2,2,72,64]{3,2,1,0:T(8,128)(2,1)S(1)}, bf16[2,2,72,64]{3,2,1,0:T(8,128)(2,1)S(1)}, u32[]{:S(2)}, u32[]{:S(2)}) collective-permute-start(bf16[2,2,72,64]{3,2,1,0:T(8,128)(2,1)S(1)} %get-tuple-element.8), channel_id=1, source_target_pairs={{0,16},{16,32},{32,48},{48,64},{64,80},{80,96},{96,112},{1,17},{17... | collective-permute-start | bytes 110600 | tf_op jit(solution)/shard_map/ppermute | solution.py:35
  64.0 7.1 %collective-permute-start.3 = (bf16[2,2,72,64]{3,2,1,0:T(8,128)(2,1)S(1)}, bf16[2,2,72,64]{3,2,1,0:T(8,128)(2,1)S(1)}, u32[]{:S(2)}, u32[]{:S(2)}) collective-permute-start(bf16[2,2,72,64]{3,2,1,0:T(8,128)(2,1)S(1)} %get-tuple-element.9), channel_id=1, source_target_pairs={{16,0},{32,16},{48,32},{64,48},{80,64},{96,80},{112,96},{17,1},{33... | collective-permute-start | bytes 110600 | tf_op jit(solution)/shard_map/ppermute | solution.py:37

commit v24 on v19

--- a/solution.py
+++ b/solution.py
@@ -79,7 +79,7 @@
         f1_ref[pl.ds(pl.multiple_of(q * wp, 8), wp), :] = f1
         return carry
 
-    lax.fori_loop(1, rows - 1, body1, 0, unroll=2)
+    lax.fori_loop(1, rows - 1, body1, 0)
     for q in (1, rows - 2):
         f1_ref[pl.ds(q * wp, wp), :] = f1_ref[pl.ds(q * wp, wp), :] * rm_ref[t * TR + q]
 

time: 116 us -> 116 us (level)
  no operation moved by 1% of the time
where the time goes in v24:
time: 116 us
  Pallas kernels  39.3 us (34%)
  waiting for transfers between devices  33.6 us (29%)
  starting transfers between devices  20.7 us (18%)
  local copies, waits for them, and re-layouts  15.1 us (13%)
  other arithmetic  6.25 us (5%)
    pallas_call x1, Pallas kernels, per_device(): pl.pallas_call(functools.partial(fit_kernel, wp), out_shape=jax.ShapeDtyp...  39.3 us
    all_to_all x1, waiting for transfers between devices, per_device(): x = lax.all_to_all(images, 'gy', split_axis=3, concat_axis=0, tiled=True)  26.8 us
    all_to_all x1, starting transfers between devices, per_device(): x = lax.all_to_all(images, 'gy', split_axis=3, concat_axis=0, tiled=True)  7.35 us
    transpose x1, local copies, waits for them, and re-layouts, per_device(): jnp.transpose(x, (1, 2, 3, 0))  6.41 us
    unnamed x7, local copies, waits for them, and re-layouts  6.19 us
    ppermute x1, starting transfers between devices, per_device(): right = lax.ppermute(head, 'gy', [(i + 1, i) for i in range(ny - 1)])  5.62 us
    concatenate x1, other arithmetic, halo(): jnp.concatenate([lax.ppermute(tail, axis, [(i, i + 1) for i in range(coun...  5.07 us
    ppermute x1, waiting for transfers between devices, halo(): lax.ppermute(head, axis, [(i + 1, i) for i in range(count - 1)])  4.75 us
  transfers between devices with their start and end apart: 5, of which 4 were waited for; matrix products, arithmetic and copies ran while one was open for 6% of the time, Pallas kernels for 0%

profile of v24, /device:TPU:42, one launch (start us, length us, event | category | flops | bytes accessed | tf_op | source)
XLA Modules:
  0.0 115.6 jit_solution(12343256156672965555)
XLA Ops:
  0.0 0.0 copy-start.2
  0.0 0.0 copy-start.1
  0.0 6.2 %copy.15 = bf16[4,2,128,1024]{2,1,0,3:T(2,128)(2,1)} copy(bf16[4,2,128,1024]{3,2,1,0:T(8,128)(2,1)} %param.3) | data formatting | bytes 4194304 | tf_op args[0]
  6.2 7.3 %all-to-all-start = ((bf16[4,2,128,1024]{2,1,0,3:T(2,128)(2,1)}), bf16[4,2,128,1024]{2,1,0,3:T(2,128)(2,1)S(1)}, u32[]{:S(2)}, u32[]{:S(2)}) async-start(bf16[4,2,128,1024]{2,1,0,3:T(2,128)(2,1)} %copy.15), calls=%async_computation | async-start | bytes 4194304 | tf_op jit(solution)/shard_map/all_to_all | solution.py:109
  13.5 0.0 copy-done.2
  13.5 0.1 multiply_reduce_fusion
  13.7 0.5 fusion.8
  14.2 0.1 copy.21
  14.3 0.0 copy-done.1
  14.4 26.8 %all-to-all-done = bf16[4,2,128,1024]{2,1,0,3:T(2,128)(2,1)S(1)} async-done(((bf16[4,2,128,1024]{2,1,0,3:T(2,128)(2,1)}), bf16[4,2,128,1024]{2,1,0,3:T(2,128)(2,1)S(1)}, u32[]{:S(2)}, u32[]{:S(2)}) %all-to-all-start) | async-done | bytes 2097184 | tf_op jit(solution)/shard_map/all_to_all | solution.py:109
  41.2 0.3 copy.16
  41.4 1.6 %copy.17 = bf16[16,4,2,128,64]{3,1,0,2,4:T(4,128)(2,1)S(1)} copy(bf16[16,4,2,128,64]{3,4,0,2,1:T(8,128)(2,1)S(1)} %bitcast.16) | data formatting | bytes 4194304 | tf_op jit(solution)/shard_map/all_to_all | solution.py:109
  43.1 0.2 copy.18
  43.3 0.2 copy.20
  43.5 5.6 %collective-permute-start.1 = (bf16[64,2,128,4]{0,3,2,1:T(4,128)(2,1)S(1)}, bf16[64,2,128,4]{0,3,2,1:T(4,128)(2,1)S(1)}, u32[]{:S(2)}, u32[]{:S(2)}) collective-permute-start(bf16[64,2,128,4]{0,3,2,1:T(4,128)(2,1)S(1)} %copy.20), channel_id=1, source_target_pairs={{1,0},{2,1},{3,2},{4,3},{5,4},{6,5},{7,6},{8,7},{9,8},{10,9},{11,1... | collective-permute-start | bytes 393224 | tf_op jit(solution)/shard_map/ppermute | solution.py:117
  49.1 1.9 %collective-permute-start = (bf16[64,2,128,4]{0,3,2,1:T(4,128)(2,1)S(1)}, bf16[64,2,128,4]{0,3,2,1:T(4,128)(2,1)S(1)}, u32[]{:S(2)}, u32[]{:S(2)}) collective-permute-start(bf16[64,2,128,4]{0,3,2,1:T(4,128)(2,1)S(1)} %copy.18), channel_id=1, source_target_pairs={{0,1},{1,2},{2,3},{3,4},{4,5},{5,6},{6,7},{7,8},{8,9},{9,10},{10,1... | collective-permute-start | bytes 393224 | tf_op jit(solution)/shard_map/ppermute | solution.py:116
  51.1 0.1 fusion.3.kb_ref
  51.2 6.4 %copy.19 = bf16[2,128,64,64]{3,2,1,0:T(8,128)(2,1)} copy(bf16[2,128,64,64]{1,3,0,2:T(8,128)(2,1)S(1)} %bitcast.15) | data formatting | bytes 4194304 | tf_op jit(solution)/shard_map/transpose | solution.py:119
  57.6 0.0 copy-start
  57.6 0.0 collective-permute-done.1
  57.6 1.6 %collective-permute-done = bf16[64,2,128,4]{0,3,2,1:T(4,128)(2,1)S(1)} collective-permute-done((bf16[64,2,128,4]{0,3,2,1:T(4,128)(2,1)S(1)}, bf16[64,2,128,4]{0,3,2,1:T(4,128)(2,1)S(1)}, u32[]{:S(2)}, u32[]{:S(2)}) %collective-permute-start) | collective-permute-done | bytes 131104 | tf_op jit(solution)/shard_map/ppermute | solution.py:116
  59.2 0.9 pad_maximum_fusion.3
  60.2 3.8 %collective-permute-start.2 = (bf16[2,2,72,64]{3,2,1,0:T(8,128)(2,1)S(1)}, bf16[2,2,72,64]{3,2,1,0:T(8,128)(2,1)S(1)}, u32[]{:S(2)}, u32[]{:S(2)}) collective-permute-start(bf16[2,2,72,64]{3,2,1,0:T(8,128)(2,1)S(1)} %get-tuple-element.8), channel_id=1, source_target_pairs={{0,16},{16,32},{32,48},{48,64},{64,80},{80,96},{96,112},{1,17},{17... | collective-permute-start | bytes 110600 | tf_op jit(solution)/shard_map/ppermute | solution.py:35
  64.0 2.0 %collective-permute-start.3 = (bf16[2,2,72,64]{3,2,1,0:T(8,128)(2,1)S(1)}, bf16[2,2,72,64]{3,2,1,0:T(8,128)(2,1)S(1)}, u32[]{:S(2)}, u32[]{:S(2)}) collective-permute-start(bf16[2,2,72,64]{3,2,1,0:T(8,128)(2,1)S(1)} %get-tuple-element.9), channel_id=1, source_target_pairs={{16,0},{32,16},{48,32},{64,48},{80,64},{96,80},{112,96},{17,1},{33... | collective-permute-start | bytes 110600 | tf_op jit(solution)/shard_map/ppermute | solution.py:37
  66.0 0.4 collective-permute-done.2
  66.4 4.7 %collective-permute-done.3 = bf16[2,2,72,64]{3,2,1,0:T(8,128)(2,1)S(1)} collective-permute-done((bf16[2,2,72,64]{3,2,1,0:T(8,128)(2,1)S(1)}, bf16[2,2,72,64]{3,2,1,0:T(8,128)(2,1)S(1)}, u32[]{:S(2)}, u32[]{:S(2)}) %collective-permute-start.3) | collective-permute-done | bytes 36896 | tf_op jit(solution)/shard_map/ppermute | solution.py:37
  71.2 0.0 copy-done
  71.2 5.1 %pad_maximum_fusion.x_ref = bf16[2,132,72,64]{3,2,1,0:T(8,128)(2,1)S(1)} fusion(bf16[2,2,72,64]{3,2,1,0:T(8,128)(2,1)S(1)} %collective-permute-done.3, bf16[2,128,4,64]{3,2,1,0:T(4,128)(2,1)S(1)} %bitcast.18, bf16[2,128,64,64]{3,2,1,0:T(8,128)(2,1)S(1)} %copy-done, bf16[2,128,4,64]{3,2,1,0:T(4,128)(2,1)S(1)} %bitcast.20, ...), kind=kLoop, calls=%fused_computation | loop fusion | flops 12165120 | bytes 4866048 | tf_op jit(solution)/shard_map/concatenate | solution.py:33
  76.2 0.1 broadcast_in_dim.22.cm_ref
  76.3 39.3 %shard_map.37 = f32[2,128,64,256]{3,2,1,0:T(8,128)} custom-call(bf16[2,132,72,64]{3,2,1,0:T(8,128)(2,1)S(1)} %pad_maximum_fusion.x_ref, bf16[64,256]{1,0:T(8,128)(2,1)S(1)} %fusion.3.kb_ref, bf16[256,256]{1,0:T(8,128)(2,1)S(1)} %multiply_convert_fusion.g3_ref, f32[1,256]{1,0:T(1,128)S(1)} %bitcast.11, f32[1,256]{1,0:T(1,128)S(1)} %bitcast.12, ...), custom_call_target="tpu_custom_call" | custom-call | flops 5775556608 | bytes 19210240 | tf_op jit(solution)/shard_map/pallas_call | solution.py:136
  (7 shorter events, 0.1 us)
Async XLA Ops:
  0.0 13.5 %copy-start.2 = (f32[256]{0:T(256)S(1)}, f32[256]{0:T(256)}, u32[]{:S(2)}) copy-start(f32[256]{0:T(256)} %param.4) | copy-start | bytes 3076
  0.0 14.3 %copy-start.1 = (f32[256]{0:T(256)S(1)}, f32[256]{0:T(256)}, u32[]{:S(2)}) copy-start(f32[256]{0:T(256)} %param.5) | copy-start | bytes 3076
  6.2 35.0 %all-to-all-start = ((bf16[4,2,128,1024]{2,1,0,3:T(2,128)(2,1)}), bf16[4,2,128,1024]{2,1,0,3:T(2,128)(2,1)S(1)}, u32[]{:S(2)}, u32[]{:S(2)}) async-start(bf16[4,2,128,1024]{2,1,0,3:T(2,128)(2,1)} %copy.15), calls=%async_computation | async-start | bytes 4194304 | tf_op jit(solution)/shard_map/all_to_all | solution.py:109
  43.5 14.1 %collective-permute-start.1 = (bf16[64,2,128,4]{0,3,2,1:T(4,128)(2,1)S(1)}, bf16[64,2,128,4]{0,3,2,1:T(4,128)(2,1)S(1)}, u32[]{:S(2)}, u32[]{:S(2)}) collective-permute-start(bf16[64,2,128,4]{0,3,2,1:T(4,128)(2,1)S(1)} %copy.20), channel_id=1, source_target_pairs={{1,0},{2,1},{3,2},{4,3},{5,4},{6,5},{7,6},{8,7},{9,8},{10,9},{11,1... | collective-permute-start | bytes 393224 | tf_op jit(solution)/shard_map/ppermute | solution.py:117
  49.1 10.1 %collective-permute-start = (bf16[64,2,128,4]{0,3,2,1:T(4,128)(2,1)S(1)}, bf16[64,2,128,4]{0,3,2,1:T(4,128)(2,1)S(1)}, u32[]{:S(2)}, u32[]{:S(2)}) collective-permute-start(bf16[64,2,128,4]{0,3,2,1:T(4,128)(2,1)S(1)} %copy.18), channel_id=1, source_target_pairs={{0,1},{1,2},{2,3},{3,4},{4,5},{5,6},{6,7},{7,8},{8,9},{9,10},{10,1... | collective-permute-start | bytes 393224 | tf_op jit(solution)/shard_map/ppermute | solution.py:116
  57.6 13.6 %copy-start = (bf16[2,128,64,64]{3,2,1,0:T(8,128)(2,1)S(1)}, bf16[2,128,64,64]{3,2,1,0:T(8,128)(2,1)}, u32[]{:S(2)}) copy-start(bf16[2,128,64,64]{3,2,1,0:T(8,128)(2,1)} %copy.19) | copy-start | bytes 6291460
  60.2 6.2 %collective-permute-start.2 = (bf16[2,2,72,64]{3,2,1,0:T(8,128)(2,1)S(1)}, bf16[2,2,72,64]{3,2,1,0:T(8,128)(2,1)S(1)}, u32[]{:S(2)}, u32[]{:S(2)}) collective-permute-start(bf16[2,2,72,64]{3,2,1,0:T(8,128)(2,1)S(1)} %get-tuple-element.8), channel_id=1, source_target_pairs={{0,16},{16,32},{32,48},{48,64},{64,80},{80,96},{96,112},{1,17},{17... | collective-permute-start | bytes 110600 | tf_op jit(solution)/shard_map/ppermute | solution.py:35
  64.0 7.1 %collective-permute-start.3 = (bf16[2,2,72,64]{3,2,1,0:T(8,128)(2,1)S(1)}, bf16[2,2,72,64]{3,2,1,0:T(8,128)(2,1)S(1)}, u32[]{:S(2)}, u32[]{:S(2)}) collective-permute-start(bf16[2,2,72,64]{3,2,1,0:T(8,128)(2,1)S(1)} %get-tuple-element.9), channel_id=1, source_target_pairs={{16,0},{32,16},{48,32},{64,48},{80,64},{96,80},{112,96},{17,1},{33... | collective-permute-start | bytes 110600 | tf_op jit(solution)/shard_map/ppermute | solution.py:37
